TPU v7x, 512 devices: a whole 4x4x16 slice. The times are simulated.
512 devices in a mesh: shot: 16 (over z_lo, core), recv: 32 (over z_hi, y, x).
Axes of the slice: x: 4, y: 4, z: 16 (z_hi: 2, z_lo: 8; z = z_hi * 8 + z_lo), core: 2. Of those that a mesh axis runs over, the one named last changes fastest.
Arguments:
- pressure: bfloat16 [2, 6144, 6144], P(None, 'recv', 'shot'), may hold values from -6 to 6
Outputs:
- multiples: float32 [2, 6144, 6144], P(None, 'recv', 'shot')
All inputs are finite; a program needn't handle non-finite values.
Results may differ from a plain program's by a relative error of at most 0.0044.
Values may be sent and summed in bfloat16 or wider, within the bound.
No kernel may reach another device: no remote copies, remote signals or barrier semaphores. Data moves between devices by JAX's collectives and lax.ppermute only.
A program may use at most 64 MiB of HBM per device.

v0:
```python
import math

import jax
import jax.numpy as jnp
from jax import lax
from jax.sharding import PartitionSpec as P

N = 6144


def partner(value, axis, apart):
    mask = 2**apart
    pairs = [(source, source ^ mask) for source in range(lax.axis_size(axis))]
    return lax.ppermute(value, axis, pairs)


def local(pressure):
    block_rows = pressure.shape[1]
    block_cols = pressure.shape[2]
    shot_index = lax.axis_index("shot")
    recv_index = lax.axis_index("recv")
    grid_row = recv_index // 2
    pair_bit = recv_index % 2
    mirror = pressure
    levels = lax.axis_size("shot").bit_length() - 1
    for bit_index in range(levels):
        stride = 2**bit_index
        agrees = shot_index // stride % 2 == grid_row // stride % 2
        transit = partner(mirror, "shot", bit_index)
        arrived = partner(transit, "recv", bit_index + 1)
        mirror = jnp.where(agrees, mirror, arrived)
    kept_cols = lax.dynamic_slice_in_dim(mirror, pair_bit * block_rows, block_rows, 2)
    given_cols = lax.dynamic_slice_in_dim(mirror, (1 - pair_bit) * block_rows, block_rows, 2)
    taken_cols = partner(given_cols, "recv", 0)
    stacked = jnp.where(
        pair_bit == 0,
        jnp.concatenate([kept_cols, taken_cols], axis=1),
        jnp.concatenate([taken_cols, kept_cols], axis=1),
    )
    symmetric = (
        (pressure.astype(jnp.float32) + jnp.swapaxes(stacked, 1, 2).astype(jnp.float32)) * 0.5
    ).astype(jnp.bfloat16)
    factor = 1.0 / math.sqrt(N)
    row_panel = lax.all_gather(symmetric, "shot", axis=2, tiled=True)
    shard_block = lax.all_gather(symmetric, "recv", axis=1, tiled=True)
    left_real = row_panel[0]
    left_imag = row_panel[1]
    upper_half = jnp.concatenate([shard_block[0], shard_block[1]], axis=1)
    lower_half = jnp.concatenate([-shard_block[1], shard_block[0]], axis=1)
    running = jnp.dot(left_real, upper_half, preferred_element_type=jnp.float32)
    running = running + jnp.dot(left_imag, lower_half, preferred_element_type=jnp.float32)
    running = running * factor
    return jnp.stack([running[:, :block_cols], running[:, block_cols:]])


def solution(mesh):
    placed = (P(None, "recv", "shot"),)
    return jax.shard_map(
        local, mesh=mesh, in_specs=placed, out_specs=P(None, "recv", "shot"), check_vma=False
    )
```

profile of v0, /device:TPU:1, one launch (start us, length us, event | category | flops | bytes accessed | tf_op | source)
XLA Modules:
  0.0 568.4 jit_solution(5705940932931412052)
XLA Ops:
  6.5 0.0 copy-start.3
  6.5 0.0 all-gather.5.cloned.1.call-start
  6.5 1.2 copy.3
  7.7 8.8 %collective-permute-start = (bf16[2,192,384]{1,2,0:T(8,128)(2,1)S(1)}, bf16[2,192,384]{1,2,0:T(8,128)(2,1)S(1)}, u32[]{:S(2)}, u32[]{:S(2)}) collective-permute-start(bf16[2,192,384]{1,2,0:T(8,128)(2,1)S(1)} %copy.3), channel_id=1, source_target_pairs={{0,32},{32,0},{64,96},{96,64},{128,160},{160,128},{192,224},{224,1... | collective-permute-start | bytes 884744 | tf_op jit(solution)/shard_map/ppermute | solution.py:14
  16.5 1.3 collective-permute-done
  17.9 1.9 collective-permute-start.1
  19.8 11.8 %collective-permute-done.1 = bf16[2,192,384]{1,2,0:T(8,128)(2,1)S(1)} collective-permute-done((bf16[2,192,384]{1,2,0:T(8,128)(2,1)S(1)}, bf16[2,192,384]{1,2,0:T(8,128)(2,1)S(1)}, u32[]{:S(2)}, u32[]{:S(2)}) %collective-permute-start.1) | collective-permute-done | bytes 294944 | tf_op jit(solution)/shard_map/ppermute | solution.py:14
  31.6 1.9 collective-permute-start.2
  33.6 9.4 %collective-permute-done.2 = bf16[2,192,384]{1,2,0:T(8,128)(2,1)S(1)} collective-permute-done((bf16[2,192,384]{1,2,0:T(8,128)(2,1)S(1)}, bf16[2,192,384]{1,2,0:T(8,128)(2,1)S(1)}, u32[]{:S(2)}, u32[]{:S(2)}) %collective-permute-start.2) | collective-permute-done | bytes 294944 | tf_op jit(solution)/shard_map/ppermute | solution.py:14
  42.9 1.9 collective-permute-start.3
  44.9 8.4 %collective-permute-done.3 = bf16[2,192,384]{1,2,0:T(8,128)(2,1)S(1)} collective-permute-done((bf16[2,192,384]{1,2,0:T(8,128)(2,1)S(1)}, bf16[2,192,384]{1,2,0:T(8,128)(2,1)S(1)}, u32[]{:S(2)}, u32[]{:S(2)}) %collective-permute-start.3) | collective-permute-done | bytes 294944 | tf_op jit(solution)/shard_map/ppermute | solution.py:14
  53.3 1.9 collective-permute-start.4
  55.3 19.9 %collective-permute-done.4 = bf16[2,192,384]{1,2,0:T(8,128)(2,1)S(1)} collective-permute-done((bf16[2,192,384]{1,2,0:T(8,128)(2,1)S(1)}, bf16[2,192,384]{1,2,0:T(8,128)(2,1)S(1)}, u32[]{:S(2)}, u32[]{:S(2)}) %collective-permute-start.4) | collective-permute-done | bytes 294944 | tf_op jit(solution)/shard_map/ppermute | solution.py:14
  75.2 1.9 collective-permute-start.5
  77.2 11.2 %collective-permute-done.5 = bf16[2,192,384]{1,2,0:T(8,128)(2,1)S(1)} collective-permute-done((bf16[2,192,384]{1,2,0:T(8,128)(2,1)S(1)}, bf16[2,192,384]{1,2,0:T(8,128)(2,1)S(1)}, u32[]{:S(2)}, u32[]{:S(2)}) %collective-permute-start.5) | collective-permute-done | bytes 294944 | tf_op jit(solution)/shard_map/ppermute | solution.py:14
  88.4 3.6 collective-permute-start.6
  92.0 36.5 %collective-permute-done.6 = bf16[2,192,384]{1,2,0:T(8,128)(2,1)S(1)} collective-permute-done((bf16[2,192,384]{1,2,0:T(8,128)(2,1)S(1)}, bf16[2,192,384]{1,2,0:T(8,128)(2,1)S(1)}, u32[]{:S(2)}, u32[]{:S(2)}) %collective-permute-start.6) | collective-permute-done | bytes 294944 | tf_op jit(solution)/shard_map/ppermute | solution.py:14
  128.6 18.8 %collective-permute-start.7 = (bf16[2,192,384]{1,2,0:T(8,128)(2,1)S(1)}, bf16[2,192,384]{1,2,0:T(8,128)(2,1)S(1)}, u32[]{:S(2)}, u32[]{:S(2)}) collective-permute-start(bf16[2,192,384]{1,2,0:T(8,128)(2,1)S(1)} %collective-permute-done.6), channel_id=1, source_target_pairs={{0,16},{1,17},{2,18},{3,19},{4,20},{5,21},{6,22},{7,23},{8,24},{9,... | collective-permute-start | bytes 884744 | tf_op jit(solution)/shard_map/ppermute | solution.py:14
  147.5 14.8 %collective-permute-done.7 = bf16[2,192,384]{1,2,0:T(8,128)(2,1)S(1)} collective-permute-done((bf16[2,192,384]{1,2,0:T(8,128)(2,1)S(1)}, bf16[2,192,384]{1,2,0:T(8,128)(2,1)S(1)}, u32[]{:S(2)}, u32[]{:S(2)}) %collective-permute-start.7) | collective-permute-done | bytes 294944 | tf_op jit(solution)/shard_map/ppermute | solution.py:14
  162.4 3.1 collective-permute-start.8
  165.5 4.7 collective-permute-done.8
  170.2 0.0 copy-done.3
  170.2 1.0 fusion.15
  171.2 0.0 all-gather.5.cloned.1.call-update
  171.2 0.0 all-gather.3.cloned.1.call-start
  171.2 0.7 all-gather.3.cloned.1.call-update
  171.9 264.8 %all-gather.5.cloned.1.call-done = bf16[2,6144,384]{2,1,0:T(8,128)(2,1)} async-done(((bf16[2,192,384]{2,1,0:T(8,128)(2,1)}), bf16[2,6144,384]{2,1,0:T(8,128)(2,1)}) %all-gather.5.cloned.1.call-update) | async-done | bytes 9437200 | tf_op jit(solution)/shard_map/all_gather | solution.py:45
  436.7 0.0 copy-start
  436.7 5.3 fusion.18
  442.0 1.5 copy-done
  443.5 4.6 slice_bitcast_fusion.1
  448.1 102.0 %all-gather.3.cloned.1.call-done = bf16[2,192,6144]{2,1,0:T(8,128)(2,1)} async-done(((bf16[2,192,384]{2,1,0:T(8,128)(2,1)}), bf16[2,192,6144]{2,1,0:T(8,128)(2,1)}) %all-gather.3.cloned.1.call-update) | async-done | bytes 4718608 | tf_op jit(solution)/shard_map/all_gather | solution.py:44
  550.2 0.0 copy-start.1
  550.2 0.0 copy-start.2
  550.2 0.0 copy-start.4
  550.2 6.5 %fusion = f32[192,768]{1,0:T(8,128)S(1)} fusion(bf16[6144,384]{1,0:T(8,128)(2,1)} %get-tuple-element.6, bf16[6144,384]{1,0:T(8,128)(2,1)} %get-tuple-element.5, bf16[2,192,6144]{2,1,0:T(8,128)(2,1)} %all-gather.3.cloned.1.call-done), kind=kOutput, calls=%fused_computation | convolution fusion | flops 1830813696 | bytes 12386304 | tf_op jit(solution)/shard_map/dot_general | solution.py:50
  556.7 0.0 copy-done.1
  556.7 0.6 copy-done.2
  557.3 1.3 copy-done.4
  558.7 2.0 fusion.11
  560.7 0.9 pad_maximum_fusion
  (6 shorter events, 0.2 us)
Async XLA Ops:
  6.5 163.6 %copy-start.3 = (bf16[2,192,384]{2,1,0:T(8,128)(2,1)S(1)}, bf16[2,192,384]{2,1,0:T(8,128)(2,1)}, u32[]{:S(2)}) copy-start(bf16[2,192,384]{2,1,0:T(8,128)(2,1)} %param.1) | copy-start | bytes 884740
  6.5 430.2 %all-gather.5.cloned.1.call-start = ((), (), s32[]{:S(2)}) async-start(), calls=%async_computation.1 | async-start | bytes 9732096 | tf_op jit(solution)/shard_map/all_gather | solution.py:45
  7.7 10.1 %collective-permute-start = (bf16[2,192,384]{1,2,0:T(8,128)(2,1)S(1)}, bf16[2,192,384]{1,2,0:T(8,128)(2,1)S(1)}, u32[]{:S(2)}, u32[]{:S(2)}) collective-permute-start(bf16[2,192,384]{1,2,0:T(8,128)(2,1)S(1)} %copy.3), channel_id=1, source_target_pairs={{0,32},{32,0},{64,96},{96,64},{128,160},{160,128},{192,224},{224,1... | collective-permute-start | bytes 884744 | tf_op jit(solution)/shard_map/ppermute | solution.py:14
  17.9 13.7 %collective-permute-start.1 = (bf16[2,192,384]{1,2,0:T(8,128)(2,1)S(1)}, bf16[2,192,384]{1,2,0:T(8,128)(2,1)S(1)}, u32[]{:S(2)}, u32[]{:S(2)}) collective-permute-start(bf16[2,192,384]{1,2,0:T(8,128)(2,1)S(1)} %collective-permute-done), channel_id=1, source_target_pairs={{0,2},{1,3},{2,0},{3,1},{4,6},{5,7},{6,4},{7,5},{8,10},{9,11},{10,... | collective-permute-start | bytes 884744 | tf_op jit(solution)/shard_map/ppermute | solution.py:14
  31.6 11.3 %collective-permute-start.2 = (bf16[2,192,384]{1,2,0:T(8,128)(2,1)S(1)}, bf16[2,192,384]{1,2,0:T(8,128)(2,1)S(1)}, u32[]{:S(2)}, u32[]{:S(2)}) collective-permute-start(bf16[2,192,384]{1,2,0:T(8,128)(2,1)S(1)} %broadcast_select_fusion), channel_id=1, source_target_pairs={{0,64},{32,96},{64,0},{96,32},{128,192},{160,224},{192,128},{224,1... | collective-permute-start | bytes 884744 | tf_op jit(solution)/shard_map/ppermute | solution.py:14
  42.9 10.4 %collective-permute-start.3 = (bf16[2,192,384]{1,2,0:T(8,128)(2,1)S(1)}, bf16[2,192,384]{1,2,0:T(8,128)(2,1)S(1)}, u32[]{:S(2)}, u32[]{:S(2)}) collective-permute-start(bf16[2,192,384]{1,2,0:T(8,128)(2,1)S(1)} %collective-permute-done.2), channel_id=1, source_target_pairs={{0,4},{1,5},{2,6},{3,7},{4,0},{5,1},{6,2},{7,3},{8,12},{9,13},{10,... | collective-permute-start | bytes 884744 | tf_op jit(solution)/shard_map/ppermute | solution.py:14
  53.3 21.9 %collective-permute-start.4 = (bf16[2,192,384]{1,2,0:T(8,128)(2,1)S(1)}, bf16[2,192,384]{1,2,0:T(8,128)(2,1)S(1)}, u32[]{:S(2)}, u32[]{:S(2)}) collective-permute-start(bf16[2,192,384]{1,2,0:T(8,128)(2,1)S(1)} %broadcast_select_fusion.1), channel_id=1, source_target_pairs={{0,128},{32,160},{64,192},{96,224},{128,0},{160,32},{192,64},{224,... | collective-permute-start | bytes 884744 | tf_op jit(solution)/shard_map/ppermute | solution.py:14
  75.2 13.1 %collective-permute-start.5 = (bf16[2,192,384]{1,2,0:T(8,128)(2,1)S(1)}, bf16[2,192,384]{1,2,0:T(8,128)(2,1)S(1)}, u32[]{:S(2)}, u32[]{:S(2)}) collective-permute-start(bf16[2,192,384]{1,2,0:T(8,128)(2,1)S(1)} %collective-permute-done.4), channel_id=1, source_target_pairs={{0,8},{1,9},{2,10},{3,11},{4,12},{5,13},{6,14},{7,15},{8,0},{9,1},... | collective-permute-start | bytes 884744 | tf_op jit(solution)/shard_map/ppermute | solution.py:14
  88.4 40.2 %collective-permute-start.6 = (bf16[2,192,384]{1,2,0:T(8,128)(2,1)S(1)}, bf16[2,192,384]{1,2,0:T(8,128)(2,1)S(1)}, u32[]{:S(2)}, u32[]{:S(2)}) collective-permute-start(bf16[2,192,384]{1,2,0:T(8,128)(2,1)S(1)} %broadcast_select_fusion.2), channel_id=1, source_target_pairs={{0,256},{32,288},{64,320},{96,352},{128,384},{160,416},{192,448},{... | collective-permute-start | bytes 884744 | tf_op jit(solution)/shard_map/ppermute | solution.py:14
  128.6 33.7 %collective-permute-start.7 = (bf16[2,192,384]{1,2,0:T(8,128)(2,1)S(1)}, bf16[2,192,384]{1,2,0:T(8,128)(2,1)S(1)}, u32[]{:S(2)}, u32[]{:S(2)}) collective-permute-start(bf16[2,192,384]{1,2,0:T(8,128)(2,1)S(1)} %collective-permute-done.6), channel_id=1, source_target_pairs={{0,16},{1,17},{2,18},{3,19},{4,20},{5,21},{6,22},{7,23},{8,24},{9,... | collective-permute-start | bytes 884744 | tf_op jit(solution)/shard_map/ppermute | solution.py:14
  162.4 7.8 %collective-permute-start.8 = (bf16[2,192,192]{1,2,0:T(8,128)(2,1)S(1)}, bf16[2,192,192]{1,2,0:T(8,128)(2,1)S(1)}, u32[]{:S(2)}, u32[]{:S(2)}) collective-permute-start(bf16[2,192,192]{1,2,0:T(8,128)(2,1)S(1)} %get-tuple-element.10), channel_id=1, source_target_pairs={{0,1},{1,0},{2,3},{3,2},{4,5},{5,4},{6,7},{7,6},{8,9},{9,8},{10,11... | collective-permute-start | bytes 442376 | tf_op jit(solution)/shard_map/ppermute | solution.py:14
  171.2 379.0 %all-gather.3.cloned.1.call-start = ((), (), s32[]{:S(2)}) async-start(), calls=%async_computation | async-start | bytes 5013504 | tf_op jit(solution)/shard_map/all_gather | solution.py:44
  436.7 6.8 %copy-start = (bf16[2,6144,384]{2,1,0:T(8,128)(2,1)S(1)}, bf16[2,6144,384]{2,1,0:T(8,128)(2,1)}, u32[]{:S(2)}) copy-start(bf16[2,6144,384]{2,1,0:T(8,128)(2,1)} %all-gather.5.cloned.1.call-done) | copy-start | bytes 28311556
  550.2 6.5 %copy-start.1 = (bf16[6144,384]{1,0:T(8,128)(2,1)S(1)}, bf16[6144,384]{1,0:T(8,128)(2,1)}, u32[]{:S(2)}) copy-start(bf16[6144,384]{1,0:T(8,128)(2,1)} %fusion.18) | copy-start | bytes 14155780
  550.2 7.2 %copy-start.2 = (bf16[6144,384]{1,0:T(8,128)(2,1)S(1)}, bf16[6144,384]{1,0:T(8,128)(2,1)}, u32[]{:S(2)}) copy-start(bf16[6144,384]{1,0:T(8,128)(2,1)} %get-tuple-element.5) | copy-start | bytes 14155780
  550.2 8.5 %copy-start.4 = (bf16[2,192,6144]{2,1,0:T(8,128)(2,1)S(1)}, bf16[2,192,6144]{2,1,0:T(8,128)(2,1)}, u32[]{:S(2)}) copy-start(bf16[2,192,6144]{2,1,0:T(8,128)(2,1)} %all-gather.3.cloned.1.call-done) | copy-start | bytes 14155780
Sparse Core Ops, SparseCore 0:
  171.3 265.3 all-gather.4
  438.8 111.3 all-gather.2
where the time goes:
time: 571 us; the launch traced here: 568 us
  waiting for transfers between devices  485 us (85%)
  starting transfers between devices  44 us (8%)
  between operations  13.8 us (2%)
  local copies, waits for them, and re-layouts  9.36 us (2%)
  matrix products  8.52 us (1%)
  other arithmetic  7.32 us (1%)
    all_gather x1, waiting for transfers between devices, local(): shard_block = lax.all_gather(symmetric, 'recv', axis=1, tiled=True)  265 us
    ppermute x9, waiting for transfers between devices, partner(): return lax.ppermute(value, axis, pairs)  118 us
    all_gather x1, waiting for transfers between devices, local(): row_panel = lax.all_gather(symmetric, 'shot', axis=2, tiled=True)  102 us
    ppermute x9, starting transfers between devices, partner(): return lax.ppermute(value, axis, pairs)  43.9 us
  transfers between devices with their start and end apart: 11, of which 11 were waited for; matrix products, arithmetic and copies ran while one was open for 2% of the time, Pallas kernels for 0%

commit v1 on v0

v1 whole, which is shorter than its diff:
```python
import math

import jax
import jax.numpy as jnp
from jax import lax
from jax.sharding import Mesh
from jax.sharding import PartitionSpec as P

N = 6144


def mirror_pairs(n_recv, n_shot, flip):
    pairs = []
    for i in range(n_recv):
        for j in range(n_shot):
            h = (i % 2) ^ flip
            pairs.append((j * n_recv + i, (i // 2) * n_recv + 2 * j + h))
    return pairs


def local(pressure):
    n_shot = lax.axis_size("shot")
    n_half = lax.axis_size("yx")
    n_recv = 2 * n_half
    block_rows = pressure.shape[1]
    shot_index = lax.axis_index("shot")
    half_index = lax.axis_index("zh")
    recv_index = half_index * n_half + lax.axis_index("yx")
    parity = recv_index % 2
    axes = ("shot", "zh", "yx")

    arrived = []
    for flip in range(2):
        sent_half = (parity + flip) % 2
        piece = lax.dynamic_slice_in_dim(pressure, sent_half * block_rows, block_rows, 2)
        arrived.append(lax.ppermute(piece, axes, mirror_pairs(n_recv, n_shot, flip)))
    upper = jnp.where(parity == 0, arrived[0], arrived[1])
    lower = jnp.where(parity == 0, arrived[1], arrived[0])
    mirror = jnp.concatenate([upper, lower], axis=1)
    symmetric = (
        (pressure.astype(jnp.float32) + jnp.swapaxes(mirror, 1, 2).astype(jnp.float32)) * 0.5
    ).astype(jnp.bfloat16)

    partner_block = lax.ppermute(symmetric, "zh", [(0, 1), (1, 0)])
    top = jnp.where(half_index == 0, symmetric, partner_block)
    bottom = jnp.where(half_index == 0, partner_block, symmetric)
    stacked = jnp.stack([top, bottom], axis=1)
    col_panel = lax.all_gather(stacked, "yx", axis=2, tiled=False)
    col_panel = col_panel.reshape(2, n_recv * block_rows, stacked.shape[-1])

    row_panel = lax.all_gather(symmetric, "shot", axis=2, tiled=True)
    factor = 1.0 / math.sqrt(N)
    upper_half = jnp.concatenate([col_panel[0], col_panel[1]], axis=1)
    lower_half = jnp.concatenate([-col_panel[1], col_panel[0]], axis=1)
    running = jnp.dot(row_panel[0], upper_half, preferred_element_type=jnp.float32)
    running = running + jnp.dot(row_panel[1], lower_half, preferred_element_type=jnp.float32)
    running = running * factor
    block_cols = pressure.shape[2]
    return jnp.stack([running[:, :block_cols], running[:, block_cols:]])


def solution(mesh):
    n_shot, n_recv = mesh.devices.shape
    split = Mesh(mesh.devices.reshape(n_shot, 2, n_recv // 2), ("shot", "zh", "yx"))
    placed = (P(None, ("zh", "yx"), "shot"),)
    return jax.shard_map(
        local, mesh=split, in_specs=placed, out_specs=P(None, ("zh", "yx"), "shot"), check_vma=False
    )
```

time: 571 us -> 316 us (0.55)
  waiting for transfers between devices: 485 us -> 215 us
  starting transfers between devices: 44 us -> 57.8 us
    all_gather x1, waiting for transfers between devices: 265 us -> 103 us  [local(): col_panel = lax.all_gather(stacked, 'yx', axis=2, tiled=False)]
    ppermute x9 -> x3, waiting for transfers between devices: 118 us -> 15.5 us  [the longest x2 7.99 us: local(): lax.ppermute(piece, axes, mirror_pairs(n_recv, n_shot, flip))]
    ppermute x9 -> x3, starting transfers between devices: 43.9 us -> 57.7 us  [the longest x1 49.2 us: local(): partner_block = lax.ppermute(symmetric, 'zh', [(0, 1), (1, 0)])]
    slice x0 -> x1, local copies, waits for them, and re-layouts: none -> 6.85 us  [local(): upper_half = jnp.concatenate([col_panel[0], col_panel[1]], axis=1)]
    all_gather x1, waiting for transfers between devices: 102 us -> 95.7 us  [local(): row_panel = lax.all_gather(symmetric, 'shot', axis=2, tiled=True)]
  transfers between devices with their start and end apart: 11 -> 5, of which waited for: 11 -> 5; matrix products, arithmetic and copies ran while one was open for 2% -> 3% of each run, Pallas kernels for 0% -> 0%
where the time goes in v1:
time: 316 us; the launch traced here: 313 us
  waiting for transfers between devices  215 us (68%)
  starting transfers between devices  57.8 us (18%)
  between operations  13.5 us (4%)
  local copies, waits for them, and re-layouts  12.3 us (4%)
  matrix products  8.52 us (3%)
  other arithmetic  6.03 us (2%)
    all_gather x1, waiting for transfers between devices, local(): col_panel = lax.all_gather(stacked, 'yx', axis=2, tiled=False)  103 us
    all_gather x1, waiting for transfers between devices, local(): row_panel = lax.all_gather(symmetric, 'shot', axis=2, tiled=True)  95.7 us
    ppermute x1, starting transfers between devices, local(): partner_block = lax.ppermute(symmetric, 'zh', [(0, 1), (1, 0)])  49.2 us
    ppermute x2, starting transfers between devices, local(): lax.ppermute(piece, axes, mirror_pairs(n_recv, n_shot, flip))  8.57 us
    ppermute x2, waiting for transfers between devices, local(): lax.ppermute(piece, axes, mirror_pairs(n_recv, n_shot, flip))  7.99 us
    ppermute x1, waiting for transfers between devices, local(): partner_block = lax.ppermute(symmetric, 'zh', [(0, 1), (1, 0)])  7.54 us
    slice x1, local copies, waits for them, and re-layouts, local(): upper_half = jnp.concatenate([col_panel[0], col_panel[1]], axis=1)  6.85 us
    dot_general x1, matrix products, local(): jnp.dot(row_panel[0], upper_half, preferred_element_type=jnp.float32)  6.53 us
  transfers between devices with their start and end apart: 5, of which 5 were waited for; matrix products, arithmetic and copies ran while one was open for 3% of the time, Pallas kernels for 0%

profile of v1, /device:TPU:1, one launch (start us, length us, event | category | flops | bytes accessed | tf_op | source)
XLA Modules:
  0.0 313.4 jit_solution(18042079084204046459)
XLA Ops:
  6.5 0.0 all-gather.6.cloned.1.call-start
  6.5 1.2 constant_dynamic-slice_fusion.1
  7.7 0.1 copy.4
  7.9 6.0 %collective-permute-start = (bf16[2,192,192]{1,2,0:T(8,128)(2,1)S(1)}, bf16[2,192,192]{1,2,0:T(8,128)(2,1)S(1)}, u32[]{:S(2)}, u32[]{:S(2)}) collective-permute-start(bf16[2,192,192]{1,2,0:T(8,128)(2,1)S(1)} %copy.4), channel_id=1, source_target_pairs={{0,0},{32,2},{64,4},{96,6},{128,8},{160,10},{192,12},{224,14},{256... | collective-permute-start | bytes 442376 | tf_op jit(solution)/shard_map/ppermute | solution.py:36
  13.9 0.1 copy.5
  14.1 2.5 collective-permute-start.1
  16.6 2.9 collective-permute-done
  19.6 5.0 %collective-permute-done.1 = bf16[2,192,192]{1,2,0:T(8,128)(2,1)S(1)} collective-permute-done((bf16[2,192,192]{1,2,0:T(8,128)(2,1)S(1)}, bf16[2,192,192]{1,2,0:T(8,128)(2,1)S(1)}, u32[]{:S(2)}, u32[]{:S(2)}) %collective-permute-start.1) | collective-permute-done | bytes 147488 | tf_op jit(solution)/shard_map/ppermute | solution.py:36
  24.6 1.1 fusion.15
  25.8 0.0 copy-start.2
  25.8 49.2 %collective-permute-start.2 = (bf16[2,192,384]{2,1,0:T(8,128)(2,1)S(1)}, bf16[2,192,384]{2,1,0:T(8,128)(2,1)S(1)}, u32[]{:S(2)}, u32[]{:S(2)}) collective-permute-start(bf16[2,192,384]{2,1,0:T(8,128)(2,1)S(1)} %fusion.15), channel_id=1, source_target_pairs={{0,16},{16,0},{1,17},{17,1},{2,18},{18,2},{3,19},{19,3},{4,20},{20... | collective-permute-start | bytes 884744 | tf_op jit(solution)/shard_map/ppermute | solution.py:44
  74.9 7.5 %collective-permute-done.2 = bf16[2,192,384]{2,1,0:T(8,128)(2,1)S(1)} collective-permute-done((bf16[2,192,384]{2,1,0:T(8,128)(2,1)S(1)}, bf16[2,192,384]{2,1,0:T(8,128)(2,1)S(1)}, u32[]{:S(2)}, u32[]{:S(2)}) %collective-permute-start.2) | collective-permute-done | bytes 294944 | tf_op jit(solution)/shard_map/ppermute | solution.py:44
  82.5 0.1 select_bitcast_fusion.1
  82.5 0.9 pad_maximum_fusion
  83.4 0.0 all-gather.6.cloned.1.call-update
  83.5 0.0 all-gather.4.cloned.1.call-start
  83.5 0.0 copy-done.2
  83.5 0.7 all-gather.4.cloned.1.call-update
  84.2 103.4 %all-gather.6.cloned.1.call-done = bf16[2,2,3072,384]{3,2,0,1:T(8,128)(2,1)} async-done(((bf16[2,2,192,384]{3,2,0,1:T(8,128)(2,1)}), bf16[2,2,3072,384]{3,2,0,1:T(8,128)(2,1)}) %all-gather.6.cloned.1.call-update) | async-done | bytes 9437200 | tf_op jit(solution)/shard_map/all_gather | solution.py:48
  187.6 6.8 %fusion.18 = (bf16[1,2,3072,384]{3,2,0,1:T(8,128)(2,1)}, bf16[1,2,3072,384]{3,2,0,1:T(8,128)(2,1)S(1)}) fusion(bf16[2,2,3072,384]{3,2,0,1:T(8,128)(2,1)} %all-gather.6.cloned.1.call-done), kind=kLoop, calls=%fused_computation.28 | loop fusion | bytes 18874368 | tf_op jit(solution)/shard_map/slice | solution.py:53
  194.4 0.0 copy-start
  194.4 2.1 copy-done
  196.5 0.0 slice-start
  196.5 3.1 bitcast_negate_fusion
  199.6 95.7 %all-gather.4.cloned.1.call-done = bf16[2,192,6144]{2,1,0:T(8,128)(2,1)} async-done(((bf16[2,192,384]{2,1,0:T(8,128)(2,1)}), bf16[2,192,6144]{2,1,0:T(8,128)(2,1)}) %all-gather.4.cloned.1.call-update) | async-done | bytes 4718608 | tf_op jit(solution)/shard_map/all_gather | solution.py:51
  295.3 0.0 copy-start.1
  295.3 0.0 slice-start.1
  295.3 0.0 copy-start.3
  295.3 6.5 %fusion = f32[192,768]{1,0:T(8,128)S(1)} fusion(bf16[6144,384]{1,0:T(8,128)(2,1)} %bitcast.27, bf16[6144,384]{1,0:T(8,128)(2,1)} %bitcast.28, bf16[2,192,6144]{2,1,0:T(8,128)(2,1)} %all-gather.4.cloned.1.call-done), kind=kOutput, calls=%fused_computation | convolution fusion | flops 1830813696 | bytes 12386304 | tf_op jit(solution)/shard_map/dot_general | solution.py:55
  301.8 0.0 slice-done
  301.9 0.0 copy-done.1
  301.9 0.5 slice-done.1
  302.3 1.3 copy-done.3
  303.7 2.0 fusion.11
  305.7 0.9 pad_maximum_fusion.1
  (3 shorter events, 0.1 us)
Async XLA Ops:
  6.5 181.0 %all-gather.6.cloned.1.call-start = ((), (), s32[]{:S(2)}) async-start(), calls=%async_computation.1 | async-start | bytes 10027008 | tf_op jit(solution)/shard_map/all_gather | solution.py:48
  7.9 11.7 %collective-permute-start = (bf16[2,192,192]{1,2,0:T(8,128)(2,1)S(1)}, bf16[2,192,192]{1,2,0:T(8,128)(2,1)S(1)}, u32[]{:S(2)}, u32[]{:S(2)}) collective-permute-start(bf16[2,192,192]{1,2,0:T(8,128)(2,1)S(1)} %copy.4), channel_id=1, source_target_pairs={{0,0},{32,2},{64,4},{96,6},{128,8},{160,10},{192,12},{224,14},{256... | collective-permute-start | bytes 442376 | tf_op jit(solution)/shard_map/ppermute | solution.py:36
  14.1 10.5 %collective-permute-start.1 = (bf16[2,192,192]{1,2,0:T(8,128)(2,1)S(1)}, bf16[2,192,192]{1,2,0:T(8,128)(2,1)S(1)}, u32[]{:S(2)}, u32[]{:S(2)}) collective-permute-start(bf16[2,192,192]{1,2,0:T(8,128)(2,1)S(1)} %copy.5), channel_id=1, source_target_pairs={{0,1},{32,3},{64,5},{96,7},{128,9},{160,11},{192,13},{224,15},{256... | collective-permute-start | bytes 442376 | tf_op jit(solution)/shard_map/ppermute | solution.py:36
  25.8 57.7 %copy-start.2 = (bf16[2,192,384]{2,1,0:T(8,128)(2,1)}, bf16[2,192,384]{2,1,0:T(8,128)(2,1)S(1)}, u32[]{:S(2)}) copy-start(bf16[2,192,384]{2,1,0:T(8,128)(2,1)S(1)} %fusion.15) | copy-start | bytes 884740
  25.8 56.7 %collective-permute-start.2 = (bf16[2,192,384]{2,1,0:T(8,128)(2,1)S(1)}, bf16[2,192,384]{2,1,0:T(8,128)(2,1)S(1)}, u32[]{:S(2)}, u32[]{:S(2)}) collective-permute-start(bf16[2,192,384]{2,1,0:T(8,128)(2,1)S(1)} %fusion.15), channel_id=1, source_target_pairs={{0,16},{16,0},{1,17},{17,1},{2,18},{18,2},{3,19},{19,3},{4,20},{20... | collective-permute-start | bytes 884744 | tf_op jit(solution)/shard_map/ppermute | solution.py:44
  83.5 211.8 %all-gather.4.cloned.1.call-start = ((), (), s32[]{:S(2)}) async-start(), calls=%async_computation | async-start | bytes 5013504 | tf_op jit(solution)/shard_map/all_gather | solution.py:51
  194.4 2.1 copy-start
  196.5 105.3 %slice-start = ((s8[4718592]{0:T(1024)(128)(4,1)}), s8[524288]{0:T(1024)(128)(4,1)S(1)}, s32[]{:S(2)}) async-start(s8[4718592]{0:T(1024)(128)(4,1)} %bitcast.29), calls=%async_computation.2 | async-start | bytes 1048576
  295.3 6.6 %copy-start.1 = (bf16[6144,384]{1,0:T(8,128)(2,1)S(1)}, bf16[6144,384]{1,0:T(8,128)(2,1)}, u32[]{:S(2)}) copy-start(bf16[6144,384]{1,0:T(8,128)(2,1)} %bitcast_negate_fusion) | copy-start | bytes 14155780
  295.3 7.0 %slice-start.1 = ((s8[4718592]{0:T(1024)(128)(4,1)}), s8[4194304]{0:T(1024)(128)(4,1)S(1)}, s32[]{:S(2)}) async-start(s8[4718592]{0:T(1024)(128)(4,1)} %bitcast.29), calls=%async_computation.3 | async-start | bytes 8388608
  295.3 8.4 %copy-start.3 = (bf16[2,192,6144]{2,1,0:T(8,128)(2,1)S(1)}, bf16[2,192,6144]{2,1,0:T(8,128)(2,1)}, u32[]{:S(2)}) copy-start(bf16[2,192,6144]{2,1,0:T(8,128)(2,1)} %all-gather.4.cloned.1.call-done) | copy-start | bytes 14155780
Sparse Core Ops, SparseCore 0:
  83.6 103.9 all-gather.5
  189.6 105.6 all-gather.3

commit v2 on v1

--- a/solution.py
+++ b/solution.py
@@ -18,16 +18,37 @@
     return pairs
 
 
+def gather_line(block):
+    n_line = lax.axis_size("zl")
+    line_index = lax.axis_index("zl")
+    core_index = lax.axis_index("core")
+    from_left, from_right = [], []
+    rightward, leftward = block, block
+    for _ in range(n_line - 1):
+        rightward = lax.ppermute(rightward, "zl", [(k, k + 1) for k in range(n_line - 1)])
+        leftward = lax.ppermute(leftward, "zl", [(k + 1, k) for k in range(n_line - 1)])
+        from_left.append(rightward)
+        from_right.append(leftward)
+    sequence = jnp.stack(from_left[::-1] + [block] + from_right)
+    mine = lax.dynamic_slice_in_dim(sequence, n_line - 1 - line_index, n_line, 0)
+    other = lax.ppermute(mine, "core", [(0, 1), (1, 0)])
+    both = jnp.where(
+        core_index == 0, jnp.stack([mine, other], axis=1), jnp.stack([other, mine], axis=1)
+    )
+    parts, rows, cols = block.shape
+    return jnp.transpose(both, (2, 3, 0, 1, 4)).reshape(parts, rows, 2 * n_line * cols)
+
+
 def local(pressure):
-    n_shot = lax.axis_size("shot")
+    n_shot = lax.axis_size("zl") * lax.axis_size("core")
     n_half = lax.axis_size("yx")
     n_recv = 2 * n_half
     block_rows = pressure.shape[1]
-    shot_index = lax.axis_index("shot")
+    shot_index = lax.axis_index("zl") * lax.axis_size("core") + lax.axis_index("core")
     half_index = lax.axis_index("zh")
     recv_index = half_index * n_half + lax.axis_index("yx")
     parity = recv_index % 2
-    axes = ("shot", "zh", "yx")
+    axes = ("zl", "core", "zh", "yx")
 
     arrived = []
     for flip in range(2):
@@ -48,7 +69,7 @@
     col_panel = lax.all_gather(stacked, "yx", axis=2, tiled=False)
     col_panel = col_panel.reshape(2, n_recv * block_rows, stacked.shape[-1])
 
-    row_panel = lax.all_gather(symmetric, "shot", axis=2, tiled=True)
+    row_panel = gather_line(symmetric)
     factor = 1.0 / math.sqrt(N)
     upper_half = jnp.concatenate([col_panel[0], col_panel[1]], axis=1)
     lower_half = jnp.concatenate([-col_panel[1], col_panel[0]], axis=1)
@@ -61,8 +82,8 @@
 
 def solution(mesh):
     n_shot, n_recv = mesh.devices.shape
-    split = Mesh(mesh.devices.reshape(n_shot, 2, n_recv // 2), ("shot", "zh", "yx"))
-    placed = (P(None, ("zh", "yx"), "shot"),)
-    return jax.shard_map(
-        local, mesh=split, in_specs=placed, out_specs=P(None, ("zh", "yx"), "shot"), check_vma=False
+    split = Mesh(
+        mesh.devices.reshape(n_shot // 2, 2, 2, n_recv // 2), ("zl", "core", "zh", "yx")
     )
+    placed = P(None, ("zh", "yx"), ("zl", "core"))
+    return jax.shard_map(local, mesh=split, in_specs=(placed,), out_specs=placed, check_vma=False)

time: 316 us -> 219 us (0.69)
  the two profiles are of different devices: /device:TPU:1 before, /device:TPU:25 now
where the time goes in v2:
time: 219 us; the launch traced here: 218 us
  starting transfers between devices  120 us (55%)
  waiting for transfers between devices  44.9 us (21%)
  local copies, waits for them, and re-layouts  28.4 us (13%)
  between operations  13.8 us (6%)
  other arithmetic  7.18 us (3%)
  matrix products  4.23 us (2%)
    ppermute x1, starting transfers between devices, local(): partner_block = lax.ppermute(symmetric, 'zh', [(0, 1), (1, 0)])  49.8 us
    ppermute x7, starting transfers between devices, gather_line(): lax.ppermute(rightward, 'zl', [(k, k + 1) for k in range(n_line - 1)])  39.7 us
    ppermute x7, waiting for transfers between devices, gather_line(): lax.ppermute(rightward, 'zl', [(k, k + 1) for k in range(n_line - 1)])  19.8 us
    ppermute x2, starting transfers between devices, local(): lax.ppermute(piece, axes, mirror_pairs(n_recv, n_shot, flip))  12 us
    ppermute x2, waiting for transfers between devices, local(): lax.ppermute(piece, axes, mirror_pairs(n_recv, n_shot, flip))  10.4 us
    ppermute x1, waiting for transfers between devices, local(): partner_block = lax.ppermute(symmetric, 'zh', [(0, 1), (1, 0)])  9.91 us
    ppermute x1, starting transfers between devices, gather_line(): other = lax.ppermute(mine, 'core', [(0, 1), (1, 0)])  9.12 us
    ppermute x7, starting transfers between devices, gather_line(): lax.ppermute(leftward, 'zl', [(k + 1, k) for k in range(n_line - 1)])  9.01 us
  transfers between devices with their start and end apart: 19, of which 12 were waited for; matrix products, arithmetic and copies ran while one was open for 10% of the time, Pallas kernels for 0%

profile of v2, /device:TPU:25, one launch (start us, length us, event | category | flops | bytes accessed | tf_op | source)
XLA Modules:
  0.0 218.1 jit_solution(15028061996165953695)
XLA Ops:
  6.5 0.0 all-gather.3.cloned.1.call-start
  6.5 1.2 constant_dynamic-slice_fusion.2
  7.7 0.1 copy.9
  7.9 8.7 %collective-permute-start.1 = (bf16[2,192,192]{1,2,0:T(8,128)(2,1)S(1)}, bf16[2,192,192]{1,2,0:T(8,128)(2,1)S(1)}, u32[]{:S(2)}, u32[]{:S(2)}) collective-permute-start(bf16[2,192,192]{1,2,0:T(8,128)(2,1)S(1)} %copy.9), channel_id=1, source_target_pairs={{0,1},{32,3},{64,5},{96,7},{128,9},{160,11},{192,13},{224,15},{256... | collective-permute-start | bytes 442376 | tf_op jit(solution)/shard_map/ppermute | solution.py:57
  16.6 0.1 copy.8
  16.7 3.2 %collective-permute-start = (bf16[2,192,192]{1,2,0:T(8,128)(2,1)S(1)}, bf16[2,192,192]{1,2,0:T(8,128)(2,1)S(1)}, u32[]{:S(2)}, u32[]{:S(2)}) collective-permute-start(bf16[2,192,192]{1,2,0:T(8,128)(2,1)S(1)} %copy.8), channel_id=1, source_target_pairs={{0,0},{32,2},{64,4},{96,6},{128,8},{160,10},{192,12},{224,14},{256... | collective-permute-start | bytes 442376 | tf_op jit(solution)/shard_map/ppermute | solution.py:57
  20.0 3.1 %collective-permute-done.1 = bf16[2,192,192]{1,2,0:T(8,128)(2,1)S(1)} collective-permute-done((bf16[2,192,192]{1,2,0:T(8,128)(2,1)S(1)}, bf16[2,192,192]{1,2,0:T(8,128)(2,1)S(1)}, u32[]{:S(2)}, u32[]{:S(2)}) %collective-permute-start.1) | collective-permute-done | bytes 147488 | tf_op jit(solution)/shard_map/ppermute | solution.py:57
  23.1 7.3 %collective-permute-done = bf16[2,192,192]{1,2,0:T(8,128)(2,1)S(1)} collective-permute-done((bf16[2,192,192]{1,2,0:T(8,128)(2,1)S(1)}, bf16[2,192,192]{1,2,0:T(8,128)(2,1)S(1)}, u32[]{:S(2)}, u32[]{:S(2)}) %collective-permute-start) | collective-permute-done | bytes 147488 | tf_op jit(solution)/shard_map/ppermute | solution.py:57
  30.5 1.1 fusion.16
  31.6 49.8 %collective-permute-start.17 = (bf16[2,192,384]{2,1,0:T(8,128)(2,1)S(1)}, bf16[2,192,384]{2,1,0:T(8,128)(2,1)S(1)}, u32[]{:S(2)}, u32[]{:S(2)}) collective-permute-start(bf16[2,192,384]{2,1,0:T(8,128)(2,1)S(1)} %fusion.16), channel_id=1, source_target_pairs={{0,16},{16,0},{1,17},{17,1},{2,18},{18,2},{3,19},{19,3},{4,20},{20... | collective-permute-start | bytes 884744 | tf_op jit(solution)/shard_map/ppermute | solution.py:65
  81.4 9.9 %collective-permute-done.17 = bf16[2,192,384]{2,1,0:T(8,128)(2,1)S(1)} collective-permute-done((bf16[2,192,384]{2,1,0:T(8,128)(2,1)S(1)}, bf16[2,192,384]{2,1,0:T(8,128)(2,1)S(1)}, u32[]{:S(2)}, u32[]{:S(2)}) %collective-permute-start.17) | collective-permute-done | bytes 294944 | tf_op jit(solution)/shard_map/ppermute | solution.py:65
  91.3 0.1 select_bitcast_fusion.1
  91.4 0.9 pad_maximum_fusion
  92.3 0.0 all-gather.3.cloned.1.call-update
  92.3 13.7 %collective-permute-start.2 = (bf16[2,192,384]{2,1,0:T(8,128)(2,1)S(1)}, bf16[2,192,384]{2,1,0:T(8,128)(2,1)S(1)}, u32[]{:S(2)}, u32[]{:S(2)}) collective-permute-start(bf16[2,192,384]{2,1,0:T(8,128)(2,1)S(1)} %fusion.16), channel_id=1, source_target_pairs={{0,64},{64,128},{128,192},{192,256},{256,320},{320,384},{384,448},... | collective-permute-start | bytes 884744 | tf_op jit(solution)/shard_map/ppermute | solution.py:28
  106.0 1.3 collective-permute-start.9
  107.3 4.3 %collective-permute-done.2 = bf16[2,192,384]{2,1,0:T(8,128)(2,1)S(1)} collective-permute-done((bf16[2,192,384]{2,1,0:T(8,128)(2,1)S(1)}, bf16[2,192,384]{2,1,0:T(8,128)(2,1)S(1)}, u32[]{:S(2)}, u32[]{:S(2)}) %collective-permute-start.2) | collective-permute-done | bytes 294944 | tf_op jit(solution)/shard_map/ppermute | solution.py:28
  111.6 4.1 %collective-permute-start.3 = (bf16[2,192,384]{2,1,0:T(8,128)(2,1)S(1)}, bf16[2,192,384]{2,1,0:T(8,128)(2,1)S(1)}, u32[]{:S(2)}, u32[]{:S(2)}) collective-permute-start(bf16[2,192,384]{2,1,0:T(8,128)(2,1)S(1)} %collective-permute-done.2), channel_id=1, source_target_pairs={{0,64},{64,128},{128,192},{192,256},{256,320},{320,384},{384,448},... | collective-permute-start | bytes 884744 | tf_op jit(solution)/shard_map/ppermute | solution.py:28
  115.7 0.0 collective-permute-done.9
  115.7 1.3 collective-permute-start.10
  117.0 3.3 %collective-permute-done.3 = bf16[2,192,384]{2,1,0:T(8,128)(2,1)S(1)} collective-permute-done((bf16[2,192,384]{2,1,0:T(8,128)(2,1)S(1)}, bf16[2,192,384]{2,1,0:T(8,128)(2,1)S(1)}, u32[]{:S(2)}, u32[]{:S(2)}) %collective-permute-start.3) | collective-permute-done | bytes 294944 | tf_op jit(solution)/shard_map/ppermute | solution.py:28
  120.3 4.2 %collective-permute-start.4 = (bf16[2,192,384]{2,1,0:T(8,128)(2,1)S(1)}, bf16[2,192,384]{2,1,0:T(8,128)(2,1)S(1)}, u32[]{:S(2)}, u32[]{:S(2)}) collective-permute-start(bf16[2,192,384]{2,1,0:T(8,128)(2,1)S(1)} %collective-permute-done.3), channel_id=1, source_target_pairs={{0,64},{64,128},{128,192},{192,256},{256,320},{320,384},{384,448},... | collective-permute-start | bytes 884744 | tf_op jit(solution)/shard_map/ppermute | solution.py:28
  124.6 0.0 collective-permute-done.10
  124.6 1.3 collective-permute-start.11
  125.9 2.3 %collective-permute-done.4 = bf16[2,192,384]{2,1,0:T(8,128)(2,1)S(1)} collective-permute-done((bf16[2,192,384]{2,1,0:T(8,128)(2,1)S(1)}, bf16[2,192,384]{2,1,0:T(8,128)(2,1)S(1)}, u32[]{:S(2)}, u32[]{:S(2)}) %collective-permute-start.4) | collective-permute-done | bytes 294944 | tf_op jit(solution)/shard_map/ppermute | solution.py:28
  128.2 4.4 %collective-permute-start.5 = (bf16[2,192,384]{2,1,0:T(8,128)(2,1)S(1)}, bf16[2,192,384]{2,1,0:T(8,128)(2,1)S(1)}, u32[]{:S(2)}, u32[]{:S(2)}) collective-permute-start(bf16[2,192,384]{2,1,0:T(8,128)(2,1)S(1)} %collective-permute-done.4), channel_id=1, source_target_pairs={{0,64},{64,128},{128,192},{192,256},{256,320},{320,384},{384,448},... | collective-permute-start | bytes 884744 | tf_op jit(solution)/shard_map/ppermute | solution.py:28
  132.6 0.0 collective-permute-done.11
  132.6 1.3 collective-permute-start.12
  133.9 2.3 %collective-permute-done.5 = bf16[2,192,384]{2,1,0:T(8,128)(2,1)S(1)} collective-permute-done((bf16[2,192,384]{2,1,0:T(8,128)(2,1)S(1)}, bf16[2,192,384]{2,1,0:T(8,128)(2,1)S(1)}, u32[]{:S(2)}, u32[]{:S(2)}) %collective-permute-start.5) | collective-permute-done | bytes 294944 | tf_op jit(solution)/shard_map/ppermute | solution.py:28
  136.2 3.8 %collective-permute-start.6 = (bf16[2,192,384]{2,1,0:T(8,128)(2,1)S(1)}, bf16[2,192,384]{2,1,0:T(8,128)(2,1)S(1)}, u32[]{:S(2)}, u32[]{:S(2)}) collective-permute-start(bf16[2,192,384]{2,1,0:T(8,128)(2,1)S(1)} %collective-permute-done.5), channel_id=1, source_target_pairs={{0,64},{64,128},{128,192},{192,256},{256,320},{320,384},{384,448},... | collective-permute-start | bytes 884744 | tf_op jit(solution)/shard_map/ppermute | solution.py:28
  140.1 0.0 collective-permute-done.12
  140.1 1.3 collective-permute-start.13
  141.4 2.3 %collective-permute-done.6 = bf16[2,192,384]{2,1,0:T(8,128)(2,1)S(1)} collective-permute-done((bf16[2,192,384]{2,1,0:T(8,128)(2,1)S(1)}, bf16[2,192,384]{2,1,0:T(8,128)(2,1)S(1)}, u32[]{:S(2)}, u32[]{:S(2)}) %collective-permute-start.6) | collective-permute-done | bytes 294944 | tf_op jit(solution)/shard_map/ppermute | solution.py:28
  143.7 4.5 %collective-permute-start.7 = (bf16[2,192,384]{2,1,0:T(8,128)(2,1)S(1)}, bf16[2,192,384]{2,1,0:T(8,128)(2,1)}, u32[]{:S(2)}, u32[]{:S(2)}) collective-permute-start(bf16[2,192,384]{2,1,0:T(8,128)(2,1)S(1)} %collective-permute-done.6), channel_id=1, source_target_pairs={{0,64},{64,128},{128,192},{192,256},{256,320},{320,384},{384,448},... | collective-permute-start | bytes 884744 | tf_op jit(solution)/shard_map/ppermute | solution.py:28
  148.2 0.0 collective-permute-done.13
  148.2 1.3 collective-permute-start.14
  149.5 2.2 %collective-permute-done.7 = bf16[2,192,384]{2,1,0:T(8,128)(2,1)} collective-permute-done((bf16[2,192,384]{2,1,0:T(8,128)(2,1)S(1)}, bf16[2,192,384]{2,1,0:T(8,128)(2,1)}, u32[]{:S(2)}, u32[]{:S(2)}) %collective-permute-start.7) | collective-permute-done | bytes 294944 | tf_op jit(solution)/shard_map/ppermute | solution.py:28
  151.7 4.9 %collective-permute-start.8 = (bf16[2,192,384]{2,1,0:T(8,128)(2,1)}, bf16[2,192,384]{2,1,0:T(8,128)(2,1)}, u32[]{:S(2)}, u32[]{:S(2)}) collective-permute-start(bf16[2,192,384]{2,1,0:T(8,128)(2,1)} %collective-permute-done.7), channel_id=1, source_target_pairs={{0,64},{64,128},{128,192},{192,256},{256,320},{320,384},{384,448},... | collective-permute-start | bytes 884744 | tf_op jit(solution)/shard_map/ppermute | solution.py:28
  156.6 0.0 collective-permute-done.14
  156.6 1.3 collective-permute-start.15
  157.9 3.0 %collective-permute-done.8 = bf16[2,192,384]{2,1,0:T(8,128)(2,1)} collective-permute-done((bf16[2,192,384]{2,1,0:T(8,128)(2,1)}, bf16[2,192,384]{2,1,0:T(8,128)(2,1)}, u32[]{:S(2)}, u32[]{:S(2)}) %collective-permute-start.8) | collective-permute-done | bytes 294944 | tf_op jit(solution)/shard_map/ppermute | solution.py:28
  160.9 1.0 bitcast_dynamic-update-slice_fusion.14
  161.9 1.0 bitcast_dynamic-update-slice_fusion.13
  163.6 2.4 %collective-permute-done.15 = bf16[2,192,384]{2,1,0:T(8,128)(2,1)S(1)} collective-permute-done((bf16[2,192,384]{2,1,0:T(8,128)(2,1)S(1)}, bf16[2,192,384]{2,1,0:T(8,128)(2,1)S(1)}, u32[]{:S(2)}, u32[]{:S(2)}) %collective-permute-start.15) | collective-permute-done | bytes 294944 | tf_op jit(solution)/shard_map/ppermute | solution.py:29
  166.1 0.0 copy-start
  166.1 2.1 copy-done
  168.2 0.2 constant_dynamic-slice_fusion
  168.5 9.1 %collective-permute-start.16 = (bf16[8,2,192,384]{3,2,1,0:T(8,128)(2,1)S(1)}, bf16[8,2,192,384]{3,2,1,0:T(8,128)(2,1)}, u32[]{:S(2)}, u32[]{:S(2)}) collective-permute-start(bf16[8,2,192,384]{3,2,1,0:T(8,128)(2,1)S(1)} %constant_dynamic-slice_fusion), channel_id=1, source_target_pairs={{0,32},{32,0},{1,33},{33,1},{2,34},{34,2},{3,35},{35,3},{4,36},{36... | collective-permute-start | bytes 7077896 | tf_op jit(solution)/shard_map/ppermute | solution.py:34
  177.6 1.9 fusion.23
  179.6 2.3 %collective-permute-done.16 = bf16[8,2,192,384]{3,2,1,0:T(8,128)(2,1)} collective-permute-done((bf16[8,2,192,384]{3,2,1,0:T(8,128)(2,1)S(1)}, bf16[8,2,192,384]{3,2,1,0:T(8,128)(2,1)}, u32[]{:S(2)}, u32[]{:S(2)}) %collective-permute-start.16) | collective-permute-done | bytes 2359328 | tf_op jit(solution)/shard_map/ppermute | solution.py:34
  181.9 3.3 %fusion.8 = bf16[2,192,8,2,384]{4,1,0,2,3:T(8,128)(2,1)S(1)} fusion(bf16[8,1,2,192,384]{4,3,2,0,1:T(8,128)(2,1)} %bitcast.17, bf16[8,1,2,192,384]{4,3,2,0,1:T(8,128)(2,1)S(1)} %fusion.23, pred[]{:T(512)S(6)} %eq.15), kind=kLoop, calls=%fused_computation.9 | loop fusion | flops 7077888 | bytes 9437185 | tf_op jit(solution)/shard_map/transpose | solution.py:39
  185.2 1.9 fusion.20
  187.1 2.4 %copy.7 = bf16[1,192,8,2,384]{4,3,2,1,0:T(2,128)(2,1)S(1)} copy(bf16[1,192,8,2,384]{4,1,0,2,3:T(8,128)(2,1)S(1)} %get-tuple-element.7) | data formatting | bytes 4718592 | tf_op jit(solution)/shard_map/slice | solution.py:77
  189.6 3.0 %squeeze.17 = bf16[192,6144]{1,0:T(8,128)(2,1)} reshape(bf16[1,192,8,2,384]{4,3,2,1,0:T(2,128)(2,1)S(1)} %copy.7) | data formatting | bytes 4718592 | tf_op jit(solution)/shard_map/squeeze | solution.py:77
  192.6 4.1 %copy.6 = bf16[1,192,8,2,384]{4,3,2,1,0:T(2,128)(2,1)S(1)} copy(bf16[1,192,8,2,384]{4,1,0,2,3:T(8,128)(2,1)} %get-tuple-element.8) | data formatting | bytes 4718592 | tf_op jit(solution)/shard_map/slice | solution.py:76
  196.7 3.0 %squeeze.14 = bf16[192,6144]{1,0:T(8,128)(2,1)} reshape(bf16[1,192,8,2,384]{4,3,2,1,0:T(2,128)(2,1)S(1)} %copy.6) | data formatting | bytes 4718592 | tf_op jit(solution)/shard_map/squeeze | solution.py:76
  199.7 4.7 %fusion.19 = (bf16[1,2,3072,384]{3,2,0,1:T(8,128)(2,1)S(1)}, bf16[1,2,3072,384]{3,2,0,1:T(8,128)(2,1)S(1)}) fusion(bf16[2,2,3072,384]{3,2,0,1:T(8,128)(2,1)} %all-gather.3.cloned.1.call-done), kind=kLoop, calls=%fused_computation.44 | loop fusion | bytes 18874368 | tf_op jit(solution)/shard_map/slice | solution.py:74
  204.4 0.0 copy-start.2
  204.4 0.9 bitcast_negate_fusion
  205.3 0.8 copy-done.2
  206.1 2.1 fusion
  208.2 0.0 copy-done.1
  208.2 2.1 fusion.12
  210.4 0.9 pad_maximum_fusion.1
  (17 shorter events, 0.7 us)
Async XLA Ops:
  6.5 193.2 %all-gather.3.cloned.1.call-start = ((), (), s32[]{:S(2)}) async-start(), calls=%async_computation | async-start | bytes 10027008 | tf_op jit(solution)/shard_map/all_gather | solution.py:69
  7.9 15.2 %collective-permute-start.1 = (bf16[2,192,192]{1,2,0:T(8,128)(2,1)S(1)}, bf16[2,192,192]{1,2,0:T(8,128)(2,1)S(1)}, u32[]{:S(2)}, u32[]{:S(2)}) collective-permute-start(bf16[2,192,192]{1,2,0:T(8,128)(2,1)S(1)} %copy.9), channel_id=1, source_target_pairs={{0,1},{32,3},{64,5},{96,7},{128,9},{160,11},{192,13},{224,15},{256... | collective-permute-start | bytes 442376 | tf_op jit(solution)/shard_map/ppermute | solution.py:57
  16.7 13.7 %collective-permute-start = (bf16[2,192,192]{1,2,0:T(8,128)(2,1)S(1)}, bf16[2,192,192]{1,2,0:T(8,128)(2,1)S(1)}, u32[]{:S(2)}, u32[]{:S(2)}) collective-permute-start(bf16[2,192,192]{1,2,0:T(8,128)(2,1)S(1)} %copy.8), channel_id=1, source_target_pairs={{0,0},{32,2},{64,4},{96,6},{128,8},{160,10},{192,12},{224,14},{256... | collective-permute-start | bytes 442376 | tf_op jit(solution)/shard_map/ppermute | solution.py:57
  31.6 59.7 %collective-permute-start.17 = (bf16[2,192,384]{2,1,0:T(8,128)(2,1)S(1)}, bf16[2,192,384]{2,1,0:T(8,128)(2,1)S(1)}, u32[]{:S(2)}, u32[]{:S(2)}) collective-permute-start(bf16[2,192,384]{2,1,0:T(8,128)(2,1)S(1)} %fusion.16), channel_id=1, source_target_pairs={{0,16},{16,0},{1,17},{17,1},{2,18},{18,2},{3,19},{19,3},{4,20},{20... | collective-permute-start | bytes 884744 | tf_op jit(solution)/shard_map/ppermute | solution.py:65
  92.3 19.3 %collective-permute-start.2 = (bf16[2,192,384]{2,1,0:T(8,128)(2,1)S(1)}, bf16[2,192,384]{2,1,0:T(8,128)(2,1)S(1)}, u32[]{:S(2)}, u32[]{:S(2)}) collective-permute-start(bf16[2,192,384]{2,1,0:T(8,128)(2,1)S(1)} %fusion.16), channel_id=1, source_target_pairs={{0,64},{64,128},{128,192},{192,256},{256,320},{320,384},{384,448},... | collective-permute-start | bytes 884744 | tf_op jit(solution)/shard_map/ppermute | solution.py:28
  106.0 9.7 %collective-permute-start.9 = (bf16[2,192,384]{2,1,0:T(8,128)(2,1)S(1)}, bf16[2,192,384]{2,1,0:T(8,128)(2,1)S(1)}, u32[]{:S(2)}, u32[]{:S(2)}) collective-permute-start(bf16[2,192,384]{2,1,0:T(8,128)(2,1)S(1)} %fusion.16), channel_id=1, source_target_pairs={{64,0},{128,64},{192,128},{256,192},{320,256},{384,320},{448,384},... | collective-permute-start | bytes 884744 | tf_op jit(solution)/shard_map/ppermute | solution.py:29
  111.6 8.8 %collective-permute-start.3 = (bf16[2,192,384]{2,1,0:T(8,128)(2,1)S(1)}, bf16[2,192,384]{2,1,0:T(8,128)(2,1)S(1)}, u32[]{:S(2)}, u32[]{:S(2)}) collective-permute-start(bf16[2,192,384]{2,1,0:T(8,128)(2,1)S(1)} %collective-permute-done.2), channel_id=1, source_target_pairs={{0,64},{64,128},{128,192},{192,256},{256,320},{320,384},{384,448},... | collective-permute-start | bytes 884744 | tf_op jit(solution)/shard_map/ppermute | solution.py:28
  115.7 8.9 %collective-permute-start.10 = (bf16[2,192,384]{2,1,0:T(8,128)(2,1)S(1)}, bf16[2,192,384]{2,1,0:T(8,128)(2,1)S(1)}, u32[]{:S(2)}, u32[]{:S(2)}) collective-permute-start(bf16[2,192,384]{2,1,0:T(8,128)(2,1)S(1)} %collective-permute-done.9), channel_id=1, source_target_pairs={{64,0},{128,64},{192,128},{256,192},{320,256},{384,320},{448,384},... | collective-permute-start | bytes 884744 | tf_op jit(solution)/shard_map/ppermute | solution.py:29
  120.3 7.9 %collective-permute-start.4 = (bf16[2,192,384]{2,1,0:T(8,128)(2,1)S(1)}, bf16[2,192,384]{2,1,0:T(8,128)(2,1)S(1)}, u32[]{:S(2)}, u32[]{:S(2)}) collective-permute-start(bf16[2,192,384]{2,1,0:T(8,128)(2,1)S(1)} %collective-permute-done.3), channel_id=1, source_target_pairs={{0,64},{64,128},{128,192},{192,256},{256,320},{320,384},{384,448},... | collective-permute-start | bytes 884744 | tf_op jit(solution)/shard_map/ppermute | solution.py:28
  124.6 8.0 %collective-permute-start.11 = (bf16[2,192,384]{2,1,0:T(8,128)(2,1)S(1)}, bf16[2,192,384]{2,1,0:T(8,128)(2,1)S(1)}, u32[]{:S(2)}, u32[]{:S(2)}) collective-permute-start(bf16[2,192,384]{2,1,0:T(8,128)(2,1)S(1)} %collective-permute-done.10), channel_id=1, source_target_pairs={{64,0},{128,64},{192,128},{256,192},{320,256},{384,320},{448,384},... | collective-permute-start | bytes 884744 | tf_op jit(solution)/shard_map/ppermute | solution.py:29
  128.2 8.0 %collective-permute-start.5 = (bf16[2,192,384]{2,1,0:T(8,128)(2,1)S(1)}, bf16[2,192,384]{2,1,0:T(8,128)(2,1)S(1)}, u32[]{:S(2)}, u32[]{:S(2)}) collective-permute-start(bf16[2,192,384]{2,1,0:T(8,128)(2,1)S(1)} %collective-permute-done.4), channel_id=1, source_target_pairs={{0,64},{64,128},{128,192},{192,256},{256,320},{320,384},{384,448},... | collective-permute-start | bytes 884744 | tf_op jit(solution)/shard_map/ppermute | solution.py:28
  132.6 7.5 %collective-permute-start.12 = (bf16[2,192,384]{2,1,0:T(8,128)(2,1)S(1)}, bf16[2,192,384]{2,1,0:T(8,128)(2,1)S(1)}, u32[]{:S(2)}, u32[]{:S(2)}) collective-permute-start(bf16[2,192,384]{2,1,0:T(8,128)(2,1)S(1)} %collective-permute-done.11), channel_id=1, source_target_pairs={{64,0},{128,64},{192,128},{256,192},{320,256},{384,320},{448,384},... | collective-permute-start | bytes 884744 | tf_op jit(solution)/shard_map/ppermute | solution.py:29
  136.2 7.5 %collective-permute-start.6 = (bf16[2,192,384]{2,1,0:T(8,128)(2,1)S(1)}, bf16[2,192,384]{2,1,0:T(8,128)(2,1)S(1)}, u32[]{:S(2)}, u32[]{:S(2)}) collective-permute-start(bf16[2,192,384]{2,1,0:T(8,128)(2,1)S(1)} %collective-permute-done.5), channel_id=1, source_target_pairs={{0,64},{64,128},{128,192},{192,256},{256,320},{320,384},{384,448},... | collective-permute-start | bytes 884744 | tf_op jit(solution)/shard_map/ppermute | solution.py:28
  140.1 8.1 %collective-permute-start.13 = (bf16[2,192,384]{2,1,0:T(8,128)(2,1)S(1)}, bf16[2,192,384]{2,1,0:T(8,128)(2,1)S(1)}, u32[]{:S(2)}, u32[]{:S(2)}) collective-permute-start(bf16[2,192,384]{2,1,0:T(8,128)(2,1)S(1)} %collective-permute-done.12), channel_id=1, source_target_pairs={{64,0},{128,64},{192,128},{256,192},{320,256},{384,320},{448,384},... | collective-permute-start | bytes 884744 | tf_op jit(solution)/shard_map/ppermute | solution.py:29
  143.7 8.0 %collective-permute-start.7 = (bf16[2,192,384]{2,1,0:T(8,128)(2,1)S(1)}, bf16[2,192,384]{2,1,0:T(8,128)(2,1)}, u32[]{:S(2)}, u32[]{:S(2)}) collective-permute-start(bf16[2,192,384]{2,1,0:T(8,128)(2,1)S(1)} %collective-permute-done.6), channel_id=1, source_target_pairs={{0,64},{64,128},{128,192},{192,256},{256,320},{320,384},{384,448},... | collective-permute-start | bytes 884744 | tf_op jit(solution)/shard_map/ppermute | solution.py:28
  148.2 8.4 %collective-permute-start.14 = (bf16[2,192,384]{2,1,0:T(8,128)(2,1)S(1)}, bf16[2,192,384]{2,1,0:T(8,128)(2,1)S(1)}, u32[]{:S(2)}, u32[]{:S(2)}) collective-permute-start(bf16[2,192,384]{2,1,0:T(8,128)(2,1)S(1)} %collective-permute-done.13), channel_id=1, source_target_pairs={{64,0},{128,64},{192,128},{256,192},{320,256},{384,320},{448,384},... | collective-permute-start | bytes 884744 | tf_op jit(solution)/shard_map/ppermute | solution.py:29
  151.7 9.2 %collective-permute-start.8 = (bf16[2,192,384]{2,1,0:T(8,128)(2,1)}, bf16[2,192,384]{2,1,0:T(8,128)(2,1)}, u32[]{:S(2)}, u32[]{:S(2)}) collective-permute-start(bf16[2,192,384]{2,1,0:T(8,128)(2,1)} %collective-permute-done.7), channel_id=1, source_target_pairs={{0,64},{64,128},{128,192},{192,256},{256,320},{320,384},{384,448},... | collective-permute-start | bytes 884744 | tf_op jit(solution)/shard_map/ppermute | solution.py:28
  156.6 9.4 %collective-permute-start.15 = (bf16[2,192,384]{2,1,0:T(8,128)(2,1)S(1)}, bf16[2,192,384]{2,1,0:T(8,128)(2,1)S(1)}, u32[]{:S(2)}, u32[]{:S(2)}) collective-permute-start(bf16[2,192,384]{2,1,0:T(8,128)(2,1)S(1)} %collective-permute-done.14), channel_id=1, source_target_pairs={{64,0},{128,64},{192,128},{256,192},{320,256},{384,320},{448,384},... | collective-permute-start | bytes 884744 | tf_op jit(solution)/shard_map/ppermute | solution.py:29
  166.1 2.1 copy-start
  168.5 13.4 %collective-permute-start.16 = (bf16[8,2,192,384]{3,2,1,0:T(8,128)(2,1)S(1)}, bf16[8,2,192,384]{3,2,1,0:T(8,128)(2,1)}, u32[]{:S(2)}, u32[]{:S(2)}) collective-permute-start(bf16[8,2,192,384]{3,2,1,0:T(8,128)(2,1)S(1)} %constant_dynamic-slice_fusion), channel_id=1, source_target_pairs={{0,32},{32,0},{1,33},{33,1},{2,34},{34,2},{3,35},{35,3},{4,36},{36... | collective-permute-start | bytes 7077896 | tf_op jit(solution)/shard_map/ppermute | solution.py:34
  204.4 1.7 copy-start.2
  206.1 2.1 copy-start.1
Sparse Core Ops, SparseCore 0:
  92.4 95.2 all-gather.2

commit v3 on v2

--- a/solution.py
+++ b/solution.py
@@ -35,8 +35,7 @@
     both = jnp.where(
         core_index == 0, jnp.stack([mine, other], axis=1), jnp.stack([other, mine], axis=1)
     )
-    parts, rows, cols = block.shape
-    return jnp.transpose(both, (2, 3, 0, 1, 4)).reshape(parts, rows, 2 * n_line * cols)
+    return both.reshape((2 * n_line,) + block.shape)
 
 
 def local(pressure):
@@ -63,21 +62,27 @@
     ).astype(jnp.bfloat16)
 
     partner_block = lax.ppermute(symmetric, "zh", [(0, 1), (1, 0)])
-    top = jnp.where(half_index == 0, symmetric, partner_block)
-    bottom = jnp.where(half_index == 0, partner_block, symmetric)
-    stacked = jnp.stack([top, bottom], axis=1)
-    col_panel = lax.all_gather(stacked, "yx", axis=2, tiled=False)
-    col_panel = col_panel.reshape(2, n_recv * block_rows, stacked.shape[-1])
+    own_panel = lax.all_gather(symmetric, "yx", axis=0, tiled=False)
+    partner_panel = lax.all_gather(partner_block, "yx", axis=0, tiled=False)
+    row_blocks = gather_line(symmetric)
 
-    row_panel = gather_line(symmetric)
+    n_blocks = row_blocks.shape[0]
+    parts, rows, cols = symmetric.shape
+    row_blocks = row_blocks.reshape(n_blocks, parts, rows, 2, cols // 2)
+    own_rows = lax.dynamic_slice_in_dim(row_blocks, half_index * (n_blocks // 2), n_blocks // 2, 0)
+    other_rows = lax.dynamic_slice_in_dim(
+        row_blocks, (1 - half_index) * (n_blocks // 2), n_blocks // 2, 0
+    )
+
+    def product(left, panel):
+        panel = panel.reshape(n_blocks // 2, 2, parts, rows, cols)
+        return jnp.einsum("jpxhr,jhqrn->pqxn", left, panel, preferred_element_type=jnp.float32)
+
+    terms = product(own_rows, own_panel) + product(other_rows, partner_panel)
     factor = 1.0 / math.sqrt(N)
-    upper_half = jnp.concatenate([col_panel[0], col_panel[1]], axis=1)
-    lower_half = jnp.concatenate([-col_panel[1], col_panel[0]], axis=1)
-    running = jnp.dot(row_panel[0], upper_half, preferred_element_type=jnp.float32)
-    running = running + jnp.dot(row_panel[1], lower_half, preferred_element_type=jnp.float32)
-    running = running * factor
-    block_cols = pressure.shape[2]
-    return jnp.stack([running[:, :block_cols], running[:, block_cols:]])
+    real = (terms[0, 0] - terms[1, 1]) * factor
+    imag = (terms[0, 1] + terms[1, 0]) * factor
+    return jnp.stack([real, imag])
 
 
 def solution(mesh):

time: 219 us -> 225 us (1.027)
  the two profiles are of different devices: /device:TPU:25 before, /device:TPU:1 now
where the time goes in v3:
time: 225 us; the launch traced here: 222 us
  starting transfers between devices  98.5 us (44%)
  waiting for transfers between devices  54.7 us (24%)
  local copies, waits for them, and re-layouts  37.7 us (17%)
  between operations  13.8 us (6%)
  matrix products  11 us (5%)
  other arithmetic  6.31 us (3%)
    ppermute x7, starting transfers between devices, gather_line(): lax.ppermute(rightward, 'zl', [(k, k + 1) for k in range(n_line - 1)])  54.9 us
    ppermute x7, waiting for transfers between devices, gather_line(): lax.ppermute(leftward, 'zl', [(k + 1, k) for k in range(n_line - 1)])  29 us
    ppermute x1, starting transfers between devices, local(): partner_block = lax.ppermute(symmetric, 'zh', [(0, 1), (1, 0)])  20.5 us
    select_n x2, local copies, waits for them, and re-layouts, gather_line(): jnp.where(core_index == 0, jnp.stack([mine, other], axis=1), jnp.stack([o...  16.9 us
    ppermute x7, waiting for transfers between devices, gather_line(): lax.ppermute(rightward, 'zl', [(k, k + 1) for k in range(n_line - 1)])  15.5 us
    dot_general x2, matrix products, product(): jnp.einsum('jpxhr,jhqrn->pqxn', left, panel, preferred_element_type=jnp.f...  11 us
    dynamic_slice x1, local copies, waits for them, and re-layouts, local(): lax.dynamic_slice_in_dim(row_blocks, half_index * (n_blocks // 2), n_bloc...  10.8 us
    ppermute x7, starting transfers between devices, gather_line(): lax.ppermute(leftward, 'zl', [(k + 1, k) for k in range(n_line - 1)])  9 us
  transfers between devices with their start and end apart: 20, of which 11 were waited for; matrix products, arithmetic and copies ran while one was open for 20% of the time, Pallas kernels for 0%

profile of v3, /device:TPU:1, one launch (start us, length us, event | category | flops | bytes accessed | tf_op | source)
XLA Modules:
  0.0 222.0 jit_solution(7108395502266304826)
XLA Ops:
  6.5 0.0 all-gather.5.cloned.1.call-start
  6.5 1.2 constant_dynamic-slice_fusion.4
  7.8 0.1 copy.34
  7.9 6.0 %collective-permute-start = (bf16[2,192,192]{1,2,0:T(8,128)(2,1)S(1)}, bf16[2,192,192]{1,2,0:T(8,128)(2,1)S(1)}, u32[]{:S(2)}, u32[]{:S(2)}) collective-permute-start(bf16[2,192,192]{1,2,0:T(8,128)(2,1)S(1)} %copy.34), channel_id=1, source_target_pairs={{0,0},{32,2},{64,4},{96,6},{128,8},{160,10},{192,12},{224,14},{256... | collective-permute-start | bytes 442376 | tf_op jit(solution)/shard_map/ppermute | solution.py:56
  13.9 0.1 copy.35
  14.1 2.5 %collective-permute-start.1 = (bf16[2,192,192]{1,2,0:T(8,128)(2,1)S(1)}, bf16[2,192,192]{1,2,0:T(8,128)(2,1)S(1)}, u32[]{:S(2)}, u32[]{:S(2)}) collective-permute-start(bf16[2,192,192]{1,2,0:T(8,128)(2,1)S(1)} %copy.35), channel_id=1, source_target_pairs={{0,1},{32,3},{64,5},{96,7},{128,9},{160,11},{192,13},{224,15},{256... | collective-permute-start | bytes 442376 | tf_op jit(solution)/shard_map/ppermute | solution.py:56
  16.6 3.0 %collective-permute-done = bf16[2,192,192]{1,2,0:T(8,128)(2,1)S(1)} collective-permute-done((bf16[2,192,192]{1,2,0:T(8,128)(2,1)S(1)}, bf16[2,192,192]{1,2,0:T(8,128)(2,1)S(1)}, u32[]{:S(2)}, u32[]{:S(2)}) %collective-permute-start) | collective-permute-done | bytes 147488 | tf_op jit(solution)/shard_map/ppermute | solution.py:56
  19.6 5.0 %collective-permute-done.1 = bf16[2,192,192]{1,2,0:T(8,128)(2,1)S(1)} collective-permute-done((bf16[2,192,192]{1,2,0:T(8,128)(2,1)S(1)}, bf16[2,192,192]{1,2,0:T(8,128)(2,1)S(1)}, u32[]{:S(2)}, u32[]{:S(2)}) %collective-permute-start.1) | collective-permute-done | bytes 147488 | tf_op jit(solution)/shard_map/ppermute | solution.py:56
  24.7 1.8 fusion.6
  26.5 0.0 all-gather.5.cloned.1.call-update
  26.5 0.0 all-gather.7.cloned.1.call-start
  26.6 17.5 %collective-permute-start.2 = (bf16[2,192,384]{2,1,0:T(8,128)(2,1)}, bf16[2,192,384]{2,1,0:T(8,128)(2,1)S(1)}, u32[]{:S(2)}, u32[]{:S(2)}) collective-permute-start(bf16[2,192,384]{2,1,0:T(8,128)(2,1)} %fusion.6), channel_id=1, source_target_pairs={{0,64},{64,128},{128,192},{192,256},{256,320},{320,384},{384,448},... | collective-permute-start | bytes 884744 | tf_op jit(solution)/shard_map/ppermute | solution.py:28
  44.1 1.3 collective-permute-start.9
  45.4 5.1 %collective-permute-done.2 = bf16[2,192,384]{2,1,0:T(8,128)(2,1)S(1)} collective-permute-done((bf16[2,192,384]{2,1,0:T(8,128)(2,1)}, bf16[2,192,384]{2,1,0:T(8,128)(2,1)S(1)}, u32[]{:S(2)}, u32[]{:S(2)}) %collective-permute-start.2) | collective-permute-done | bytes 294944 | tf_op jit(solution)/shard_map/ppermute | solution.py:28
  50.5 4.0 %collective-permute-start.3 = (bf16[2,192,384]{2,1,0:T(8,128)(2,1)S(1)}, bf16[2,192,384]{2,1,0:T(8,128)(2,1)S(1)}, u32[]{:S(2)}, u32[]{:S(2)}) collective-permute-start(bf16[2,192,384]{2,1,0:T(8,128)(2,1)S(1)} %collective-permute-done.2), channel_id=1, source_target_pairs={{0,64},{64,128},{128,192},{192,256},{256,320},{320,384},{384,448},... | collective-permute-start | bytes 884744 | tf_op jit(solution)/shard_map/ppermute | solution.py:28
  54.5 0.0 collective-permute-done.9
  54.5 1.3 collective-permute-start.10
  55.8 5.3 %collective-permute-done.3 = bf16[2,192,384]{2,1,0:T(8,128)(2,1)S(1)} collective-permute-done((bf16[2,192,384]{2,1,0:T(8,128)(2,1)S(1)}, bf16[2,192,384]{2,1,0:T(8,128)(2,1)S(1)}, u32[]{:S(2)}, u32[]{:S(2)}) %collective-permute-start.3) | collective-permute-done | bytes 294944 | tf_op jit(solution)/shard_map/ppermute | solution.py:28
  61.1 4.1 %collective-permute-start.4 = (bf16[2,192,384]{2,1,0:T(8,128)(2,1)S(1)}, bf16[2,192,384]{2,1,0:T(8,128)(2,1)S(1)}, u32[]{:S(2)}, u32[]{:S(2)}) collective-permute-start(bf16[2,192,384]{2,1,0:T(8,128)(2,1)S(1)} %collective-permute-done.3), channel_id=1, source_target_pairs={{0,64},{64,128},{128,192},{192,256},{256,320},{320,384},{384,448},... | collective-permute-start | bytes 884744 | tf_op jit(solution)/shard_map/ppermute | solution.py:28
  65.2 20.5 %collective-permute-start.17 = (bf16[2,192,384]{2,1,0:T(8,128)(2,1)}, bf16[2,192,384]{2,1,0:T(8,128)(2,1)S(1)}, u32[]{:S(2)}, u32[]{:S(2)}) collective-permute-start(bf16[2,192,384]{2,1,0:T(8,128)(2,1)} %fusion.6), channel_id=1, source_target_pairs={{0,16},{16,0},{1,17},{17,1},{2,18},{18,2},{3,19},{19,3},{4,20},{20... | collective-permute-start | bytes 884744 | tf_op jit(solution)/shard_map/ppermute | solution.py:64
  85.7 0.0 collective-permute-done.10
  85.7 1.3 collective-permute-start.11
  87.0 0.0 collective-permute-done.4
  87.0 9.2 %collective-permute-start.5 = (bf16[2,192,384]{2,1,0:T(8,128)(2,1)S(1)}, bf16[2,192,384]{2,1,0:T(8,128)(2,1)S(1)}, u32[]{:S(2)}, u32[]{:S(2)}) collective-permute-start(bf16[2,192,384]{2,1,0:T(8,128)(2,1)S(1)} %collective-permute-done.4), channel_id=1, source_target_pairs={{0,64},{64,128},{128,192},{192,256},{256,320},{320,384},{384,448},... | collective-permute-start | bytes 884744 | tf_op jit(solution)/shard_map/ppermute | solution.py:28
  96.3 0.0 collective-permute-done.17
  96.3 0.0 copy-start.3
  96.3 0.7 copy-done.3
  97.0 0.0 all-gather.7.cloned.1.call-update
  97.0 20.4 %collective-permute-done.11 = bf16[2,192,384]{2,1,0:T(8,128)(2,1)S(1)} collective-permute-done((bf16[2,192,384]{2,1,0:T(8,128)(2,1)S(1)}, bf16[2,192,384]{2,1,0:T(8,128)(2,1)S(1)}, u32[]{:S(2)}, u32[]{:S(2)}) %collective-permute-start.11) | collective-permute-done | bytes 294944 | tf_op jit(solution)/shard_map/ppermute | solution.py:29
  117.4 1.3 collective-permute-start.12
  118.7 3.1 %collective-permute-done.5 = bf16[2,192,384]{2,1,0:T(8,128)(2,1)S(1)} collective-permute-done((bf16[2,192,384]{2,1,0:T(8,128)(2,1)S(1)}, bf16[2,192,384]{2,1,0:T(8,128)(2,1)S(1)}, u32[]{:S(2)}, u32[]{:S(2)}) %collective-permute-start.5) | collective-permute-done | bytes 294944 | tf_op jit(solution)/shard_map/ppermute | solution.py:28
  121.8 4.6 %collective-permute-start.6 = (bf16[2,192,384]{2,1,0:T(8,128)(2,1)S(1)}, bf16[2,192,384]{2,1,0:T(8,128)(2,1)S(1)}, u32[]{:S(2)}, u32[]{:S(2)}) collective-permute-start(bf16[2,192,384]{2,1,0:T(8,128)(2,1)S(1)} %collective-permute-done.5), channel_id=1, source_target_pairs={{0,64},{64,128},{128,192},{192,256},{256,320},{320,384},{384,448},... | collective-permute-start | bytes 884744 | tf_op jit(solution)/shard_map/ppermute | solution.py:28
  126.4 2.6 %collective-permute-done.12 = bf16[2,192,384]{2,1,0:T(8,128)(2,1)S(1)} collective-permute-done((bf16[2,192,384]{2,1,0:T(8,128)(2,1)S(1)}, bf16[2,192,384]{2,1,0:T(8,128)(2,1)S(1)}, u32[]{:S(2)}, u32[]{:S(2)}) %collective-permute-start.12) | collective-permute-done | bytes 294944 | tf_op jit(solution)/shard_map/ppermute | solution.py:29
  129.0 1.3 collective-permute-start.13
  130.2 0.0 collective-permute-done.6
  130.3 0.0 copy-start.4
  130.3 8.6 %collective-permute-start.7 = (bf16[2,192,384]{2,1,0:T(8,128)(2,1)S(1)}, bf16[2,192,384]{2,1,0:T(8,128)(2,1)}, u32[]{:S(2)}, u32[]{:S(2)}) collective-permute-start(bf16[2,192,384]{2,1,0:T(8,128)(2,1)S(1)} %collective-permute-done.6), channel_id=1, source_target_pairs={{0,64},{64,128},{128,192},{192,256},{256,320},{320,384},{384,448},... | collective-permute-start | bytes 884744 | tf_op jit(solution)/shard_map/ppermute | solution.py:28
  138.9 0.0 collective-permute-done.13
  138.9 0.0 copy-done.4
  138.9 1.3 collective-permute-start.14
  140.2 2.0 collective-permute-done.7
  142.2 6.9 %collective-permute-start.8 = (bf16[2,192,384]{2,1,0:T(8,128)(2,1)}, bf16[2,192,384]{2,1,0:T(8,128)(2,1)}, u32[]{:S(2)}, u32[]{:S(2)}) collective-permute-start(bf16[2,192,384]{2,1,0:T(8,128)(2,1)} %collective-permute-done.7), channel_id=1, source_target_pairs={{0,64},{64,128},{128,192},{192,256},{256,320},{320,384},{384,448},... | collective-permute-start | bytes 884744 | tf_op jit(solution)/shard_map/ppermute | solution.py:28
  149.1 3.0 %collective-permute-done.14 = bf16[2,192,384]{2,1,0:T(8,128)(2,1)S(1)} collective-permute-done((bf16[2,192,384]{2,1,0:T(8,128)(2,1)S(1)}, bf16[2,192,384]{2,1,0:T(8,128)(2,1)S(1)}, u32[]{:S(2)}, u32[]{:S(2)}) %collective-permute-start.14) | collective-permute-done | bytes 294944 | tf_op jit(solution)/shard_map/ppermute | solution.py:29
  152.1 1.3 collective-permute-start.15
  153.4 0.0 collective-permute-done.8
  153.4 1.0 bitcast_dynamic-update-slice_fusion.14
  154.4 1.0 bitcast_dynamic-update-slice_fusion.13
  155.4 1.0 bitcast_dynamic-update-slice_fusion.12
  156.7 0.0 copy-done.1
  157.1 3.0 %collective-permute-done.15 = bf16[2,192,384]{2,1,0:T(8,128)(2,1)S(1)} collective-permute-done((bf16[2,192,384]{2,1,0:T(8,128)(2,1)S(1)}, bf16[2,192,384]{2,1,0:T(8,128)(2,1)S(1)}, u32[]{:S(2)}, u32[]{:S(2)}) %collective-permute-start.15) | collective-permute-done | bytes 294944 | tf_op jit(solution)/shard_map/ppermute | solution.py:29
  160.1 2.0 copy-done
  162.2 0.2 constant_dynamic-slice_fusion.2
  162.4 5.5 %collective-permute-start.16 = (bf16[8,2,192,384]{3,2,1,0:T(8,128)(2,1)S(1)}, bf16[8,2,192,384]{3,2,1,0:T(8,128)(2,1)}, u32[]{:S(2)}, u32[]{:S(2)}) collective-permute-start(bf16[8,2,192,384]{3,2,1,0:T(8,128)(2,1)S(1)} %constant_dynamic-slice_fusion.2), channel_id=1, source_target_pairs={{0,32},{32,0},{1,33},{33,1},{2,34},{34,2},{3,35},{35,3},{4,36},{36... | collective-permute-start | bytes 7077896 | tf_op jit(solution)/shard_map/ppermute | solution.py:34
  167.9 1.9 fusion.11
  169.8 2.1 collective-permute-done.16
  172.0 3.4 %maximum_select_fusion = bf16[8,2,2,192,384]{4,3,2,0,1:T(8,128)(2,1)S(1)} fusion(bf16[8,1,2,192,384]{4,3,2,0,1:T(8,128)(2,1)} %bitcast.19, bf16[8,1,2,192,384]{4,3,2,0,1:T(8,128)(2,1)S(1)} %fusion.11, pred[]{:T(512)S(6)} %eq.12), kind=kLoop, calls=%fused_computation | loop fusion | flops 7077888 | bytes 9437185 | tf_op jit(solution)/shard_map/jit(_where)/select_n | solution.py:35
  175.4 2.6 %copy.19 = bf16[8,2,2,192,384]{4,3,2,1,0:T(8,128)(2,1)} copy(bf16[8,2,2,192,384]{4,3,2,0,1:T(8,128)(2,1)S(1)} %maximum_select_fusion) | data formatting | bytes 9437184 | tf_op jit(solution)/shard_map/jit(_where)/select_n | solution.py:35
  178.0 14.3 %select_n.65 = bf16[16,2,192,2,192]{4,3,2,1,0:T(2,128)(2,1)} reshape(bf16[8,2,2,192,384]{4,3,2,1,0:T(8,128)(2,1)} %copy.19) | data formatting | bytes 9437184 | tf_op jit(solution)/shard_map/jit(_where)/select_n | solution.py:35
  192.3 10.8 %constant_dynamic-slice_fusion.1 = (bf16[8,2,192,2,192]{4,3,2,1,0:T(2,128)(2,1)}, bf16[8,2,192,2,192]{4,3,2,1,0:T(2,128)(2,1)S(1)}) fusion(bf16[16,2,192,2,192]{4,3,2,1,0:T(2,128)(2,1)} %select_n.65, s32[]{:T(128)S(6)} %select_n.66, s32[]{:T(128)S(6)} %select_n.67), kind=kLoop, calls=%fused_computation.37 | loop fusion | bytes 9437192 | tf_op jit(solution)/shard_map/dynamic_slice | solution.py:72
  203.0 6.4 %fusion.2 = f32[2,384,2,192,1,1]{1,3,4,2,0,5:T(8,128)} fusion(bf16[8,2,2,192,384,1]{4,3,2,1,0,5:T(8,128)(2,1)} %bitcast.69, bf16[8,2,192,2,192]{4,3,2,1,0:T(2,128)(2,1)} %get-tuple-element.5), kind=kOutput, calls=%fused_computation.3 | convolution fusion | flops 1811939328 | bytes 8257536 | tf_op jit(solution)/shard_map/jpxhr,jhqrn->pqxn/dot_general | solution.py:79
  209.4 4.7 %fusion = f32[2,384,2,192,1,1]{1,3,4,2,0,5:T(8,128)S(1)} fusion(bf16[8,2,2,192,384,1]{4,3,2,1,0,5:T(8,128)(2,1)} %bitcast.70, bf16[8,2,192,2,192]{4,3,2,1,0:T(2,128)(2,1)S(1)} %get-tuple-element.6), kind=kOutput, calls=%fused_computation.1 | convolution fusion | flops 1811939328 | bytes 8257536 | tf_op jit(solution)/shard_map/jpxhr,jhqrn->pqxn/dot_general | solution.py:79
  214.1 0.1 fusion.4
  214.2 0.1 fusion.10
  214.3 0.9 pad_maximum_fusion
  (19 shorter events, 0.6 us)
Async XLA Ops:
  6.5 196.5 %all-gather.5.cloned.1.call-start = ((), (), s32[]{:S(2)}) async-start(), calls=%async_computation | async-start | bytes 5013504 | tf_op jit(solution)/shard_map/all_gather | solution.py:65
  7.9 11.7 %collective-permute-start = (bf16[2,192,192]{1,2,0:T(8,128)(2,1)S(1)}, bf16[2,192,192]{1,2,0:T(8,128)(2,1)S(1)}, u32[]{:S(2)}, u32[]{:S(2)}) collective-permute-start(bf16[2,192,192]{1,2,0:T(8,128)(2,1)S(1)} %copy.34), channel_id=1, source_target_pairs={{0,0},{32,2},{64,4},{96,6},{128,8},{160,10},{192,12},{224,14},{256... | collective-permute-start | bytes 442376 | tf_op jit(solution)/shard_map/ppermute | solution.py:56
  14.1 10.5 %collective-permute-start.1 = (bf16[2,192,192]{1,2,0:T(8,128)(2,1)S(1)}, bf16[2,192,192]{1,2,0:T(8,128)(2,1)S(1)}, u32[]{:S(2)}, u32[]{:S(2)}) collective-permute-start(bf16[2,192,192]{1,2,0:T(8,128)(2,1)S(1)} %copy.35), channel_id=1, source_target_pairs={{0,1},{32,3},{64,5},{96,7},{128,9},{160,11},{192,13},{224,15},{256... | collective-permute-start | bytes 442376 | tf_op jit(solution)/shard_map/ppermute | solution.py:56
  26.5 130.2 %copy-start.1 = (bf16[2,192,384]{2,1,0:T(8,128)(2,1)S(1)}, bf16[2,192,384]{2,1,0:T(8,128)(2,1)}, u32[]{:S(2)}) copy-start(bf16[2,192,384]{2,1,0:T(8,128)(2,1)} %fusion.6) | copy-start | bytes 884740
  26.5 182.9 %all-gather.7.cloned.1.call-start = ((), (), s32[]{:S(2)}) async-start(), calls=%async_computation.1 | async-start | bytes 5013504 | tf_op jit(solution)/shard_map/all_gather | solution.py:66
  26.6 23.9 %collective-permute-start.2 = (bf16[2,192,384]{2,1,0:T(8,128)(2,1)}, bf16[2,192,384]{2,1,0:T(8,128)(2,1)S(1)}, u32[]{:S(2)}, u32[]{:S(2)}) collective-permute-start(bf16[2,192,384]{2,1,0:T(8,128)(2,1)} %fusion.6), channel_id=1, source_target_pairs={{0,64},{64,128},{128,192},{192,256},{256,320},{320,384},{384,448},... | collective-permute-start | bytes 884744 | tf_op jit(solution)/shard_map/ppermute | solution.py:28
  44.1 10.4 %collective-permute-start.9 = (bf16[2,192,384]{2,1,0:T(8,128)(2,1)}, bf16[2,192,384]{2,1,0:T(8,128)(2,1)S(1)}, u32[]{:S(2)}, u32[]{:S(2)}) collective-permute-start(bf16[2,192,384]{2,1,0:T(8,128)(2,1)} %fusion.6), channel_id=1, source_target_pairs={{64,0},{128,64},{192,128},{256,192},{320,256},{384,320},{448,384},... | collective-permute-start | bytes 884744 | tf_op jit(solution)/shard_map/ppermute | solution.py:29
  50.5 10.6 %collective-permute-start.3 = (bf16[2,192,384]{2,1,0:T(8,128)(2,1)S(1)}, bf16[2,192,384]{2,1,0:T(8,128)(2,1)S(1)}, u32[]{:S(2)}, u32[]{:S(2)}) collective-permute-start(bf16[2,192,384]{2,1,0:T(8,128)(2,1)S(1)} %collective-permute-done.2), channel_id=1, source_target_pairs={{0,64},{64,128},{128,192},{192,256},{256,320},{320,384},{384,448},... | collective-permute-start | bytes 884744 | tf_op jit(solution)/shard_map/ppermute | solution.py:28
  54.5 31.2 %collective-permute-start.10 = (bf16[2,192,384]{2,1,0:T(8,128)(2,1)S(1)}, bf16[2,192,384]{2,1,0:T(8,128)(2,1)S(1)}, u32[]{:S(2)}, u32[]{:S(2)}) collective-permute-start(bf16[2,192,384]{2,1,0:T(8,128)(2,1)S(1)} %collective-permute-done.9), channel_id=1, source_target_pairs={{64,0},{128,64},{192,128},{256,192},{320,256},{384,320},{448,384},... | collective-permute-start | bytes 884744 | tf_op jit(solution)/shard_map/ppermute | solution.py:29
  61.1 25.9 %collective-permute-start.4 = (bf16[2,192,384]{2,1,0:T(8,128)(2,1)S(1)}, bf16[2,192,384]{2,1,0:T(8,128)(2,1)S(1)}, u32[]{:S(2)}, u32[]{:S(2)}) collective-permute-start(bf16[2,192,384]{2,1,0:T(8,128)(2,1)S(1)} %collective-permute-done.3), channel_id=1, source_target_pairs={{0,64},{64,128},{128,192},{192,256},{256,320},{320,384},{384,448},... | collective-permute-start | bytes 884744 | tf_op jit(solution)/shard_map/ppermute | solution.py:28
  65.2 31.1 %collective-permute-start.17 = (bf16[2,192,384]{2,1,0:T(8,128)(2,1)}, bf16[2,192,384]{2,1,0:T(8,128)(2,1)S(1)}, u32[]{:S(2)}, u32[]{:S(2)}) collective-permute-start(bf16[2,192,384]{2,1,0:T(8,128)(2,1)} %fusion.6), channel_id=1, source_target_pairs={{0,16},{16,0},{1,17},{17,1},{2,18},{18,2},{3,19},{19,3},{4,20},{20... | collective-permute-start | bytes 884744 | tf_op jit(solution)/shard_map/ppermute | solution.py:64
  85.7 31.7 %collective-permute-start.11 = (bf16[2,192,384]{2,1,0:T(8,128)(2,1)S(1)}, bf16[2,192,384]{2,1,0:T(8,128)(2,1)S(1)}, u32[]{:S(2)}, u32[]{:S(2)}) collective-permute-start(bf16[2,192,384]{2,1,0:T(8,128)(2,1)S(1)} %collective-permute-done.10), channel_id=1, source_target_pairs={{64,0},{128,64},{192,128},{256,192},{320,256},{384,320},{448,384},... | collective-permute-start | bytes 884744 | tf_op jit(solution)/shard_map/ppermute | solution.py:29
  87.0 34.8 %collective-permute-start.5 = (bf16[2,192,384]{2,1,0:T(8,128)(2,1)S(1)}, bf16[2,192,384]{2,1,0:T(8,128)(2,1)S(1)}, u32[]{:S(2)}, u32[]{:S(2)}) collective-permute-start(bf16[2,192,384]{2,1,0:T(8,128)(2,1)S(1)} %collective-permute-done.4), channel_id=1, source_target_pairs={{0,64},{64,128},{128,192},{192,256},{256,320},{320,384},{384,448},... | collective-permute-start | bytes 884744 | tf_op jit(solution)/shard_map/ppermute | solution.py:28
  96.3 0.7 copy-start.3
  117.4 11.5 %collective-permute-start.12 = (bf16[2,192,384]{2,1,0:T(8,128)(2,1)S(1)}, bf16[2,192,384]{2,1,0:T(8,128)(2,1)S(1)}, u32[]{:S(2)}, u32[]{:S(2)}) collective-permute-start(bf16[2,192,384]{2,1,0:T(8,128)(2,1)S(1)} %collective-permute-done.11), channel_id=1, source_target_pairs={{64,0},{128,64},{192,128},{256,192},{320,256},{384,320},{448,384},... | collective-permute-start | bytes 884744 | tf_op jit(solution)/shard_map/ppermute | solution.py:29
  121.8 8.4 %collective-permute-start.6 = (bf16[2,192,384]{2,1,0:T(8,128)(2,1)S(1)}, bf16[2,192,384]{2,1,0:T(8,128)(2,1)S(1)}, u32[]{:S(2)}, u32[]{:S(2)}) collective-permute-start(bf16[2,192,384]{2,1,0:T(8,128)(2,1)S(1)} %collective-permute-done.5), channel_id=1, source_target_pairs={{0,64},{64,128},{128,192},{192,256},{256,320},{320,384},{384,448},... | collective-permute-start | bytes 884744 | tf_op jit(solution)/shard_map/ppermute | solution.py:28
  129.0 9.9 %collective-permute-start.13 = (bf16[2,192,384]{2,1,0:T(8,128)(2,1)S(1)}, bf16[2,192,384]{2,1,0:T(8,128)(2,1)S(1)}, u32[]{:S(2)}, u32[]{:S(2)}) collective-permute-start(bf16[2,192,384]{2,1,0:T(8,128)(2,1)S(1)} %collective-permute-done.12), channel_id=1, source_target_pairs={{64,0},{128,64},{192,128},{256,192},{320,256},{384,320},{448,384},... | collective-permute-start | bytes 884744 | tf_op jit(solution)/shard_map/ppermute | solution.py:29
  130.3 8.6 %copy-start.4 = (bf16[2,192,384]{2,1,0:T(8,128)(2,1)}, bf16[2,192,384]{2,1,0:T(8,128)(2,1)S(1)}, u32[]{:S(2)}) copy-start(bf16[2,192,384]{2,1,0:T(8,128)(2,1)S(1)} %collective-permute-done.6) | copy-start | bytes 884740
  130.3 11.9 %collective-permute-start.7 = (bf16[2,192,384]{2,1,0:T(8,128)(2,1)S(1)}, bf16[2,192,384]{2,1,0:T(8,128)(2,1)}, u32[]{:S(2)}, u32[]{:S(2)}) collective-permute-start(bf16[2,192,384]{2,1,0:T(8,128)(2,1)S(1)} %collective-permute-done.6), channel_id=1, source_target_pairs={{0,64},{64,128},{128,192},{192,256},{256,320},{320,384},{384,448},... | collective-permute-start | bytes 884744 | tf_op jit(solution)/shard_map/ppermute | solution.py:28
  138.9 13.2 %collective-permute-start.14 = (bf16[2,192,384]{2,1,0:T(8,128)(2,1)S(1)}, bf16[2,192,384]{2,1,0:T(8,128)(2,1)S(1)}, u32[]{:S(2)}, u32[]{:S(2)}) collective-permute-start(bf16[2,192,384]{2,1,0:T(8,128)(2,1)S(1)} %collective-permute-done.13), channel_id=1, source_target_pairs={{64,0},{128,64},{192,128},{256,192},{320,256},{384,320},{448,384},... | collective-permute-start | bytes 884744 | tf_op jit(solution)/shard_map/ppermute | solution.py:29
  142.2 11.2 %collective-permute-start.8 = (bf16[2,192,384]{2,1,0:T(8,128)(2,1)}, bf16[2,192,384]{2,1,0:T(8,128)(2,1)}, u32[]{:S(2)}, u32[]{:S(2)}) collective-permute-start(bf16[2,192,384]{2,1,0:T(8,128)(2,1)} %collective-permute-done.7), channel_id=1, source_target_pairs={{0,64},{64,128},{128,192},{192,256},{256,320},{320,384},{384,448},... | collective-permute-start | bytes 884744 | tf_op jit(solution)/shard_map/ppermute | solution.py:28
  152.1 8.0 %collective-permute-start.15 = (bf16[2,192,384]{2,1,0:T(8,128)(2,1)S(1)}, bf16[2,192,384]{2,1,0:T(8,128)(2,1)S(1)}, u32[]{:S(2)}, u32[]{:S(2)}) collective-permute-start(bf16[2,192,384]{2,1,0:T(8,128)(2,1)S(1)} %collective-permute-done.14), channel_id=1, source_target_pairs={{64,0},{128,64},{192,128},{256,192},{320,256},{384,320},{448,384},... | collective-permute-start | bytes 884744 | tf_op jit(solution)/shard_map/ppermute | solution.py:29
  160.1 2.0 copy-start
  162.4 9.6 %collective-permute-start.16 = (bf16[8,2,192,384]{3,2,1,0:T(8,128)(2,1)S(1)}, bf16[8,2,192,384]{3,2,1,0:T(8,128)(2,1)}, u32[]{:S(2)}, u32[]{:S(2)}) collective-permute-start(bf16[8,2,192,384]{3,2,1,0:T(8,128)(2,1)S(1)} %constant_dynamic-slice_fusion.2), channel_id=1, source_target_pairs={{0,32},{32,0},{1,33},{33,1},{2,34},{34,2},{3,35},{35,3},{4,36},{36... | collective-permute-start | bytes 7077896 | tf_op jit(solution)/shard_map/ppermute | solution.py:34
  209.4 4.7 %copy-start.2 = (f32[2,384,2,192,1,1]{1,3,4,2,0,5:T(8,128)S(1)}, f32[2,384,2,192,1,1]{1,3,4,2,0,5:T(8,128)}, u32[]{:S(2)}) copy-start(f32[2,384,2,192,1,1]{1,3,4,2,0,5:T(8,128)} %fusion.2) | copy-start | bytes 3538948
Sparse Core Ops, SparseCore 0:
  26.6 101.0 all-gather.4
  130.7 69.1 all-gather.6

commit v4 on v3

v4 whole, which is shorter than its diff:
```python
import math

import jax
import jax.numpy as jnp
from jax import lax
from jax.sharding import Mesh
from jax.sharding import PartitionSpec as P

N = 6144


def mirror_pairs(n_recv, n_shot, flip):
    pairs = []
    for i in range(n_recv):
        for j in range(n_shot):
            h = (i % 2) ^ flip
            pairs.append((j * n_recv + i, (i // 2) * n_recv + 2 * j + h))
    return pairs


def gather_line(block):
    n_line = lax.axis_size("zl")
    line_index = lax.axis_index("zl")
    from_left, from_right = [], []
    rightward, leftward = block, block
    for _ in range(n_line - 1):
        rightward = lax.ppermute(rightward, "zl", [(k, k + 1) for k in range(n_line - 1)])
        leftward = lax.ppermute(leftward, "zl", [(k + 1, k) for k in range(n_line - 1)])
        from_left.append(rightward)
        from_right.append(leftward)
    sequence = jnp.stack(from_left[::-1] + [block] + from_right)
    mine = lax.dynamic_slice_in_dim(sequence, n_line - 1 - line_index, n_line, 0)
    other = lax.ppermute(mine, "core", [(0, 1), (1, 0)])
    return mine, other


def gather_plane(block):
    n_y = lax.axis_size("y")
    n_x = lax.axis_size("x")
    rows = []
    for dy in range(n_y):
        row = []
        for dx in range(n_x):
            if dy == 0 and dx == 0:
                row.append(block)
                continue
            pairs = [
                (y * n_x + x, ((y - dy) % n_y) * n_x + (x - dx) % n_x)
                for y in range(n_y)
                for x in range(n_x)
            ]
            row.append(lax.ppermute(block, ("y", "x"), pairs))
        rows.append(jnp.stack(row))
    relative = jnp.stack(rows)
    placed = jnp.roll(relative, (lax.axis_index("y"), lax.axis_index("x")), axis=(0, 1))
    return placed.reshape((n_y * n_x,) + block.shape)


def local(pressure):
    n_shot = lax.axis_size("zl") * lax.axis_size("core")
    n_half = lax.axis_size("y") * lax.axis_size("x")
    n_recv = 2 * n_half
    block_rows = pressure.shape[1]
    shot_index = lax.axis_index("zl") * lax.axis_size("core") + lax.axis_index("core")
    half_index = lax.axis_index("zh")
    recv_index = half_index * n_half + lax.axis_index("y") * lax.axis_size("x") + lax.axis_index("x")
    parity = recv_index % 2
    axes = ("zl", "core", "zh", "y", "x")

    arrived = []
    for flip in range(2):
        sent_half = (parity + flip) % 2
        piece = lax.dynamic_slice_in_dim(pressure, sent_half * block_rows, block_rows, 2)
        arrived.append(lax.ppermute(piece, axes, mirror_pairs(n_recv, n_shot, flip)))
    upper = jnp.where(parity == 0, arrived[0], arrived[1])
    lower = jnp.where(parity == 0, arrived[1], arrived[0])
    mirror = jnp.concatenate([upper, lower], axis=1)
    symmetric = (
        (pressure.astype(jnp.float32) + jnp.swapaxes(mirror, 1, 2).astype(jnp.float32)) * 0.5
    ).astype(jnp.bfloat16)

    partner_block = lax.ppermute(symmetric, "zh", [(0, 1), (1, 0)])
    own_panel = gather_plane(symmetric)
    partner_panel = gather_plane(partner_block)
    mine, other = gather_line(symmetric)
    core_index = lax.axis_index("core")
    n_line = mine.shape[0]
    parts, rows, cols = symmetric.shape

    def product(left, panel, parity):
        panel = panel.reshape(n_line // 2, 2, 2, parts, rows, cols)
        panel = lax.dynamic_index_in_dim(panel, parity, 1, keepdims=False)
        panel = jnp.swapaxes(panel, 1, 2).reshape(n_line // 2, parts, 2 * rows, cols)
        return jnp.einsum("zpxc,zqcn->pqxn", left, panel, preferred_element_type=jnp.float32)

    quarter = n_line // 2
    own_start = half_index * quarter
    other_start = (1 - half_index) * quarter
    terms = (
        product(lax.dynamic_slice_in_dim(mine, own_start, quarter, 0), own_panel, core_index)
        + product(lax.dynamic_slice_in_dim(other, own_start, quarter, 0), own_panel, 1 - core_index)
        + product(lax.dynamic_slice_in_dim(mine, other_start, quarter, 0), partner_panel, core_index)
        + product(lax.dynamic_slice_in_dim(other, other_start, quarter, 0), partner_panel, 1 - core_index)
    )
    factor = 1.0 / math.sqrt(N)
    real = (terms[0, 0] - terms[1, 1]) * factor
    imag = (terms[0, 1] + terms[1, 0]) * factor
    return jnp.stack([real, imag])


def solution(mesh):
    n_shot, n_recv = mesh.devices.shape
    n_x = 4
    split = Mesh(
        mesh.devices.reshape(n_shot // 2, 2, 2, n_recv // (2 * n_x), n_x),
        ("zl", "core", "zh", "y", "x"),
    )
    placed = P(None, ("zh", "y", "x"), ("zl", "core"))
    return jax.shard_map(local, mesh=split, in_specs=(placed,), out_specs=placed, check_vma=False)
```

time: 225 us -> 316 us (1.40)
  starting transfers between devices: 98.5 us -> 235 us
  local copies, waits for them, and re-layouts: 37.7 us -> 9.32 us
  other arithmetic: 6.31 us -> 19.3 us
  between operations: 13.8 us -> 1.27 us
  waiting for transfers between devices: 54.7 us -> 45.1 us
  matrix products: 11 us -> 4.57 us
    ppermute x0 -> x30, starting transfers between devices: none -> 124 us  [gather_plane(): row.append(lax.ppermute(block, ('y', 'x'), pairs))]
    ppermute x0 -> x30, waiting for transfers between devices: none -> 33.2 us  [gather_plane(): row.append(lax.ppermute(block, ('y', 'x'), pairs))]
    ppermute x1, starting transfers between devices: 20.5 us -> 49.2 us  [local(): partner_block = lax.ppermute(symmetric, 'zh', [(0, 1), (1, 0)])]
    ppermute x7, waiting for transfers between devices: 29 us -> 3.9 us  [gather_line(): lax.ppermute(leftward, 'zl', [(k + 1, k) for k in range(n_line - 1)])]
    select_n x2 -> x0, local copies, waits for them, and re-layouts: 16.9 us -> none  [gather_line(): jnp.where(core_index == 0, jnp.stack([mine, other], axis=1), jnp.stack([o...]
    concatenate x0 -> x3, other arithmetic: none -> 15.5 us  [gather_plane(): jnp.roll(relative, (lax.axis_index('y'), lax.axis_index('x')), axis=(0, 1))]
    ppermute x7, waiting for transfers between devices: 15.5 us -> 0.02 us  [gather_line(): lax.ppermute(rightward, 'zl', [(k, k + 1) for k in range(n_line - 1)])]
    ppermute x7, starting transfers between devices: 54.9 us -> 40.4 us  [gather_line(): lax.ppermute(rightward, 'zl', [(k, k + 1) for k in range(n_line - 1)])]
  transfers between devices with their start and end apart: 20 -> 48, of which waited for: 11 -> 8; matrix products, arithmetic and copies ran while one was open for 20% -> 8% of each run, Pallas kernels for 0% -> 0%
where the time goes in v4:
time: 316 us; the launch traced here: 314 us
  starting transfers between devices  235 us (74%)
  waiting for transfers between devices  45.1 us (14%)
  other arithmetic  19.3 us (6%)
  local copies, waits for them, and re-layouts  9.32 us (3%)
  matrix products  4.57 us (1%)
    ppermute x30, starting transfers between devices, gather_plane(): row.append(lax.ppermute(block, ('y', 'x'), pairs))  124 us
    ppermute x1, starting transfers between devices, local(): partner_block = lax.ppermute(symmetric, 'zh', [(0, 1), (1, 0)])  49.2 us
    ppermute x7, starting transfers between devices, gather_line(): lax.ppermute(rightward, 'zl', [(k, k + 1) for k in range(n_line - 1)])  40.4 us
    ppermute x30, waiting for transfers between devices, gather_plane(): row.append(lax.ppermute(block, ('y', 'x'), pairs))  33.2 us
    concatenate x3, other arithmetic, gather_plane(): jnp.roll(relative, (lax.axis_index('y'), lax.axis_index('x')), axis=(0, 1))  15.5 us
    ppermute x7, starting transfers between devices, gather_line(): lax.ppermute(leftward, 'zl', [(k + 1, k) for k in range(n_line - 1)])  9.18 us
    ppermute x2, starting transfers between devices, local(): lax.ppermute(piece, axes, mirror_pairs(n_recv, n_shot, flip))  8.56 us
    ppermute x2, waiting for transfers between devices, local(): lax.ppermute(piece, axes, mirror_pairs(n_recv, n_shot, flip))  8 us
  transfers between devices with their start and end apart: 48, of which 8 were waited for; matrix products, arithmetic and copies ran while one was open for 8% of the time, Pallas kernels for 0%

profile of v4, /device:TPU:1, one launch (start us, length us, event | category | flops | bytes accessed | tf_op | source)
XLA Modules:
  0.0 314.1 jit_solution(18382397841701153370)
XLA Ops:
  0.0 1.2 constant_dynamic-slice_fusion.6
  1.4 6.0 %collective-permute-start = (bf16[2,192,192]{1,2,0:T(8,128)(2,1)S(1)}, bf16[2,192,192]{1,2,0:T(8,128)(2,1)S(1)}, u32[]{:S(2)}, u32[]{:S(2)}) collective-permute-start(bf16[2,192,192]{1,2,0:T(8,128)(2,1)S(1)} %copy.33), channel_id=1, source_target_pairs={{0,0},{32,2},{64,4},{96,6},{128,8},{160,10},{192,12},{224,14},{256... | collective-permute-start | bytes 442376 | tf_op jit(solution)/shard_map/ppermute | solution.py:74
  7.6 2.5 collective-permute-start.1
  10.1 3.0 collective-permute-done
  13.1 5.0 %collective-permute-done.1 = bf16[2,192,192]{1,2,0:T(8,128)(2,1)S(1)} collective-permute-done((bf16[2,192,192]{1,2,0:T(8,128)(2,1)S(1)}, bf16[2,192,192]{1,2,0:T(8,128)(2,1)S(1)}, u32[]{:S(2)}, u32[]{:S(2)}) %collective-permute-start.1) | collective-permute-done | bytes 147488 | tf_op jit(solution)/shard_map/ppermute | solution.py:74
  18.3 49.2 %collective-permute-start.32 = (bf16[2,192,384]{2,1,0:T(8,128)(2,1)S(1)}, bf16[2,192,384]{2,1,0:T(8,128)(2,1)S(1)}, u32[]{:S(2)}, u32[]{:S(2)}) collective-permute-start(bf16[2,192,384]{2,1,0:T(8,128)(2,1)S(1)} %fusion.29), channel_id=1, source_target_pairs={{0,16},{16,0},{1,17},{17,1},{2,18},{18,2},{3,19},{19,3},{4,20},{20... | collective-permute-start | bytes 884744 | tf_op jit(solution)/shard_map/ppermute | solution.py:82
  67.5 2.6 collective-permute-start.4
  70.1 3.7 %collective-permute-start.3 = (bf16[2,192,384]{2,1,0:T(8,128)(2,1)S(1)}, bf16[2,192,384]{2,1,0:T(8,128)(2,1)S(1)}, u32[]{:S(2)}, u32[]{:S(2)}) collective-permute-start(bf16[2,192,384]{2,1,0:T(8,128)(2,1)S(1)} %fusion.29), channel_id=1, source_target_pairs={{0,2},{1,3},{2,0},{3,1},{4,6},{5,7},{6,4},{7,5},{8,10},{9,11},{10,... | collective-permute-start | bytes 884744 | tf_op jit(solution)/shard_map/ppermute | solution.py:52
  73.8 3.0 collective-permute-start.2
  76.8 7.5 %collective-permute-start.8 = (bf16[2,192,384]{2,1,0:T(8,128)(2,1)S(1)}, bf16[2,192,384]{2,1,0:T(8,128)(2,1)S(1)}, u32[]{:S(2)}, u32[]{:S(2)}) collective-permute-start(bf16[2,192,384]{2,1,0:T(8,128)(2,1)S(1)} %fusion.29), channel_id=1, source_target_pairs={{0,13},{1,14},{2,15},{3,12},{4,1},{5,2},{6,3},{7,0},{8,5},{9,6},{1... | collective-permute-start | bytes 884744 | tf_op jit(solution)/shard_map/ppermute | solution.py:52
  84.3 3.7 %collective-permute-start.7 = (bf16[2,192,384]{2,1,0:T(8,128)(2,1)S(1)}, bf16[2,192,384]{2,1,0:T(8,128)(2,1)S(1)}, u32[]{:S(2)}, u32[]{:S(2)}) collective-permute-start(bf16[2,192,384]{2,1,0:T(8,128)(2,1)S(1)} %fusion.29), channel_id=1, source_target_pairs={{0,14},{1,15},{2,12},{3,13},{4,2},{5,3},{6,0},{7,1},{8,6},{9,7},{1... | collective-permute-start | bytes 884744 | tf_op jit(solution)/shard_map/ppermute | solution.py:52
  88.0 4.9 %collective-permute-start.6 = (bf16[2,192,384]{2,1,0:T(8,128)(2,1)S(1)}, bf16[2,192,384]{2,1,0:T(8,128)(2,1)S(1)}, u32[]{:S(2)}, u32[]{:S(2)}) collective-permute-start(bf16[2,192,384]{2,1,0:T(8,128)(2,1)S(1)} %fusion.29), channel_id=1, source_target_pairs={{0,15},{1,12},{2,13},{3,14},{4,3},{5,0},{6,1},{7,2},{8,7},{9,4},{1... | collective-permute-start | bytes 884744 | tf_op jit(solution)/shard_map/ppermute | solution.py:52
  93.0 2.8 collective-permute-start.5
  95.8 2.2 collective-permute-start.12
  98.0 4.9 %collective-permute-start.11 = (bf16[2,192,384]{2,1,0:T(8,128)(2,1)S(1)}, bf16[2,192,384]{2,1,0:T(8,128)(2,1)S(1)}, u32[]{:S(2)}, u32[]{:S(2)}) collective-permute-start(bf16[2,192,384]{2,1,0:T(8,128)(2,1)S(1)} %fusion.29), channel_id=1, source_target_pairs={{0,10},{1,11},{2,8},{3,9},{4,14},{5,15},{6,12},{7,13},{8,2},{9,3},... | collective-permute-start | bytes 884744 | tf_op jit(solution)/shard_map/ppermute | solution.py:52
  102.8 4.9 %collective-permute-start.10 = (bf16[2,192,384]{2,1,0:T(8,128)(2,1)S(1)}, bf16[2,192,384]{2,1,0:T(8,128)(2,1)S(1)}, u32[]{:S(2)}, u32[]{:S(2)}) collective-permute-start(bf16[2,192,384]{2,1,0:T(8,128)(2,1)S(1)} %fusion.29), channel_id=1, source_target_pairs={{0,11},{1,8},{2,9},{3,10},{4,15},{5,12},{6,13},{7,14},{8,3},{9,0},... | collective-permute-start | bytes 884744 | tf_op jit(solution)/shard_map/ppermute | solution.py:52
  107.8 8.1 %collective-permute-start.9 = (bf16[2,192,384]{2,1,0:T(8,128)(2,1)S(1)}, bf16[2,192,384]{2,1,0:T(8,128)(2,1)S(1)}, u32[]{:S(2)}, u32[]{:S(2)}) collective-permute-start(bf16[2,192,384]{2,1,0:T(8,128)(2,1)S(1)} %fusion.29), channel_id=1, source_target_pairs={{0,8},{1,9},{2,10},{3,11},{4,12},{5,13},{6,14},{7,15},{8,0},{9,1},... | collective-permute-start | bytes 884744 | tf_op jit(solution)/shard_map/ppermute | solution.py:52
  115.9 21.0 %collective-permute-done.5 = bf16[2,192,384]{2,1,0:T(8,128)(2,1)S(1)} collective-permute-done((bf16[2,192,384]{2,1,0:T(8,128)(2,1)S(1)}, bf16[2,192,384]{2,1,0:T(8,128)(2,1)S(1)}, u32[]{:S(2)}, u32[]{:S(2)}) %collective-permute-start.5) | collective-permute-done | bytes 294944 | tf_op jit(solution)/shard_map/ppermute | solution.py:52
  136.9 1.9 collective-permute-start.16
  138.8 14.2 %collective-permute-start.17 = (bf16[2,192,384]{2,1,0:T(8,128)(2,1)S(1)}, bf16[2,192,384]{2,1,0:T(8,128)(2,1)S(1)}, u32[]{:S(2)}, u32[]{:S(2)}) collective-permute-start(bf16[2,192,384]{2,1,0:T(8,128)(2,1)S(1)} %fusion.29), channel_id=1, source_target_pairs={{0,64},{64,128},{128,192},{192,256},{256,320},{320,384},{384,448},... | collective-permute-start | bytes 884744 | tf_op jit(solution)/shard_map/ppermute | solution.py:27
  153.0 1.9 collective-permute-start.15
  155.0 8.5 %collective-permute-start.14 = (bf16[2,192,384]{2,1,0:T(8,128)(2,1)S(1)}, bf16[2,192,384]{2,1,0:T(8,128)(2,1)S(1)}, u32[]{:S(2)}, u32[]{:S(2)}) collective-permute-start(bf16[2,192,384]{2,1,0:T(8,128)(2,1)S(1)} %fusion.29), channel_id=1, source_target_pairs={{0,7},{1,4},{2,5},{3,6},{4,11},{5,8},{6,9},{7,10},{8,15},{9,12},{1... | collective-permute-start | bytes 884744 | tf_op jit(solution)/shard_map/ppermute | solution.py:52
  163.5 1.9 collective-permute-start.13
  165.4 1.3 collective-permute-start.24
  166.8 4.0 %collective-permute-start.18 = (bf16[2,192,384]{2,1,0:T(8,128)(2,1)S(1)}, bf16[2,192,384]{2,1,0:T(8,128)(2,1)S(1)}, u32[]{:S(2)}, u32[]{:S(2)}) collective-permute-start(bf16[2,192,384]{2,1,0:T(8,128)(2,1)S(1)} %collective-permute-done.17), channel_id=1, source_target_pairs={{0,64},{64,128},{128,192},{192,256},{256,320},{320,384},{384,448},... | collective-permute-start | bytes 884744 | tf_op jit(solution)/shard_map/ppermute | solution.py:27
  170.8 2.3 collective-permute-start.35
  173.1 3.4 %collective-permute-start.34 = (bf16[2,192,384]{2,1,0:T(8,128)(2,1)S(1)}, bf16[2,192,384]{2,1,0:T(8,128)(2,1)S(1)}, u32[]{:S(2)}, u32[]{:S(2)}) collective-permute-start(bf16[2,192,384]{2,1,0:T(8,128)(2,1)S(1)} %collective-permute-done.32), channel_id=1, source_target_pairs={{0,2},{1,3},{2,0},{3,1},{4,6},{5,7},{6,4},{7,5},{8,10},{9,11},{10,... | collective-permute-start | bytes 884744 | tf_op jit(solution)/shard_map/ppermute | solution.py:52
  176.6 3.6 %collective-permute-done.13 = bf16[2,192,384]{2,1,0:T(8,128)(2,1)S(1)} collective-permute-done((bf16[2,192,384]{2,1,0:T(8,128)(2,1)S(1)}, bf16[2,192,384]{2,1,0:T(8,128)(2,1)S(1)}, u32[]{:S(2)}, u32[]{:S(2)}) %collective-permute-start.13) | collective-permute-done | bytes 294944 | tf_op jit(solution)/shard_map/ppermute | solution.py:52
  180.1 2.1 collective-permute-start.33
  182.2 1.3 collective-permute-start.25
  183.6 5.2 %collective-permute-start.19 = (bf16[2,192,384]{2,1,0:T(8,128)(2,1)S(1)}, bf16[2,192,384]{2,1,0:T(8,128)(2,1)}, u32[]{:S(2)}, u32[]{:S(2)}) collective-permute-start(bf16[2,192,384]{2,1,0:T(8,128)(2,1)S(1)} %collective-permute-done.18), channel_id=1, source_target_pairs={{0,64},{64,128},{128,192},{192,256},{256,320},{320,384},{384,448},... | collective-permute-start | bytes 884744 | tf_op jit(solution)/shard_map/ppermute | solution.py:27
  188.8 5.3 %collective-permute-start.39 = (bf16[2,192,384]{2,1,0:T(8,128)(2,1)S(1)}, bf16[2,192,384]{2,1,0:T(8,128)(2,1)}, u32[]{:S(2)}, u32[]{:S(2)}) collective-permute-start(bf16[2,192,384]{2,1,0:T(8,128)(2,1)S(1)} %collective-permute-done.32), channel_id=1, source_target_pairs={{0,13},{1,14},{2,15},{3,12},{4,1},{5,2},{6,3},{7,0},{8,5},{9,6},{1... | collective-permute-start | bytes 884744 | tf_op jit(solution)/shard_map/ppermute | solution.py:52
  194.1 4.5 %collective-permute-start.38 = (bf16[2,192,384]{2,1,0:T(8,128)(2,1)S(1)}, bf16[2,192,384]{2,1,0:T(8,128)(2,1)}, u32[]{:S(2)}, u32[]{:S(2)}) collective-permute-start(bf16[2,192,384]{2,1,0:T(8,128)(2,1)S(1)} %collective-permute-done.32), channel_id=1, source_target_pairs={{0,14},{1,15},{2,12},{3,13},{4,2},{5,3},{6,0},{7,1},{8,6},{9,7},{1... | collective-permute-start | bytes 884744 | tf_op jit(solution)/shard_map/ppermute | solution.py:52
  198.6 3.4 %collective-permute-start.37 = (bf16[2,192,384]{2,1,0:T(8,128)(2,1)S(1)}, bf16[2,192,384]{2,1,0:T(8,128)(2,1)}, u32[]{:S(2)}, u32[]{:S(2)}) collective-permute-start(bf16[2,192,384]{2,1,0:T(8,128)(2,1)S(1)} %collective-permute-done.32), channel_id=1, source_target_pairs={{0,15},{1,12},{2,13},{3,14},{4,3},{5,0},{6,1},{7,2},{8,7},{9,4},{1... | collective-permute-start | bytes 884744 | tf_op jit(solution)/shard_map/ppermute | solution.py:52
  202.1 1.3 collective-permute-start.26
  203.4 4.7 %collective-permute-start.20 = (bf16[2,192,384]{2,1,0:T(8,128)(2,1)}, bf16[2,192,384]{2,1,0:T(8,128)(2,1)}, u32[]{:S(2)}, u32[]{:S(2)}) collective-permute-start(bf16[2,192,384]{2,1,0:T(8,128)(2,1)} %collective-permute-done.19), channel_id=1, source_target_pairs={{0,64},{64,128},{128,192},{192,256},{256,320},{320,384},{384,448},... | collective-permute-start | bytes 884744 | tf_op jit(solution)/shard_map/ppermute | solution.py:27
  208.3 1.9 collective-permute-start.36
  210.3 4.6 %collective-permute-start.43 = (bf16[2,192,384]{2,1,0:T(8,128)(2,1)S(1)}, bf16[2,192,384]{2,1,0:T(8,128)(2,1)S(1)}, u32[]{:S(2)}, u32[]{:S(2)}) collective-permute-start(bf16[2,192,384]{2,1,0:T(8,128)(2,1)S(1)} %collective-permute-done.32), channel_id=1, source_target_pairs={{0,9},{1,10},{2,11},{3,8},{4,13},{5,14},{6,15},{7,12},{8,1},{9,2},... | collective-permute-start | bytes 884744 | tf_op jit(solution)/shard_map/ppermute | solution.py:52
  214.9 4.3 %collective-permute-start.42 = (bf16[2,192,384]{2,1,0:T(8,128)(2,1)S(1)}, bf16[2,192,384]{2,1,0:T(8,128)(2,1)S(1)}, u32[]{:S(2)}, u32[]{:S(2)}) collective-permute-start(bf16[2,192,384]{2,1,0:T(8,128)(2,1)S(1)} %collective-permute-done.32), channel_id=1, source_target_pairs={{0,10},{1,11},{2,8},{3,9},{4,14},{5,15},{6,12},{7,13},{8,2},{9,3},... | collective-permute-start | bytes 884744 | tf_op jit(solution)/shard_map/ppermute | solution.py:52
  219.2 1.3 collective-permute-start.27
  220.5 4.0 %collective-permute-start.21 = (bf16[2,192,384]{2,1,0:T(8,128)(2,1)}, bf16[2,192,384]{2,1,0:T(8,128)(2,1)S(1)}, u32[]{:S(2)}, u32[]{:S(2)}) collective-permute-start(bf16[2,192,384]{2,1,0:T(8,128)(2,1)} %collective-permute-done.20), channel_id=1, source_target_pairs={{0,64},{64,128},{128,192},{192,256},{256,320},{320,384},{384,448},... | collective-permute-start | bytes 884744 | tf_op jit(solution)/shard_map/ppermute | solution.py:27
  226.0 9.8 %collective-permute-start.41 = (bf16[2,192,384]{2,1,0:T(8,128)(2,1)S(1)}, bf16[2,192,384]{2,1,0:T(8,128)(2,1)S(1)}, u32[]{:S(2)}, u32[]{:S(2)}) collective-permute-start(bf16[2,192,384]{2,1,0:T(8,128)(2,1)S(1)} %collective-permute-done.32), channel_id=1, source_target_pairs={{0,11},{1,8},{2,9},{3,10},{4,15},{5,12},{6,13},{7,14},{8,3},{9,0},... | collective-permute-start | bytes 884744 | tf_op jit(solution)/shard_map/ppermute | solution.py:52
  235.7 6.5 %collective-permute-start.40 = (bf16[2,192,384]{2,1,0:T(8,128)(2,1)S(1)}, bf16[2,192,384]{2,1,0:T(8,128)(2,1)S(1)}, u32[]{:S(2)}, u32[]{:S(2)}) collective-permute-start(bf16[2,192,384]{2,1,0:T(8,128)(2,1)S(1)} %collective-permute-done.32), channel_id=1, source_target_pairs={{0,8},{1,9},{2,10},{3,11},{4,12},{5,13},{6,14},{7,15},{8,0},{9,1},... | collective-permute-start | bytes 884744 | tf_op jit(solution)/shard_map/ppermute | solution.py:52
  242.2 1.9 collective-permute-start.47
  244.2 1.3 collective-permute-start.28
  245.5 4.3 %collective-permute-start.22 = (bf16[2,192,384]{2,1,0:T(8,128)(2,1)S(1)}, bf16[2,192,384]{2,1,0:T(8,128)(2,1)S(1)}, u32[]{:S(2)}, u32[]{:S(2)}) collective-permute-start(bf16[2,192,384]{2,1,0:T(8,128)(2,1)S(1)} %collective-permute-done.21), channel_id=1, source_target_pairs={{0,64},{64,128},{128,192},{192,256},{256,320},{320,384},{384,448},... | collective-permute-start | bytes 884744 | tf_op jit(solution)/shard_map/ppermute | solution.py:27
  249.7 5.8 %fusion.12 = bf16[4,4,2,192,384]{4,3,2,1,0:T(8,128)(2,1)S(1)} fusion(s32[]{:T(128)S(6)} %select_n.96, bf16[1,4,2,192,384]{4,3,2,1,0:T(8,128)(2,1)S(1)} %maximum_bitcast_fusion, bf16[1,4,2,192,384]{4,3,2,1,0:T(8,128)(2,1)S(1)} %maximum_bitcast_fusion.1, bf16[1,4,2,192,384]{4,3,2,1,0:T(8,128)(2,1)S(1)} %maximum_bitcast_fusion.2, ...), kind=kLoop, calls=%fused_computation.32 | loop fusion | flops 16515072 | bytes 9437188 | tf_op jit(solution)/shard_map/jit(_roll_dynamic)/concatenate | solution.py:55
  255.5 3.9 %collective-permute-start.46 = (bf16[2,192,384]{2,1,0:T(8,128)(2,1)S(1)}, bf16[2,192,384]{2,1,0:T(8,128)(2,1)S(1)}, u32[]{:S(2)}, u32[]{:S(2)}) collective-permute-start(bf16[2,192,384]{2,1,0:T(8,128)(2,1)S(1)} %collective-permute-done.32), channel_id=1, source_target_pairs={{0,6},{1,7},{2,4},{3,5},{4,10},{5,11},{6,8},{7,9},{8,14},{9,15},{1... | collective-permute-start | bytes 884744 | tf_op jit(solution)/shard_map/ppermute | solution.py:52
  260.1 4.4 %collective-permute-start.45 = (bf16[2,192,384]{2,1,0:T(8,128)(2,1)S(1)}, bf16[2,192,384]{2,1,0:T(8,128)(2,1)S(1)}, u32[]{:S(2)}, u32[]{:S(2)}) collective-permute-start(bf16[2,192,384]{2,1,0:T(8,128)(2,1)S(1)} %collective-permute-done.32), channel_id=1, source_target_pairs={{0,7},{1,4},{2,5},{3,6},{4,11},{5,8},{6,9},{7,10},{8,15},{9,12},{1... | collective-permute-start | bytes 884744 | tf_op jit(solution)/shard_map/ppermute | solution.py:52
  264.5 2.9 collective-permute-start.44
  267.7 1.3 collective-permute-start.29
  269.0 4.0 %collective-permute-start.23 = (bf16[2,192,384]{2,1,0:T(8,128)(2,1)S(1)}, bf16[2,192,384]{2,1,0:T(8,128)(2,1)S(1)}, u32[]{:S(2)}, u32[]{:S(2)}) collective-permute-start(bf16[2,192,384]{2,1,0:T(8,128)(2,1)S(1)} %collective-permute-done.22), channel_id=1, source_target_pairs={{0,64},{64,128},{128,192},{192,256},{256,320},{320,384},{384,448},... | collective-permute-start | bytes 884744 | tf_op jit(solution)/shard_map/ppermute | solution.py:27
  273.0 1.3 maximum_bitcast_fusion.5
  275.0 7.4 %collective-permute-done.44 = bf16[2,192,384]{2,1,0:T(8,128)(2,1)S(1)} collective-permute-done((bf16[2,192,384]{2,1,0:T(8,128)(2,1)S(1)}, bf16[2,192,384]{2,1,0:T(8,128)(2,1)S(1)}, u32[]{:S(2)}, u32[]{:S(2)}) %collective-permute-start.44) | collective-permute-done | bytes 294944 | tf_op jit(solution)/shard_map/ppermute | solution.py:52
  282.6 1.4 collective-permute-start.30
  284.2 1.0 bitcast_dynamic-update-slice_fusion.10
  288.7 3.9 %collective-permute-done.30 = bf16[2,192,384]{2,1,0:T(8,128)(2,1)S(1)} collective-permute-done((bf16[2,192,384]{2,1,0:T(8,128)(2,1)S(1)}, bf16[2,192,384]{2,1,0:T(8,128)(2,1)S(1)}, u32[]{:S(2)}, u32[]{:S(2)}) %collective-permute-start.30) | collective-permute-done | bytes 294944 | tf_op jit(solution)/shard_map/ppermute | solution.py:28
  292.9 3.8 %collective-permute-start.31 = (bf16[8,2,192,384]{3,2,0,1:T(8,128)(2,1)S(1)}, bf16[8,2,192,384]{3,2,0,1:T(8,128)(2,1)S(1)}, u32[]{:S(2)}, u32[]{:S(2)}) collective-permute-start(bf16[8,2,192,384]{3,2,0,1:T(8,128)(2,1)S(1)} %constant_dynamic-slice_fusion.2), channel_id=1, source_target_pairs={{0,32},{32,0},{1,33},{33,1},{2,34},{34,2},{3,35},{35,3},{4,36},{36... | collective-permute-start | bytes 7077896 | tf_op jit(solution)/shard_map/ppermute | solution.py:33
  296.7 5.8 %fusion.4 = bf16[4,4,2,192,384]{4,3,2,1,0:T(8,128)(2,1)S(1)} fusion(s32[]{:T(128)S(6)} %select_n.96, bf16[1,4,2,192,384]{4,3,2,1,0:T(8,128)(2,1)S(1)} %maximum_bitcast_fusion.4, bf16[1,4,2,192,384]{4,3,2,1,0:T(8,128)(2,1)S(1)} %maximum_bitcast_fusion.5, bf16[1,4,2,192,384]{4,3,2,1,0:T(8,128)(2,1)S(1)} %maximum_bitcast_fusion.6, ...), kind=kLoop, calls=%fused_computation.24 | loop fusion | flops 16515072 | bytes 9437188 | tf_op jit(solution)/shard_map/jit(_roll_dynamic)/concatenate | solution.py:55
  302.5 4.0 %fusion = (bf16[4,4,2,192,384]{4,3,2,1,0:T(8,128)(2,1)S(1)}, bf16[4,4,2,192,384]{4,3,2,1,0:T(8,128)(2,1)S(1)}) fusion(s32[]{:T(128)S(6)} %select_n.98, bf16[4,4,2,192,384]{4,3,2,1,0:T(8,128)(2,1)S(1)} %fusion.4, bf16[4,4,2,192,384]{4,3,2,1,0:T(8,128)(2,1)S(1)} %fusion.12), kind=kLoop, calls=%fused_computation.20 | loop fusion | flops 4718592 | bytes 18874372 | tf_op jit(solution)/shard_map/jit(_roll_dynamic)/concatenate | solution.py:55
  308.6 1.1 convolution_bitcast_fusion.1
  309.7 1.1 convolution_bitcast_fusion
  310.8 1.1 convolution_bitcast_fusion.2
  311.9 1.3 fusion.19
  (123 shorter events, 10.7 us)
Async XLA Ops:
  0.0 18.2 %copy-start = (bf16[2,192,384]{2,1,0:T(8,128)(2,1)S(1)}, bf16[2,192,384]{2,1,0:T(8,128)(2,1)}, u32[]{:S(2)}) copy-start(bf16[2,192,384]{2,1,0:T(8,128)(2,1)} %param.3) | copy-start | bytes 884740
  1.4 11.7 %collective-permute-start = (bf16[2,192,192]{1,2,0:T(8,128)(2,1)S(1)}, bf16[2,192,192]{1,2,0:T(8,128)(2,1)S(1)}, u32[]{:S(2)}, u32[]{:S(2)}) collective-permute-start(bf16[2,192,192]{1,2,0:T(8,128)(2,1)S(1)} %copy.33), channel_id=1, source_target_pairs={{0,0},{32,2},{64,4},{96,6},{128,8},{160,10},{192,12},{224,14},{256... | collective-permute-start | bytes 442376 | tf_op jit(solution)/shard_map/ppermute | solution.py:74
  7.6 10.5 %collective-permute-start.1 = (bf16[2,192,192]{1,2,0:T(8,128)(2,1)S(1)}, bf16[2,192,192]{1,2,0:T(8,128)(2,1)S(1)}, u32[]{:S(2)}, u32[]{:S(2)}) collective-permute-start(bf16[2,192,192]{1,2,0:T(8,128)(2,1)S(1)} %copy.34), channel_id=1, source_target_pairs={{0,1},{32,3},{64,5},{96,7},{128,9},{160,11},{192,13},{224,15},{256... | collective-permute-start | bytes 442376 | tf_op jit(solution)/shard_map/ppermute | solution.py:74
  18.3 66.0 %collective-permute-start.32 = (bf16[2,192,384]{2,1,0:T(8,128)(2,1)S(1)}, bf16[2,192,384]{2,1,0:T(8,128)(2,1)S(1)}, u32[]{:S(2)}, u32[]{:S(2)}) collective-permute-start(bf16[2,192,384]{2,1,0:T(8,128)(2,1)S(1)} %fusion.29), channel_id=1, source_target_pairs={{0,16},{16,0},{1,17},{17,1},{2,18},{18,2},{3,19},{19,3},{4,20},{20... | collective-permute-start | bytes 884744 | tf_op jit(solution)/shard_map/ppermute | solution.py:82
  67.5 20.5 %collective-permute-start.4 = (bf16[2,192,384]{2,1,0:T(8,128)(2,1)S(1)}, bf16[2,192,384]{2,1,0:T(8,128)(2,1)S(1)}, u32[]{:S(2)}, u32[]{:S(2)}) collective-permute-start(bf16[2,192,384]{2,1,0:T(8,128)(2,1)S(1)} %fusion.29), channel_id=1, source_target_pairs={{0,1},{1,2},{2,3},{3,0},{4,5},{5,6},{6,7},{7,4},{8,9},{9,10},{10,1... | collective-permute-start | bytes 884744 | tf_op jit(solution)/shard_map/ppermute | solution.py:52
  70.1 22.9 %collective-permute-start.3 = (bf16[2,192,384]{2,1,0:T(8,128)(2,1)S(1)}, bf16[2,192,384]{2,1,0:T(8,128)(2,1)S(1)}, u32[]{:S(2)}, u32[]{:S(2)}) collective-permute-start(bf16[2,192,384]{2,1,0:T(8,128)(2,1)S(1)} %fusion.29), channel_id=1, source_target_pairs={{0,2},{1,3},{2,0},{3,1},{4,6},{5,7},{6,4},{7,5},{8,10},{9,11},{10,... | collective-permute-start | bytes 884744 | tf_op jit(solution)/shard_map/ppermute | solution.py:52
  73.8 21.9 %collective-permute-start.2 = (bf16[2,192,384]{2,1,0:T(8,128)(2,1)S(1)}, bf16[2,192,384]{2,1,0:T(8,128)(2,1)S(1)}, u32[]{:S(2)}, u32[]{:S(2)}) collective-permute-start(bf16[2,192,384]{2,1,0:T(8,128)(2,1)S(1)} %fusion.29), channel_id=1, source_target_pairs={{0,3},{1,0},{2,1},{3,2},{4,7},{5,4},{6,5},{7,6},{8,11},{9,8},{10,9... | collective-permute-start | bytes 884744 | tf_op jit(solution)/shard_map/ppermute | solution.py:52
  76.8 21.1 %collective-permute-start.8 = (bf16[2,192,384]{2,1,0:T(8,128)(2,1)S(1)}, bf16[2,192,384]{2,1,0:T(8,128)(2,1)S(1)}, u32[]{:S(2)}, u32[]{:S(2)}) collective-permute-start(bf16[2,192,384]{2,1,0:T(8,128)(2,1)S(1)} %fusion.29), channel_id=1, source_target_pairs={{0,13},{1,14},{2,15},{3,12},{4,1},{5,2},{6,3},{7,0},{8,5},{9,6},{1... | collective-permute-start | bytes 884744 | tf_op jit(solution)/shard_map/ppermute | solution.py:52
  84.3 18.5 %collective-permute-start.7 = (bf16[2,192,384]{2,1,0:T(8,128)(2,1)S(1)}, bf16[2,192,384]{2,1,0:T(8,128)(2,1)S(1)}, u32[]{:S(2)}, u32[]{:S(2)}) collective-permute-start(bf16[2,192,384]{2,1,0:T(8,128)(2,1)S(1)} %fusion.29), channel_id=1, source_target_pairs={{0,14},{1,15},{2,12},{3,13},{4,2},{5,3},{6,0},{7,1},{8,6},{9,7},{1... | collective-permute-start | bytes 884744 | tf_op jit(solution)/shard_map/ppermute | solution.py:52
  88.0 19.7 %collective-permute-start.6 = (bf16[2,192,384]{2,1,0:T(8,128)(2,1)S(1)}, bf16[2,192,384]{2,1,0:T(8,128)(2,1)S(1)}, u32[]{:S(2)}, u32[]{:S(2)}) collective-permute-start(bf16[2,192,384]{2,1,0:T(8,128)(2,1)S(1)} %fusion.29), channel_id=1, source_target_pairs={{0,15},{1,12},{2,13},{3,14},{4,3},{5,0},{6,1},{7,2},{8,7},{9,4},{1... | collective-permute-start | bytes 884744 | tf_op jit(solution)/shard_map/ppermute | solution.py:52
  93.0 44.0 %collective-permute-start.5 = (bf16[2,192,384]{2,1,0:T(8,128)(2,1)S(1)}, bf16[2,192,384]{2,1,0:T(8,128)(2,1)S(1)}, u32[]{:S(2)}, u32[]{:S(2)}) collective-permute-start(bf16[2,192,384]{2,1,0:T(8,128)(2,1)S(1)} %fusion.29), channel_id=1, source_target_pairs={{0,12},{1,13},{2,14},{3,15},{4,0},{5,1},{6,2},{7,3},{8,4},{9,5},{1... | collective-permute-start | bytes 884744 | tf_op jit(solution)/shard_map/ppermute | solution.py:52
  95.8 43.1 %collective-permute-start.12 = (bf16[2,192,384]{2,1,0:T(8,128)(2,1)S(1)}, bf16[2,192,384]{2,1,0:T(8,128)(2,1)S(1)}, u32[]{:S(2)}, u32[]{:S(2)}) collective-permute-start(bf16[2,192,384]{2,1,0:T(8,128)(2,1)S(1)} %fusion.29), channel_id=1, source_target_pairs={{0,9},{1,10},{2,11},{3,8},{4,13},{5,14},{6,15},{7,12},{8,1},{9,2},... | collective-permute-start | bytes 884744 | tf_op jit(solution)/shard_map/ppermute | solution.py:52
  98.0 55.1 %collective-permute-start.11 = (bf16[2,192,384]{2,1,0:T(8,128)(2,1)S(1)}, bf16[2,192,384]{2,1,0:T(8,128)(2,1)S(1)}, u32[]{:S(2)}, u32[]{:S(2)}) collective-permute-start(bf16[2,192,384]{2,1,0:T(8,128)(2,1)S(1)} %fusion.29), channel_id=1, source_target_pairs={{0,10},{1,11},{2,8},{3,9},{4,14},{5,15},{6,12},{7,13},{8,2},{9,3},... | collective-permute-start | bytes 884744 | tf_op jit(solution)/shard_map/ppermute | solution.py:52
  102.8 52.1 %collective-permute-start.10 = (bf16[2,192,384]{2,1,0:T(8,128)(2,1)S(1)}, bf16[2,192,384]{2,1,0:T(8,128)(2,1)S(1)}, u32[]{:S(2)}, u32[]{:S(2)}) collective-permute-start(bf16[2,192,384]{2,1,0:T(8,128)(2,1)S(1)} %fusion.29), channel_id=1, source_target_pairs={{0,11},{1,8},{2,9},{3,10},{4,15},{5,12},{6,13},{7,14},{8,3},{9,0},... | collective-permute-start | bytes 884744 | tf_op jit(solution)/shard_map/ppermute | solution.py:52
  107.8 55.7 %collective-permute-start.9 = (bf16[2,192,384]{2,1,0:T(8,128)(2,1)S(1)}, bf16[2,192,384]{2,1,0:T(8,128)(2,1)S(1)}, u32[]{:S(2)}, u32[]{:S(2)}) collective-permute-start(bf16[2,192,384]{2,1,0:T(8,128)(2,1)S(1)} %fusion.29), channel_id=1, source_target_pairs={{0,8},{1,9},{2,10},{3,11},{4,12},{5,13},{6,14},{7,15},{8,0},{9,1},... | collective-permute-start | bytes 884744 | tf_op jit(solution)/shard_map/ppermute | solution.py:52
  136.9 28.5 %collective-permute-start.16 = (bf16[2,192,384]{2,1,0:T(8,128)(2,1)S(1)}, bf16[2,192,384]{2,1,0:T(8,128)(2,1)S(1)}, u32[]{:S(2)}, u32[]{:S(2)}) collective-permute-start(bf16[2,192,384]{2,1,0:T(8,128)(2,1)S(1)} %fusion.29), channel_id=1, source_target_pairs={{0,5},{1,6},{2,7},{3,4},{4,9},{5,10},{6,11},{7,8},{8,13},{9,14},{1... | collective-permute-start | bytes 884744 | tf_op jit(solution)/shard_map/ppermute | solution.py:52
  138.8 27.9 %collective-permute-start.17 = (bf16[2,192,384]{2,1,0:T(8,128)(2,1)S(1)}, bf16[2,192,384]{2,1,0:T(8,128)(2,1)S(1)}, u32[]{:S(2)}, u32[]{:S(2)}) collective-permute-start(bf16[2,192,384]{2,1,0:T(8,128)(2,1)S(1)} %fusion.29), channel_id=1, source_target_pairs={{0,64},{64,128},{128,192},{192,256},{256,320},{320,384},{384,448},... | collective-permute-start | bytes 884744 | tf_op jit(solution)/shard_map/ppermute | solution.py:27
  153.0 17.7 %collective-permute-start.15 = (bf16[2,192,384]{2,1,0:T(8,128)(2,1)S(1)}, bf16[2,192,384]{2,1,0:T(8,128)(2,1)S(1)}, u32[]{:S(2)}, u32[]{:S(2)}) collective-permute-start(bf16[2,192,384]{2,1,0:T(8,128)(2,1)S(1)} %fusion.29), channel_id=1, source_target_pairs={{0,6},{1,7},{2,4},{3,5},{4,10},{5,11},{6,8},{7,9},{8,14},{9,15},{1... | collective-permute-start | bytes 884744 | tf_op jit(solution)/shard_map/ppermute | solution.py:52
  155.0 15.8 %copy-start.1 = (bf16[2,192,384]{2,1,0:T(8,128)(2,1)}, bf16[2,192,384]{2,1,0:T(8,128)(2,1)S(1)}, u32[]{:S(2)}) copy-start(bf16[2,192,384]{2,1,0:T(8,128)(2,1)S(1)} %collective-permute-done.10) | copy-start | bytes 884740
  155.0 18.1 %collective-permute-start.14 = (bf16[2,192,384]{2,1,0:T(8,128)(2,1)S(1)}, bf16[2,192,384]{2,1,0:T(8,128)(2,1)S(1)}, u32[]{:S(2)}, u32[]{:S(2)}) collective-permute-start(bf16[2,192,384]{2,1,0:T(8,128)(2,1)S(1)} %fusion.29), channel_id=1, source_target_pairs={{0,7},{1,4},{2,5},{3,6},{4,11},{5,8},{6,9},{7,10},{8,15},{9,12},{1... | collective-permute-start | bytes 884744 | tf_op jit(solution)/shard_map/ppermute | solution.py:52
  163.5 9.6 %copy-start.5 = (bf16[2,192,384]{2,1,0:T(8,128)(2,1)}, bf16[2,192,384]{2,1,0:T(8,128)(2,1)S(1)}, u32[]{:S(2)}) copy-start(bf16[2,192,384]{2,1,0:T(8,128)(2,1)S(1)} %collective-permute-done.9) | copy-start | bytes 884740
  163.5 16.6 %collective-permute-start.13 = (bf16[2,192,384]{2,1,0:T(8,128)(2,1)S(1)}, bf16[2,192,384]{2,1,0:T(8,128)(2,1)S(1)}, u32[]{:S(2)}, u32[]{:S(2)}) collective-permute-start(bf16[2,192,384]{2,1,0:T(8,128)(2,1)S(1)} %fusion.29), channel_id=1, source_target_pairs={{0,4},{1,5},{2,6},{3,7},{4,8},{5,9},{6,10},{7,11},{8,12},{9,13},{1... | collective-permute-start | bytes 884744 | tf_op jit(solution)/shard_map/ppermute | solution.py:52
  165.4 11.1 %copy-start.9 = (bf16[2,192,384]{2,1,0:T(8,128)(2,1)}, bf16[2,192,384]{2,1,0:T(8,128)(2,1)S(1)}, u32[]{:S(2)}) copy-start(bf16[2,192,384]{2,1,0:T(8,128)(2,1)S(1)} %collective-permute-done.16) | copy-start | bytes 884740
  165.4 16.8 %collective-permute-start.24 = (bf16[2,192,384]{2,1,0:T(8,128)(2,1)S(1)}, bf16[2,192,384]{2,1,0:T(8,128)(2,1)S(1)}, u32[]{:S(2)}, u32[]{:S(2)}) collective-permute-start(bf16[2,192,384]{2,1,0:T(8,128)(2,1)S(1)} %fusion.29), channel_id=1, source_target_pairs={{64,0},{128,64},{192,128},{256,192},{320,256},{384,320},{448,384},... | collective-permute-start | bytes 884744 | tf_op jit(solution)/shard_map/ppermute | solution.py:28
  166.7 36.6 %copy-start.17 = (bf16[2,192,384]{2,1,0:T(8,128)(2,1)}, bf16[2,192,384]{2,1,0:T(8,128)(2,1)S(1)}, u32[]{:S(2)}) copy-start(bf16[2,192,384]{2,1,0:T(8,128)(2,1)S(1)} %collective-permute-done.17) | copy-start | bytes 884740
  166.8 16.8 %collective-permute-start.18 = (bf16[2,192,384]{2,1,0:T(8,128)(2,1)S(1)}, bf16[2,192,384]{2,1,0:T(8,128)(2,1)S(1)}, u32[]{:S(2)}, u32[]{:S(2)}) collective-permute-start(bf16[2,192,384]{2,1,0:T(8,128)(2,1)S(1)} %collective-permute-done.17), channel_id=1, source_target_pairs={{0,64},{64,128},{128,192},{192,256},{256,320},{320,384},{384,448},... | collective-permute-start | bytes 884744 | tf_op jit(solution)/shard_map/ppermute | solution.py:27
  170.8 31.3 %copy-start.11 = (bf16[2,192,384]{2,1,0:T(8,128)(2,1)}, bf16[2,192,384]{2,1,0:T(8,128)(2,1)S(1)}, u32[]{:S(2)}) copy-start(bf16[2,192,384]{2,1,0:T(8,128)(2,1)S(1)} %collective-permute-done.15) | copy-start | bytes 884740
  170.8 18.0 %collective-permute-start.35 = (bf16[2,192,384]{2,1,0:T(8,128)(2,1)S(1)}, bf16[2,192,384]{2,1,0:T(8,128)(2,1)S(1)}, u32[]{:S(2)}, u32[]{:S(2)}) collective-permute-start(bf16[2,192,384]{2,1,0:T(8,128)(2,1)S(1)} %collective-permute-done.32), channel_id=1, source_target_pairs={{0,1},{1,2},{2,3},{3,0},{4,5},{5,6},{6,7},{7,4},{8,9},{9,10},{10,1... | collective-permute-start | bytes 884744 | tf_op jit(solution)/shard_map/ppermute | solution.py:52
  173.1 30.3 %copy-start.13 = (bf16[2,192,384]{2,1,0:T(8,128)(2,1)}, bf16[2,192,384]{2,1,0:T(8,128)(2,1)S(1)}, u32[]{:S(2)}) copy-start(bf16[2,192,384]{2,1,0:T(8,128)(2,1)S(1)} %collective-permute-done.14) | copy-start | bytes 884740
  173.1 20.9 %collective-permute-start.34 = (bf16[2,192,384]{2,1,0:T(8,128)(2,1)S(1)}, bf16[2,192,384]{2,1,0:T(8,128)(2,1)S(1)}, u32[]{:S(2)}, u32[]{:S(2)}) collective-permute-start(bf16[2,192,384]{2,1,0:T(8,128)(2,1)S(1)} %collective-permute-done.32), channel_id=1, source_target_pairs={{0,2},{1,3},{2,0},{3,1},{4,6},{5,7},{6,4},{7,5},{8,10},{9,11},{10,... | collective-permute-start | bytes 884744 | tf_op jit(solution)/shard_map/ppermute | solution.py:52
  180.1 23.3 %copy-start.15 = (bf16[2,192,384]{2,1,0:T(8,128)(2,1)}, bf16[2,192,384]{2,1,0:T(8,128)(2,1)S(1)}, u32[]{:S(2)}) copy-start(bf16[2,192,384]{2,1,0:T(8,128)(2,1)S(1)} %collective-permute-done.13) | copy-start | bytes 884740
  180.1 18.5 %collective-permute-start.33 = (bf16[2,192,384]{2,1,0:T(8,128)(2,1)S(1)}, bf16[2,192,384]{2,1,0:T(8,128)(2,1)S(1)}, u32[]{:S(2)}, u32[]{:S(2)}) collective-permute-start(bf16[2,192,384]{2,1,0:T(8,128)(2,1)S(1)} %collective-permute-done.32), channel_id=1, source_target_pairs={{0,3},{1,0},{2,1},{3,2},{4,7},{5,4},{6,5},{7,6},{8,11},{9,8},{10,9... | collective-permute-start | bytes 884744 | tf_op jit(solution)/shard_map/ppermute | solution.py:52
  182.2 21.2 %copy-start.19 = (bf16[2,192,384]{2,1,0:T(8,128)(2,1)}, bf16[2,192,384]{2,1,0:T(8,128)(2,1)S(1)}, u32[]{:S(2)}) copy-start(bf16[2,192,384]{2,1,0:T(8,128)(2,1)S(1)} %collective-permute-done.24) | copy-start | bytes 884740
  182.2 19.8 %collective-permute-start.25 = (bf16[2,192,384]{2,1,0:T(8,128)(2,1)S(1)}, bf16[2,192,384]{2,1,0:T(8,128)(2,1)}, u32[]{:S(2)}, u32[]{:S(2)}) collective-permute-start(bf16[2,192,384]{2,1,0:T(8,128)(2,1)S(1)} %collective-permute-done.24), channel_id=1, source_target_pairs={{64,0},{128,64},{192,128},{256,192},{320,256},{384,320},{448,384},... | collective-permute-start | bytes 884744 | tf_op jit(solution)/shard_map/ppermute | solution.py:28
  183.6 19.9 %copy-start.21 = (bf16[2,192,384]{2,1,0:T(8,128)(2,1)}, bf16[2,192,384]{2,1,0:T(8,128)(2,1)S(1)}, u32[]{:S(2)}) copy-start(bf16[2,192,384]{2,1,0:T(8,128)(2,1)S(1)} %collective-permute-done.18) | copy-start | bytes 884740
  183.6 19.8 %collective-permute-start.19 = (bf16[2,192,384]{2,1,0:T(8,128)(2,1)S(1)}, bf16[2,192,384]{2,1,0:T(8,128)(2,1)}, u32[]{:S(2)}, u32[]{:S(2)}) collective-permute-start(bf16[2,192,384]{2,1,0:T(8,128)(2,1)S(1)} %collective-permute-done.18), channel_id=1, source_target_pairs={{0,64},{64,128},{128,192},{192,256},{256,320},{320,384},{384,448},... | collective-permute-start | bytes 884744 | tf_op jit(solution)/shard_map/ppermute | solution.py:27
  188.8 19.6 %collective-permute-start.39 = (bf16[2,192,384]{2,1,0:T(8,128)(2,1)S(1)}, bf16[2,192,384]{2,1,0:T(8,128)(2,1)}, u32[]{:S(2)}, u32[]{:S(2)}) collective-permute-start(bf16[2,192,384]{2,1,0:T(8,128)(2,1)S(1)} %collective-permute-done.32), channel_id=1, source_target_pairs={{0,13},{1,14},{2,15},{3,12},{4,1},{5,2},{6,3},{7,0},{8,5},{9,6},{1... | collective-permute-start | bytes 884744 | tf_op jit(solution)/shard_map/ppermute | solution.py:52
  194.1 4.5 %copy-start.3 = (bf16[2,192,384]{2,1,0:T(8,128)(2,1)}, bf16[2,192,384]{2,1,0:T(8,128)(2,1)S(1)}, u32[]{:S(2)}) copy-start(bf16[2,192,384]{2,1,0:T(8,128)(2,1)S(1)} %collective-permute-done.34) | copy-start | bytes 884740
  194.1 16.2 %collective-permute-start.38 = (bf16[2,192,384]{2,1,0:T(8,128)(2,1)S(1)}, bf16[2,192,384]{2,1,0:T(8,128)(2,1)}, u32[]{:S(2)}, u32[]{:S(2)}) collective-permute-start(bf16[2,192,384]{2,1,0:T(8,128)(2,1)S(1)} %collective-permute-done.32), channel_id=1, source_target_pairs={{0,14},{1,15},{2,12},{3,13},{4,2},{5,3},{6,0},{7,1},{8,6},{9,7},{1... | collective-permute-start | bytes 884744 | tf_op jit(solution)/shard_map/ppermute | solution.py:52
  198.6 16.2 %collective-permute-start.37 = (bf16[2,192,384]{2,1,0:T(8,128)(2,1)S(1)}, bf16[2,192,384]{2,1,0:T(8,128)(2,1)}, u32[]{:S(2)}, u32[]{:S(2)}) collective-permute-start(bf16[2,192,384]{2,1,0:T(8,128)(2,1)S(1)} %collective-permute-done.32), channel_id=1, source_target_pairs={{0,15},{1,12},{2,13},{3,14},{4,3},{5,0},{6,1},{7,2},{8,7},{9,4},{1... | collective-permute-start | bytes 884744 | tf_op jit(solution)/shard_map/ppermute | solution.py:52
  202.1 17.1 %collective-permute-start.26 = (bf16[2,192,384]{2,1,0:T(8,128)(2,1)}, bf16[2,192,384]{2,1,0:T(8,128)(2,1)}, u32[]{:S(2)}, u32[]{:S(2)}) collective-permute-start(bf16[2,192,384]{2,1,0:T(8,128)(2,1)} %collective-permute-done.25), channel_id=1, source_target_pairs={{64,0},{128,64},{192,128},{256,192},{320,256},{384,320},{448,384},... | collective-permute-start | bytes 884744 | tf_op jit(solution)/shard_map/ppermute | solution.py:28
  203.4 17.1 %collective-permute-start.20 = (bf16[2,192,384]{2,1,0:T(8,128)(2,1)}, bf16[2,192,384]{2,1,0:T(8,128)(2,1)}, u32[]{:S(2)}, u32[]{:S(2)}) collective-permute-start(bf16[2,192,384]{2,1,0:T(8,128)(2,1)} %collective-permute-done.19), channel_id=1, source_target_pairs={{0,64},{64,128},{128,192},{192,256},{256,320},{320,384},{384,448},... | collective-permute-start | bytes 884744 | tf_op jit(solution)/shard_map/ppermute | solution.py:27
  208.1 16.6 %copy-start.2 = (bf16[2,192,384]{2,1,0:T(8,128)(2,1)S(1)}, bf16[2,192,384]{2,1,0:T(8,128)(2,1)}, u32[]{:S(2)}) copy-start(bf16[2,192,384]{2,1,0:T(8,128)(2,1)} %copy-done.1) | copy-start | bytes 884740
  208.1 16.6 %copy-start.6 = (bf16[2,192,384]{2,1,0:T(8,128)(2,1)S(1)}, bf16[2,192,384]{2,1,0:T(8,128)(2,1)}, u32[]{:S(2)}) copy-start(bf16[2,192,384]{2,1,0:T(8,128)(2,1)} %copy-done.5) | copy-start | bytes 884740
  208.3 17.6 %collective-permute-start.36 = (bf16[2,192,384]{2,1,0:T(8,128)(2,1)S(1)}, bf16[2,192,384]{2,1,0:T(8,128)(2,1)S(1)}, u32[]{:S(2)}, u32[]{:S(2)}) collective-permute-start(bf16[2,192,384]{2,1,0:T(8,128)(2,1)S(1)} %collective-permute-done.32), channel_id=1, source_target_pairs={{0,12},{1,13},{2,14},{3,15},{4,0},{5,1},{6,2},{7,3},{8,4},{9,5},{1... | collective-permute-start | bytes 884744 | tf_op jit(solution)/shard_map/ppermute | solution.py:52
  210.3 25.4 %collective-permute-start.43 = (bf16[2,192,384]{2,1,0:T(8,128)(2,1)S(1)}, bf16[2,192,384]{2,1,0:T(8,128)(2,1)S(1)}, u32[]{:S(2)}, u32[]{:S(2)}) collective-permute-start(bf16[2,192,384]{2,1,0:T(8,128)(2,1)S(1)} %collective-permute-done.32), channel_id=1, source_target_pairs={{0,9},{1,10},{2,11},{3,8},{4,13},{5,14},{6,15},{7,12},{8,1},{9,2},... | collective-permute-start | bytes 884744 | tf_op jit(solution)/shard_map/ppermute | solution.py:52
  214.9 27.3 %collective-permute-start.42 = (bf16[2,192,384]{2,1,0:T(8,128)(2,1)S(1)}, bf16[2,192,384]{2,1,0:T(8,128)(2,1)S(1)}, u32[]{:S(2)}, u32[]{:S(2)}) collective-permute-start(bf16[2,192,384]{2,1,0:T(8,128)(2,1)S(1)} %collective-permute-done.32), channel_id=1, source_target_pairs={{0,10},{1,11},{2,8},{3,9},{4,14},{5,15},{6,12},{7,13},{8,2},{9,3},... | collective-permute-start | bytes 884744 | tf_op jit(solution)/shard_map/ppermute | solution.py:52
  219.2 25.0 %collective-permute-start.27 = (bf16[2,192,384]{2,1,0:T(8,128)(2,1)}, bf16[2,192,384]{2,1,0:T(8,128)(2,1)S(1)}, u32[]{:S(2)}, u32[]{:S(2)}) collective-permute-start(bf16[2,192,384]{2,1,0:T(8,128)(2,1)} %collective-permute-done.26), channel_id=1, source_target_pairs={{64,0},{128,64},{192,128},{256,192},{320,256},{384,320},{448,384},... | collective-permute-start | bytes 884744 | tf_op jit(solution)/shard_map/ppermute | solution.py:28
  220.5 25.0 %collective-permute-start.21 = (bf16[2,192,384]{2,1,0:T(8,128)(2,1)}, bf16[2,192,384]{2,1,0:T(8,128)(2,1)S(1)}, u32[]{:S(2)}, u32[]{:S(2)}) collective-permute-start(bf16[2,192,384]{2,1,0:T(8,128)(2,1)} %collective-permute-done.20), channel_id=1, source_target_pairs={{0,64},{64,128},{128,192},{192,256},{256,320},{320,384},{384,448},... | collective-permute-start | bytes 884744 | tf_op jit(solution)/shard_map/ppermute | solution.py:27
  225.9 41.5 %copy-start.4 = (bf16[2,192,384]{2,1,0:T(8,128)(2,1)S(1)}, bf16[2,192,384]{2,1,0:T(8,128)(2,1)}, u32[]{:S(2)}) copy-start(bf16[2,192,384]{2,1,0:T(8,128)(2,1)} %copy-done.3) | copy-start | bytes 884740
  225.9 41.5 %copy-start.8 = (bf16[2,192,384]{2,1,0:T(8,128)(2,1)S(1)}, bf16[2,192,384]{2,1,0:T(8,128)(2,1)}, u32[]{:S(2)}) copy-start(bf16[2,192,384]{2,1,0:T(8,128)(2,1)} %copy-done.7) | copy-start | bytes 884740
  226.0 29.6 %collective-permute-start.41 = (bf16[2,192,384]{2,1,0:T(8,128)(2,1)S(1)}, bf16[2,192,384]{2,1,0:T(8,128)(2,1)S(1)}, u32[]{:S(2)}, u32[]{:S(2)}) collective-permute-start(bf16[2,192,384]{2,1,0:T(8,128)(2,1)S(1)} %collective-permute-done.32), channel_id=1, source_target_pairs={{0,11},{1,8},{2,9},{3,10},{4,15},{5,12},{6,13},{7,14},{8,3},{9,0},... | collective-permute-start | bytes 884744 | tf_op jit(solution)/shard_map/ppermute | solution.py:52
  235.7 24.4 %collective-permute-start.40 = (bf16[2,192,384]{2,1,0:T(8,128)(2,1)S(1)}, bf16[2,192,384]{2,1,0:T(8,128)(2,1)S(1)}, u32[]{:S(2)}, u32[]{:S(2)}) collective-permute-start(bf16[2,192,384]{2,1,0:T(8,128)(2,1)S(1)} %collective-permute-done.32), channel_id=1, source_target_pairs={{0,8},{1,9},{2,10},{3,11},{4,12},{5,13},{6,14},{7,15},{8,0},{9,1},... | collective-permute-start | bytes 884744 | tf_op jit(solution)/shard_map/ppermute | solution.py:52
  242.2 22.3 %collective-permute-start.47 = (bf16[2,192,384]{2,1,0:T(8,128)(2,1)S(1)}, bf16[2,192,384]{2,1,0:T(8,128)(2,1)S(1)}, u32[]{:S(2)}, u32[]{:S(2)}) collective-permute-start(bf16[2,192,384]{2,1,0:T(8,128)(2,1)S(1)} %collective-permute-done.32), channel_id=1, source_target_pairs={{0,5},{1,6},{2,7},{3,4},{4,9},{5,10},{6,11},{7,8},{8,13},{9,14},{1... | collective-permute-start | bytes 884744 | tf_op jit(solution)/shard_map/ppermute | solution.py:52
  244.2 23.5 %collective-permute-start.28 = (bf16[2,192,384]{2,1,0:T(8,128)(2,1)S(1)}, bf16[2,192,384]{2,1,0:T(8,128)(2,1)S(1)}, u32[]{:S(2)}, u32[]{:S(2)}) collective-permute-start(bf16[2,192,384]{2,1,0:T(8,128)(2,1)S(1)} %collective-permute-done.27), channel_id=1, source_target_pairs={{64,0},{128,64},{192,128},{256,192},{320,256},{384,320},{448,384},... | collective-permute-start | bytes 884744 | tf_op jit(solution)/shard_map/ppermute | solution.py:28
  245.5 23.5 %collective-permute-start.22 = (bf16[2,192,384]{2,1,0:T(8,128)(2,1)S(1)}, bf16[2,192,384]{2,1,0:T(8,128)(2,1)S(1)}, u32[]{:S(2)}, u32[]{:S(2)}) collective-permute-start(bf16[2,192,384]{2,1,0:T(8,128)(2,1)S(1)} %collective-permute-done.21), channel_id=1, source_target_pairs={{0,64},{64,128},{128,192},{192,256},{256,320},{320,384},{384,448},... | collective-permute-start | bytes 884744 | tf_op jit(solution)/shard_map/ppermute | solution.py:27
  255.5 19.0 %collective-permute-start.46 = (bf16[2,192,384]{2,1,0:T(8,128)(2,1)S(1)}, bf16[2,192,384]{2,1,0:T(8,128)(2,1)S(1)}, u32[]{:S(2)}, u32[]{:S(2)}) collective-permute-start(bf16[2,192,384]{2,1,0:T(8,128)(2,1)S(1)} %collective-permute-done.32), channel_id=1, source_target_pairs={{0,6},{1,7},{2,4},{3,5},{4,10},{5,11},{6,8},{7,9},{8,14},{9,15},{1... | collective-permute-start | bytes 884744 | tf_op jit(solution)/shard_map/ppermute | solution.py:52
  260.1 14.9 %collective-permute-start.45 = (bf16[2,192,384]{2,1,0:T(8,128)(2,1)S(1)}, bf16[2,192,384]{2,1,0:T(8,128)(2,1)S(1)}, u32[]{:S(2)}, u32[]{:S(2)}) collective-permute-start(bf16[2,192,384]{2,1,0:T(8,128)(2,1)S(1)} %collective-permute-done.32), channel_id=1, source_target_pairs={{0,7},{1,4},{2,5},{3,6},{4,11},{5,8},{6,9},{7,10},{8,15},{9,12},{1... | collective-permute-start | bytes 884744 | tf_op jit(solution)/shard_map/ppermute | solution.py:52
  264.5 17.8 %collective-permute-start.44 = (bf16[2,192,384]{2,1,0:T(8,128)(2,1)S(1)}, bf16[2,192,384]{2,1,0:T(8,128)(2,1)S(1)}, u32[]{:S(2)}, u32[]{:S(2)}) collective-permute-start(bf16[2,192,384]{2,1,0:T(8,128)(2,1)S(1)} %collective-permute-done.32), channel_id=1, source_target_pairs={{0,4},{1,5},{2,6},{3,7},{4,8},{5,9},{6,10},{7,11},{8,12},{9,13},{1... | collective-permute-start | bytes 884744 | tf_op jit(solution)/shard_map/ppermute | solution.py:52
  267.7 14.9 %collective-permute-start.29 = (bf16[2,192,384]{2,1,0:T(8,128)(2,1)S(1)}, bf16[2,192,384]{2,1,0:T(8,128)(2,1)S(1)}, u32[]{:S(2)}, u32[]{:S(2)}) collective-permute-start(bf16[2,192,384]{2,1,0:T(8,128)(2,1)S(1)} %collective-permute-done.28), channel_id=1, source_target_pairs={{64,0},{128,64},{192,128},{256,192},{320,256},{384,320},{448,384},... | collective-permute-start | bytes 884744 | tf_op jit(solution)/shard_map/ppermute | solution.py:28
  269.0 15.1 %collective-permute-start.23 = (bf16[2,192,384]{2,1,0:T(8,128)(2,1)S(1)}, bf16[2,192,384]{2,1,0:T(8,128)(2,1)S(1)}, u32[]{:S(2)}, u32[]{:S(2)}) collective-permute-start(bf16[2,192,384]{2,1,0:T(8,128)(2,1)S(1)} %collective-permute-done.22), channel_id=1, source_target_pairs={{0,64},{64,128},{128,192},{192,256},{256,320},{320,384},{384,448},... | collective-permute-start | bytes 884744 | tf_op jit(solution)/shard_map/ppermute | solution.py:27
  282.4 3.8 %copy-start.22 = (bf16[2,192,384]{2,1,0:T(8,128)(2,1)S(1)}, bf16[2,192,384]{2,1,0:T(8,128)(2,1)}, u32[]{:S(2)}) copy-start(bf16[2,192,384]{2,1,0:T(8,128)(2,1)} %copy-done.21) | copy-start | bytes 884740
  282.6 10.0 %collective-permute-start.30 = (bf16[2,192,384]{2,1,0:T(8,128)(2,1)S(1)}, bf16[2,192,384]{2,1,0:T(8,128)(2,1)S(1)}, u32[]{:S(2)}, u32[]{:S(2)}) collective-permute-start(bf16[2,192,384]{2,1,0:T(8,128)(2,1)S(1)} %collective-permute-done.29), channel_id=1, source_target_pairs={{64,0},{128,64},{192,128},{256,192},{320,256},{384,320},{448,384},... | collective-permute-start | bytes 884744 | tf_op jit(solution)/shard_map/ppermute | solution.py:28
  292.9 16.8 %collective-permute-start.31 = (bf16[8,2,192,384]{3,2,0,1:T(8,128)(2,1)S(1)}, bf16[8,2,192,384]{3,2,0,1:T(8,128)(2,1)S(1)}, u32[]{:S(2)}, u32[]{:S(2)}) collective-permute-start(bf16[8,2,192,384]{3,2,0,1:T(8,128)(2,1)S(1)} %constant_dynamic-slice_fusion.2), channel_id=1, source_target_pairs={{0,32},{32,0},{1,33},{33,1},{2,34},{34,2},{3,35},{35,3},{4,36},{36... | collective-permute-start | bytes 7077896 | tf_op jit(solution)/shard_map/ppermute | solution.py:33
  (7 other events, 15.3 us)

commit v5 on v4

--- a/solution.py
+++ b/solution.py
@@ -34,28 +34,6 @@
     return mine, other
 
 
-def gather_plane(block):
-    n_y = lax.axis_size("y")
-    n_x = lax.axis_size("x")
-    rows = []
-    for dy in range(n_y):
-        row = []
-        for dx in range(n_x):
-            if dy == 0 and dx == 0:
-                row.append(block)
-                continue
-            pairs = [
-                (y * n_x + x, ((y - dy) % n_y) * n_x + (x - dx) % n_x)
-                for y in range(n_y)
-                for x in range(n_x)
-            ]
-            row.append(lax.ppermute(block, ("y", "x"), pairs))
-        rows.append(jnp.stack(row))
-    relative = jnp.stack(rows)
-    placed = jnp.roll(relative, (lax.axis_index("y"), lax.axis_index("x")), axis=(0, 1))
-    return placed.reshape((n_y * n_x,) + block.shape)
-
-
 def local(pressure):
     n_shot = lax.axis_size("zl") * lax.axis_size("core")
     n_half = lax.axis_size("y") * lax.axis_size("x")
@@ -80,8 +58,9 @@
     ).astype(jnp.bfloat16)
 
     partner_block = lax.ppermute(symmetric, "zh", [(0, 1), (1, 0)])
-    own_panel = gather_plane(symmetric)
-    partner_panel = gather_plane(partner_block)
+    top = jnp.where(half_index == 0, symmetric, partner_block)
+    bottom = jnp.where(half_index == 0, partner_block, symmetric)
+    panels = lax.all_gather(jnp.stack([top, bottom]), ("y", "x"), axis=1, tiled=False)
     mine, other = gather_line(symmetric)
     core_index = lax.axis_index("core")
     n_line = mine.shape[0]
@@ -94,13 +73,11 @@
         return jnp.einsum("zpxc,zqcn->pqxn", left, panel, preferred_element_type=jnp.float32)
 
     quarter = n_line // 2
-    own_start = half_index * quarter
-    other_start = (1 - half_index) * quarter
     terms = (
-        product(lax.dynamic_slice_in_dim(mine, own_start, quarter, 0), own_panel, core_index)
-        + product(lax.dynamic_slice_in_dim(other, own_start, quarter, 0), own_panel, 1 - core_index)
-        + product(lax.dynamic_slice_in_dim(mine, other_start, quarter, 0), partner_panel, core_index)
-        + product(lax.dynamic_slice_in_dim(other, other_start, quarter, 0), partner_panel, 1 - core_index)
+        product(mine[:quarter], panels[0], core_index)
+        + product(other[:quarter], panels[0], 1 - core_index)
+        + product(mine[quarter:], panels[1], core_index)
+        + product(other[quarter:], panels[1], 1 - core_index)
     )
     factor = 1.0 / math.sqrt(N)
     real = (terms[0, 0] - terms[1, 1]) * factor

time: 316 us -> 216 us (0.68)
  starting transfers between devices: 235 us -> 103 us
  waiting for transfers between devices: 45.1 us -> 67.9 us
  other arithmetic: 19.3 us -> 3.02 us
  between operations: 1.27 us -> 13.8 us
  local copies, waits for them, and re-layouts: 9.32 us -> 20.5 us
    ppermute x30 -> x0, starting transfers between devices: 124 us -> none  [gather_plane(): row.append(lax.ppermute(block, ('y', 'x'), pairs))]
    ppermute x30 -> x0, waiting for transfers between devices: 33.2 us -> none  [gather_plane(): row.append(lax.ppermute(block, ('y', 'x'), pairs))]
    ppermute x7, waiting for transfers between devices: 0.02 us -> 26.4 us  [gather_line(): lax.ppermute(rightward, 'zl', [(k, k + 1) for k in range(n_line - 1)])]
    all_gather x0 -> x1, waiting for transfers between devices: none -> 18.1 us  [local(): lax.all_gather(jnp.stack([top, bottom]), ('y', 'x'), axis=1, tiled=False)]
    concatenate x3 -> x0, other arithmetic: 15.5 us -> none  [gather_plane(): jnp.roll(relative, (lax.axis_index('y'), lax.axis_index('x')), axis=(0, 1))]
    ppermute x7, starting transfers between devices: 40.4 us -> 29.1 us  [gather_line(): lax.ppermute(rightward, 'zl', [(k, k + 1) for k in range(n_line - 1)])]
    ppermute x1, waiting for transfers between devices: 0.01 us -> 7.62 us  [local(): partner_block = lax.ppermute(symmetric, 'zh', [(0, 1), (1, 0)])]
    transpose x0 -> x5, local copies, waits for them, and re-layouts: none -> 6.08 us  [product(): jnp.swapaxes(panel, 1, 2).reshape(n_line // 2, parts, 2 * rows, cols)]
  transfers between devices with their start and end apart: 48 -> 19, of which waited for: 8 -> 16; matrix products, arithmetic and copies ran while one was open for 8% -> 8% of each run, Pallas kernels for 0% -> 0%
where the time goes in v5:
time: 216 us; the launch traced here: 215 us
  starting transfers between devices  103 us (48%)
  waiting for transfers between devices  67.9 us (31%)
  local copies, waits for them, and re-layouts  20.5 us (9%)
  between operations  13.8 us (6%)
  matrix products  7.1 us (3%)
  other arithmetic  3.02 us (1%)
    ppermute x1, starting transfers between devices, local(): partner_block = lax.ppermute(symmetric, 'zh', [(0, 1), (1, 0)])  49.2 us
    ppermute x7, starting transfers between devices, gather_line(): lax.ppermute(rightward, 'zl', [(k, k + 1) for k in range(n_line - 1)])  29.1 us
    ppermute x7, waiting for transfers between devices, gather_line(): lax.ppermute(rightward, 'zl', [(k, k + 1) for k in range(n_line - 1)])  26.4 us
    all_gather x1, waiting for transfers between devices, local(): lax.all_gather(jnp.stack([top, bottom]), ('y', 'x'), axis=1, tiled=False)  18.1 us
    ppermute x7, starting transfers between devices, gather_line(): lax.ppermute(leftward, 'zl', [(k + 1, k) for k in range(n_line - 1)])  9 us
    ppermute x2, starting transfers between devices, local(): lax.ppermute(piece, axes, mirror_pairs(n_recv, n_shot, flip))  8.57 us
    ppermute x2, waiting for transfers between devices, local(): lax.ppermute(piece, axes, mirror_pairs(n_recv, n_shot, flip))  7.99 us
    ppermute x7, waiting for transfers between devices, gather_line(): lax.ppermute(leftward, 'zl', [(k + 1, k) for k in range(n_line - 1)])  7.76 us
  transfers between devices with their start and end apart: 19, of which 16 were waited for; matrix products, arithmetic and copies ran while one was open for 8% of the time, Pallas kernels for 0%

profile of v5, /device:TPU:1, one launch (start us, length us, event | category | flops | bytes accessed | tf_op | source)
XLA Modules:
  0.0 215.5 jit_solution(5251815016670926813)
XLA Ops:
  6.5 0.0 all-gather.3.cloned.1.call-start
  6.5 1.2 constant_dynamic-slice_fusion.2
  7.7 0.1 copy.56
  7.9 6.0 %collective-permute-start = (bf16[2,192,192]{1,2,0:T(8,128)(2,1)S(1)}, bf16[2,192,192]{1,2,0:T(8,128)(2,1)S(1)}, u32[]{:S(2)}, u32[]{:S(2)}) collective-permute-start(bf16[2,192,192]{1,2,0:T(8,128)(2,1)S(1)} %copy.56), channel_id=1, source_target_pairs={{0,0},{32,2},{64,4},{96,6},{128,8},{160,10},{192,12},{224,14},{256... | collective-permute-start | bytes 442376 | tf_op jit(solution)/shard_map/ppermute | solution.py:52
  13.9 0.1 copy.57
  14.1 2.5 %collective-permute-start.1 = (bf16[2,192,192]{1,2,0:T(8,128)(2,1)S(1)}, bf16[2,192,192]{1,2,0:T(8,128)(2,1)S(1)}, u32[]{:S(2)}, u32[]{:S(2)}) collective-permute-start(bf16[2,192,192]{1,2,0:T(8,128)(2,1)S(1)} %copy.57), channel_id=1, source_target_pairs={{0,1},{32,3},{64,5},{96,7},{128,9},{160,11},{192,13},{224,15},{256... | collective-permute-start | bytes 442376 | tf_op jit(solution)/shard_map/ppermute | solution.py:52
  16.6 2.9 %collective-permute-done = bf16[2,192,192]{1,2,0:T(8,128)(2,1)S(1)} collective-permute-done((bf16[2,192,192]{1,2,0:T(8,128)(2,1)S(1)}, bf16[2,192,192]{1,2,0:T(8,128)(2,1)S(1)}, u32[]{:S(2)}, u32[]{:S(2)}) %collective-permute-start) | collective-permute-done | bytes 147488 | tf_op jit(solution)/shard_map/ppermute | solution.py:52
  19.6 5.0 %collective-permute-done.1 = bf16[2,192,192]{1,2,0:T(8,128)(2,1)S(1)} collective-permute-done((bf16[2,192,192]{1,2,0:T(8,128)(2,1)S(1)}, bf16[2,192,192]{1,2,0:T(8,128)(2,1)S(1)}, u32[]{:S(2)}, u32[]{:S(2)}) %collective-permute-start.1) | collective-permute-done | bytes 147488 | tf_op jit(solution)/shard_map/ppermute | solution.py:52
  24.6 1.1 fusion.5
  25.8 49.2 %collective-permute-start.2 = (bf16[2,192,384]{2,1,0:T(8,128)(2,1)S(1)}, bf16[2,192,384]{2,1,0:T(8,128)(2,1)S(1)}, u32[]{:S(2)}, u32[]{:S(2)}) collective-permute-start(bf16[2,192,384]{2,1,0:T(8,128)(2,1)S(1)} %fusion.5), channel_id=1, source_target_pairs={{0,16},{16,0},{1,17},{17,1},{2,18},{18,2},{3,19},{19,3},{4,20},{20... | collective-permute-start | bytes 884744 | tf_op jit(solution)/shard_map/ppermute | solution.py:60
  74.9 7.6 %collective-permute-done.2 = bf16[2,192,384]{2,1,0:T(8,128)(2,1)S(1)} collective-permute-done((bf16[2,192,384]{2,1,0:T(8,128)(2,1)S(1)}, bf16[2,192,384]{2,1,0:T(8,128)(2,1)S(1)}, u32[]{:S(2)}, u32[]{:S(2)}) %collective-permute-start.2) | collective-permute-done | bytes 294944 | tf_op jit(solution)/shard_map/ppermute | solution.py:60
  82.6 0.1 select_bitcast_fusion.1
  82.6 0.9 pad_maximum_fusion
  83.5 0.0 all-gather.3.cloned.1.call-update
  83.5 1.3 collective-permute-start.3
  84.8 1.3 collective-permute-start.10
  86.2 12.5 %collective-permute-done.3 = bf16[2,192,384]{2,1,0:T(8,128)(2,1)S(1)} collective-permute-done((bf16[2,192,384]{2,1,0:T(8,128)(2,1)S(1)}, bf16[2,192,384]{2,1,0:T(8,128)(2,1)S(1)}, u32[]{:S(2)}, u32[]{:S(2)}) %collective-permute-start.3) | collective-permute-done | bytes 294944 | tf_op jit(solution)/shard_map/ppermute | solution.py:27
  98.6 4.1 %collective-permute-start.4 = (bf16[2,192,384]{2,1,0:T(8,128)(2,1)S(1)}, bf16[2,192,384]{2,1,0:T(8,128)(2,1)S(1)}, u32[]{:S(2)}, u32[]{:S(2)}) collective-permute-start(bf16[2,192,384]{2,1,0:T(8,128)(2,1)S(1)} %collective-permute-done.3), channel_id=1, source_target_pairs={{0,64},{64,128},{128,192},{192,256},{256,320},{320,384},{384,448},... | collective-permute-start | bytes 884744 | tf_op jit(solution)/shard_map/ppermute | solution.py:27
  102.7 0.0 collective-permute-done.10
  102.7 1.3 collective-permute-start.11
  104.0 4.6 %collective-permute-done.4 = bf16[2,192,384]{2,1,0:T(8,128)(2,1)S(1)} collective-permute-done((bf16[2,192,384]{2,1,0:T(8,128)(2,1)S(1)}, bf16[2,192,384]{2,1,0:T(8,128)(2,1)S(1)}, u32[]{:S(2)}, u32[]{:S(2)}) %collective-permute-start.4) | collective-permute-done | bytes 294944 | tf_op jit(solution)/shard_map/ppermute | solution.py:27
  108.6 4.1 %collective-permute-start.5 = (bf16[2,192,384]{2,1,0:T(8,128)(2,1)S(1)}, bf16[2,192,384]{2,1,0:T(8,128)(2,1)S(1)}, u32[]{:S(2)}, u32[]{:S(2)}) collective-permute-start(bf16[2,192,384]{2,1,0:T(8,128)(2,1)S(1)} %collective-permute-done.4), channel_id=1, source_target_pairs={{0,64},{64,128},{128,192},{192,256},{256,320},{320,384},{384,448},... | collective-permute-start | bytes 884744 | tf_op jit(solution)/shard_map/ppermute | solution.py:27
  112.7 0.0 collective-permute-done.11
  112.7 1.3 collective-permute-start.12
  114.0 3.6 %collective-permute-done.5 = bf16[2,192,384]{2,1,0:T(8,128)(2,1)S(1)} collective-permute-done((bf16[2,192,384]{2,1,0:T(8,128)(2,1)S(1)}, bf16[2,192,384]{2,1,0:T(8,128)(2,1)S(1)}, u32[]{:S(2)}, u32[]{:S(2)}) %collective-permute-start.5) | collective-permute-done | bytes 294944 | tf_op jit(solution)/shard_map/ppermute | solution.py:27
  117.7 4.2 %collective-permute-start.6 = (bf16[2,192,384]{2,1,0:T(8,128)(2,1)S(1)}, bf16[2,192,384]{2,1,0:T(8,128)(2,1)S(1)}, u32[]{:S(2)}, u32[]{:S(2)}) collective-permute-start(bf16[2,192,384]{2,1,0:T(8,128)(2,1)S(1)} %collective-permute-done.5), channel_id=1, source_target_pairs={{0,64},{64,128},{128,192},{192,256},{256,320},{320,384},{384,448},... | collective-permute-start | bytes 884744 | tf_op jit(solution)/shard_map/ppermute | solution.py:27
  121.9 0.8 collective-permute-done.12
  122.7 1.3 collective-permute-start.13
  124.0 2.1 collective-permute-done.6
  126.1 4.2 %collective-permute-start.7 = (bf16[2,192,384]{2,1,0:T(8,128)(2,1)S(1)}, bf16[2,192,384]{2,1,0:T(8,128)(2,1)S(1)}, u32[]{:S(2)}, u32[]{:S(2)}) collective-permute-start(bf16[2,192,384]{2,1,0:T(8,128)(2,1)S(1)} %collective-permute-done.6), channel_id=1, source_target_pairs={{0,64},{64,128},{128,192},{192,256},{256,320},{320,384},{384,448},... | collective-permute-start | bytes 884744 | tf_op jit(solution)/shard_map/ppermute | solution.py:27
  130.3 0.6 collective-permute-done.13
  130.9 1.3 collective-permute-start.14
  132.2 1.7 collective-permute-done.7
  133.9 4.8 %collective-permute-start.8 = (bf16[2,192,384]{2,1,0:T(8,128)(2,1)S(1)}, bf16[2,192,384]{2,1,0:T(8,128)(2,1)}, u32[]{:S(2)}, u32[]{:S(2)}) collective-permute-start(bf16[2,192,384]{2,1,0:T(8,128)(2,1)S(1)} %collective-permute-done.7), channel_id=1, source_target_pairs={{0,64},{64,128},{128,192},{192,256},{256,320},{320,384},{384,448},... | collective-permute-start | bytes 884744 | tf_op jit(solution)/shard_map/ppermute | solution.py:27
  138.7 1.0 collective-permute-done.14
  139.8 1.3 collective-permute-start.15
  141.0 0.6 collective-permute-done.8
  141.7 6.3 %collective-permute-start.9 = (bf16[2,192,384]{2,1,0:T(8,128)(2,1)}, bf16[2,192,384]{2,1,0:T(8,128)(2,1)}, u32[]{:S(2)}, u32[]{:S(2)}) collective-permute-start(bf16[2,192,384]{2,1,0:T(8,128)(2,1)} %collective-permute-done.8), channel_id=1, source_target_pairs={{0,64},{64,128},{128,192},{192,256},{256,320},{320,384},{384,448},... | collective-permute-start | bytes 884744 | tf_op jit(solution)/shard_map/ppermute | solution.py:27
  148.0 0.7 collective-permute-done.15
  148.6 1.3 collective-permute-start.16
  149.9 1.3 collective-permute-done.9
  151.2 1.0 bitcast_dynamic-update-slice_fusion.13
  152.2 1.0 bitcast_dynamic-update-slice_fusion.12
  153.9 4.7 %collective-permute-done.16 = bf16[2,192,384]{2,1,0:T(8,128)(2,1)S(1)} collective-permute-done((bf16[2,192,384]{2,1,0:T(8,128)(2,1)S(1)}, bf16[2,192,384]{2,1,0:T(8,128)(2,1)S(1)}, u32[]{:S(2)}, u32[]{:S(2)}) %collective-permute-start.16) | collective-permute-done | bytes 294944 | tf_op jit(solution)/shard_map/ppermute | solution.py:28
  158.7 2.1 copy-done.1
  160.8 1.7 constant_dynamic-slice_fusion
  162.5 7.4 %collective-permute-start.17 = (bf16[8,2,192,384]{3,2,0,1:T(8,128)(2,1)}, bf16[8,2,192,384]{3,2,0,1:T(8,128)(2,1)}, u32[]{:S(2)}, u32[]{:S(2)}) collective-permute-start(bf16[8,2,192,384]{3,2,0,1:T(8,128)(2,1)} %constant_dynamic-slice_fusion), channel_id=1, source_target_pairs={{0,32},{32,0},{1,33},{33,1},{2,34},{34,2},{3,35},{35,3},{4,36},{36... | collective-permute-start | bytes 7077896 | tf_op jit(solution)/shard_map/ppermute | solution.py:33
  169.8 18.1 %all-gather.3.cloned.1.call-done = bf16[2,32,192,384]{3,2,1,0:T(8,128)(2,1)} async-done(((bf16[2,2,192,384]{3,2,1,0:T(8,128)(2,1)}), bf16[2,32,192,384]{3,2,1,0:T(8,128)(2,1)}) %all-gather.3.cloned.1.call-update) | async-done | bytes 9437200 | tf_op jit(solution)/shard_map/all_gather | solution.py:63
  187.9 4.7 %fusion.13 = (bf16[1,32,192,384]{3,2,1,0:T(8,128)(2,1)S(1)}, bf16[1,32,192,384]{3,2,1,0:T(8,128)(2,1)S(1)}) fusion(bf16[2,32,192,384]{3,2,1,0:T(8,128)(2,1)} %all-gather.3.cloned.1.call-done), kind=kLoop, calls=%fused_computation.53 | loop fusion | bytes 18874368 | tf_op jit(solution)/shard_map/slice | solution.py:77
  192.6 3.3 %dynamic-slice_bitcast_fusion.1 = (bf16[4,2,2,192,384]{4,3,1,2,0:T(8,128)(2,1)}, bf16[4,2,2,192,384]{4,3,1,2,0:T(8,128)(2,1)}, bf16[4,2,2,192,384]{4,3,1,2,0:T(8,128)(2,1)S(1)}, bf16[4,2,2,192,384]{4,3,1,2,0:T(8,128)(2,1)S(1)}) fusion(bf16[4,2,2,2,192,384]{5,4,3,2,1,0:T(8,128)(2,1)S(1)} %bitcast.170, s32[]{:T(128)S(6)} %select_n.68, s32[]{:T(128)S(6)} %select_n.70, ...), kind=kLoop, calls=%fused_computation.1 | loop fusion | bytes 18874376 | tf_op jit(solution)/shard_map/transpose | solution.py:72
  195.9 2.1 copy.44
  198.0 0.3 copy-done
  198.3 0.3 copy.42
  198.5 0.0 slice-start.1
  198.6 0.2 copy.40
  198.8 0.2 copy.24
  199.1 1.4 slice-done
  200.5 0.1 slice-done.1
  200.5 1.1 convolution_bitcast_fusion.1
  201.6 0.0 collective-permute-done.17
  201.7 2.4 %convolution_bitcast_fusion = f32[2,384,2,192]{1,3,2,0:T(8,128)S(1)} fusion(bf16[4,2,384,384,1]{3,2,0,4,1:T(8,128)(2,1)S(1)} %bitcast.174, bf16[8,2,192,384]{3,2,0,1:T(8,128)(2,1)} %collective-permute-done.17), kind=kOutput, calls=%fused_computation.4 | convolution fusion | flops 905969664 | bytes 4718592 | tf_op jit(solution)/shard_map/zpxc,zqcn->pqxn/dot_general | solution.py:73
  204.0 2.4 %convolution_bitcast_fusion.2 = f32[2,384,2,192]{1,3,2,0:T(8,128)S(1)} fusion(bf16[4,2,384,384,1]{3,2,0,4,1:T(8,128)(2,1)S(1)} %bitcast.175, bf16[8,2,192,384]{3,2,0,1:T(8,128)(2,1)} %collective-permute-done.17), kind=kOutput, calls=%fused_computation.6 | convolution fusion | flops 905969664 | bytes 4718592 | tf_op jit(solution)/shard_map/zpxc,zqcn->pqxn/dot_general | solution.py:73
  206.4 1.2 fusion.3
  207.8 0.9 pad_maximum_fusion.1
  (20 shorter events, 0.7 us)
Async XLA Ops:
  6.5 181.3 %all-gather.3.cloned.1.call-start = ((), (), s32[]{:S(2)}) async-start(), calls=%async_computation | async-start | bytes 10027008 | tf_op jit(solution)/shard_map/all_gather | solution.py:63
  7.9 11.7 %collective-permute-start = (bf16[2,192,192]{1,2,0:T(8,128)(2,1)S(1)}, bf16[2,192,192]{1,2,0:T(8,128)(2,1)S(1)}, u32[]{:S(2)}, u32[]{:S(2)}) collective-permute-start(bf16[2,192,192]{1,2,0:T(8,128)(2,1)S(1)} %copy.56), channel_id=1, source_target_pairs={{0,0},{32,2},{64,4},{96,6},{128,8},{160,10},{192,12},{224,14},{256... | collective-permute-start | bytes 442376 | tf_op jit(solution)/shard_map/ppermute | solution.py:52
  14.1 10.5 %collective-permute-start.1 = (bf16[2,192,192]{1,2,0:T(8,128)(2,1)S(1)}, bf16[2,192,192]{1,2,0:T(8,128)(2,1)S(1)}, u32[]{:S(2)}, u32[]{:S(2)}) collective-permute-start(bf16[2,192,192]{1,2,0:T(8,128)(2,1)S(1)} %copy.57), channel_id=1, source_target_pairs={{0,1},{32,3},{64,5},{96,7},{128,9},{160,11},{192,13},{224,15},{256... | collective-permute-start | bytes 442376 | tf_op jit(solution)/shard_map/ppermute | solution.py:52
  25.8 56.8 %collective-permute-start.2 = (bf16[2,192,384]{2,1,0:T(8,128)(2,1)S(1)}, bf16[2,192,384]{2,1,0:T(8,128)(2,1)S(1)}, u32[]{:S(2)}, u32[]{:S(2)}) collective-permute-start(bf16[2,192,384]{2,1,0:T(8,128)(2,1)S(1)} %fusion.5), channel_id=1, source_target_pairs={{0,16},{16,0},{1,17},{17,1},{2,18},{18,2},{3,19},{19,3},{4,20},{20... | collective-permute-start | bytes 884744 | tf_op jit(solution)/shard_map/ppermute | solution.py:60
  83.5 15.1 %collective-permute-start.3 = (bf16[2,192,384]{2,1,0:T(8,128)(2,1)S(1)}, bf16[2,192,384]{2,1,0:T(8,128)(2,1)S(1)}, u32[]{:S(2)}, u32[]{:S(2)}) collective-permute-start(bf16[2,192,384]{2,1,0:T(8,128)(2,1)S(1)} %fusion.5), channel_id=1, source_target_pairs={{0,64},{64,128},{128,192},{192,256},{256,320},{320,384},{384,448},... | collective-permute-start | bytes 884744 | tf_op jit(solution)/shard_map/ppermute | solution.py:27
  84.8 17.9 %collective-permute-start.10 = (bf16[2,192,384]{2,1,0:T(8,128)(2,1)S(1)}, bf16[2,192,384]{2,1,0:T(8,128)(2,1)S(1)}, u32[]{:S(2)}, u32[]{:S(2)}) collective-permute-start(bf16[2,192,384]{2,1,0:T(8,128)(2,1)S(1)} %fusion.5), channel_id=1, source_target_pairs={{64,0},{128,64},{192,128},{256,192},{320,256},{384,320},{448,384},... | collective-permute-start | bytes 884744 | tf_op jit(solution)/shard_map/ppermute | solution.py:28
  98.6 10.0 %collective-permute-start.4 = (bf16[2,192,384]{2,1,0:T(8,128)(2,1)S(1)}, bf16[2,192,384]{2,1,0:T(8,128)(2,1)S(1)}, u32[]{:S(2)}, u32[]{:S(2)}) collective-permute-start(bf16[2,192,384]{2,1,0:T(8,128)(2,1)S(1)} %collective-permute-done.3), channel_id=1, source_target_pairs={{0,64},{64,128},{128,192},{192,256},{256,320},{320,384},{384,448},... | collective-permute-start | bytes 884744 | tf_op jit(solution)/shard_map/ppermute | solution.py:27
  102.7 10.0 %collective-permute-start.11 = (bf16[2,192,384]{2,1,0:T(8,128)(2,1)S(1)}, bf16[2,192,384]{2,1,0:T(8,128)(2,1)S(1)}, u32[]{:S(2)}, u32[]{:S(2)}) collective-permute-start(bf16[2,192,384]{2,1,0:T(8,128)(2,1)S(1)} %collective-permute-done.10), channel_id=1, source_target_pairs={{64,0},{128,64},{192,128},{256,192},{320,256},{384,320},{448,384},... | collective-permute-start | bytes 884744 | tf_op jit(solution)/shard_map/ppermute | solution.py:28
  108.6 9.1 %collective-permute-start.5 = (bf16[2,192,384]{2,1,0:T(8,128)(2,1)S(1)}, bf16[2,192,384]{2,1,0:T(8,128)(2,1)S(1)}, u32[]{:S(2)}, u32[]{:S(2)}) collective-permute-start(bf16[2,192,384]{2,1,0:T(8,128)(2,1)S(1)} %collective-permute-done.4), channel_id=1, source_target_pairs={{0,64},{64,128},{128,192},{192,256},{256,320},{320,384},{384,448},... | collective-permute-start | bytes 884744 | tf_op jit(solution)/shard_map/ppermute | solution.py:27
  112.7 9.9 %collective-permute-start.12 = (bf16[2,192,384]{2,1,0:T(8,128)(2,1)S(1)}, bf16[2,192,384]{2,1,0:T(8,128)(2,1)S(1)}, u32[]{:S(2)}, u32[]{:S(2)}) collective-permute-start(bf16[2,192,384]{2,1,0:T(8,128)(2,1)S(1)} %collective-permute-done.11), channel_id=1, source_target_pairs={{64,0},{128,64},{192,128},{256,192},{320,256},{384,320},{448,384},... | collective-permute-start | bytes 884744 | tf_op jit(solution)/shard_map/ppermute | solution.py:28
  117.7 8.4 %collective-permute-start.6 = (bf16[2,192,384]{2,1,0:T(8,128)(2,1)S(1)}, bf16[2,192,384]{2,1,0:T(8,128)(2,1)S(1)}, u32[]{:S(2)}, u32[]{:S(2)}) collective-permute-start(bf16[2,192,384]{2,1,0:T(8,128)(2,1)S(1)} %collective-permute-done.5), channel_id=1, source_target_pairs={{0,64},{64,128},{128,192},{192,256},{256,320},{320,384},{384,448},... | collective-permute-start | bytes 884744 | tf_op jit(solution)/shard_map/ppermute | solution.py:27
  122.7 8.2 %collective-permute-start.13 = (bf16[2,192,384]{2,1,0:T(8,128)(2,1)S(1)}, bf16[2,192,384]{2,1,0:T(8,128)(2,1)S(1)}, u32[]{:S(2)}, u32[]{:S(2)}) collective-permute-start(bf16[2,192,384]{2,1,0:T(8,128)(2,1)S(1)} %collective-permute-done.12), channel_id=1, source_target_pairs={{64,0},{128,64},{192,128},{256,192},{320,256},{384,320},{448,384},... | collective-permute-start | bytes 884744 | tf_op jit(solution)/shard_map/ppermute | solution.py:28
  126.1 7.9 %collective-permute-start.7 = (bf16[2,192,384]{2,1,0:T(8,128)(2,1)S(1)}, bf16[2,192,384]{2,1,0:T(8,128)(2,1)S(1)}, u32[]{:S(2)}, u32[]{:S(2)}) collective-permute-start(bf16[2,192,384]{2,1,0:T(8,128)(2,1)S(1)} %collective-permute-done.6), channel_id=1, source_target_pairs={{0,64},{64,128},{128,192},{192,256},{256,320},{320,384},{384,448},... | collective-permute-start | bytes 884744 | tf_op jit(solution)/shard_map/ppermute | solution.py:27
  130.9 8.8 %collective-permute-start.14 = (bf16[2,192,384]{2,1,0:T(8,128)(2,1)S(1)}, bf16[2,192,384]{2,1,0:T(8,128)(2,1)S(1)}, u32[]{:S(2)}, u32[]{:S(2)}) collective-permute-start(bf16[2,192,384]{2,1,0:T(8,128)(2,1)S(1)} %collective-permute-done.13), channel_id=1, source_target_pairs={{64,0},{128,64},{192,128},{256,192},{320,256},{384,320},{448,384},... | collective-permute-start | bytes 884744 | tf_op jit(solution)/shard_map/ppermute | solution.py:28
  133.9 7.8 %collective-permute-start.8 = (bf16[2,192,384]{2,1,0:T(8,128)(2,1)S(1)}, bf16[2,192,384]{2,1,0:T(8,128)(2,1)}, u32[]{:S(2)}, u32[]{:S(2)}) collective-permute-start(bf16[2,192,384]{2,1,0:T(8,128)(2,1)S(1)} %collective-permute-done.7), channel_id=1, source_target_pairs={{0,64},{64,128},{128,192},{192,256},{256,320},{320,384},{384,448},... | collective-permute-start | bytes 884744 | tf_op jit(solution)/shard_map/ppermute | solution.py:27
  139.8 8.9 %collective-permute-start.15 = (bf16[2,192,384]{2,1,0:T(8,128)(2,1)S(1)}, bf16[2,192,384]{2,1,0:T(8,128)(2,1)S(1)}, u32[]{:S(2)}, u32[]{:S(2)}) collective-permute-start(bf16[2,192,384]{2,1,0:T(8,128)(2,1)S(1)} %collective-permute-done.14), channel_id=1, source_target_pairs={{64,0},{128,64},{192,128},{256,192},{320,256},{384,320},{448,384},... | collective-permute-start | bytes 884744 | tf_op jit(solution)/shard_map/ppermute | solution.py:28
  141.7 9.6 %collective-permute-start.9 = (bf16[2,192,384]{2,1,0:T(8,128)(2,1)}, bf16[2,192,384]{2,1,0:T(8,128)(2,1)}, u32[]{:S(2)}, u32[]{:S(2)}) collective-permute-start(bf16[2,192,384]{2,1,0:T(8,128)(2,1)} %collective-permute-done.8), channel_id=1, source_target_pairs={{0,64},{64,128},{128,192},{192,256},{256,320},{320,384},{384,448},... | collective-permute-start | bytes 884744 | tf_op jit(solution)/shard_map/ppermute | solution.py:27
  148.6 10.0 %collective-permute-start.16 = (bf16[2,192,384]{2,1,0:T(8,128)(2,1)S(1)}, bf16[2,192,384]{2,1,0:T(8,128)(2,1)S(1)}, u32[]{:S(2)}, u32[]{:S(2)}) collective-permute-start(bf16[2,192,384]{2,1,0:T(8,128)(2,1)S(1)} %collective-permute-done.15), channel_id=1, source_target_pairs={{64,0},{128,64},{192,128},{256,192},{320,256},{384,320},{448,384},... | collective-permute-start | bytes 884744 | tf_op jit(solution)/shard_map/ppermute | solution.py:28
  158.7 2.1 copy-start.1
  162.5 39.2 %collective-permute-start.17 = (bf16[8,2,192,384]{3,2,0,1:T(8,128)(2,1)}, bf16[8,2,192,384]{3,2,0,1:T(8,128)(2,1)}, u32[]{:S(2)}, u32[]{:S(2)}) collective-permute-start(bf16[8,2,192,384]{3,2,0,1:T(8,128)(2,1)} %constant_dynamic-slice_fusion), channel_id=1, source_target_pairs={{0,32},{32,0},{1,33},{33,1},{2,34},{34,2},{3,35},{35,3},{4,36},{36... | collective-permute-start | bytes 7077896 | tf_op jit(solution)/shard_map/ppermute | solution.py:33
  195.9 2.4 %copy-start = (bf16[4,2,2,192,384]{4,3,1,2,0:T(8,128)(2,1)S(1)}, bf16[4,2,2,192,384]{4,3,1,2,0:T(8,128)(2,1)}, u32[]{:S(2)}) copy-start(bf16[4,2,2,192,384]{4,3,1,2,0:T(8,128)(2,1)} %get-tuple-element.9) | copy-start | bytes 7077892
  198.3 2.2 %slice-start = ((s8[4423680]{0:T(1024)(128)(4,1)}), s8[4194304]{0:T(1024)(128)(4,1)S(1)}, s32[]{:S(2)}) async-start(s8[4423680]{0:T(1024)(128)(4,1)} %bitcast.172), calls=%async_computation.1 | async-start | bytes 8388608
  198.5 2.0 slice-start.1
Sparse Core Ops, SparseCore 0:
  83.7 104.1 all-gather.2

commit v6 on v5

--- a/solution.py
+++ b/solution.py
@@ -60,7 +60,9 @@
     partner_block = lax.ppermute(symmetric, "zh", [(0, 1), (1, 0)])
     top = jnp.where(half_index == 0, symmetric, partner_block)
     bottom = jnp.where(half_index == 0, partner_block, symmetric)
-    panels = lax.all_gather(jnp.stack([top, bottom]), ("y", "x"), axis=1, tiled=False)
+    panels = lax.all_gather(jnp.stack([top, bottom]), "x", axis=1, tiled=False)
+    panels = lax.all_gather(panels, "y", axis=1, tiled=False)
+    panels = panels.reshape((2, -1) + symmetric.shape)
     mine, other = gather_line(symmetric)
     core_index = lax.axis_index("core")
     n_line = mine.shape[0]

time: 216 us -> 268 us (1.24)
  waiting for transfers between devices: 67.9 us -> 116 us
  starting transfers between devices: 103 us -> 106 us
    all_gather x1 -> x2, waiting for transfers between devices: 18.1 us -> 77.3 us  [the longest x1 53.7 us: local(): panels = lax.all_gather(jnp.stack([top, bottom]), 'x', axis=1, tiled=False)]
    ppermute x7, waiting for transfers between devices: 26.4 us -> 11.2 us  [gather_line(): lax.ppermute(rightward, 'zl', [(k, k + 1) for k in range(n_line - 1)])]
    transpose x5 -> x0, local copies, waits for them, and re-layouts: 6.08 us -> none  [product(): jnp.swapaxes(panel, 1, 2).reshape(n_line // 2, parts, 2 * rows, cols)]
    dynamic_slice x0 -> x5, local copies, waits for them, and re-layouts: none -> 6.06 us  [product(): panel = lax.dynamic_index_in_dim(panel, parity, 1, keepdims=False)]
    ppermute x7, waiting for transfers between devices: 7.76 us -> 12.3 us  [gather_line(): lax.ppermute(leftward, 'zl', [(k + 1, k) for k in range(n_line - 1)])]
  transfers between devices with their start and end apart: 19 -> 20, of which waited for: 16 -> 16; matrix products, arithmetic and copies ran while one was open for 8% -> 6% of each run, Pallas kernels for 0% -> 0%
where the time goes in v6:
time: 268 us; the launch traced here: 267 us
  waiting for transfers between devices  116 us (43%)
  starting transfers between devices  106 us (40%)
  local copies, waits for them, and re-layouts  20.8 us (8%)
  between operations  13.8 us (5%)
  matrix products  7.1 us (3%)
  other arithmetic  3.02 us (1%)
    all_gather x1, waiting for transfers between devices, local(): panels = lax.all_gather(jnp.stack([top, bottom]), 'x', axis=1, tiled=False)  53.7 us
    ppermute x1, starting transfers between devices, local(): partner_block = lax.ppermute(symmetric, 'zh', [(0, 1), (1, 0)])  49.2 us
    ppermute x7, starting transfers between devices, gather_line(): lax.ppermute(rightward, 'zl', [(k, k + 1) for k in range(n_line - 1)])  31.4 us
    all_gather x1, waiting for transfers between devices, local(): panels = lax.all_gather(panels, 'y', axis=1, tiled=False)  23.6 us
    ppermute x7, waiting for transfers between devices, gather_line(): lax.ppermute(leftward, 'zl', [(k + 1, k) for k in range(n_line - 1)])  12.3 us
    ppermute x7, waiting for transfers between devices, gather_line(): lax.ppermute(rightward, 'zl', [(k, k + 1) for k in range(n_line - 1)])  11.2 us
    ppermute x7, starting transfers between devices, gather_line(): lax.ppermute(leftward, 'zl', [(k + 1, k) for k in range(n_line - 1)])  9 us
    ppermute x2, starting transfers between devices, local(): lax.ppermute(piece, axes, mirror_pairs(n_recv, n_shot, flip))  8.55 us
  transfers between devices with their start and end apart: 20, of which 16 were waited for; matrix products, arithmetic and copies ran while one was open for 6% of the time, Pallas kernels for 0%

profile of v6, /device:TPU:1, one launch (start us, length us, event | category | flops | bytes accessed | tf_op | source)
XLA Modules:
  0.0 266.9 jit_solution(7328656980334131815)
XLA Ops:
  6.5 1.2 constant_dynamic-slice_fusion.6
  7.8 0.1 copy.33
  7.9 6.0 %collective-permute-start = (bf16[2,192,192]{1,2,0:T(8,128)(2,1)S(1)}, bf16[2,192,192]{1,2,0:T(8,128)(2,1)S(1)}, u32[]{:S(2)}, u32[]{:S(2)}) collective-permute-start(bf16[2,192,192]{1,2,0:T(8,128)(2,1)S(1)} %copy.33), channel_id=1, source_target_pairs={{0,0},{32,2},{64,4},{96,6},{128,8},{160,10},{192,12},{224,14},{256... | collective-permute-start | bytes 442376 | tf_op jit(solution)/shard_map/ppermute | solution.py:52
  13.9 0.1 copy.34
  14.1 2.5 collective-permute-start.1
  16.6 3.0 %collective-permute-done = bf16[2,192,192]{1,2,0:T(8,128)(2,1)S(1)} collective-permute-done((bf16[2,192,192]{1,2,0:T(8,128)(2,1)S(1)}, bf16[2,192,192]{1,2,0:T(8,128)(2,1)S(1)}, u32[]{:S(2)}, u32[]{:S(2)}) %collective-permute-start) | collective-permute-done | bytes 147488 | tf_op jit(solution)/shard_map/ppermute | solution.py:52
  19.6 5.0 %collective-permute-done.1 = bf16[2,192,192]{1,2,0:T(8,128)(2,1)S(1)} collective-permute-done((bf16[2,192,192]{1,2,0:T(8,128)(2,1)S(1)}, bf16[2,192,192]{1,2,0:T(8,128)(2,1)S(1)}, u32[]{:S(2)}, u32[]{:S(2)}) %collective-permute-start.1) | collective-permute-done | bytes 147488 | tf_op jit(solution)/shard_map/ppermute | solution.py:52
  24.7 1.1 fusion.5
  25.8 49.2 %collective-permute-start.2 = (bf16[2,192,384]{2,1,0:T(8,128)(2,1)S(1)}, bf16[2,192,384]{2,1,0:T(8,128)(2,1)S(1)}, u32[]{:S(2)}, u32[]{:S(2)}) collective-permute-start(bf16[2,192,384]{2,1,0:T(8,128)(2,1)S(1)} %fusion.5), channel_id=1, source_target_pairs={{0,16},{16,0},{1,17},{17,1},{2,18},{18,2},{3,19},{19,3},{4,20},{20... | collective-permute-start | bytes 884744 | tf_op jit(solution)/shard_map/ppermute | solution.py:60
  75.0 7.5 %collective-permute-done.2 = bf16[2,192,384]{2,1,0:T(8,128)(2,1)S(1)} collective-permute-done((bf16[2,192,384]{2,1,0:T(8,128)(2,1)S(1)}, bf16[2,192,384]{2,1,0:T(8,128)(2,1)S(1)}, u32[]{:S(2)}, u32[]{:S(2)}) %collective-permute-start.2) | collective-permute-done | bytes 294944 | tf_op jit(solution)/shard_map/ppermute | solution.py:60
  82.5 0.1 select_bitcast_fusion.1
  82.6 0.9 pad_maximum_fusion
  83.4 0.0 all-gather.5.cloned.1.call-update
  83.5 0.0 all-gather.7.cloned.1.call-start
  83.5 53.7 %all-gather.5.cloned.1.call-done = bf16[2,8,192,384]{3,2,1,0:T(8,128)(2,1)} async-done(((bf16[2,2,192,384]{3,2,1,0:T(8,128)(2,1)}), bf16[2,8,192,384]{3,2,1,0:T(8,128)(2,1)}) %all-gather.5.cloned.1.call-update) | async-done | bytes 2359312 | tf_op jit(solution)/shard_map/all_gather | solution.py:63
  137.2 0.0 all-gather.7.cloned.1.call-update
  137.2 3.2 %collective-permute-start.3 = (bf16[2,192,384]{2,1,0:T(8,128)(2,1)S(1)}, bf16[2,192,384]{2,1,0:T(8,128)(2,1)S(1)}, u32[]{:S(2)}, u32[]{:S(2)}) collective-permute-start(bf16[2,192,384]{2,1,0:T(8,128)(2,1)S(1)} %fusion.5), channel_id=1, source_target_pairs={{0,64},{64,128},{128,192},{192,256},{256,320},{320,384},{384,448},... | collective-permute-start | bytes 884744 | tf_op jit(solution)/shard_map/ppermute | solution.py:27
  140.4 1.3 collective-permute-start.10
  141.7 4.3 %collective-permute-done.3 = bf16[2,192,384]{2,1,0:T(8,128)(2,1)S(1)} collective-permute-done((bf16[2,192,384]{2,1,0:T(8,128)(2,1)S(1)}, bf16[2,192,384]{2,1,0:T(8,128)(2,1)S(1)}, u32[]{:S(2)}, u32[]{:S(2)}) %collective-permute-start.3) | collective-permute-done | bytes 294944 | tf_op jit(solution)/shard_map/ppermute | solution.py:27
  146.1 4.1 %collective-permute-start.4 = (bf16[2,192,384]{2,1,0:T(8,128)(2,1)S(1)}, bf16[2,192,384]{2,1,0:T(8,128)(2,1)S(1)}, u32[]{:S(2)}, u32[]{:S(2)}) collective-permute-start(bf16[2,192,384]{2,1,0:T(8,128)(2,1)S(1)} %collective-permute-done.3), channel_id=1, source_target_pairs={{0,64},{64,128},{128,192},{192,256},{256,320},{320,384},{384,448},... | collective-permute-start | bytes 884744 | tf_op jit(solution)/shard_map/ppermute | solution.py:27
  150.2 0.0 collective-permute-done.10
  150.2 1.3 collective-permute-start.11
  151.5 3.4 %collective-permute-done.4 = bf16[2,192,384]{2,1,0:T(8,128)(2,1)S(1)} collective-permute-done((bf16[2,192,384]{2,1,0:T(8,128)(2,1)S(1)}, bf16[2,192,384]{2,1,0:T(8,128)(2,1)S(1)}, u32[]{:S(2)}, u32[]{:S(2)}) %collective-permute-start.4) | collective-permute-done | bytes 294944 | tf_op jit(solution)/shard_map/ppermute | solution.py:27
  154.9 4.1 %collective-permute-start.5 = (bf16[2,192,384]{2,1,0:T(8,128)(2,1)S(1)}, bf16[2,192,384]{2,1,0:T(8,128)(2,1)S(1)}, u32[]{:S(2)}, u32[]{:S(2)}) collective-permute-start(bf16[2,192,384]{2,1,0:T(8,128)(2,1)S(1)} %collective-permute-done.4), channel_id=1, source_target_pairs={{0,64},{64,128},{128,192},{192,256},{256,320},{320,384},{384,448},... | collective-permute-start | bytes 884744 | tf_op jit(solution)/shard_map/ppermute | solution.py:27
  159.0 0.0 collective-permute-done.11
  159.0 1.3 collective-permute-start.12
  160.3 2.3 collective-permute-done.5
  162.7 4.4 %collective-permute-start.6 = (bf16[2,192,384]{2,1,0:T(8,128)(2,1)S(1)}, bf16[2,192,384]{2,1,0:T(8,128)(2,1)S(1)}, u32[]{:S(2)}, u32[]{:S(2)}) collective-permute-start(bf16[2,192,384]{2,1,0:T(8,128)(2,1)S(1)} %collective-permute-done.5), channel_id=1, source_target_pairs={{0,64},{64,128},{128,192},{192,256},{256,320},{320,384},{384,448},... | collective-permute-start | bytes 884744 | tf_op jit(solution)/shard_map/ppermute | solution.py:27
  167.0 1.5 collective-permute-done.12
  168.5 1.3 collective-permute-start.13
  169.8 0.8 collective-permute-done.6
  170.7 4.2 %collective-permute-start.7 = (bf16[2,192,384]{2,1,0:T(8,128)(2,1)S(1)}, bf16[2,192,384]{2,1,0:T(8,128)(2,1)S(1)}, u32[]{:S(2)}, u32[]{:S(2)}) collective-permute-start(bf16[2,192,384]{2,1,0:T(8,128)(2,1)S(1)} %collective-permute-done.6), channel_id=1, source_target_pairs={{0,64},{64,128},{128,192},{192,256},{256,320},{320,384},{384,448},... | collective-permute-start | bytes 884744 | tf_op jit(solution)/shard_map/ppermute | solution.py:27
  174.9 2.2 collective-permute-done.13
  177.1 1.3 collective-permute-start.14
  178.4 0.2 collective-permute-done.7
  178.5 5.5 %collective-permute-start.8 = (bf16[2,192,384]{2,1,0:T(8,128)(2,1)S(1)}, bf16[2,192,384]{2,1,0:T(8,128)(2,1)}, u32[]{:S(2)}, u32[]{:S(2)}) collective-permute-start(bf16[2,192,384]{2,1,0:T(8,128)(2,1)S(1)} %collective-permute-done.7), channel_id=1, source_target_pairs={{0,64},{64,128},{128,192},{192,256},{256,320},{320,384},{384,448},... | collective-permute-start | bytes 884744 | tf_op jit(solution)/shard_map/ppermute | solution.py:27
  184.0 1.8 collective-permute-done.14
  185.9 1.3 collective-permute-start.15
  187.1 0.0 collective-permute-done.8
  187.2 5.9 %collective-permute-start.9 = (bf16[2,192,384]{2,1,0:T(8,128)(2,1)}, bf16[2,192,384]{2,1,0:T(8,128)(2,1)}, u32[]{:S(2)}, u32[]{:S(2)}) collective-permute-start(bf16[2,192,384]{2,1,0:T(8,128)(2,1)} %collective-permute-done.8), channel_id=1, source_target_pairs={{0,64},{64,128},{128,192},{192,256},{256,320},{320,384},{384,448},... | collective-permute-start | bytes 884744 | tf_op jit(solution)/shard_map/ppermute | solution.py:27
  193.1 1.8 collective-permute-done.15
  194.9 1.3 collective-permute-start.16
  196.2 0.1 collective-permute-done.9
  196.3 1.0 bitcast_dynamic-update-slice_fusion.13
  197.3 1.0 bitcast_dynamic-update-slice_fusion.12
  199.0 5.0 %collective-permute-done.16 = bf16[2,192,384]{2,1,0:T(8,128)(2,1)S(1)} collective-permute-done((bf16[2,192,384]{2,1,0:T(8,128)(2,1)S(1)}, bf16[2,192,384]{2,1,0:T(8,128)(2,1)S(1)}, u32[]{:S(2)}, u32[]{:S(2)}) %collective-permute-start.16) | collective-permute-done | bytes 294944 | tf_op jit(solution)/shard_map/ppermute | solution.py:28
  204.0 2.1 copy-done.1
  206.2 1.7 constant_dynamic-slice_fusion.3
  207.8 7.6 %collective-permute-start.17 = (bf16[8,2,192,384]{3,2,0,1:T(8,128)(2,1)}, bf16[8,2,192,384]{3,2,0,1:T(8,128)(2,1)}, u32[]{:S(2)}, u32[]{:S(2)}) collective-permute-start(bf16[8,2,192,384]{3,2,0,1:T(8,128)(2,1)} %constant_dynamic-slice_fusion.3), channel_id=1, source_target_pairs={{0,32},{32,0},{1,33},{33,1},{2,34},{34,2},{3,35},{35,3},{4,36},{36... | collective-permute-start | bytes 7077896 | tf_op jit(solution)/shard_map/ppermute | solution.py:33
  215.5 23.6 %all-gather.7.cloned.1.call-done = bf16[2,16,2,192,384]{4,3,2,1,0:T(8,128)(2,1)} async-done(((bf16[2,4,2,192,384]{4,3,2,1,0:T(8,128)(2,1)}), bf16[2,16,2,192,384]{4,3,2,1,0:T(8,128)(2,1)}) %all-gather.7.cloned.1.call-update) | async-done | bytes 9437200 | tf_op jit(solution)/shard_map/all_gather | solution.py:64
  239.1 5.0 %fusion.13 = (bf16[1,16,2,192,384]{4,3,2,1,0:T(8,128)(2,1)S(1)}, bf16[1,16,2,192,384]{4,3,2,1,0:T(8,128)(2,1)S(1)}) fusion(bf16[2,16,2,192,384]{4,3,2,1,0:T(8,128)(2,1)} %all-gather.7.cloned.1.call-done), kind=kLoop, calls=%fused_computation.53 | loop fusion | bytes 18874368 | tf_op jit(solution)/shard_map/slice | solution.py:79
  244.1 3.3 %constant_dynamic-slice_fusion.1 = (bf16[4,1,2,2,192,384]{5,4,3,2,1,0:T(8,128)(2,1)}, bf16[4,1,2,2,192,384]{5,4,3,2,1,0:T(8,128)(2,1)}, bf16[4,1,2,2,192,384]{5,...) fusion(bf16[4,2,2,2,192,384]{5,4,3,2,1,0:T(8,128)(2,1)S(1)} %bitcast.163, s32[]{:T(128)S(6)} %select_n.68, ...), kind=kLoop, calls=%fused_computation.47 | loop fusion | bytes 18874376 | tf_op jit(solution)/shard_map/jit(dynamic_index_in_dim)/dynamic_slice | solution.py:73
  247.4 2.1 copy.21
  249.4 0.3 copy-done
  249.8 0.3 copy.20
  250.0 0.2 copy.19
  250.3 0.2 copy.4
  250.5 1.4 slice-done
  251.9 0.1 slice-done.1
  252.0 1.1 convolution_bitcast_fusion.1
  253.1 2.4 convolution_bitcast_fusion
  255.5 2.4 convolution_bitcast_fusion.2
  257.9 1.2 fusion.3
  259.2 0.9 pad_maximum_fusion.1
  (23 shorter events, 0.8 us)
Async XLA Ops:
  6.5 130.7 %all-gather.5.cloned.1.call-start = ((), (), s32[]{:S(2)}) async-start(), calls=%async_computation | async-start | bytes 2949120 | tf_op jit(solution)/shard_map/all_gather | solution.py:63
  7.9 11.7 %collective-permute-start = (bf16[2,192,192]{1,2,0:T(8,128)(2,1)S(1)}, bf16[2,192,192]{1,2,0:T(8,128)(2,1)S(1)}, u32[]{:S(2)}, u32[]{:S(2)}) collective-permute-start(bf16[2,192,192]{1,2,0:T(8,128)(2,1)S(1)} %copy.33), channel_id=1, source_target_pairs={{0,0},{32,2},{64,4},{96,6},{128,8},{160,10},{192,12},{224,14},{256... | collective-permute-start | bytes 442376 | tf_op jit(solution)/shard_map/ppermute | solution.py:52
  14.1 10.5 %collective-permute-start.1 = (bf16[2,192,192]{1,2,0:T(8,128)(2,1)S(1)}, bf16[2,192,192]{1,2,0:T(8,128)(2,1)S(1)}, u32[]{:S(2)}, u32[]{:S(2)}) collective-permute-start(bf16[2,192,192]{1,2,0:T(8,128)(2,1)S(1)} %copy.34), channel_id=1, source_target_pairs={{0,1},{32,3},{64,5},{96,7},{128,9},{160,11},{192,13},{224,15},{256... | collective-permute-start | bytes 442376 | tf_op jit(solution)/shard_map/ppermute | solution.py:52
  25.8 56.7 %collective-permute-start.2 = (bf16[2,192,384]{2,1,0:T(8,128)(2,1)S(1)}, bf16[2,192,384]{2,1,0:T(8,128)(2,1)S(1)}, u32[]{:S(2)}, u32[]{:S(2)}) collective-permute-start(bf16[2,192,384]{2,1,0:T(8,128)(2,1)S(1)} %fusion.5), channel_id=1, source_target_pairs={{0,16},{16,0},{1,17},{17,1},{2,18},{18,2},{3,19},{19,3},{4,20},{20... | collective-permute-start | bytes 884744 | tf_op jit(solution)/shard_map/ppermute | solution.py:60
  83.5 155.6 %all-gather.7.cloned.1.call-start = ((), (), s32[]{:S(2)}) async-start(), calls=%async_computation.1 | async-start | bytes 11796480 | tf_op jit(solution)/shard_map/all_gather | solution.py:64
  137.2 8.8 %collective-permute-start.3 = (bf16[2,192,384]{2,1,0:T(8,128)(2,1)S(1)}, bf16[2,192,384]{2,1,0:T(8,128)(2,1)S(1)}, u32[]{:S(2)}, u32[]{:S(2)}) collective-permute-start(bf16[2,192,384]{2,1,0:T(8,128)(2,1)S(1)} %fusion.5), channel_id=1, source_target_pairs={{0,64},{64,128},{128,192},{192,256},{256,320},{320,384},{384,448},... | collective-permute-start | bytes 884744 | tf_op jit(solution)/shard_map/ppermute | solution.py:27
  140.4 9.8 %collective-permute-start.10 = (bf16[2,192,384]{2,1,0:T(8,128)(2,1)S(1)}, bf16[2,192,384]{2,1,0:T(8,128)(2,1)S(1)}, u32[]{:S(2)}, u32[]{:S(2)}) collective-permute-start(bf16[2,192,384]{2,1,0:T(8,128)(2,1)S(1)} %fusion.5), channel_id=1, source_target_pairs={{64,0},{128,64},{192,128},{256,192},{320,256},{384,320},{448,384},... | collective-permute-start | bytes 884744 | tf_op jit(solution)/shard_map/ppermute | solution.py:28
  146.1 8.8 %collective-permute-start.4 = (bf16[2,192,384]{2,1,0:T(8,128)(2,1)S(1)}, bf16[2,192,384]{2,1,0:T(8,128)(2,1)S(1)}, u32[]{:S(2)}, u32[]{:S(2)}) collective-permute-start(bf16[2,192,384]{2,1,0:T(8,128)(2,1)S(1)} %collective-permute-done.3), channel_id=1, source_target_pairs={{0,64},{64,128},{128,192},{192,256},{256,320},{320,384},{384,448},... | collective-permute-start | bytes 884744 | tf_op jit(solution)/shard_map/ppermute | solution.py:27
  150.2 8.8 %collective-permute-start.11 = (bf16[2,192,384]{2,1,0:T(8,128)(2,1)S(1)}, bf16[2,192,384]{2,1,0:T(8,128)(2,1)S(1)}, u32[]{:S(2)}, u32[]{:S(2)}) collective-permute-start(bf16[2,192,384]{2,1,0:T(8,128)(2,1)S(1)} %collective-permute-done.10), channel_id=1, source_target_pairs={{64,0},{128,64},{192,128},{256,192},{320,256},{384,320},{448,384},... | collective-permute-start | bytes 884744 | tf_op jit(solution)/shard_map/ppermute | solution.py:28
  154.9 7.8 %collective-permute-start.5 = (bf16[2,192,384]{2,1,0:T(8,128)(2,1)S(1)}, bf16[2,192,384]{2,1,0:T(8,128)(2,1)S(1)}, u32[]{:S(2)}, u32[]{:S(2)}) collective-permute-start(bf16[2,192,384]{2,1,0:T(8,128)(2,1)S(1)} %collective-permute-done.4), channel_id=1, source_target_pairs={{0,64},{64,128},{128,192},{192,256},{256,320},{320,384},{384,448},... | collective-permute-start | bytes 884744 | tf_op jit(solution)/shard_map/ppermute | solution.py:27
  159.0 9.5 %collective-permute-start.12 = (bf16[2,192,384]{2,1,0:T(8,128)(2,1)S(1)}, bf16[2,192,384]{2,1,0:T(8,128)(2,1)S(1)}, u32[]{:S(2)}, u32[]{:S(2)}) collective-permute-start(bf16[2,192,384]{2,1,0:T(8,128)(2,1)S(1)} %collective-permute-done.11), channel_id=1, source_target_pairs={{64,0},{128,64},{192,128},{256,192},{320,256},{384,320},{448,384},... | collective-permute-start | bytes 884744 | tf_op jit(solution)/shard_map/ppermute | solution.py:28
  162.7 8.0 %collective-permute-start.6 = (bf16[2,192,384]{2,1,0:T(8,128)(2,1)S(1)}, bf16[2,192,384]{2,1,0:T(8,128)(2,1)S(1)}, u32[]{:S(2)}, u32[]{:S(2)}) collective-permute-start(bf16[2,192,384]{2,1,0:T(8,128)(2,1)S(1)} %collective-permute-done.5), channel_id=1, source_target_pairs={{0,64},{64,128},{128,192},{192,256},{256,320},{320,384},{384,448},... | collective-permute-start | bytes 884744 | tf_op jit(solution)/shard_map/ppermute | solution.py:27
  168.5 8.5 %collective-permute-start.13 = (bf16[2,192,384]{2,1,0:T(8,128)(2,1)S(1)}, bf16[2,192,384]{2,1,0:T(8,128)(2,1)S(1)}, u32[]{:S(2)}, u32[]{:S(2)}) collective-permute-start(bf16[2,192,384]{2,1,0:T(8,128)(2,1)S(1)} %collective-permute-done.12), channel_id=1, source_target_pairs={{64,0},{128,64},{192,128},{256,192},{320,256},{384,320},{448,384},... | collective-permute-start | bytes 884744 | tf_op jit(solution)/shard_map/ppermute | solution.py:28
  170.7 7.9 %collective-permute-start.7 = (bf16[2,192,384]{2,1,0:T(8,128)(2,1)S(1)}, bf16[2,192,384]{2,1,0:T(8,128)(2,1)S(1)}, u32[]{:S(2)}, u32[]{:S(2)}) collective-permute-start(bf16[2,192,384]{2,1,0:T(8,128)(2,1)S(1)} %collective-permute-done.6), channel_id=1, source_target_pairs={{0,64},{64,128},{128,192},{192,256},{256,320},{320,384},{384,448},... | collective-permute-start | bytes 884744 | tf_op jit(solution)/shard_map/ppermute | solution.py:27
  177.1 8.8 %collective-permute-start.14 = (bf16[2,192,384]{2,1,0:T(8,128)(2,1)S(1)}, bf16[2,192,384]{2,1,0:T(8,128)(2,1)S(1)}, u32[]{:S(2)}, u32[]{:S(2)}) collective-permute-start(bf16[2,192,384]{2,1,0:T(8,128)(2,1)S(1)} %collective-permute-done.13), channel_id=1, source_target_pairs={{64,0},{128,64},{192,128},{256,192},{320,256},{384,320},{448,384},... | collective-permute-start | bytes 884744 | tf_op jit(solution)/shard_map/ppermute | solution.py:28
  178.5 8.6 %collective-permute-start.8 = (bf16[2,192,384]{2,1,0:T(8,128)(2,1)S(1)}, bf16[2,192,384]{2,1,0:T(8,128)(2,1)}, u32[]{:S(2)}, u32[]{:S(2)}) collective-permute-start(bf16[2,192,384]{2,1,0:T(8,128)(2,1)S(1)} %collective-permute-done.7), channel_id=1, source_target_pairs={{0,64},{64,128},{128,192},{192,256},{256,320},{320,384},{384,448},... | collective-permute-start | bytes 884744 | tf_op jit(solution)/shard_map/ppermute | solution.py:27
  185.9 9.1 %collective-permute-start.15 = (bf16[2,192,384]{2,1,0:T(8,128)(2,1)S(1)}, bf16[2,192,384]{2,1,0:T(8,128)(2,1)S(1)}, u32[]{:S(2)}, u32[]{:S(2)}) collective-permute-start(bf16[2,192,384]{2,1,0:T(8,128)(2,1)S(1)} %collective-permute-done.14), channel_id=1, source_target_pairs={{64,0},{128,64},{192,128},{256,192},{320,256},{384,320},{448,384},... | collective-permute-start | bytes 884744 | tf_op jit(solution)/shard_map/ppermute | solution.py:28
  187.2 9.2 %collective-permute-start.9 = (bf16[2,192,384]{2,1,0:T(8,128)(2,1)}, bf16[2,192,384]{2,1,0:T(8,128)(2,1)}, u32[]{:S(2)}, u32[]{:S(2)}) collective-permute-start(bf16[2,192,384]{2,1,0:T(8,128)(2,1)} %collective-permute-done.8), channel_id=1, source_target_pairs={{0,64},{64,128},{128,192},{192,256},{256,320},{320,384},{384,448},... | collective-permute-start | bytes 884744 | tf_op jit(solution)/shard_map/ppermute | solution.py:27
  194.9 9.1 %collective-permute-start.16 = (bf16[2,192,384]{2,1,0:T(8,128)(2,1)S(1)}, bf16[2,192,384]{2,1,0:T(8,128)(2,1)S(1)}, u32[]{:S(2)}, u32[]{:S(2)}) collective-permute-start(bf16[2,192,384]{2,1,0:T(8,128)(2,1)S(1)} %collective-permute-done.15), channel_id=1, source_target_pairs={{64,0},{128,64},{192,128},{256,192},{320,256},{384,320},{448,384},... | collective-permute-start | bytes 884744 | tf_op jit(solution)/shard_map/ppermute | solution.py:28
  204.0 2.2 copy-start.1
  207.8 45.3 %collective-permute-start.17 = (bf16[8,2,192,384]{3,2,0,1:T(8,128)(2,1)}, bf16[8,2,192,384]{3,2,0,1:T(8,128)(2,1)}, u32[]{:S(2)}, u32[]{:S(2)}) collective-permute-start(bf16[8,2,192,384]{3,2,0,1:T(8,128)(2,1)} %constant_dynamic-slice_fusion.3), channel_id=1, source_target_pairs={{0,32},{32,0},{1,33},{33,1},{2,34},{34,2},{3,35},{35,3},{4,36},{36... | collective-permute-start | bytes 7077896 | tf_op jit(solution)/shard_map/ppermute | solution.py:33
  247.4 2.4 copy-start
  249.8 2.2 slice-start
  250.0 2.0 slice-start.1
Sparse Core Ops, SparseCore 0:
  83.6 53.5 all-gather.4
  139.3 99.7 all-gather.6

commit v7 on v5

--- a/solution.py
+++ b/solution.py
@@ -34,6 +34,24 @@
     return mine, other
 
 
+def ring_shift(value, shift):
+    n_line = lax.axis_size("zl")
+    n_ring = 2 * n_line
+    pairs = []
+    for line in range(n_line):
+        for half in range(2):
+            target = (half * n_line + line + shift) % n_ring
+            pairs.append((line * 2 + half, (target % n_line) * 2 + target // n_line))
+    return lax.ppermute(value, ("zl", "zh"), pairs)
+
+
+def cross_halves(block):
+    quarter = lax.axis_size("zl") // 2
+    forward = ring_shift(ring_shift(block[0], quarter), quarter)
+    backward = ring_shift(ring_shift(block[1], -quarter), -quarter)
+    return jnp.stack([forward, backward])
+
+
 def local(pressure):
     n_shot = lax.axis_size("zl") * lax.axis_size("core")
     n_half = lax.axis_size("y") * lax.axis_size("x")
@@ -57,7 +75,7 @@
         (pressure.astype(jnp.float32) + jnp.swapaxes(mirror, 1, 2).astype(jnp.float32)) * 0.5
     ).astype(jnp.bfloat16)
 
-    partner_block = lax.ppermute(symmetric, "zh", [(0, 1), (1, 0)])
+    partner_block = cross_halves(symmetric)
     top = jnp.where(half_index == 0, symmetric, partner_block)
     bottom = jnp.where(half_index == 0, partner_block, symmetric)
     panels = lax.all_gather(jnp.stack([top, bottom]), ("y", "x"), axis=1, tiled=False)

time: 216 us -> 219 us (1.014)
  starting transfers between devices: 103 us -> 118 us
  waiting for transfers between devices: 67.9 us -> 56.2 us
    ppermute x7, waiting for transfers between devices: 26.4 us -> 8.53 us  [gather_line(): lax.ppermute(rightward, 'zl', [(k, k + 1) for k in range(n_line - 1)])]
    ppermute x1 -> x4, waiting for transfers between devices: 7.62 us -> 14.7 us  [ring_shift(): return lax.ppermute(value, ('zl', 'zh'), pairs)]
    ppermute x1 -> x4, starting transfers between devices: 49.2 us -> 55.7 us  [ring_shift(): return lax.ppermute(value, ('zl', 'zh'), pairs)]
    all_gather x1, waiting for transfers between devices: 18.1 us -> 12.3 us  [local(): lax.all_gather(jnp.stack([top, bottom]), ('y', 'x'), axis=1, tiled=False)]
    ppermute x7, waiting for transfers between devices: 7.76 us -> 12.6 us  [gather_line(): lax.ppermute(leftward, 'zl', [(k + 1, k) for k in range(n_line - 1)])]
    ppermute x7, starting transfers between devices: 29.1 us -> 33.3 us  [gather_line(): lax.ppermute(rightward, 'zl', [(k, k + 1) for k in range(n_line - 1)])]
    ppermute x1, starting transfers between devices: 7.36 us -> 11.1 us  [gather_line(): other = lax.ppermute(mine, 'core', [(0, 1), (1, 0)])]
  transfers between devices with their start and end apart: 19 -> 22, of which waited for: 16 -> 18; matrix products, arithmetic and copies ran while one was open for 8% -> 7% of each run, Pallas kernels for 0% -> 0%
where the time goes in v7:
time: 219 us; the launch traced here: 218 us
  starting transfers between devices  118 us (54%)
  waiting for transfers between devices  56.2 us (26%)
  local copies, waits for them, and re-layouts  20.5 us (9%)
  between operations  13.8 us (6%)
  matrix products  7.1 us (3%)
  other arithmetic  3.04 us (1%)
    ppermute x4, starting transfers between devices, ring_shift(): return lax.ppermute(value, ('zl', 'zh'), pairs)  55.7 us
    ppermute x7, starting transfers between devices, gather_line(): lax.ppermute(rightward, 'zl', [(k, k + 1) for k in range(n_line - 1)])  33.3 us
    ppermute x4, waiting for transfers between devices, ring_shift(): return lax.ppermute(value, ('zl', 'zh'), pairs)  14.7 us
    ppermute x7, waiting for transfers between devices, gather_line(): lax.ppermute(leftward, 'zl', [(k + 1, k) for k in range(n_line - 1)])  12.6 us
    all_gather x1, waiting for transfers between devices, local(): lax.all_gather(jnp.stack([top, bottom]), ('y', 'x'), axis=1, tiled=False)  12.3 us
    ppermute x1, starting transfers between devices, gather_line(): other = lax.ppermute(mine, 'core', [(0, 1), (1, 0)])  11.1 us
    ppermute x7, starting transfers between devices, gather_line(): lax.ppermute(leftward, 'zl', [(k + 1, k) for k in range(n_line - 1)])  8.99 us
    ppermute x2, starting transfers between devices, local(): lax.ppermute(piece, axes, mirror_pairs(n_recv, n_shot, flip))  8.57 us
  transfers between devices with their start and end apart: 22, of which 18 were waited for; matrix products, arithmetic and copies ran while one was open for 7% of the time, Pallas kernels for 0%

profile of v7, /device:TPU:1, one launch (start us, length us, event | category | flops | bytes accessed | tf_op | source)
XLA Modules:
  0.0 218.4 jit_solution(9314649778709224332)
XLA Ops:
  6.5 1.2 constant_dynamic-slice_fusion.2
  7.7 0.1 copy.56
  7.9 6.0 %collective-permute-start = (bf16[2,192,192]{1,2,0:T(8,128)(2,1)S(1)}, bf16[2,192,192]{1,2,0:T(8,128)(2,1)S(1)}, u32[]{:S(2)}, u32[]{:S(2)}) collective-permute-start(bf16[2,192,192]{1,2,0:T(8,128)(2,1)S(1)} %copy.56), channel_id=1, source_target_pairs={{0,0},{32,2},{64,4},{96,6},{128,8},{160,10},{192,12},{224,14},{256... | collective-permute-start | bytes 442376 | tf_op jit(solution)/shard_map/ppermute | solution.py:70
  13.9 0.1 copy.57
  14.1 2.5 %collective-permute-start.1 = (bf16[2,192,192]{1,2,0:T(8,128)(2,1)S(1)}, bf16[2,192,192]{1,2,0:T(8,128)(2,1)S(1)}, u32[]{:S(2)}, u32[]{:S(2)}) collective-permute-start(bf16[2,192,192]{1,2,0:T(8,128)(2,1)S(1)} %copy.57), channel_id=1, source_target_pairs={{0,1},{32,3},{64,5},{96,7},{128,9},{160,11},{192,13},{224,15},{256... | collective-permute-start | bytes 442376 | tf_op jit(solution)/shard_map/ppermute | solution.py:70
  16.6 2.9 %collective-permute-done = bf16[2,192,192]{1,2,0:T(8,128)(2,1)S(1)} collective-permute-done((bf16[2,192,192]{1,2,0:T(8,128)(2,1)S(1)}, bf16[2,192,192]{1,2,0:T(8,128)(2,1)S(1)}, u32[]{:S(2)}, u32[]{:S(2)}) %collective-permute-start) | collective-permute-done | bytes 147488 | tf_op jit(solution)/shard_map/ppermute | solution.py:70
  19.6 5.0 %collective-permute-done.1 = bf16[2,192,192]{1,2,0:T(8,128)(2,1)S(1)} collective-permute-done((bf16[2,192,192]{1,2,0:T(8,128)(2,1)S(1)}, bf16[2,192,192]{1,2,0:T(8,128)(2,1)S(1)}, u32[]{:S(2)}, u32[]{:S(2)}) %collective-permute-start.1) | collective-permute-done | bytes 147488 | tf_op jit(solution)/shard_map/ppermute | solution.py:70
  24.6 1.1 fusion.5
  25.8 12.2 %collective-permute-start.4 = (bf16[192,384]{1,0:T(8,128)(2,1)S(1)}, bf16[192,384]{1,0:T(8,128)(2,1)S(1)}, u32[]{:S(2)}, u32[]{:S(2)}) collective-permute-start(bf16[192,384]{1,0:T(8,128)(2,1)S(1)} %get-tuple-element.16), channel_id=1, source_target_pairs={{0,272},{16,256},{64,336},{80,320},{128,400},{144,384},{192,464},{... | collective-permute-start | bytes 442376 | tf_op jit(solution)/shard_map/ppermute | solution.py:45
  38.0 28.7 %collective-permute-start.2 = (bf16[192,384]{1,0:T(8,128)(2,1)S(1)}, bf16[192,384]{1,0:T(8,128)(2,1)S(1)}, u32[]{:S(2)}, u32[]{:S(2)}) collective-permute-start(bf16[192,384]{1,0:T(8,128)(2,1)S(1)} %get-tuple-element.15), channel_id=1, source_target_pairs={{0,256},{16,272},{64,320},{80,336},{128,384},{144,400},{192,448},{... | collective-permute-start | bytes 442376 | tf_op jit(solution)/shard_map/ppermute | solution.py:45
  66.7 6.2 %collective-permute-done.4 = bf16[192,384]{1,0:T(8,128)(2,1)S(1)} collective-permute-done((bf16[192,384]{1,0:T(8,128)(2,1)S(1)}, bf16[192,384]{1,0:T(8,128)(2,1)S(1)}, u32[]{:S(2)}, u32[]{:S(2)}) %collective-permute-start.4) | collective-permute-done | bytes 147488 | tf_op jit(solution)/shard_map/ppermute | solution.py:45
  72.9 1.9 collective-permute-start.5
  74.8 12.9 %collective-permute-start.3 = (bf16[192,384]{1,0:T(8,128)(2,1)S(1)}, bf16[192,384]{1,0:T(8,128)(2,1)S(1)}, u32[]{:S(2)}, u32[]{:S(2)}) collective-permute-start(bf16[192,384]{1,0:T(8,128)(2,1)S(1)} %collective-permute-done.2), channel_id=1, source_target_pairs={{0,256},{16,272},{64,320},{80,336},{128,384},{144,400},{192,448},{... | collective-permute-start | bytes 442376 | tf_op jit(solution)/shard_map/ppermute | solution.py:45
  87.8 8.5 %collective-permute-done.5 = bf16[192,384]{1,0:T(8,128)(2,1)S(1)} collective-permute-done((bf16[192,384]{1,0:T(8,128)(2,1)S(1)}, bf16[192,384]{1,0:T(8,128)(2,1)S(1)}, u32[]{:S(2)}, u32[]{:S(2)}) %collective-permute-start.5) | collective-permute-done | bytes 147488 | tf_op jit(solution)/shard_map/ppermute | solution.py:45
  96.3 0.1 select_bitcast_fusion.1
  96.4 0.9 pad_maximum_fusion
  97.3 0.0 all-gather.3.cloned.1.call-update
  97.3 2.1 collective-permute-start.6
  99.4 1.3 collective-permute-start.13
  100.7 2.7 %collective-permute-done.6 = bf16[2,192,384]{2,1,0:T(8,128)(2,1)S(1)} collective-permute-done((bf16[2,192,384]{2,1,0:T(8,128)(2,1)S(1)}, bf16[2,192,384]{2,1,0:T(8,128)(2,1)S(1)}, u32[]{:S(2)}, u32[]{:S(2)}) %collective-permute-start.6) | collective-permute-done | bytes 294944 | tf_op jit(solution)/shard_map/ppermute | solution.py:27
  103.4 4.7 %collective-permute-start.7 = (bf16[2,192,384]{2,1,0:T(8,128)(2,1)S(1)}, bf16[2,192,384]{2,1,0:T(8,128)(2,1)S(1)}, u32[]{:S(2)}, u32[]{:S(2)}) collective-permute-start(bf16[2,192,384]{2,1,0:T(8,128)(2,1)S(1)} %collective-permute-done.6), channel_id=1, source_target_pairs={{0,64},{64,128},{128,192},{192,256},{256,320},{320,384},{384,448},... | collective-permute-start | bytes 884744 | tf_op jit(solution)/shard_map/ppermute | solution.py:27
  108.2 1.3 collective-permute-start.14
  109.5 2.3 %collective-permute-done.7 = bf16[2,192,384]{2,1,0:T(8,128)(2,1)S(1)} collective-permute-done((bf16[2,192,384]{2,1,0:T(8,128)(2,1)S(1)}, bf16[2,192,384]{2,1,0:T(8,128)(2,1)S(1)}, u32[]{:S(2)}, u32[]{:S(2)}) %collective-permute-start.7) | collective-permute-done | bytes 294944 | tf_op jit(solution)/shard_map/ppermute | solution.py:27
  111.8 8.5 %collective-permute-start.8 = (bf16[2,192,384]{2,1,0:T(8,128)(2,1)S(1)}, bf16[2,192,384]{2,1,0:T(8,128)(2,1)S(1)}, u32[]{:S(2)}, u32[]{:S(2)}) collective-permute-start(bf16[2,192,384]{2,1,0:T(8,128)(2,1)S(1)} %collective-permute-done.7), channel_id=1, source_target_pairs={{0,64},{64,128},{128,192},{192,256},{256,320},{320,384},{384,448},... | collective-permute-start | bytes 884744 | tf_op jit(solution)/shard_map/ppermute | solution.py:27
  120.3 1.9 collective-permute-done.14
  122.1 1.3 collective-permute-start.15
  123.4 0.8 collective-permute-done.8
  124.2 4.2 %collective-permute-start.9 = (bf16[2,192,384]{2,1,0:T(8,128)(2,1)S(1)}, bf16[2,192,384]{2,1,0:T(8,128)(2,1)S(1)}, u32[]{:S(2)}, u32[]{:S(2)}) collective-permute-start(bf16[2,192,384]{2,1,0:T(8,128)(2,1)S(1)} %collective-permute-done.8), channel_id=1, source_target_pairs={{0,64},{64,128},{128,192},{192,256},{256,320},{320,384},{384,448},... | collective-permute-start | bytes 884744 | tf_op jit(solution)/shard_map/ppermute | solution.py:27
  128.5 2.3 %collective-permute-done.15 = bf16[2,192,384]{2,1,0:T(8,128)(2,1)S(1)} collective-permute-done((bf16[2,192,384]{2,1,0:T(8,128)(2,1)S(1)}, bf16[2,192,384]{2,1,0:T(8,128)(2,1)S(1)}, u32[]{:S(2)}, u32[]{:S(2)}) %collective-permute-start.15) | collective-permute-done | bytes 294944 | tf_op jit(solution)/shard_map/ppermute | solution.py:28
  130.7 1.3 collective-permute-start.16
  132.0 0.1 collective-permute-done.9
  132.1 4.2 %collective-permute-start.10 = (bf16[2,192,384]{2,1,0:T(8,128)(2,1)S(1)}, bf16[2,192,384]{2,1,0:T(8,128)(2,1)S(1)}, u32[]{:S(2)}, u32[]{:S(2)}) collective-permute-start(bf16[2,192,384]{2,1,0:T(8,128)(2,1)S(1)} %collective-permute-done.9), channel_id=1, source_target_pairs={{0,64},{64,128},{128,192},{192,256},{256,320},{320,384},{384,448},... | collective-permute-start | bytes 884744 | tf_op jit(solution)/shard_map/ppermute | solution.py:27
  136.3 1.9 collective-permute-done.16
  138.2 1.3 collective-permute-start.17
  139.5 0.5 collective-permute-done.10
  140.0 4.8 %collective-permute-start.11 = (bf16[2,192,384]{2,1,0:T(8,128)(2,1)S(1)}, bf16[2,192,384]{2,1,0:T(8,128)(2,1)}, u32[]{:S(2)}, u32[]{:S(2)}) collective-permute-start(bf16[2,192,384]{2,1,0:T(8,128)(2,1)S(1)} %collective-permute-done.10), channel_id=1, source_target_pairs={{0,64},{64,128},{128,192},{192,256},{256,320},{320,384},{384,448},... | collective-permute-start | bytes 884744 | tf_op jit(solution)/shard_map/ppermute | solution.py:27
  144.8 0.9 collective-permute-done.17
  145.6 1.3 collective-permute-start.18
  146.9 0.8 collective-permute-done.11
  147.7 4.8 %collective-permute-start.12 = (bf16[2,192,384]{2,1,0:T(8,128)(2,1)}, bf16[2,192,384]{2,1,0:T(8,128)(2,1)}, u32[]{:S(2)}, u32[]{:S(2)}) collective-permute-start(bf16[2,192,384]{2,1,0:T(8,128)(2,1)} %collective-permute-done.11), channel_id=1, source_target_pairs={{0,64},{64,128},{128,192},{192,256},{256,320},{320,384},{384,448},... | collective-permute-start | bytes 884744 | tf_op jit(solution)/shard_map/ppermute | solution.py:27
  152.5 1.0 collective-permute-done.18
  153.5 1.3 collective-permute-start.19
  154.8 1.3 collective-permute-done.12
  156.1 1.0 bitcast_dynamic-update-slice_fusion.13
  157.1 1.0 bitcast_dynamic-update-slice_fusion.12
  158.9 4.7 %collective-permute-done.19 = bf16[2,192,384]{2,1,0:T(8,128)(2,1)S(1)} collective-permute-done((bf16[2,192,384]{2,1,0:T(8,128)(2,1)S(1)}, bf16[2,192,384]{2,1,0:T(8,128)(2,1)S(1)}, u32[]{:S(2)}, u32[]{:S(2)}) %collective-permute-start.19) | collective-permute-done | bytes 294944 | tf_op jit(solution)/shard_map/ppermute | solution.py:28
  163.7 2.1 copy-done.1
  165.8 1.6 constant_dynamic-slice_fusion
  167.4 11.1 %collective-permute-start.20 = (bf16[8,2,192,384]{3,2,0,1:T(8,128)(2,1)}, bf16[8,2,192,384]{3,2,0,1:T(8,128)(2,1)}, u32[]{:S(2)}, u32[]{:S(2)}) collective-permute-start(bf16[8,2,192,384]{3,2,0,1:T(8,128)(2,1)} %constant_dynamic-slice_fusion), channel_id=1, source_target_pairs={{0,32},{32,0},{1,33},{33,1},{2,34},{34,2},{3,35},{35,3},{4,36},{36... | collective-permute-start | bytes 7077896 | tf_op jit(solution)/shard_map/ppermute | solution.py:33
  178.5 12.3 %all-gather.3.cloned.1.call-done = bf16[2,32,192,384]{3,2,1,0:T(8,128)(2,1)} async-done(((bf16[2,2,192,384]{3,2,1,0:T(8,128)(2,1)}), bf16[2,32,192,384]{3,2,1,0:T(8,128)(2,1)}) %all-gather.3.cloned.1.call-update) | async-done | bytes 9437200 | tf_op jit(solution)/shard_map/all_gather | solution.py:81
  190.8 4.7 %fusion.13 = (bf16[1,32,192,384]{3,2,1,0:T(8,128)(2,1)S(1)}, bf16[1,32,192,384]{3,2,1,0:T(8,128)(2,1)S(1)}) fusion(bf16[2,32,192,384]{3,2,1,0:T(8,128)(2,1)} %all-gather.3.cloned.1.call-done), kind=kLoop, calls=%fused_computation.56 | loop fusion | bytes 18874368 | tf_op jit(solution)/shard_map/slice | solution.py:95
  195.5 3.3 %dynamic-slice_bitcast_fusion.1 = (bf16[4,2,2,192,384]{4,3,1,2,0:T(8,128)(2,1)}, bf16[4,2,2,192,384]{4,3,1,2,0:T(8,128)(2,1)}, bf16[4,2,2,192,384]{4,3,1,2,0:T(8,128)(2,1)S(1)}, bf16[4,2,2,192,384]{4,3,1,2,0:T(8,128)(2,1)S(1)}) fusion(bf16[4,2,2,2,192,384]{5,4,3,2,1,0:T(8,128)(2,1)S(1)} %bitcast.176, s32[]{:T(128)S(6)} %select_n.68, s32[]{:T(128)S(6)} %select_n.70, ...), kind=kLoop, calls=%fused_computation.1 | loop fusion | bytes 18874376 | tf_op jit(solution)/shard_map/transpose | solution.py:90
  198.8 2.1 copy.44
  200.9 0.3 copy-done
  201.2 0.3 copy.42
  201.5 0.2 copy.40
  201.7 0.2 copy.24
  202.0 1.4 slice-done
  203.4 0.1 slice-done.1
  203.4 1.1 convolution_bitcast_fusion.1
  204.6 2.4 %convolution_bitcast_fusion = f32[2,384,2,192]{1,3,2,0:T(8,128)S(1)} fusion(bf16[4,2,384,384,1]{3,2,0,4,1:T(8,128)(2,1)S(1)} %bitcast.180, bf16[8,2,192,384]{3,2,0,1:T(8,128)(2,1)} %collective-permute-done.20), kind=kOutput, calls=%fused_computation.4 | convolution fusion | flops 905969664 | bytes 4718592 | tf_op jit(solution)/shard_map/zpxc,zqcn->pqxn/dot_general | solution.py:91
  207.0 2.4 %convolution_bitcast_fusion.2 = f32[2,384,2,192]{1,3,2,0:T(8,128)S(1)} fusion(bf16[4,2,384,384,1]{3,2,0,4,1:T(8,128)(2,1)S(1)} %bitcast.181, bf16[8,2,192,384]{3,2,0,1:T(8,128)(2,1)} %collective-permute-done.20), kind=kOutput, calls=%fused_computation.6 | convolution fusion | flops 905969664 | bytes 4718592 | tf_op jit(solution)/shard_map/zpxc,zqcn->pqxn/dot_general | solution.py:91
  209.3 1.2 fusion.3
  210.7 0.9 pad_maximum_fusion.1
  (27 shorter events, 0.8 us)
Async XLA Ops:
  6.5 184.3 %all-gather.3.cloned.1.call-start = ((), (), s32[]{:S(2)}) async-start(), calls=%async_computation | async-start | bytes 10027008 | tf_op jit(solution)/shard_map/all_gather | solution.py:81
  7.9 11.7 %collective-permute-start = (bf16[2,192,192]{1,2,0:T(8,128)(2,1)S(1)}, bf16[2,192,192]{1,2,0:T(8,128)(2,1)S(1)}, u32[]{:S(2)}, u32[]{:S(2)}) collective-permute-start(bf16[2,192,192]{1,2,0:T(8,128)(2,1)S(1)} %copy.56), channel_id=1, source_target_pairs={{0,0},{32,2},{64,4},{96,6},{128,8},{160,10},{192,12},{224,14},{256... | collective-permute-start | bytes 442376 | tf_op jit(solution)/shard_map/ppermute | solution.py:70
  14.1 10.5 %collective-permute-start.1 = (bf16[2,192,192]{1,2,0:T(8,128)(2,1)S(1)}, bf16[2,192,192]{1,2,0:T(8,128)(2,1)S(1)}, u32[]{:S(2)}, u32[]{:S(2)}) collective-permute-start(bf16[2,192,192]{1,2,0:T(8,128)(2,1)S(1)} %copy.57), channel_id=1, source_target_pairs={{0,1},{32,3},{64,5},{96,7},{128,9},{160,11},{192,13},{224,15},{256... | collective-permute-start | bytes 442376 | tf_op jit(solution)/shard_map/ppermute | solution.py:70
  25.8 47.1 %collective-permute-start.4 = (bf16[192,384]{1,0:T(8,128)(2,1)S(1)}, bf16[192,384]{1,0:T(8,128)(2,1)S(1)}, u32[]{:S(2)}, u32[]{:S(2)}) collective-permute-start(bf16[192,384]{1,0:T(8,128)(2,1)S(1)} %get-tuple-element.16), channel_id=1, source_target_pairs={{0,272},{16,256},{64,336},{80,320},{128,400},{144,384},{192,464},{... | collective-permute-start | bytes 442376 | tf_op jit(solution)/shard_map/ppermute | solution.py:45
  38.0 36.8 %collective-permute-start.2 = (bf16[192,384]{1,0:T(8,128)(2,1)S(1)}, bf16[192,384]{1,0:T(8,128)(2,1)S(1)}, u32[]{:S(2)}, u32[]{:S(2)}) collective-permute-start(bf16[192,384]{1,0:T(8,128)(2,1)S(1)} %get-tuple-element.15), channel_id=1, source_target_pairs={{0,256},{16,272},{64,320},{80,336},{128,384},{144,400},{192,448},{... | collective-permute-start | bytes 442376 | tf_op jit(solution)/shard_map/ppermute | solution.py:45
  72.9 23.4 %collective-permute-start.5 = (bf16[192,384]{1,0:T(8,128)(2,1)S(1)}, bf16[192,384]{1,0:T(8,128)(2,1)S(1)}, u32[]{:S(2)}, u32[]{:S(2)}) collective-permute-start(bf16[192,384]{1,0:T(8,128)(2,1)S(1)} %collective-permute-done.4), channel_id=1, source_target_pairs={{0,272},{16,256},{64,336},{80,320},{128,400},{144,384},{192,464},{... | collective-permute-start | bytes 442376 | tf_op jit(solution)/shard_map/ppermute | solution.py:45
  74.8 21.5 %collective-permute-start.3 = (bf16[192,384]{1,0:T(8,128)(2,1)S(1)}, bf16[192,384]{1,0:T(8,128)(2,1)S(1)}, u32[]{:S(2)}, u32[]{:S(2)}) collective-permute-start(bf16[192,384]{1,0:T(8,128)(2,1)S(1)} %collective-permute-done.2), channel_id=1, source_target_pairs={{0,256},{16,272},{64,320},{80,336},{128,384},{144,400},{192,448},{... | collective-permute-start | bytes 442376 | tf_op jit(solution)/shard_map/ppermute | solution.py:45
  97.3 6.1 %collective-permute-start.6 = (bf16[2,192,384]{2,1,0:T(8,128)(2,1)S(1)}, bf16[2,192,384]{2,1,0:T(8,128)(2,1)S(1)}, u32[]{:S(2)}, u32[]{:S(2)}) collective-permute-start(bf16[2,192,384]{2,1,0:T(8,128)(2,1)S(1)} %fusion.5), channel_id=1, source_target_pairs={{0,64},{64,128},{128,192},{192,256},{256,320},{320,384},{384,448},... | collective-permute-start | bytes 884744 | tf_op jit(solution)/shard_map/ppermute | solution.py:27
  99.4 8.8 %collective-permute-start.13 = (bf16[2,192,384]{2,1,0:T(8,128)(2,1)S(1)}, bf16[2,192,384]{2,1,0:T(8,128)(2,1)S(1)}, u32[]{:S(2)}, u32[]{:S(2)}) collective-permute-start(bf16[2,192,384]{2,1,0:T(8,128)(2,1)S(1)} %fusion.5), channel_id=1, source_target_pairs={{64,0},{128,64},{192,128},{256,192},{320,256},{384,320},{448,384},... | collective-permute-start | bytes 884744 | tf_op jit(solution)/shard_map/ppermute | solution.py:28
  103.4 8.4 %collective-permute-start.7 = (bf16[2,192,384]{2,1,0:T(8,128)(2,1)S(1)}, bf16[2,192,384]{2,1,0:T(8,128)(2,1)S(1)}, u32[]{:S(2)}, u32[]{:S(2)}) collective-permute-start(bf16[2,192,384]{2,1,0:T(8,128)(2,1)S(1)} %collective-permute-done.6), channel_id=1, source_target_pairs={{0,64},{64,128},{128,192},{192,256},{256,320},{320,384},{384,448},... | collective-permute-start | bytes 884744 | tf_op jit(solution)/shard_map/ppermute | solution.py:27
  108.2 14.0 %collective-permute-start.14 = (bf16[2,192,384]{2,1,0:T(8,128)(2,1)S(1)}, bf16[2,192,384]{2,1,0:T(8,128)(2,1)S(1)}, u32[]{:S(2)}, u32[]{:S(2)}) collective-permute-start(bf16[2,192,384]{2,1,0:T(8,128)(2,1)S(1)} %collective-permute-done.13), channel_id=1, source_target_pairs={{64,0},{128,64},{192,128},{256,192},{320,256},{384,320},{448,384},... | collective-permute-start | bytes 884744 | tf_op jit(solution)/shard_map/ppermute | solution.py:28
  111.8 12.4 %collective-permute-start.8 = (bf16[2,192,384]{2,1,0:T(8,128)(2,1)S(1)}, bf16[2,192,384]{2,1,0:T(8,128)(2,1)S(1)}, u32[]{:S(2)}, u32[]{:S(2)}) collective-permute-start(bf16[2,192,384]{2,1,0:T(8,128)(2,1)S(1)} %collective-permute-done.7), channel_id=1, source_target_pairs={{0,64},{64,128},{128,192},{192,256},{256,320},{320,384},{384,448},... | collective-permute-start | bytes 884744 | tf_op jit(solution)/shard_map/ppermute | solution.py:27
  122.1 8.6 %collective-permute-start.15 = (bf16[2,192,384]{2,1,0:T(8,128)(2,1)S(1)}, bf16[2,192,384]{2,1,0:T(8,128)(2,1)S(1)}, u32[]{:S(2)}, u32[]{:S(2)}) collective-permute-start(bf16[2,192,384]{2,1,0:T(8,128)(2,1)S(1)} %collective-permute-done.14), channel_id=1, source_target_pairs={{64,0},{128,64},{192,128},{256,192},{320,256},{384,320},{448,384},... | collective-permute-start | bytes 884744 | tf_op jit(solution)/shard_map/ppermute | solution.py:28
  124.2 7.9 %collective-permute-start.9 = (bf16[2,192,384]{2,1,0:T(8,128)(2,1)S(1)}, bf16[2,192,384]{2,1,0:T(8,128)(2,1)S(1)}, u32[]{:S(2)}, u32[]{:S(2)}) collective-permute-start(bf16[2,192,384]{2,1,0:T(8,128)(2,1)S(1)} %collective-permute-done.8), channel_id=1, source_target_pairs={{0,64},{64,128},{128,192},{192,256},{256,320},{320,384},{384,448},... | collective-permute-start | bytes 884744 | tf_op jit(solution)/shard_map/ppermute | solution.py:27
  130.7 7.5 %collective-permute-start.16 = (bf16[2,192,384]{2,1,0:T(8,128)(2,1)S(1)}, bf16[2,192,384]{2,1,0:T(8,128)(2,1)S(1)}, u32[]{:S(2)}, u32[]{:S(2)}) collective-permute-start(bf16[2,192,384]{2,1,0:T(8,128)(2,1)S(1)} %collective-permute-done.15), channel_id=1, source_target_pairs={{64,0},{128,64},{192,128},{256,192},{320,256},{384,320},{448,384},... | collective-permute-start | bytes 884744 | tf_op jit(solution)/shard_map/ppermute | solution.py:28
  132.1 7.9 %collective-permute-start.10 = (bf16[2,192,384]{2,1,0:T(8,128)(2,1)S(1)}, bf16[2,192,384]{2,1,0:T(8,128)(2,1)S(1)}, u32[]{:S(2)}, u32[]{:S(2)}) collective-permute-start(bf16[2,192,384]{2,1,0:T(8,128)(2,1)S(1)} %collective-permute-done.9), channel_id=1, source_target_pairs={{0,64},{64,128},{128,192},{192,256},{256,320},{320,384},{384,448},... | collective-permute-start | bytes 884744 | tf_op jit(solution)/shard_map/ppermute | solution.py:27
  138.2 7.5 %collective-permute-start.17 = (bf16[2,192,384]{2,1,0:T(8,128)(2,1)S(1)}, bf16[2,192,384]{2,1,0:T(8,128)(2,1)S(1)}, u32[]{:S(2)}, u32[]{:S(2)}) collective-permute-start(bf16[2,192,384]{2,1,0:T(8,128)(2,1)S(1)} %collective-permute-done.16), channel_id=1, source_target_pairs={{64,0},{128,64},{192,128},{256,192},{320,256},{384,320},{448,384},... | collective-permute-start | bytes 884744 | tf_op jit(solution)/shard_map/ppermute | solution.py:28
  140.0 7.8 %collective-permute-start.11 = (bf16[2,192,384]{2,1,0:T(8,128)(2,1)S(1)}, bf16[2,192,384]{2,1,0:T(8,128)(2,1)}, u32[]{:S(2)}, u32[]{:S(2)}) collective-permute-start(bf16[2,192,384]{2,1,0:T(8,128)(2,1)S(1)} %collective-permute-done.10), channel_id=1, source_target_pairs={{0,64},{64,128},{128,192},{192,256},{256,320},{320,384},{384,448},... | collective-permute-start | bytes 884744 | tf_op jit(solution)/shard_map/ppermute | solution.py:27
  145.6 7.9 %collective-permute-start.18 = (bf16[2,192,384]{2,1,0:T(8,128)(2,1)S(1)}, bf16[2,192,384]{2,1,0:T(8,128)(2,1)S(1)}, u32[]{:S(2)}, u32[]{:S(2)}) collective-permute-start(bf16[2,192,384]{2,1,0:T(8,128)(2,1)S(1)} %collective-permute-done.17), channel_id=1, source_target_pairs={{64,0},{128,64},{192,128},{256,192},{320,256},{384,320},{448,384},... | collective-permute-start | bytes 884744 | tf_op jit(solution)/shard_map/ppermute | solution.py:28
  147.7 8.4 %collective-permute-start.12 = (bf16[2,192,384]{2,1,0:T(8,128)(2,1)}, bf16[2,192,384]{2,1,0:T(8,128)(2,1)}, u32[]{:S(2)}, u32[]{:S(2)}) collective-permute-start(bf16[2,192,384]{2,1,0:T(8,128)(2,1)} %collective-permute-done.11), channel_id=1, source_target_pairs={{0,64},{64,128},{128,192},{192,256},{256,320},{320,384},{384,448},... | collective-permute-start | bytes 884744 | tf_op jit(solution)/shard_map/ppermute | solution.py:27
  153.5 10.1 %collective-permute-start.19 = (bf16[2,192,384]{2,1,0:T(8,128)(2,1)S(1)}, bf16[2,192,384]{2,1,0:T(8,128)(2,1)S(1)}, u32[]{:S(2)}, u32[]{:S(2)}) collective-permute-start(bf16[2,192,384]{2,1,0:T(8,128)(2,1)S(1)} %collective-permute-done.18), channel_id=1, source_target_pairs={{64,0},{128,64},{192,128},{256,192},{320,256},{384,320},{448,384},... | collective-permute-start | bytes 884744 | tf_op jit(solution)/shard_map/ppermute | solution.py:28
  163.6 2.1 copy-start.1
  167.4 37.1 %collective-permute-start.20 = (bf16[8,2,192,384]{3,2,0,1:T(8,128)(2,1)}, bf16[8,2,192,384]{3,2,0,1:T(8,128)(2,1)}, u32[]{:S(2)}, u32[]{:S(2)}) collective-permute-start(bf16[8,2,192,384]{3,2,0,1:T(8,128)(2,1)} %constant_dynamic-slice_fusion), channel_id=1, source_target_pairs={{0,32},{32,0},{1,33},{33,1},{2,34},{34,2},{3,35},{35,3},{4,36},{36... | collective-permute-start | bytes 7077896 | tf_op jit(solution)/shard_map/ppermute | solution.py:33
  198.8 2.4 %copy-start = (bf16[4,2,2,192,384]{4,3,1,2,0:T(8,128)(2,1)S(1)}, bf16[4,2,2,192,384]{4,3,1,2,0:T(8,128)(2,1)}, u32[]{:S(2)}) copy-start(bf16[4,2,2,192,384]{4,3,1,2,0:T(8,128)(2,1)} %get-tuple-element.9) | copy-start | bytes 7077892
  201.2 2.2 %slice-start = ((s8[4423680]{0:T(1024)(128)(4,1)}), s8[4194304]{0:T(1024)(128)(4,1)S(1)}, s32[]{:S(2)}) async-start(s8[4423680]{0:T(1024)(128)(4,1)} %bitcast.178), calls=%async_computation.1 | async-start | bytes 8388608
  201.4 2.0 slice-start.1
Sparse Core Ops, SparseCore 0:
  97.4 93.3 all-gather.2

commit v8 on v5

--- a/solution.py
+++ b/solution.py
@@ -9,12 +9,13 @@
 N = 6144
 
 
-def mirror_pairs(n_recv, n_shot, flip):
+def mirror_pairs(n_recv, n_shot, flip, across):
     pairs = []
     for i in range(n_recv):
         for j in range(n_shot):
             h = (i % 2) ^ flip
-            pairs.append((j * n_recv + i, (i // 2) * n_recv + 2 * j + h))
+            target = (2 * j + h + across * n_recv // 2) % n_recv
+            pairs.append((j * n_recv + i, (i // 2) * n_recv + target))
     return pairs
 
 
@@ -45,19 +46,23 @@
     parity = recv_index % 2
     axes = ("zl", "core", "zh", "y", "x")
 
-    arrived = []
-    for flip in range(2):
-        sent_half = (parity + flip) % 2
-        piece = lax.dynamic_slice_in_dim(pressure, sent_half * block_rows, block_rows, 2)
-        arrived.append(lax.ppermute(piece, axes, mirror_pairs(n_recv, n_shot, flip)))
-    upper = jnp.where(parity == 0, arrived[0], arrived[1])
-    lower = jnp.where(parity == 0, arrived[1], arrived[0])
-    mirror = jnp.concatenate([upper, lower], axis=1)
-    symmetric = (
-        (pressure.astype(jnp.float32) + jnp.swapaxes(mirror, 1, 2).astype(jnp.float32)) * 0.5
-    ).astype(jnp.bfloat16)
+    partner_raw = lax.ppermute(pressure, "zh", [(0, 1), (1, 0)])
 
-    partner_block = lax.ppermute(symmetric, "zh", [(0, 1), (1, 0)])
+    def symmetrize(raw, across):
+        arrived = []
+        for flip in range(2):
+            sent_half = (parity + flip) % 2
+            piece = lax.dynamic_slice_in_dim(pressure, sent_half * block_rows, block_rows, 2)
+            arrived.append(lax.ppermute(piece, axes, mirror_pairs(n_recv, n_shot, flip, across)))
+        upper = jnp.where(parity == 0, arrived[0], arrived[1])
+        lower = jnp.where(parity == 0, arrived[1], arrived[0])
+        mirror = jnp.concatenate([upper, lower], axis=1)
+        return (
+            (raw.astype(jnp.float32) + jnp.swapaxes(mirror, 1, 2).astype(jnp.float32)) * 0.5
+        ).astype(jnp.bfloat16)
+
+    symmetric = symmetrize(pressure, 0)
+    partner_block = symmetrize(partner_raw, 1)
     top = jnp.where(half_index == 0, symmetric, partner_block)
     bottom = jnp.where(half_index == 0, partner_block, symmetric)
     panels = lax.all_gather(jnp.stack([top, bottom]), ("y", "x"), axis=1, tiled=False)

time: 216 us -> 247 us (1.14)
  waiting for transfers between devices: 67.9 us -> 87.7 us
  starting transfers between devices: 103 us -> 113 us
    ppermute x7, starting transfers between devices: 29.1 us -> 64.3 us  [gather_line(): lax.ppermute(rightward, 'zl', [(k, k + 1) for k in range(n_line - 1)])]
    ppermute x3 -> x5, waiting for transfers between devices: 15.6 us -> 49.9 us  [the longest x4 43.6 us: symmetrize(): lax.ppermute(piece, axes, mirror_pairs(n_recv, n_shot, flip, across))]
    ppermute x3 -> x5, starting transfers between devices: 57.7 us -> 33.4 us  [the longest x4 30.1 us: symmetrize(): lax.ppermute(piece, axes, mirror_pairs(n_recv, n_shot, flip, across))]
    ppermute x7, waiting for transfers between devices: 26.4 us -> 9.66 us  [gather_line(): lax.ppermute(rightward, 'zl', [(k, k + 1) for k in range(n_line - 1)])]
    ppermute x7, waiting for transfers between devices: 7.76 us -> 15.6 us  [gather_line(): lax.ppermute(leftward, 'zl', [(k + 1, k) for k in range(n_line - 1)])]
    all_gather x1, waiting for transfers between devices: 18.1 us -> 12.5 us  [local(): lax.all_gather(jnp.stack([top, bottom]), ('y', 'x'), axis=1, tiled=False)]
  transfers between devices with their start and end apart: 19 -> 21, of which waited for: 16 -> 17; matrix products, arithmetic and copies ran while one was open for 8% -> 7% of each run, Pallas kernels for 0% -> 0%
where the time goes in v8:
time: 247 us; the launch traced here: 246 us
  starting transfers between devices  113 us (46%)
  waiting for transfers between devices  87.7 us (36%)
  local copies, waits for them, and re-layouts  20.5 us (8%)
  between operations  13.8 us (6%)
  matrix products  7.09 us (3%)
  other arithmetic  3.35 us (1%)
    ppermute x7, starting transfers between devices, gather_line(): lax.ppermute(rightward, 'zl', [(k, k + 1) for k in range(n_line - 1)])  64.3 us
    ppermute x4, waiting for transfers between devices, symmetrize(): lax.ppermute(piece, axes, mirror_pairs(n_recv, n_shot, flip, across))  43.6 us
    ppermute x4, starting transfers between devices, symmetrize(): lax.ppermute(piece, axes, mirror_pairs(n_recv, n_shot, flip, across))  30.1 us
    ppermute x7, waiting for transfers between devices, gather_line(): lax.ppermute(leftward, 'zl', [(k + 1, k) for k in range(n_line - 1)])  15.6 us
    all_gather x1, waiting for transfers between devices, local(): lax.all_gather(jnp.stack([top, bottom]), ('y', 'x'), axis=1, tiled=False)  12.5 us
    ppermute x7, waiting for transfers between devices, gather_line(): lax.ppermute(rightward, 'zl', [(k, k + 1) for k in range(n_line - 1)])  9.66 us
    ppermute x7, starting transfers between devices, gather_line(): lax.ppermute(leftward, 'zl', [(k + 1, k) for k in range(n_line - 1)])  8.98 us
    dot_general x4, matrix products, product(): jnp.einsum('zpxc,zqcn->pqxn', left, panel, preferred_element_type=jnp.flo...  7.09 us
  transfers between devices with their start and end apart: 21, of which 17 were waited for; matrix products, arithmetic and copies ran while one was open for 7% of the time, Pallas kernels for 0%

profile of v8, /device:TPU:1, one launch (start us, length us, event | category | flops | bytes accessed | tf_op | source)
XLA Modules:
  0.0 245.8 jit_solution(14562222543080118994)
XLA Ops:
  6.5 1.2 constant_dynamic-slice_fusion.2
  7.7 0.1 copy.56
  7.9 19.3 %collective-permute-start.3 = (bf16[2,192,192]{1,2,0:T(8,128)(2,1)S(1)}, bf16[2,192,192]{1,2,0:T(8,128)(2,1)S(1)}, u32[]{:S(2)}, u32[]{:S(2)}) collective-permute-start(bf16[2,192,192]{1,2,0:T(8,128)(2,1)S(1)} %copy.56), channel_id=1, source_target_pairs={{0,16},{32,18},{64,20},{96,22},{128,24},{160,26},{192,28},{224,30}... | collective-permute-start | bytes 442376 | tf_op jit(solution)/shard_map/ppermute | solution.py:56
  27.2 0.1 copy.57
  27.3 4.4 %collective-permute-start.4 = (bf16[2,192,192]{1,2,0:T(8,128)(2,1)S(1)}, bf16[2,192,192]{1,2,0:T(8,128)(2,1)S(1)}, u32[]{:S(2)}, u32[]{:S(2)}) collective-permute-start(bf16[2,192,192]{1,2,0:T(8,128)(2,1)S(1)} %copy.57), channel_id=1, source_target_pairs={{0,17},{32,19},{64,21},{96,23},{128,25},{160,27},{192,29},{224,31}... | collective-permute-start | bytes 442376 | tf_op jit(solution)/shard_map/ppermute | solution.py:56
  31.7 3.4 %collective-permute-start.2 = (bf16[2,192,384]{2,1,0:T(8,128)(2,1)}, bf16[2,192,384]{2,1,0:T(8,128)(2,1)S(1)}, u32[]{:S(2)}, u32[]{:S(2)}) collective-permute-start(bf16[2,192,384]{2,1,0:T(8,128)(2,1)} %param.1), channel_id=1, source_target_pairs={{0,16},{16,0},{1,17},{17,1},{2,18},{18,2},{3,19},{19,3},{4,20},{20... | collective-permute-start | bytes 884744 | tf_op jit(solution)/shard_map/ppermute | solution.py:49
  35.0 4.0 %collective-permute-start = (bf16[2,192,192]{1,2,0:T(8,128)(2,1)S(1)}, bf16[2,192,192]{1,2,0:T(8,128)(2,1)S(1)}, u32[]{:S(2)}, u32[]{:S(2)}) collective-permute-start(bf16[2,192,192]{1,2,0:T(8,128)(2,1)S(1)} %copy.56), channel_id=1, source_target_pairs={{0,0},{32,2},{64,4},{96,6},{128,8},{160,10},{192,12},{224,14},{256... | collective-permute-start | bytes 442376 | tf_op jit(solution)/shard_map/ppermute | solution.py:56
  39.0 2.5 collective-permute-start.1
  41.5 26.6 %collective-permute-done.3 = bf16[2,192,192]{1,2,0:T(8,128)(2,1)S(1)} collective-permute-done((bf16[2,192,192]{1,2,0:T(8,128)(2,1)S(1)}, bf16[2,192,192]{1,2,0:T(8,128)(2,1)S(1)}, u32[]{:S(2)}, u32[]{:S(2)}) %collective-permute-start.3) | collective-permute-done | bytes 147488 | tf_op jit(solution)/shard_map/ppermute | solution.py:56
  68.1 17.0 %collective-permute-done.4 = bf16[2,192,192]{1,2,0:T(8,128)(2,1)S(1)} collective-permute-done((bf16[2,192,192]{1,2,0:T(8,128)(2,1)S(1)}, bf16[2,192,192]{1,2,0:T(8,128)(2,1)S(1)}, u32[]{:S(2)}, u32[]{:S(2)}) %collective-permute-start.4) | collective-permute-done | bytes 147488 | tf_op jit(solution)/shard_map/ppermute | solution.py:56
  85.2 0.0 collective-permute-done.1
  85.2 6.3 %collective-permute-done.2 = bf16[2,192,384]{2,1,0:T(8,128)(2,1)S(1)} collective-permute-done((bf16[2,192,384]{2,1,0:T(8,128)(2,1)}, bf16[2,192,384]{2,1,0:T(8,128)(2,1)S(1)}, u32[]{:S(2)}, u32[]{:S(2)}) %collective-permute-start.2) | collective-permute-done | bytes 294944 | tf_op jit(solution)/shard_map/ppermute | solution.py:49
  91.5 1.3 select_bitcast_fusion.1
  92.8 0.2 select_bitcast_fusion
  93.0 0.9 pad_maximum_fusion
  93.8 0.0 all-gather.3.cloned.1.call-update
  93.9 11.6 %collective-permute-start.5 = (bf16[2,192,384]{2,1,0:T(8,128)(2,1)S(1)}, bf16[2,192,384]{2,1,0:T(8,128)(2,1)S(1)}, u32[]{:S(2)}, u32[]{:S(2)}) collective-permute-start(bf16[2,192,384]{2,1,0:T(8,128)(2,1)S(1)} %get-tuple-element.6), channel_id=1, source_target_pairs={{0,64},{64,128},{128,192},{192,256},{256,320},{320,384},{384,448},... | collective-permute-start | bytes 884744 | tf_op jit(solution)/shard_map/ppermute | solution.py:28
  105.4 1.3 collective-permute-start.12
  106.7 4.9 %collective-permute-done.5 = bf16[2,192,384]{2,1,0:T(8,128)(2,1)S(1)} collective-permute-done((bf16[2,192,384]{2,1,0:T(8,128)(2,1)S(1)}, bf16[2,192,384]{2,1,0:T(8,128)(2,1)S(1)}, u32[]{:S(2)}, u32[]{:S(2)}) %collective-permute-start.5) | collective-permute-done | bytes 294944 | tf_op jit(solution)/shard_map/ppermute | solution.py:28
  111.6 11.2 %collective-permute-start.6 = (bf16[2,192,384]{2,1,0:T(8,128)(2,1)S(1)}, bf16[2,192,384]{2,1,0:T(8,128)(2,1)S(1)}, u32[]{:S(2)}, u32[]{:S(2)}) collective-permute-start(bf16[2,192,384]{2,1,0:T(8,128)(2,1)S(1)} %collective-permute-done.5), channel_id=1, source_target_pairs={{0,64},{64,128},{128,192},{192,256},{256,320},{320,384},{384,448},... | collective-permute-start | bytes 884744 | tf_op jit(solution)/shard_map/ppermute | solution.py:28
  122.8 0.7 collective-permute-done.12
  123.6 1.3 collective-permute-start.13
  124.9 3.1 %collective-permute-done.6 = bf16[2,192,384]{2,1,0:T(8,128)(2,1)S(1)} collective-permute-done((bf16[2,192,384]{2,1,0:T(8,128)(2,1)S(1)}, bf16[2,192,384]{2,1,0:T(8,128)(2,1)S(1)}, u32[]{:S(2)}, u32[]{:S(2)}) %collective-permute-start.6) | collective-permute-done | bytes 294944 | tf_op jit(solution)/shard_map/ppermute | solution.py:28
  128.0 11.7 %collective-permute-start.7 = (bf16[2,192,384]{2,1,0:T(8,128)(2,1)S(1)}, bf16[2,192,384]{2,1,0:T(8,128)(2,1)S(1)}, u32[]{:S(2)}, u32[]{:S(2)}) collective-permute-start(bf16[2,192,384]{2,1,0:T(8,128)(2,1)S(1)} %collective-permute-done.6), channel_id=1, source_target_pairs={{0,64},{64,128},{128,192},{192,256},{256,320},{320,384},{384,448},... | collective-permute-start | bytes 884744 | tf_op jit(solution)/shard_map/ppermute | solution.py:28
  139.8 1.8 collective-permute-done.13
  141.6 1.3 collective-permute-start.14
  142.9 1.2 collective-permute-done.7
  144.1 4.1 %collective-permute-start.8 = (bf16[2,192,384]{2,1,0:T(8,128)(2,1)S(1)}, bf16[2,192,384]{2,1,0:T(8,128)(2,1)S(1)}, u32[]{:S(2)}, u32[]{:S(2)}) collective-permute-start(bf16[2,192,384]{2,1,0:T(8,128)(2,1)S(1)} %collective-permute-done.7), channel_id=1, source_target_pairs={{0,64},{64,128},{128,192},{192,256},{256,320},{320,384},{384,448},... | collective-permute-start | bytes 884744 | tf_op jit(solution)/shard_map/ppermute | solution.py:28
  148.2 2.2 collective-permute-done.14
  150.4 1.3 collective-permute-start.15
  151.7 0.1 collective-permute-done.8
  151.8 4.2 %collective-permute-start.9 = (bf16[2,192,384]{2,1,0:T(8,128)(2,1)S(1)}, bf16[2,192,384]{2,1,0:T(8,128)(2,1)S(1)}, u32[]{:S(2)}, u32[]{:S(2)}) collective-permute-start(bf16[2,192,384]{2,1,0:T(8,128)(2,1)S(1)} %collective-permute-done.8), channel_id=1, source_target_pairs={{0,64},{64,128},{128,192},{192,256},{256,320},{320,384},{384,448},... | collective-permute-start | bytes 884744 | tf_op jit(solution)/shard_map/ppermute | solution.py:28
  156.1 2.5 collective-permute-done.15
  158.5 1.3 collective-permute-start.16
  159.8 0.0 collective-permute-done.9
  159.8 6.4 %collective-permute-start.10 = (bf16[2,192,384]{2,1,0:T(8,128)(2,1)S(1)}, bf16[2,192,384]{2,1,0:T(8,128)(2,1)}, u32[]{:S(2)}, u32[]{:S(2)}) collective-permute-start(bf16[2,192,384]{2,1,0:T(8,128)(2,1)S(1)} %collective-permute-done.9), channel_id=1, source_target_pairs={{0,64},{64,128},{128,192},{192,256},{256,320},{320,384},{384,448},... | collective-permute-start | bytes 884744 | tf_op jit(solution)/shard_map/ppermute | solution.py:28
  166.2 1.4 collective-permute-done.16
  167.7 1.3 collective-permute-start.17
  169.0 0.2 collective-permute-done.10
  169.2 15.0 %collective-permute-start.11 = (bf16[2,192,384]{2,1,0:T(8,128)(2,1)}, bf16[2,192,384]{2,1,0:T(8,128)(2,1)}, u32[]{:S(2)}, u32[]{:S(2)}) collective-permute-start(bf16[2,192,384]{2,1,0:T(8,128)(2,1)} %collective-permute-done.10), channel_id=1, source_target_pairs={{0,64},{64,128},{128,192},{192,256},{256,320},{320,384},{384,448},... | collective-permute-start | bytes 884744 | tf_op jit(solution)/shard_map/ppermute | solution.py:28
  184.2 1.8 collective-permute-done.17
  186.0 1.3 collective-permute-start.18
  187.3 0.1 collective-permute-done.11
  187.4 1.0 bitcast_dynamic-update-slice_fusion.13
  188.5 1.0 bitcast_dynamic-update-slice_fusion.12
  190.2 5.1 %collective-permute-done.18 = bf16[2,192,384]{2,1,0:T(8,128)(2,1)S(1)} collective-permute-done((bf16[2,192,384]{2,1,0:T(8,128)(2,1)S(1)}, bf16[2,192,384]{2,1,0:T(8,128)(2,1)S(1)}, u32[]{:S(2)}, u32[]{:S(2)}) %collective-permute-start.18) | collective-permute-done | bytes 294944 | tf_op jit(solution)/shard_map/ppermute | solution.py:29
  195.3 2.1 copy-done.1
  197.4 1.6 constant_dynamic-slice_fusion
  199.1 6.6 %collective-permute-start.19 = (bf16[8,2,192,384]{3,2,0,1:T(8,128)(2,1)}, bf16[8,2,192,384]{3,2,0,1:T(8,128)(2,1)}, u32[]{:S(2)}, u32[]{:S(2)}) collective-permute-start(bf16[8,2,192,384]{3,2,0,1:T(8,128)(2,1)} %constant_dynamic-slice_fusion), channel_id=1, source_target_pairs={{0,32},{32,0},{1,33},{33,1},{2,34},{34,2},{3,35},{35,3},{4,36},{36... | collective-permute-start | bytes 7077896 | tf_op jit(solution)/shard_map/ppermute | solution.py:34
  205.7 12.5 %all-gather.3.cloned.1.call-done = bf16[2,32,192,384]{3,2,1,0:T(8,128)(2,1)} async-done(((bf16[2,2,192,384]{3,2,1,0:T(8,128)(2,1)}), bf16[2,32,192,384]{3,2,1,0:T(8,128)(2,1)}) %all-gather.3.cloned.1.call-update) | async-done | bytes 9437200 | tf_op jit(solution)/shard_map/all_gather | solution.py:68
  218.2 4.7 %fusion.16 = (bf16[1,32,192,384]{3,2,1,0:T(8,128)(2,1)S(1)}, bf16[1,32,192,384]{3,2,1,0:T(8,128)(2,1)S(1)}) fusion(bf16[2,32,192,384]{3,2,1,0:T(8,128)(2,1)} %all-gather.3.cloned.1.call-done), kind=kLoop, calls=%fused_computation.58 | loop fusion | bytes 18874368 | tf_op jit(solution)/shard_map/slice | solution.py:82
  222.9 3.3 %dynamic-slice_bitcast_fusion.1 = (bf16[4,2,2,192,384]{4,3,1,2,0:T(8,128)(2,1)}, bf16[4,2,2,192,384]{4,3,1,2,0:T(8,128)(2,1)}, bf16[4,2,2,192,384]{4,3,1,2,0:T(8,128)(2,1)S(1)}, bf16[4,2,2,192,384]{4,3,1,2,0:T(8,128)(2,1)S(1)}) fusion(bf16[4,2,2,2,192,384]{5,4,3,2,1,0:T(8,128)(2,1)S(1)} %bitcast.181, s32[]{:T(128)S(6)} %select_n.84, s32[]{:T(128)S(6)} %select_n.86, ...), kind=kLoop, calls=%fused_computation.1 | loop fusion | bytes 18874376 | tf_op jit(solution)/shard_map/transpose | solution.py:77
  226.2 2.1 copy.44
  228.3 0.3 copy-done
  228.6 0.3 copy.42
  228.9 0.2 copy.40
  229.1 0.2 copy.24
  229.4 1.4 slice-done
  230.8 0.1 slice-done.1
  230.8 1.1 convolution_bitcast_fusion.1
  232.0 2.4 convolution_bitcast_fusion
  234.4 2.4 convolution_bitcast_fusion.2
  236.7 1.2 fusion.3
  238.1 0.9 pad_maximum_fusion.1
  (25 shorter events, 0.8 us)
Async XLA Ops:
  6.5 211.7 %all-gather.3.cloned.1.call-start = ((), (), s32[]{:S(2)}) async-start(), calls=%async_computation | async-start | bytes 10027008 | tf_op jit(solution)/shard_map/all_gather | solution.py:68
  7.9 60.2 %collective-permute-start.3 = (bf16[2,192,192]{1,2,0:T(8,128)(2,1)S(1)}, bf16[2,192,192]{1,2,0:T(8,128)(2,1)S(1)}, u32[]{:S(2)}, u32[]{:S(2)}) collective-permute-start(bf16[2,192,192]{1,2,0:T(8,128)(2,1)S(1)} %copy.56), channel_id=1, source_target_pairs={{0,16},{32,18},{64,20},{96,22},{128,24},{160,26},{192,28},{224,30}... | collective-permute-start | bytes 442376 | tf_op jit(solution)/shard_map/ppermute | solution.py:56
  27.3 57.8 %collective-permute-start.4 = (bf16[2,192,192]{1,2,0:T(8,128)(2,1)S(1)}, bf16[2,192,192]{1,2,0:T(8,128)(2,1)S(1)}, u32[]{:S(2)}, u32[]{:S(2)}) collective-permute-start(bf16[2,192,192]{1,2,0:T(8,128)(2,1)S(1)} %copy.57), channel_id=1, source_target_pairs={{0,17},{32,19},{64,21},{96,23},{128,25},{160,27},{192,29},{224,31}... | collective-permute-start | bytes 442376 | tf_op jit(solution)/shard_map/ppermute | solution.py:56
  31.7 59.8 %collective-permute-start.2 = (bf16[2,192,384]{2,1,0:T(8,128)(2,1)}, bf16[2,192,384]{2,1,0:T(8,128)(2,1)S(1)}, u32[]{:S(2)}, u32[]{:S(2)}) collective-permute-start(bf16[2,192,384]{2,1,0:T(8,128)(2,1)} %param.1), channel_id=1, source_target_pairs={{0,16},{16,0},{1,17},{17,1},{2,18},{18,2},{3,19},{19,3},{4,20},{20... | collective-permute-start | bytes 884744 | tf_op jit(solution)/shard_map/ppermute | solution.py:49
  35.0 50.1 %collective-permute-start = (bf16[2,192,192]{1,2,0:T(8,128)(2,1)S(1)}, bf16[2,192,192]{1,2,0:T(8,128)(2,1)S(1)}, u32[]{:S(2)}, u32[]{:S(2)}) collective-permute-start(bf16[2,192,192]{1,2,0:T(8,128)(2,1)S(1)} %copy.56), channel_id=1, source_target_pairs={{0,0},{32,2},{64,4},{96,6},{128,8},{160,10},{192,12},{224,14},{256... | collective-permute-start | bytes 442376 | tf_op jit(solution)/shard_map/ppermute | solution.py:56
  39.0 46.1 %collective-permute-start.1 = (bf16[2,192,192]{1,2,0:T(8,128)(2,1)S(1)}, bf16[2,192,192]{1,2,0:T(8,128)(2,1)S(1)}, u32[]{:S(2)}, u32[]{:S(2)}) collective-permute-start(bf16[2,192,192]{1,2,0:T(8,128)(2,1)S(1)} %copy.57), channel_id=1, source_target_pairs={{0,1},{32,3},{64,5},{96,7},{128,9},{160,11},{192,13},{224,15},{256... | collective-permute-start | bytes 442376 | tf_op jit(solution)/shard_map/ppermute | solution.py:56
  93.9 17.8 %collective-permute-start.5 = (bf16[2,192,384]{2,1,0:T(8,128)(2,1)S(1)}, bf16[2,192,384]{2,1,0:T(8,128)(2,1)S(1)}, u32[]{:S(2)}, u32[]{:S(2)}) collective-permute-start(bf16[2,192,384]{2,1,0:T(8,128)(2,1)S(1)} %get-tuple-element.6), channel_id=1, source_target_pairs={{0,64},{64,128},{128,192},{192,256},{256,320},{320,384},{384,448},... | collective-permute-start | bytes 884744 | tf_op jit(solution)/shard_map/ppermute | solution.py:28
  105.4 18.2 %collective-permute-start.12 = (bf16[2,192,384]{2,1,0:T(8,128)(2,1)S(1)}, bf16[2,192,384]{2,1,0:T(8,128)(2,1)S(1)}, u32[]{:S(2)}, u32[]{:S(2)}) collective-permute-start(bf16[2,192,384]{2,1,0:T(8,128)(2,1)S(1)} %get-tuple-element.6), channel_id=1, source_target_pairs={{64,0},{128,64},{192,128},{256,192},{320,256},{384,320},{448,384},... | collective-permute-start | bytes 884744 | tf_op jit(solution)/shard_map/ppermute | solution.py:29
  111.6 16.4 %collective-permute-start.6 = (bf16[2,192,384]{2,1,0:T(8,128)(2,1)S(1)}, bf16[2,192,384]{2,1,0:T(8,128)(2,1)S(1)}, u32[]{:S(2)}, u32[]{:S(2)}) collective-permute-start(bf16[2,192,384]{2,1,0:T(8,128)(2,1)S(1)} %collective-permute-done.5), channel_id=1, source_target_pairs={{0,64},{64,128},{128,192},{192,256},{256,320},{320,384},{384,448},... | collective-permute-start | bytes 884744 | tf_op jit(solution)/shard_map/ppermute | solution.py:28
  123.6 18.0 %collective-permute-start.13 = (bf16[2,192,384]{2,1,0:T(8,128)(2,1)S(1)}, bf16[2,192,384]{2,1,0:T(8,128)(2,1)S(1)}, u32[]{:S(2)}, u32[]{:S(2)}) collective-permute-start(bf16[2,192,384]{2,1,0:T(8,128)(2,1)S(1)} %collective-permute-done.12), channel_id=1, source_target_pairs={{64,0},{128,64},{192,128},{256,192},{320,256},{384,320},{448,384},... | collective-permute-start | bytes 884744 | tf_op jit(solution)/shard_map/ppermute | solution.py:29
  128.0 16.1 %collective-permute-start.7 = (bf16[2,192,384]{2,1,0:T(8,128)(2,1)S(1)}, bf16[2,192,384]{2,1,0:T(8,128)(2,1)S(1)}, u32[]{:S(2)}, u32[]{:S(2)}) collective-permute-start(bf16[2,192,384]{2,1,0:T(8,128)(2,1)S(1)} %collective-permute-done.6), channel_id=1, source_target_pairs={{0,64},{64,128},{128,192},{192,256},{256,320},{320,384},{384,448},... | collective-permute-start | bytes 884744 | tf_op jit(solution)/shard_map/ppermute | solution.py:28
  141.6 8.9 %collective-permute-start.14 = (bf16[2,192,384]{2,1,0:T(8,128)(2,1)S(1)}, bf16[2,192,384]{2,1,0:T(8,128)(2,1)S(1)}, u32[]{:S(2)}, u32[]{:S(2)}) collective-permute-start(bf16[2,192,384]{2,1,0:T(8,128)(2,1)S(1)} %collective-permute-done.13), channel_id=1, source_target_pairs={{64,0},{128,64},{192,128},{256,192},{320,256},{384,320},{448,384},... | collective-permute-start | bytes 884744 | tf_op jit(solution)/shard_map/ppermute | solution.py:29
  144.1 7.8 %collective-permute-start.8 = (bf16[2,192,384]{2,1,0:T(8,128)(2,1)S(1)}, bf16[2,192,384]{2,1,0:T(8,128)(2,1)S(1)}, u32[]{:S(2)}, u32[]{:S(2)}) collective-permute-start(bf16[2,192,384]{2,1,0:T(8,128)(2,1)S(1)} %collective-permute-done.7), channel_id=1, source_target_pairs={{0,64},{64,128},{128,192},{192,256},{256,320},{320,384},{384,448},... | collective-permute-start | bytes 884744 | tf_op jit(solution)/shard_map/ppermute | solution.py:28
  150.4 8.1 %collective-permute-start.15 = (bf16[2,192,384]{2,1,0:T(8,128)(2,1)S(1)}, bf16[2,192,384]{2,1,0:T(8,128)(2,1)S(1)}, u32[]{:S(2)}, u32[]{:S(2)}) collective-permute-start(bf16[2,192,384]{2,1,0:T(8,128)(2,1)S(1)} %collective-permute-done.14), channel_id=1, source_target_pairs={{64,0},{128,64},{192,128},{256,192},{320,256},{384,320},{448,384},... | collective-permute-start | bytes 884744 | tf_op jit(solution)/shard_map/ppermute | solution.py:29
  151.8 8.0 %collective-permute-start.9 = (bf16[2,192,384]{2,1,0:T(8,128)(2,1)S(1)}, bf16[2,192,384]{2,1,0:T(8,128)(2,1)S(1)}, u32[]{:S(2)}, u32[]{:S(2)}) collective-permute-start(bf16[2,192,384]{2,1,0:T(8,128)(2,1)S(1)} %collective-permute-done.8), channel_id=1, source_target_pairs={{0,64},{64,128},{128,192},{192,256},{256,320},{320,384},{384,448},... | collective-permute-start | bytes 884744 | tf_op jit(solution)/shard_map/ppermute | solution.py:28
  158.5 9.2 %collective-permute-start.16 = (bf16[2,192,384]{2,1,0:T(8,128)(2,1)S(1)}, bf16[2,192,384]{2,1,0:T(8,128)(2,1)S(1)}, u32[]{:S(2)}, u32[]{:S(2)}) collective-permute-start(bf16[2,192,384]{2,1,0:T(8,128)(2,1)S(1)} %collective-permute-done.15), channel_id=1, source_target_pairs={{64,0},{128,64},{192,128},{256,192},{320,256},{384,320},{448,384},... | collective-permute-start | bytes 884744 | tf_op jit(solution)/shard_map/ppermute | solution.py:29
  159.8 9.4 %collective-permute-start.10 = (bf16[2,192,384]{2,1,0:T(8,128)(2,1)S(1)}, bf16[2,192,384]{2,1,0:T(8,128)(2,1)}, u32[]{:S(2)}, u32[]{:S(2)}) collective-permute-start(bf16[2,192,384]{2,1,0:T(8,128)(2,1)S(1)} %collective-permute-done.9), channel_id=1, source_target_pairs={{0,64},{64,128},{128,192},{192,256},{256,320},{320,384},{384,448},... | collective-permute-start | bytes 884744 | tf_op jit(solution)/shard_map/ppermute | solution.py:28
  167.7 18.4 %collective-permute-start.17 = (bf16[2,192,384]{2,1,0:T(8,128)(2,1)S(1)}, bf16[2,192,384]{2,1,0:T(8,128)(2,1)S(1)}, u32[]{:S(2)}, u32[]{:S(2)}) collective-permute-start(bf16[2,192,384]{2,1,0:T(8,128)(2,1)S(1)} %collective-permute-done.16), channel_id=1, source_target_pairs={{64,0},{128,64},{192,128},{256,192},{320,256},{384,320},{448,384},... | collective-permute-start | bytes 884744 | tf_op jit(solution)/shard_map/ppermute | solution.py:29
  169.2 18.3 %collective-permute-start.11 = (bf16[2,192,384]{2,1,0:T(8,128)(2,1)}, bf16[2,192,384]{2,1,0:T(8,128)(2,1)}, u32[]{:S(2)}, u32[]{:S(2)}) collective-permute-start(bf16[2,192,384]{2,1,0:T(8,128)(2,1)} %collective-permute-done.10), channel_id=1, source_target_pairs={{0,64},{64,128},{128,192},{192,256},{256,320},{320,384},{384,448},... | collective-permute-start | bytes 884744 | tf_op jit(solution)/shard_map/ppermute | solution.py:28
  186.0 9.2 %collective-permute-start.18 = (bf16[2,192,384]{2,1,0:T(8,128)(2,1)S(1)}, bf16[2,192,384]{2,1,0:T(8,128)(2,1)S(1)}, u32[]{:S(2)}, u32[]{:S(2)}) collective-permute-start(bf16[2,192,384]{2,1,0:T(8,128)(2,1)S(1)} %collective-permute-done.17), channel_id=1, source_target_pairs={{64,0},{128,64},{192,128},{256,192},{320,256},{384,320},{448,384},... | collective-permute-start | bytes 884744 | tf_op jit(solution)/shard_map/ppermute | solution.py:29
  195.3 2.2 copy-start.1
  199.1 32.9 %collective-permute-start.19 = (bf16[8,2,192,384]{3,2,0,1:T(8,128)(2,1)}, bf16[8,2,192,384]{3,2,0,1:T(8,128)(2,1)}, u32[]{:S(2)}, u32[]{:S(2)}) collective-permute-start(bf16[8,2,192,384]{3,2,0,1:T(8,128)(2,1)} %constant_dynamic-slice_fusion), channel_id=1, source_target_pairs={{0,32},{32,0},{1,33},{33,1},{2,34},{34,2},{3,35},{35,3},{4,36},{36... | collective-permute-start | bytes 7077896 | tf_op jit(solution)/shard_map/ppermute | solution.py:34
  226.2 2.4 copy-start
  228.6 2.2 slice-start
  228.9 2.0 slice-start.1
Sparse Core Ops, SparseCore 0:
  94.0 124.1 all-gather.2

commit v9 on v5

--- a/solution.py
+++ b/solution.py
@@ -60,25 +60,21 @@
     partner_block = lax.ppermute(symmetric, "zh", [(0, 1), (1, 0)])
     top = jnp.where(half_index == 0, symmetric, partner_block)
     bottom = jnp.where(half_index == 0, partner_block, symmetric)
-    panels = lax.all_gather(jnp.stack([top, bottom]), ("y", "x"), axis=1, tiled=False)
+    pieces = jnp.swapaxes(jnp.stack([top, bottom]), 1, 2)
+    panels = lax.all_gather(pieces, ("y", "x"), axis=1, tiled=False)
     mine, other = gather_line(symmetric)
     core_index = lax.axis_index("core")
     n_line = mine.shape[0]
     parts, rows, cols = symmetric.shape
+    natural = jnp.where(
+        core_index == 0, jnp.stack([mine, other], axis=1), jnp.stack([other, mine], axis=1)
+    ).reshape((2 * n_line,) + symmetric.shape)
 
-    def product(left, panel, parity):
-        panel = panel.reshape(n_line // 2, 2, 2, parts, rows, cols)
-        panel = lax.dynamic_index_in_dim(panel, parity, 1, keepdims=False)
-        panel = jnp.swapaxes(panel, 1, 2).reshape(n_line // 2, parts, 2 * rows, cols)
-        return jnp.einsum("zpxc,zqcn->pqxn", left, panel, preferred_element_type=jnp.float32)
+    def product(left, panel):
+        panel = panel.reshape(n_line, 2 * rows, parts, cols)
+        return jnp.einsum("jpxc,jcqn->pqxn", left, panel, preferred_element_type=jnp.float32)
 
-    quarter = n_line // 2
-    terms = (
-        product(mine[:quarter], panels[0], core_index)
-        + product(other[:quarter], panels[0], 1 - core_index)
-        + product(mine[quarter:], panels[1], core_index)
-        + product(other[quarter:], panels[1], 1 - core_index)
-    )
+    terms = product(natural[:n_line], panels[0]) + product(natural[n_line:], panels[1])
     factor = 1.0 / math.sqrt(N)
     real = (terms[0, 0] - terms[1, 1]) * factor
     imag = (terms[0, 1] + terms[1, 0]) * factor

time: 216 us -> 209 us (0.968)
  waiting for transfers between devices: 67.9 us -> 59.9 us
  other arithmetic: 3.02 us -> 6.35 us
  local copies, waits for them, and re-layouts: 20.5 us -> 17.2 us
    all_gather x1, waiting for transfers between devices: 18.1 us -> 7.79 us  [local(): panels = lax.all_gather(pieces, ('y', 'x'), axis=1, tiled=False)]
    transpose x5 -> x0, local copies, waits for them, and re-layouts: 6.08 us -> none  [product(): jnp.swapaxes(panel, 1, 2).reshape(n_line // 2, parts, 2 * rows, cols)]
    slice x0 -> x3, local copies, waits for them, and re-layouts: none -> 4.01 us  [the longest x2 2.36 us: local(): natural[:n_line]]
    select_n x0 -> x1, other arithmetic: none -> 3.32 us  [local(): jnp.where(core_index == 0, jnp.stack([mine, other], axis=1), jnp.stack([o...]
    ppermute x1, waiting for transfers between devices: 0.01 us -> 2.27 us  [gather_line(): other = lax.ppermute(mine, 'core', [(0, 1), (1, 0)])]
    unnamed x24 -> x20, local copies, waits for them, and re-layouts: 6.78 us -> 4.98 us
    dot_general x4 -> x2, matrix products: 7.1 us -> 5.99 us  [product(): jnp.einsum('jpxc,jcqn->pqxn', left, panel, preferred_element_type=jnp.flo...]
  transfers between devices with their start and end apart: 19 -> 19, of which waited for: 16 -> 17; matrix products, arithmetic and copies ran while one was open for 8% -> 6% of each run, Pallas kernels for 0% -> 0%
where the time goes in v9:
time: 209 us; the launch traced here: 206 us
  starting transfers between devices  103 us (49%)
  waiting for transfers between devices  59.9 us (29%)
  local copies, waits for them, and re-layouts  17.2 us (8%)
  between operations  13.8 us (7%)
  other arithmetic  6.35 us (3%)
  matrix products  5.99 us (3%)
    ppermute x1, starting transfers between devices, local(): partner_block = lax.ppermute(symmetric, 'zh', [(0, 1), (1, 0)])  49.2 us
    ppermute x7, starting transfers between devices, gather_line(): lax.ppermute(rightward, 'zl', [(k, k + 1) for k in range(n_line - 1)])  29.2 us
    ppermute x7, waiting for transfers between devices, gather_line(): lax.ppermute(rightward, 'zl', [(k, k + 1) for k in range(n_line - 1)])  25.9 us
    ppermute x7, starting transfers between devices, gather_line(): lax.ppermute(leftward, 'zl', [(k + 1, k) for k in range(n_line - 1)])  9 us
    ppermute x2, starting transfers between devices, local(): lax.ppermute(piece, axes, mirror_pairs(n_recv, n_shot, flip))  8.58 us
    ppermute x7, waiting for transfers between devices, gather_line(): lax.ppermute(leftward, 'zl', [(k + 1, k) for k in range(n_line - 1)])  8.3 us
    ppermute x2, waiting for transfers between devices, local(): lax.ppermute(piece, axes, mirror_pairs(n_recv, n_shot, flip))  7.99 us
    all_gather x1, waiting for transfers between devices, local(): panels = lax.all_gather(pieces, ('y', 'x'), axis=1, tiled=False)  7.79 us
  transfers between devices with their start and end apart: 19, of which 17 were waited for; matrix products, arithmetic and copies ran while one was open for 6% of the time, Pallas kernels for 0%

profile of v9, /device:TPU:1, one launch (start us, length us, event | category | flops | bytes accessed | tf_op | source)
XLA Modules:
  0.0 206.4 jit_solution(3513834565831142835)
XLA Ops:
  6.5 0.0 all-gather.3.cloned.1.call-start
  6.5 1.2 constant_dynamic-slice_fusion.2
  7.7 0.1 copy.13
  7.9 6.0 %collective-permute-start = (bf16[2,192,192]{1,2,0:T(8,128)(2,1)S(1)}, bf16[2,192,192]{1,2,0:T(8,128)(2,1)S(1)}, u32[]{:S(2)}, u32[]{:S(2)}) collective-permute-start(bf16[2,192,192]{1,2,0:T(8,128)(2,1)S(1)} %copy.13), channel_id=1, source_target_pairs={{0,0},{32,2},{64,4},{96,6},{128,8},{160,10},{192,12},{224,14},{256... | collective-permute-start | bytes 442376 | tf_op jit(solution)/shard_map/ppermute | solution.py:52
  13.9 0.1 copy.14
  14.1 2.5 %collective-permute-start.1 = (bf16[2,192,192]{1,2,0:T(8,128)(2,1)S(1)}, bf16[2,192,192]{1,2,0:T(8,128)(2,1)S(1)}, u32[]{:S(2)}, u32[]{:S(2)}) collective-permute-start(bf16[2,192,192]{1,2,0:T(8,128)(2,1)S(1)} %copy.14), channel_id=1, source_target_pairs={{0,1},{32,3},{64,5},{96,7},{128,9},{160,11},{192,13},{224,15},{256... | collective-permute-start | bytes 442376 | tf_op jit(solution)/shard_map/ppermute | solution.py:52
  16.6 2.9 %collective-permute-done = bf16[2,192,192]{1,2,0:T(8,128)(2,1)S(1)} collective-permute-done((bf16[2,192,192]{1,2,0:T(8,128)(2,1)S(1)}, bf16[2,192,192]{1,2,0:T(8,128)(2,1)S(1)}, u32[]{:S(2)}, u32[]{:S(2)}) %collective-permute-start) | collective-permute-done | bytes 147488 | tf_op jit(solution)/shard_map/ppermute | solution.py:52
  19.5 5.1 %collective-permute-done.1 = bf16[2,192,192]{1,2,0:T(8,128)(2,1)S(1)} collective-permute-done((bf16[2,192,192]{1,2,0:T(8,128)(2,1)S(1)}, bf16[2,192,192]{1,2,0:T(8,128)(2,1)S(1)}, u32[]{:S(2)}, u32[]{:S(2)}) %collective-permute-start.1) | collective-permute-done | bytes 147488 | tf_op jit(solution)/shard_map/ppermute | solution.py:52
  24.6 1.1 fusion.3
  25.8 49.2 %collective-permute-start.2 = (bf16[2,192,384]{2,1,0:T(8,128)(2,1)S(1)}, bf16[2,192,384]{2,1,0:T(8,128)(2,1)S(1)}, u32[]{:S(2)}, u32[]{:S(2)}) collective-permute-start(bf16[2,192,384]{2,1,0:T(8,128)(2,1)S(1)} %fusion.3), channel_id=1, source_target_pairs={{0,16},{16,0},{1,17},{17,1},{2,18},{18,2},{3,19},{19,3},{4,20},{20... | collective-permute-start | bytes 884744 | tf_op jit(solution)/shard_map/ppermute | solution.py:60
  74.9 7.6 %collective-permute-done.2 = bf16[2,192,384]{2,1,0:T(8,128)(2,1)S(1)} collective-permute-done((bf16[2,192,384]{2,1,0:T(8,128)(2,1)S(1)}, bf16[2,192,384]{2,1,0:T(8,128)(2,1)S(1)}, u32[]{:S(2)}, u32[]{:S(2)}) %collective-permute-start.2) | collective-permute-done | bytes 294944 | tf_op jit(solution)/shard_map/ppermute | solution.py:60
  82.6 0.1 select_bitcast_fusion.1
  82.6 0.9 maximum_bitcast_fusion
  83.5 0.0 all-gather.3.cloned.1.call-update
  83.5 1.3 collective-permute-start.3
  84.8 1.3 collective-permute-start.10
  86.1 12.5 %collective-permute-done.3 = bf16[2,192,384]{2,1,0:T(8,128)(2,1)S(1)} collective-permute-done((bf16[2,192,384]{2,1,0:T(8,128)(2,1)S(1)}, bf16[2,192,384]{2,1,0:T(8,128)(2,1)S(1)}, u32[]{:S(2)}, u32[]{:S(2)}) %collective-permute-start.3) | collective-permute-done | bytes 294944 | tf_op jit(solution)/shard_map/ppermute | solution.py:27
  98.6 4.1 %collective-permute-start.4 = (bf16[2,192,384]{2,1,0:T(8,128)(2,1)S(1)}, bf16[2,192,384]{2,1,0:T(8,128)(2,1)S(1)}, u32[]{:S(2)}, u32[]{:S(2)}) collective-permute-start(bf16[2,192,384]{2,1,0:T(8,128)(2,1)S(1)} %collective-permute-done.3), channel_id=1, source_target_pairs={{0,64},{64,128},{128,192},{192,256},{256,320},{320,384},{384,448},... | collective-permute-start | bytes 884744 | tf_op jit(solution)/shard_map/ppermute | solution.py:27
  102.7 0.0 collective-permute-done.10
  102.7 1.3 collective-permute-start.11
  104.0 4.6 %collective-permute-done.4 = bf16[2,192,384]{2,1,0:T(8,128)(2,1)S(1)} collective-permute-done((bf16[2,192,384]{2,1,0:T(8,128)(2,1)S(1)}, bf16[2,192,384]{2,1,0:T(8,128)(2,1)S(1)}, u32[]{:S(2)}, u32[]{:S(2)}) %collective-permute-start.4) | collective-permute-done | bytes 294944 | tf_op jit(solution)/shard_map/ppermute | solution.py:27
  108.6 4.1 %collective-permute-start.5 = (bf16[2,192,384]{2,1,0:T(8,128)(2,1)S(1)}, bf16[2,192,384]{2,1,0:T(8,128)(2,1)S(1)}, u32[]{:S(2)}, u32[]{:S(2)}) collective-permute-start(bf16[2,192,384]{2,1,0:T(8,128)(2,1)S(1)} %collective-permute-done.4), channel_id=1, source_target_pairs={{0,64},{64,128},{128,192},{192,256},{256,320},{320,384},{384,448},... | collective-permute-start | bytes 884744 | tf_op jit(solution)/shard_map/ppermute | solution.py:27
  112.7 0.0 collective-permute-done.11
  112.7 1.3 collective-permute-start.12
  114.0 3.6 %collective-permute-done.5 = bf16[2,192,384]{2,1,0:T(8,128)(2,1)S(1)} collective-permute-done((bf16[2,192,384]{2,1,0:T(8,128)(2,1)S(1)}, bf16[2,192,384]{2,1,0:T(8,128)(2,1)S(1)}, u32[]{:S(2)}, u32[]{:S(2)}) %collective-permute-start.5) | collective-permute-done | bytes 294944 | tf_op jit(solution)/shard_map/ppermute | solution.py:27
  117.7 4.2 %collective-permute-start.6 = (bf16[2,192,384]{2,1,0:T(8,128)(2,1)S(1)}, bf16[2,192,384]{2,1,0:T(8,128)(2,1)S(1)}, u32[]{:S(2)}, u32[]{:S(2)}) collective-permute-start(bf16[2,192,384]{2,1,0:T(8,128)(2,1)S(1)} %collective-permute-done.5), channel_id=1, source_target_pairs={{0,64},{64,128},{128,192},{192,256},{256,320},{320,384},{384,448},... | collective-permute-start | bytes 884744 | tf_op jit(solution)/shard_map/ppermute | solution.py:27
  121.9 0.9 collective-permute-done.12
  122.8 1.3 collective-permute-start.13
  124.1 2.0 collective-permute-done.6
  126.1 4.2 %collective-permute-start.7 = (bf16[2,192,384]{2,1,0:T(8,128)(2,1)S(1)}, bf16[2,192,384]{2,1,0:T(8,128)(2,1)S(1)}, u32[]{:S(2)}, u32[]{:S(2)}) collective-permute-start(bf16[2,192,384]{2,1,0:T(8,128)(2,1)S(1)} %collective-permute-done.6), channel_id=1, source_target_pairs={{0,64},{64,128},{128,192},{192,256},{256,320},{320,384},{384,448},... | collective-permute-start | bytes 884744 | tf_op jit(solution)/shard_map/ppermute | solution.py:27
  130.3 0.6 collective-permute-done.13
  130.9 1.3 collective-permute-start.14
  132.2 1.7 collective-permute-done.7
  133.9 4.8 %collective-permute-start.8 = (bf16[2,192,384]{2,1,0:T(8,128)(2,1)S(1)}, bf16[2,192,384]{2,1,0:T(8,128)(2,1)}, u32[]{:S(2)}, u32[]{:S(2)}) collective-permute-start(bf16[2,192,384]{2,1,0:T(8,128)(2,1)S(1)} %collective-permute-done.7), channel_id=1, source_target_pairs={{0,64},{64,128},{128,192},{192,256},{256,320},{320,384},{384,448},... | collective-permute-start | bytes 884744 | tf_op jit(solution)/shard_map/ppermute | solution.py:27
  138.7 1.0 collective-permute-done.14
  139.8 1.3 collective-permute-start.15
  141.1 0.6 collective-permute-done.8
  141.7 6.4 %collective-permute-start.9 = (bf16[2,192,384]{2,1,0:T(8,128)(2,1)}, bf16[2,192,384]{2,1,0:T(8,128)(2,1)}, u32[]{:S(2)}, u32[]{:S(2)}) collective-permute-start(bf16[2,192,384]{2,1,0:T(8,128)(2,1)} %collective-permute-done.8), channel_id=1, source_target_pairs={{0,64},{64,128},{128,192},{192,256},{256,320},{320,384},{384,448},... | collective-permute-start | bytes 884744 | tf_op jit(solution)/shard_map/ppermute | solution.py:27
  148.0 1.1 collective-permute-done.15
  149.1 1.3 collective-permute-start.16
  150.4 0.9 collective-permute-done.9
  151.3 1.0 bitcast_dynamic-update-slice_fusion.14
  152.3 1.0 bitcast_dynamic-update-slice_fusion.13
  154.0 4.7 %collective-permute-done.16 = bf16[2,192,384]{2,1,0:T(8,128)(2,1)S(1)} collective-permute-done((bf16[2,192,384]{2,1,0:T(8,128)(2,1)S(1)}, bf16[2,192,384]{2,1,0:T(8,128)(2,1)S(1)}, u32[]{:S(2)}, u32[]{:S(2)}) %collective-permute-start.16) | collective-permute-done | bytes 294944 | tf_op jit(solution)/shard_map/ppermute | solution.py:28
  158.7 0.0 copy-start
  158.7 2.1 %copy-done = bf16[15,2,192,384]{3,2,1,0:T(8,128)(2,1)} copy-done((bf16[15,2,192,384]{3,2,1,0:T(8,128)(2,1)}, bf16[15,2,192,384]{3,2,1,0:T(8,128)(2,1)S(1)}, u32[]{:S(2)}) %copy-start) | copy-done | bytes 4423704
  160.9 0.2 constant_dynamic-slice_fusion
  161.1 7.3 %collective-permute-start.17 = (bf16[8,2,192,384]{3,2,1,0:T(8,128)(2,1)S(1)}, bf16[8,2,192,384]{3,2,1,0:T(8,128)(2,1)}, u32[]{:S(2)}, u32[]{:S(2)}) collective-permute-start(bf16[8,2,192,384]{3,2,1,0:T(8,128)(2,1)S(1)} %constant_dynamic-slice_fusion), channel_id=1, source_target_pairs={{0,32},{32,0},{1,33},{33,1},{2,34},{34,2},{3,35},{35,3},{4,36},{36... | collective-permute-start | bytes 7077896 | tf_op jit(solution)/shard_map/ppermute | solution.py:33
  168.5 2.0 fusion.15
  170.5 2.3 %collective-permute-done.17 = bf16[8,2,192,384]{3,2,1,0:T(8,128)(2,1)} collective-permute-done((bf16[8,2,192,384]{3,2,1,0:T(8,128)(2,1)S(1)}, bf16[8,2,192,384]{3,2,1,0:T(8,128)(2,1)}, u32[]{:S(2)}, u32[]{:S(2)}) %collective-permute-start.17) | collective-permute-done | bytes 2359328 | tf_op jit(solution)/shard_map/ppermute | solution.py:33
  172.7 3.3 %maximum_select_fusion = bf16[8,2,2,192,384]{4,3,2,0,1:T(8,128)(2,1)S(1)} fusion(bf16[8,1,2,192,384]{4,3,2,0,1:T(8,128)(2,1)} %bitcast.23, bf16[8,1,2,192,384]{4,3,2,0,1:T(8,128)(2,1)S(1)} %fusion.15, pred[]{:T(512)S(6)} %eq.17), kind=kLoop, calls=%fused_computation | loop fusion | flops 7077888 | bytes 9437185 | tf_op jit(solution)/shard_map/jit(_where)/select_n | solution.py:69
  176.1 0.7 fusion.10
  176.8 1.6 copy.5
  178.4 1.7 copy.4
  180.1 7.8 %all-gather.3.cloned.1.call-done = bf16[2,3072,2,384]{3,1,2,0:T(8,128)(2,1)} async-done(((bf16[2,192,2,384]{3,1,2,0:T(8,128)(2,1)}), bf16[2,3072,2,384]{3,1,2,0:T(8,128)(2,1)}) %all-gather.3.cloned.1.call-update) | async-done | bytes 9437200 | tf_op jit(solution)/shard_map/all_gather | solution.py:64
  187.9 4.7 %fusion.9 = (bf16[1,3072,2,384]{3,1,2,0:T(8,128)(2,1)S(1)}, bf16[1,3072,2,384]{3,1,2,0:T(8,128)(2,1)S(1)}) fusion(bf16[2,3072,2,384]{3,1,2,0:T(8,128)(2,1)} %all-gather.3.cloned.1.call-done), kind=kLoop, calls=%fused_computation.40 | loop fusion | bytes 18874368 | tf_op jit(solution)/shard_map/slice | solution.py:77
  192.6 0.0 copy-start.1
  192.6 3.9 %convolution_bitcast_fusion = f32[2,384,2,192]{1,3,2,0:T(8,128)S(1)} fusion(bf16[8,384,2,384,1]{3,1,0,4,2:T(8,128)(2,1)S(1)} %bitcast.95, bf16[8,2,192,384,1]{3,2,0,1,4:T(8,128)(2,1)} %bitcast.97), kind=kOutput, calls=%fused_computation.1 | convolution fusion | flops 1811939328 | bytes 8257536 | tf_op jit(solution)/shard_map/jpxc,jcqn->pqxn/dot_general | solution.py:75
  196.5 0.0 copy-done.1
  196.5 2.1 %fusion.1 = f32[2,2,192,384]{3,2,0,1:T(8,128)S(1)} fusion(f32[2,384,2,192]{1,3,2,0:T(8,128)S(1)} %convolution_bitcast_fusion, bf16[8,384,2,384,1]{3,1,0,4,2:T(8,128)(2,1)S(1)} %bitcast.94, bf16[8,2,192,384,1]{3,2,0,1,4:T(8,128)(2,1)S(1)} %bitcast.96), kind=kOutput, calls=%fused_computation.4 | convolution fusion | flops 1812234240 | bytes 9437184 | tf_op jit(solution)/shard_map/jpxc,jcqn->pqxn/dot_general | solution.py:75
  198.7 0.9 pad_maximum_fusion
  (16 shorter events, 0.7 us)
Async XLA Ops:
  6.5 181.3 %all-gather.3.cloned.1.call-start = ((), (), s32[]{:S(2)}) async-start(), calls=%async_computation | async-start | bytes 10027008 | tf_op jit(solution)/shard_map/all_gather | solution.py:64
  7.9 11.7 %collective-permute-start = (bf16[2,192,192]{1,2,0:T(8,128)(2,1)S(1)}, bf16[2,192,192]{1,2,0:T(8,128)(2,1)S(1)}, u32[]{:S(2)}, u32[]{:S(2)}) collective-permute-start(bf16[2,192,192]{1,2,0:T(8,128)(2,1)S(1)} %copy.13), channel_id=1, source_target_pairs={{0,0},{32,2},{64,4},{96,6},{128,8},{160,10},{192,12},{224,14},{256... | collective-permute-start | bytes 442376 | tf_op jit(solution)/shard_map/ppermute | solution.py:52
  14.1 10.5 %collective-permute-start.1 = (bf16[2,192,192]{1,2,0:T(8,128)(2,1)S(1)}, bf16[2,192,192]{1,2,0:T(8,128)(2,1)S(1)}, u32[]{:S(2)}, u32[]{:S(2)}) collective-permute-start(bf16[2,192,192]{1,2,0:T(8,128)(2,1)S(1)} %copy.14), channel_id=1, source_target_pairs={{0,1},{32,3},{64,5},{96,7},{128,9},{160,11},{192,13},{224,15},{256... | collective-permute-start | bytes 442376 | tf_op jit(solution)/shard_map/ppermute | solution.py:52
  25.8 56.8 %collective-permute-start.2 = (bf16[2,192,384]{2,1,0:T(8,128)(2,1)S(1)}, bf16[2,192,384]{2,1,0:T(8,128)(2,1)S(1)}, u32[]{:S(2)}, u32[]{:S(2)}) collective-permute-start(bf16[2,192,384]{2,1,0:T(8,128)(2,1)S(1)} %fusion.3), channel_id=1, source_target_pairs={{0,16},{16,0},{1,17},{17,1},{2,18},{18,2},{3,19},{19,3},{4,20},{20... | collective-permute-start | bytes 884744 | tf_op jit(solution)/shard_map/ppermute | solution.py:60
  83.5 15.1 %collective-permute-start.3 = (bf16[2,192,384]{2,1,0:T(8,128)(2,1)S(1)}, bf16[2,192,384]{2,1,0:T(8,128)(2,1)S(1)}, u32[]{:S(2)}, u32[]{:S(2)}) collective-permute-start(bf16[2,192,384]{2,1,0:T(8,128)(2,1)S(1)} %fusion.3), channel_id=1, source_target_pairs={{0,64},{64,128},{128,192},{192,256},{256,320},{320,384},{384,448},... | collective-permute-start | bytes 884744 | tf_op jit(solution)/shard_map/ppermute | solution.py:27
  84.8 17.9 %collective-permute-start.10 = (bf16[2,192,384]{2,1,0:T(8,128)(2,1)S(1)}, bf16[2,192,384]{2,1,0:T(8,128)(2,1)S(1)}, u32[]{:S(2)}, u32[]{:S(2)}) collective-permute-start(bf16[2,192,384]{2,1,0:T(8,128)(2,1)S(1)} %fusion.3), channel_id=1, source_target_pairs={{64,0},{128,64},{192,128},{256,192},{320,256},{384,320},{448,384},... | collective-permute-start | bytes 884744 | tf_op jit(solution)/shard_map/ppermute | solution.py:28
  98.6 10.0 %collective-permute-start.4 = (bf16[2,192,384]{2,1,0:T(8,128)(2,1)S(1)}, bf16[2,192,384]{2,1,0:T(8,128)(2,1)S(1)}, u32[]{:S(2)}, u32[]{:S(2)}) collective-permute-start(bf16[2,192,384]{2,1,0:T(8,128)(2,1)S(1)} %collective-permute-done.3), channel_id=1, source_target_pairs={{0,64},{64,128},{128,192},{192,256},{256,320},{320,384},{384,448},... | collective-permute-start | bytes 884744 | tf_op jit(solution)/shard_map/ppermute | solution.py:27
  102.7 10.0 %collective-permute-start.11 = (bf16[2,192,384]{2,1,0:T(8,128)(2,1)S(1)}, bf16[2,192,384]{2,1,0:T(8,128)(2,1)S(1)}, u32[]{:S(2)}, u32[]{:S(2)}) collective-permute-start(bf16[2,192,384]{2,1,0:T(8,128)(2,1)S(1)} %collective-permute-done.10), channel_id=1, source_target_pairs={{64,0},{128,64},{192,128},{256,192},{320,256},{384,320},{448,384},... | collective-permute-start | bytes 884744 | tf_op jit(solution)/shard_map/ppermute | solution.py:28
  108.6 9.1 %collective-permute-start.5 = (bf16[2,192,384]{2,1,0:T(8,128)(2,1)S(1)}, bf16[2,192,384]{2,1,0:T(8,128)(2,1)S(1)}, u32[]{:S(2)}, u32[]{:S(2)}) collective-permute-start(bf16[2,192,384]{2,1,0:T(8,128)(2,1)S(1)} %collective-permute-done.4), channel_id=1, source_target_pairs={{0,64},{64,128},{128,192},{192,256},{256,320},{320,384},{384,448},... | collective-permute-start | bytes 884744 | tf_op jit(solution)/shard_map/ppermute | solution.py:27
  112.7 10.0 %collective-permute-start.12 = (bf16[2,192,384]{2,1,0:T(8,128)(2,1)S(1)}, bf16[2,192,384]{2,1,0:T(8,128)(2,1)S(1)}, u32[]{:S(2)}, u32[]{:S(2)}) collective-permute-start(bf16[2,192,384]{2,1,0:T(8,128)(2,1)S(1)} %collective-permute-done.11), channel_id=1, source_target_pairs={{64,0},{128,64},{192,128},{256,192},{320,256},{384,320},{448,384},... | collective-permute-start | bytes 884744 | tf_op jit(solution)/shard_map/ppermute | solution.py:28
  117.7 8.4 %collective-permute-start.6 = (bf16[2,192,384]{2,1,0:T(8,128)(2,1)S(1)}, bf16[2,192,384]{2,1,0:T(8,128)(2,1)S(1)}, u32[]{:S(2)}, u32[]{:S(2)}) collective-permute-start(bf16[2,192,384]{2,1,0:T(8,128)(2,1)S(1)} %collective-permute-done.5), channel_id=1, source_target_pairs={{0,64},{64,128},{128,192},{192,256},{256,320},{320,384},{384,448},... | collective-permute-start | bytes 884744 | tf_op jit(solution)/shard_map/ppermute | solution.py:27
  122.8 8.1 %collective-permute-start.13 = (bf16[2,192,384]{2,1,0:T(8,128)(2,1)S(1)}, bf16[2,192,384]{2,1,0:T(8,128)(2,1)S(1)}, u32[]{:S(2)}, u32[]{:S(2)}) collective-permute-start(bf16[2,192,384]{2,1,0:T(8,128)(2,1)S(1)} %collective-permute-done.12), channel_id=1, source_target_pairs={{64,0},{128,64},{192,128},{256,192},{320,256},{384,320},{448,384},... | collective-permute-start | bytes 884744 | tf_op jit(solution)/shard_map/ppermute | solution.py:28
  126.1 7.9 %collective-permute-start.7 = (bf16[2,192,384]{2,1,0:T(8,128)(2,1)S(1)}, bf16[2,192,384]{2,1,0:T(8,128)(2,1)S(1)}, u32[]{:S(2)}, u32[]{:S(2)}) collective-permute-start(bf16[2,192,384]{2,1,0:T(8,128)(2,1)S(1)} %collective-permute-done.6), channel_id=1, source_target_pairs={{0,64},{64,128},{128,192},{192,256},{256,320},{320,384},{384,448},... | collective-permute-start | bytes 884744 | tf_op jit(solution)/shard_map/ppermute | solution.py:27
  130.9 8.9 %collective-permute-start.14 = (bf16[2,192,384]{2,1,0:T(8,128)(2,1)S(1)}, bf16[2,192,384]{2,1,0:T(8,128)(2,1)S(1)}, u32[]{:S(2)}, u32[]{:S(2)}) collective-permute-start(bf16[2,192,384]{2,1,0:T(8,128)(2,1)S(1)} %collective-permute-done.13), channel_id=1, source_target_pairs={{64,0},{128,64},{192,128},{256,192},{320,256},{384,320},{448,384},... | collective-permute-start | bytes 884744 | tf_op jit(solution)/shard_map/ppermute | solution.py:28
  133.9 7.8 %collective-permute-start.8 = (bf16[2,192,384]{2,1,0:T(8,128)(2,1)S(1)}, bf16[2,192,384]{2,1,0:T(8,128)(2,1)}, u32[]{:S(2)}, u32[]{:S(2)}) collective-permute-start(bf16[2,192,384]{2,1,0:T(8,128)(2,1)S(1)} %collective-permute-done.7), channel_id=1, source_target_pairs={{0,64},{64,128},{128,192},{192,256},{256,320},{320,384},{384,448},... | collective-permute-start | bytes 884744 | tf_op jit(solution)/shard_map/ppermute | solution.py:27
  139.8 9.3 %collective-permute-start.15 = (bf16[2,192,384]{2,1,0:T(8,128)(2,1)S(1)}, bf16[2,192,384]{2,1,0:T(8,128)(2,1)S(1)}, u32[]{:S(2)}, u32[]{:S(2)}) collective-permute-start(bf16[2,192,384]{2,1,0:T(8,128)(2,1)S(1)} %collective-permute-done.14), channel_id=1, source_target_pairs={{64,0},{128,64},{192,128},{256,192},{320,256},{384,320},{448,384},... | collective-permute-start | bytes 884744 | tf_op jit(solution)/shard_map/ppermute | solution.py:28
  141.7 9.6 %collective-permute-start.9 = (bf16[2,192,384]{2,1,0:T(8,128)(2,1)}, bf16[2,192,384]{2,1,0:T(8,128)(2,1)}, u32[]{:S(2)}, u32[]{:S(2)}) collective-permute-start(bf16[2,192,384]{2,1,0:T(8,128)(2,1)} %collective-permute-done.8), channel_id=1, source_target_pairs={{0,64},{64,128},{128,192},{192,256},{256,320},{320,384},{384,448},... | collective-permute-start | bytes 884744 | tf_op jit(solution)/shard_map/ppermute | solution.py:27
  149.1 9.6 %collective-permute-start.16 = (bf16[2,192,384]{2,1,0:T(8,128)(2,1)S(1)}, bf16[2,192,384]{2,1,0:T(8,128)(2,1)S(1)}, u32[]{:S(2)}, u32[]{:S(2)}) collective-permute-start(bf16[2,192,384]{2,1,0:T(8,128)(2,1)S(1)} %collective-permute-done.15), channel_id=1, source_target_pairs={{64,0},{128,64},{192,128},{256,192},{320,256},{384,320},{448,384},... | collective-permute-start | bytes 884744 | tf_op jit(solution)/shard_map/ppermute | solution.py:28
  158.7 2.1 %copy-start = (bf16[15,2,192,384]{3,2,1,0:T(8,128)(2,1)}, bf16[15,2,192,384]{3,2,1,0:T(8,128)(2,1)S(1)}, u32[]{:S(2)}) copy-start(bf16[15,2,192,384]{3,2,1,0:T(8,128)(2,1)S(1)} %bitcast_dynamic-update-slice_fusion) | copy-start | bytes 13271044
  161.1 11.6 %collective-permute-start.17 = (bf16[8,2,192,384]{3,2,1,0:T(8,128)(2,1)S(1)}, bf16[8,2,192,384]{3,2,1,0:T(8,128)(2,1)}, u32[]{:S(2)}, u32[]{:S(2)}) collective-permute-start(bf16[8,2,192,384]{3,2,1,0:T(8,128)(2,1)S(1)} %constant_dynamic-slice_fusion), channel_id=1, source_target_pairs={{0,32},{32,0},{1,33},{33,1},{2,34},{34,2},{3,35},{35,3},{4,36},{36... | collective-permute-start | bytes 7077896 | tf_op jit(solution)/shard_map/ppermute | solution.py:33
  192.6 3.9 %copy-start.1 = (bf16[4,2,2,192,384]{4,3,1,0,2:T(8,128)(2,1)S(1)}, bf16[4,2,2,192,384]{4,3,1,0,2:T(8,128)(2,1)}, u32[]{:S(2)}) copy-start(bf16[4,2,2,192,384]{4,3,1,0,2:T(8,128)(2,1)} %copy.4) | copy-start | bytes 7077892
Sparse Core Ops, SparseCore 0:
  83.6 104.1 all-gather.2

commit v10 on v9

--- a/solution.py
+++ b/solution.py
@@ -9,12 +9,16 @@
 N = 6144
 
 
-def mirror_pairs(n_recv, n_shot, flip):
+def mirror_pairs(n_recv, n_shot, flip, across=0):
     pairs = []
+    n_half = n_recv // 2
     for i in range(n_recv):
         for j in range(n_shot):
             h = (i % 2) ^ flip
-            pairs.append((j * n_recv + i, (i // 2) * n_recv + 2 * j + h))
+            target = (2 * j + h + across * n_half) % n_recv
+            if across and target // n_half != i // n_half:
+                continue
+            pairs.append((j * n_recv + i, (i // 2) * n_recv + target))
     return pairs
 
 
@@ -57,7 +61,23 @@
         (pressure.astype(jnp.float32) + jnp.swapaxes(mirror, 1, 2).astype(jnp.float32)) * 0.5
     ).astype(jnp.bfloat16)
 
-    partner_block = lax.ppermute(symmetric, "zh", [(0, 1), (1, 0)])
+    arrived = []
+    for flip in range(2):
+        sent_half = (parity + flip) % 2
+        piece = lax.dynamic_slice_in_dim(symmetric, sent_half * block_rows, block_rows, 2)
+        arrived.append(lax.ppermute(piece, axes, mirror_pairs(n_recv, n_shot, flip, 1)))
+    upper = jnp.where(parity == 0, arrived[0], arrived[1])
+    lower = jnp.where(parity == 0, arrived[1], arrived[0])
+    transposed = jnp.swapaxes(jnp.concatenate([upper, lower], axis=1), 1, 2)
+    shot_half = n_shot // 2
+    crossing = [
+        (j * 2 + half, j * 2 + 1 - half)
+        for j in range(n_shot)
+        for half in range(2)
+        if j // shot_half == half
+    ]
+    crossed = lax.ppermute(symmetric, ("zl", "core", "zh"), crossing)
+    partner_block = jnp.where(shot_index // shot_half == half_index, transposed, crossed)
     top = jnp.where(half_index == 0, symmetric, partner_block)
     bottom = jnp.where(half_index == 0, partner_block, symmetric)
     pieces = jnp.swapaxes(jnp.stack([top, bottom]), 1, 2)

time: 209 us -> 214 us (1.024)
  waiting for transfers between devices: 59.9 us -> 69.5 us
  starting transfers between devices: 103 us -> 98.4 us
    ppermute x1 -> x3, waiting for transfers between devices: 7.63 us -> 33.8 us  [the longest x2 33.8 us: local(): lax.ppermute(piece, axes, mirror_pairs(n_recv, n_shot, flip, 1))]
    ppermute x1 -> x3, starting transfers between devices: 49.2 us -> 39.1 us  [the longest x1 36.6 us: local(): crossed = lax.ppermute(symmetric, ('zl', 'core', 'zh'), crossing)]
    ppermute x7, waiting for transfers between devices: 8.3 us -> 2.47 us  [gather_line(): lax.ppermute(leftward, 'zl', [(k + 1, k) for k in range(n_line - 1)])]
    all_gather x1, waiting for transfers between devices: 7.79 us -> 2.15 us  [local(): panels = lax.all_gather(pieces, ('y', 'x'), axis=1, tiled=False)]
    ppermute x7, waiting for transfers between devices: 25.9 us -> 20.7 us  [gather_line(): lax.ppermute(rightward, 'zl', [(k, k + 1) for k in range(n_line - 1)])]
    ppermute x7, starting transfers between devices: 29.2 us -> 33.4 us  [gather_line(): lax.ppermute(rightward, 'zl', [(k, k + 1) for k in range(n_line - 1)])]
    unnamed x20 -> x22, local copies, waits for them, and re-layouts: 4.98 us -> 5.25 us
  transfers between devices with their start and end apart: 19 -> 21, of which waited for: 17 -> 14; matrix products, arithmetic and copies ran while one was open for 6% -> 6% of each run, Pallas kernels for 0% -> 0%
where the time goes in v10:
time: 214 us; the launch traced here: 212 us
  starting transfers between devices  98.4 us (46%)
  waiting for transfers between devices  69.5 us (32%)
  local copies, waits for them, and re-layouts  17.6 us (8%)
  between operations  13.9 us (6%)
  other arithmetic  6.54 us (3%)
  matrix products  5.99 us (3%)
    ppermute x1, starting transfers between devices, local(): crossed = lax.ppermute(symmetric, ('zl', 'core', 'zh'), crossing)  36.6 us
    ppermute x2, waiting for transfers between devices, local(): lax.ppermute(piece, axes, mirror_pairs(n_recv, n_shot, flip, 1))  33.8 us
    ppermute x7, starting transfers between devices, gather_line(): lax.ppermute(rightward, 'zl', [(k, k + 1) for k in range(n_line - 1)])  33.4 us
    ppermute x7, waiting for transfers between devices, gather_line(): lax.ppermute(rightward, 'zl', [(k, k + 1) for k in range(n_line - 1)])  20.7 us
    ppermute x7, starting transfers between devices, gather_line(): lax.ppermute(leftward, 'zl', [(k + 1, k) for k in range(n_line - 1)])  9.01 us
    ppermute x2, starting transfers between devices, local(): lax.ppermute(piece, axes, mirror_pairs(n_recv, n_shot, flip))  8.58 us
    ppermute x1, starting transfers between devices, gather_line(): other = lax.ppermute(mine, 'core', [(0, 1), (1, 0)])  8.31 us
    ppermute x2, waiting for transfers between devices, local(): lax.ppermute(piece, axes, mirror_pairs(n_recv, n_shot, flip))  7.98 us
  transfers between devices with their start and end apart: 21, of which 14 were waited for; matrix products, arithmetic and copies ran while one was open for 6% of the time, Pallas kernels for 0%

profile of v10, /device:TPU:1, one launch (start us, length us, event | category | flops | bytes accessed | tf_op | source)
XLA Modules:
  0.0 211.8 jit_solution(5077549982475911960)
XLA Ops:
  6.5 1.2 constant_dynamic-slice_fusion.4
  7.7 0.1 copy.15
  7.9 6.0 %collective-permute-start = (bf16[2,192,192]{1,2,0:T(8,128)(2,1)S(1)}, bf16[2,192,192]{1,2,0:T(8,128)(2,1)S(1)}, u32[]{:S(2)}, u32[]{:S(2)}) collective-permute-start(bf16[2,192,192]{1,2,0:T(8,128)(2,1)S(1)} %copy.15), channel_id=1, source_target_pairs={{0,0},{32,2},{64,4},{96,6},{128,8},{160,10},{192,12},{224,14},{256... | collective-permute-start | bytes 442376 | tf_op jit(solution)/shard_map/ppermute | solution.py:56
  13.9 0.1 copy.16
  14.1 2.5 %collective-permute-start.1 = (bf16[2,192,192]{1,2,0:T(8,128)(2,1)S(1)}, bf16[2,192,192]{1,2,0:T(8,128)(2,1)S(1)}, u32[]{:S(2)}, u32[]{:S(2)}) collective-permute-start(bf16[2,192,192]{1,2,0:T(8,128)(2,1)S(1)} %copy.16), channel_id=1, source_target_pairs={{0,1},{32,3},{64,5},{96,7},{128,9},{160,11},{192,13},{224,15},{256... | collective-permute-start | bytes 442376 | tf_op jit(solution)/shard_map/ppermute | solution.py:56
  16.6 2.9 %collective-permute-done = bf16[2,192,192]{1,2,0:T(8,128)(2,1)S(1)} collective-permute-done((bf16[2,192,192]{1,2,0:T(8,128)(2,1)S(1)}, bf16[2,192,192]{1,2,0:T(8,128)(2,1)S(1)}, u32[]{:S(2)}, u32[]{:S(2)}) %collective-permute-start) | collective-permute-done | bytes 147488 | tf_op jit(solution)/shard_map/ppermute | solution.py:56
  19.5 5.1 %collective-permute-done.1 = bf16[2,192,192]{1,2,0:T(8,128)(2,1)S(1)} collective-permute-done((bf16[2,192,192]{1,2,0:T(8,128)(2,1)S(1)}, bf16[2,192,192]{1,2,0:T(8,128)(2,1)S(1)}, u32[]{:S(2)}, u32[]{:S(2)}) %collective-permute-start.1) | collective-permute-done | bytes 147488 | tf_op jit(solution)/shard_map/ppermute | solution.py:56
  24.6 1.1 fusion.3
  25.8 0.2 constant_dynamic-slice_fusion.2
  25.9 0.1 copy.17
  26.1 1.3 collective-permute-start.2
  27.4 0.1 copy.18
  27.5 1.3 collective-permute-start.3
  28.8 36.6 %collective-permute-start.4 = (bf16[2,192,384]{2,1,0:T(8,128)(2,1)S(1)}, bf16[2,192,384]{2,1,0:T(8,128)(2,1)S(1)}, u32[]{:S(2)}, u32[]{:S(2)}) collective-permute-start(bf16[2,192,384]{2,1,0:T(8,128)(2,1)S(1)} %fusion.3), channel_id=1, source_target_pairs={{0,16},{32,48},{64,80},{96,112},{128,144},{160,176},{192,208},{224... | collective-permute-start | bytes 884744 | tf_op jit(solution)/shard_map/ppermute | solution.py:79
  65.4 30.5 %collective-permute-done.2 = bf16[2,192,192]{1,2,0:T(8,128)(2,1)S(1)} collective-permute-done((bf16[2,192,192]{1,2,0:T(8,128)(2,1)S(1)}, bf16[2,192,192]{1,2,0:T(8,128)(2,1)S(1)}, u32[]{:S(2)}, u32[]{:S(2)}) %collective-permute-start.2) | collective-permute-done | bytes 147488 | tf_op jit(solution)/shard_map/ppermute | solution.py:68
  96.0 3.2 %collective-permute-done.3 = bf16[2,192,192]{1,2,0:T(8,128)(2,1)S(1)} collective-permute-done((bf16[2,192,192]{1,2,0:T(8,128)(2,1)S(1)}, bf16[2,192,192]{1,2,0:T(8,128)(2,1)S(1)}, u32[]{:S(2)}, u32[]{:S(2)}) %collective-permute-start.3) | collective-permute-done | bytes 147488 | tf_op jit(solution)/shard_map/ppermute | solution.py:68
  99.2 0.0 collective-permute-done.4
  99.3 0.2 select_bitcast_fusion.1
  99.5 0.9 maximum_bitcast_fusion
  100.4 0.0 all-gather.3.cloned.1.call-update
  100.4 7.6 %collective-permute-start.5 = (bf16[2,192,384]{2,1,0:T(8,128)(2,1)S(1)}, bf16[2,192,384]{2,1,0:T(8,128)(2,1)S(1)}, u32[]{:S(2)}, u32[]{:S(2)}) collective-permute-start(bf16[2,192,384]{2,1,0:T(8,128)(2,1)S(1)} %fusion.3), channel_id=1, source_target_pairs={{0,64},{64,128},{128,192},{192,256},{256,320},{320,384},{384,448},... | collective-permute-start | bytes 884744 | tf_op jit(solution)/shard_map/ppermute | solution.py:31
  108.0 1.3 collective-permute-start.12
  109.3 4.9 %collective-permute-done.5 = bf16[2,192,384]{2,1,0:T(8,128)(2,1)S(1)} collective-permute-done((bf16[2,192,384]{2,1,0:T(8,128)(2,1)S(1)}, bf16[2,192,384]{2,1,0:T(8,128)(2,1)S(1)}, u32[]{:S(2)}, u32[]{:S(2)}) %collective-permute-start.5) | collective-permute-done | bytes 294944 | tf_op jit(solution)/shard_map/ppermute | solution.py:31
  114.1 4.1 %collective-permute-start.6 = (bf16[2,192,384]{2,1,0:T(8,128)(2,1)S(1)}, bf16[2,192,384]{2,1,0:T(8,128)(2,1)S(1)}, u32[]{:S(2)}, u32[]{:S(2)}) collective-permute-start(bf16[2,192,384]{2,1,0:T(8,128)(2,1)S(1)} %collective-permute-done.5), channel_id=1, source_target_pairs={{0,64},{64,128},{128,192},{192,256},{256,320},{320,384},{384,448},... | collective-permute-start | bytes 884744 | tf_op jit(solution)/shard_map/ppermute | solution.py:31
  118.3 0.0 collective-permute-done.12
  118.3 1.3 collective-permute-start.13
  119.6 3.9 %collective-permute-done.6 = bf16[2,192,384]{2,1,0:T(8,128)(2,1)S(1)} collective-permute-done((bf16[2,192,384]{2,1,0:T(8,128)(2,1)S(1)}, bf16[2,192,384]{2,1,0:T(8,128)(2,1)S(1)}, u32[]{:S(2)}, u32[]{:S(2)}) %collective-permute-start.6) | collective-permute-done | bytes 294944 | tf_op jit(solution)/shard_map/ppermute | solution.py:31
  123.5 4.2 %collective-permute-start.7 = (bf16[2,192,384]{2,1,0:T(8,128)(2,1)S(1)}, bf16[2,192,384]{2,1,0:T(8,128)(2,1)S(1)}, u32[]{:S(2)}, u32[]{:S(2)}) collective-permute-start(bf16[2,192,384]{2,1,0:T(8,128)(2,1)S(1)} %collective-permute-done.6), channel_id=1, source_target_pairs={{0,64},{64,128},{128,192},{192,256},{256,320},{320,384},{384,448},... | collective-permute-start | bytes 884744 | tf_op jit(solution)/shard_map/ppermute | solution.py:31
  127.7 0.0 collective-permute-done.13
  127.7 1.3 collective-permute-start.14
  129.0 3.1 %collective-permute-done.7 = bf16[2,192,384]{2,1,0:T(8,128)(2,1)S(1)} collective-permute-done((bf16[2,192,384]{2,1,0:T(8,128)(2,1)S(1)}, bf16[2,192,384]{2,1,0:T(8,128)(2,1)S(1)}, u32[]{:S(2)}, u32[]{:S(2)}) %collective-permute-start.7) | collective-permute-done | bytes 294944 | tf_op jit(solution)/shard_map/ppermute | solution.py:31
  132.2 4.2 %collective-permute-start.8 = (bf16[2,192,384]{2,1,0:T(8,128)(2,1)S(1)}, bf16[2,192,384]{2,1,0:T(8,128)(2,1)S(1)}, u32[]{:S(2)}, u32[]{:S(2)}) collective-permute-start(bf16[2,192,384]{2,1,0:T(8,128)(2,1)S(1)} %collective-permute-done.7), channel_id=1, source_target_pairs={{0,64},{64,128},{128,192},{192,256},{256,320},{320,384},{384,448},... | collective-permute-start | bytes 884744 | tf_op jit(solution)/shard_map/ppermute | solution.py:31
  136.4 0.0 collective-permute-done.14
  136.4 1.3 collective-permute-start.15
  137.7 2.3 %collective-permute-done.8 = bf16[2,192,384]{2,1,0:T(8,128)(2,1)S(1)} collective-permute-done((bf16[2,192,384]{2,1,0:T(8,128)(2,1)S(1)}, bf16[2,192,384]{2,1,0:T(8,128)(2,1)S(1)}, u32[]{:S(2)}, u32[]{:S(2)}) %collective-permute-start.8) | collective-permute-done | bytes 294944 | tf_op jit(solution)/shard_map/ppermute | solution.py:31
  140.0 3.8 %collective-permute-start.9 = (bf16[2,192,384]{2,1,0:T(8,128)(2,1)S(1)}, bf16[2,192,384]{2,1,0:T(8,128)(2,1)S(1)}, u32[]{:S(2)}, u32[]{:S(2)}) collective-permute-start(bf16[2,192,384]{2,1,0:T(8,128)(2,1)S(1)} %collective-permute-done.8), channel_id=1, source_target_pairs={{0,64},{64,128},{128,192},{192,256},{256,320},{320,384},{384,448},... | collective-permute-start | bytes 884744 | tf_op jit(solution)/shard_map/ppermute | solution.py:31
  143.9 0.0 collective-permute-done.15
  143.9 1.3 collective-permute-start.16
  145.2 2.3 %collective-permute-done.9 = bf16[2,192,384]{2,1,0:T(8,128)(2,1)S(1)} collective-permute-done((bf16[2,192,384]{2,1,0:T(8,128)(2,1)S(1)}, bf16[2,192,384]{2,1,0:T(8,128)(2,1)S(1)}, u32[]{:S(2)}, u32[]{:S(2)}) %collective-permute-start.9) | collective-permute-done | bytes 294944 | tf_op jit(solution)/shard_map/ppermute | solution.py:31
  147.5 4.5 %collective-permute-start.10 = (bf16[2,192,384]{2,1,0:T(8,128)(2,1)S(1)}, bf16[2,192,384]{2,1,0:T(8,128)(2,1)}, u32[]{:S(2)}, u32[]{:S(2)}) collective-permute-start(bf16[2,192,384]{2,1,0:T(8,128)(2,1)S(1)} %collective-permute-done.9), channel_id=1, source_target_pairs={{0,64},{64,128},{128,192},{192,256},{256,320},{320,384},{384,448},... | collective-permute-start | bytes 884744 | tf_op jit(solution)/shard_map/ppermute | solution.py:31
  152.0 0.0 collective-permute-done.16
  152.0 1.3 collective-permute-start.17
  153.3 1.6 collective-permute-done.10
  155.0 4.9 %collective-permute-start.11 = (bf16[2,192,384]{2,1,0:T(8,128)(2,1)}, bf16[2,192,384]{2,1,0:T(8,128)(2,1)}, u32[]{:S(2)}, u32[]{:S(2)}) collective-permute-start(bf16[2,192,384]{2,1,0:T(8,128)(2,1)} %collective-permute-done.10), channel_id=1, source_target_pairs={{0,64},{64,128},{128,192},{192,256},{256,320},{320,384},{384,448},... | collective-permute-start | bytes 884744 | tf_op jit(solution)/shard_map/ppermute | solution.py:31
  159.9 0.0 collective-permute-done.17
  159.9 1.3 collective-permute-start.18
  161.2 2.5 %collective-permute-done.11 = bf16[2,192,384]{2,1,0:T(8,128)(2,1)} collective-permute-done((bf16[2,192,384]{2,1,0:T(8,128)(2,1)}, bf16[2,192,384]{2,1,0:T(8,128)(2,1)}, u32[]{:S(2)}, u32[]{:S(2)}) %collective-permute-start.11) | collective-permute-done | bytes 294944 | tf_op jit(solution)/shard_map/ppermute | solution.py:31
  163.7 1.0 bitcast_dynamic-update-slice_fusion.14
  164.7 1.0 bitcast_dynamic-update-slice_fusion.13
  166.4 2.4 %collective-permute-done.18 = bf16[2,192,384]{2,1,0:T(8,128)(2,1)S(1)} collective-permute-done((bf16[2,192,384]{2,1,0:T(8,128)(2,1)S(1)}, bf16[2,192,384]{2,1,0:T(8,128)(2,1)S(1)}, u32[]{:S(2)}, u32[]{:S(2)}) %collective-permute-start.18) | collective-permute-done | bytes 294944 | tf_op jit(solution)/shard_map/ppermute | solution.py:32
  168.8 2.1 %copy-done = bf16[15,2,192,384]{3,2,1,0:T(8,128)(2,1)} copy-done((bf16[15,2,192,384]{3,2,1,0:T(8,128)(2,1)}, bf16[15,2,192,384]{3,2,1,0:T(8,128)(2,1)S(1)}, u32[]{:S(2)}) %copy-start) | copy-done | bytes 4423704
  171.0 0.2 constant_dynamic-slice_fusion
  171.2 8.3 %collective-permute-start.19 = (bf16[8,2,192,384]{3,2,1,0:T(8,128)(2,1)S(1)}, bf16[8,2,192,384]{3,2,1,0:T(8,128)(2,1)}, u32[]{:S(2)}, u32[]{:S(2)}) collective-permute-start(bf16[8,2,192,384]{3,2,1,0:T(8,128)(2,1)S(1)} %constant_dynamic-slice_fusion), channel_id=1, source_target_pairs={{0,32},{32,0},{1,33},{33,1},{2,34},{34,2},{3,35},{35,3},{4,36},{36... | collective-permute-start | bytes 7077896 | tf_op jit(solution)/shard_map/ppermute | solution.py:37
  179.5 1.9 fusion.16
  181.5 2.3 %collective-permute-done.19 = bf16[8,2,192,384]{3,2,1,0:T(8,128)(2,1)} collective-permute-done((bf16[8,2,192,384]{3,2,1,0:T(8,128)(2,1)S(1)}, bf16[8,2,192,384]{3,2,1,0:T(8,128)(2,1)}, u32[]{:S(2)}, u32[]{:S(2)}) %collective-permute-start.19) | collective-permute-done | bytes 2359328 | tf_op jit(solution)/shard_map/ppermute | solution.py:37
  183.8 3.3 %maximum_select_fusion = bf16[8,2,2,192,384]{4,3,2,0,1:T(8,128)(2,1)S(1)} fusion(bf16[8,1,2,192,384]{4,3,2,0,1:T(8,128)(2,1)} %bitcast.24, bf16[8,1,2,192,384]{4,3,2,0,1:T(8,128)(2,1)S(1)} %fusion.16, pred[]{:T(512)S(6)} %eq.25), kind=kLoop, calls=%fused_computation | loop fusion | flops 7077888 | bytes 9437185 | tf_op jit(solution)/shard_map/jit(_where)/select_n | solution.py:89
  187.2 0.7 fusion.11
  187.8 1.6 copy.7
  189.5 1.7 copy.6
  191.2 2.2 %all-gather.3.cloned.1.call-done = bf16[2,3072,2,384]{3,1,2,0:T(8,128)(2,1)} async-done(((bf16[2,192,2,384]{3,1,2,0:T(8,128)(2,1)}), bf16[2,3072,2,384]{3,1,2,0:T(8,128)(2,1)}) %all-gather.3.cloned.1.call-update) | async-done | bytes 9437200 | tf_op jit(solution)/shard_map/all_gather | solution.py:84
  193.3 4.7 %fusion.10 = (bf16[1,3072,2,384]{3,1,2,0:T(8,128)(2,1)S(1)}, bf16[1,3072,2,384]{3,1,2,0:T(8,128)(2,1)S(1)}) fusion(bf16[2,3072,2,384]{3,1,2,0:T(8,128)(2,1)} %all-gather.3.cloned.1.call-done), kind=kLoop, calls=%fused_computation.46 | loop fusion | bytes 18874368 | tf_op jit(solution)/shard_map/slice | solution.py:97
  198.0 3.9 %convolution_bitcast_fusion = f32[2,384,2,192]{1,3,2,0:T(8,128)S(1)} fusion(bf16[8,384,2,384,1]{3,1,0,4,2:T(8,128)(2,1)S(1)} %bitcast.103, bf16[8,2,192,384,1]{3,2,0,1,4:T(8,128)(2,1)} %bitcast.105), kind=kOutput, calls=%fused_computation.1 | convolution fusion | flops 1811939328 | bytes 8257536 | tf_op jit(solution)/shard_map/jpxc,jcqn->pqxn/dot_general | solution.py:95
  202.0 2.1 fusion.1
  204.1 0.9 pad_maximum_fusion
  (21 shorter events, 0.8 us)
Async XLA Ops:
  6.5 186.8 %all-gather.3.cloned.1.call-start = ((), (), s32[]{:S(2)}) async-start(), calls=%async_computation | async-start | bytes 10027008 | tf_op jit(solution)/shard_map/all_gather | solution.py:84
  7.9 11.7 %collective-permute-start = (bf16[2,192,192]{1,2,0:T(8,128)(2,1)S(1)}, bf16[2,192,192]{1,2,0:T(8,128)(2,1)S(1)}, u32[]{:S(2)}, u32[]{:S(2)}) collective-permute-start(bf16[2,192,192]{1,2,0:T(8,128)(2,1)S(1)} %copy.15), channel_id=1, source_target_pairs={{0,0},{32,2},{64,4},{96,6},{128,8},{160,10},{192,12},{224,14},{256... | collective-permute-start | bytes 442376 | tf_op jit(solution)/shard_map/ppermute | solution.py:56
  14.1 10.5 %collective-permute-start.1 = (bf16[2,192,192]{1,2,0:T(8,128)(2,1)S(1)}, bf16[2,192,192]{1,2,0:T(8,128)(2,1)S(1)}, u32[]{:S(2)}, u32[]{:S(2)}) collective-permute-start(bf16[2,192,192]{1,2,0:T(8,128)(2,1)S(1)} %copy.16), channel_id=1, source_target_pairs={{0,1},{32,3},{64,5},{96,7},{128,9},{160,11},{192,13},{224,15},{256... | collective-permute-start | bytes 442376 | tf_op jit(solution)/shard_map/ppermute | solution.py:56
  26.1 69.9 %collective-permute-start.2 = (bf16[2,192,192]{1,2,0:T(8,128)(2,1)S(1)}, bf16[2,192,192]{1,2,0:T(8,128)(2,1)S(1)}, u32[]{:S(2)}, u32[]{:S(2)}) collective-permute-start(bf16[2,192,192]{1,2,0:T(8,128)(2,1)S(1)} %copy.17), channel_id=1, source_target_pairs={{256,0},{288,2},{320,4},{352,6},{384,8},{416,10},{448,12},{480,14}... | collective-permute-start | bytes 442376 | tf_op jit(solution)/shard_map/ppermute | solution.py:68
  27.5 71.7 %collective-permute-start.3 = (bf16[2,192,192]{1,2,0:T(8,128)(2,1)S(1)}, bf16[2,192,192]{1,2,0:T(8,128)(2,1)S(1)}, u32[]{:S(2)}, u32[]{:S(2)}) collective-permute-start(bf16[2,192,192]{1,2,0:T(8,128)(2,1)S(1)} %copy.18), channel_id=1, source_target_pairs={{256,1},{288,3},{320,5},{352,7},{384,9},{416,11},{448,13},{480,15}... | collective-permute-start | bytes 442376 | tf_op jit(solution)/shard_map/ppermute | solution.py:68
  28.8 70.4 %collective-permute-start.4 = (bf16[2,192,384]{2,1,0:T(8,128)(2,1)S(1)}, bf16[2,192,384]{2,1,0:T(8,128)(2,1)S(1)}, u32[]{:S(2)}, u32[]{:S(2)}) collective-permute-start(bf16[2,192,384]{2,1,0:T(8,128)(2,1)S(1)} %fusion.3), channel_id=1, source_target_pairs={{0,16},{32,48},{64,80},{96,112},{128,144},{160,176},{192,208},{224... | collective-permute-start | bytes 884744 | tf_op jit(solution)/shard_map/ppermute | solution.py:79
  100.4 13.7 %collective-permute-start.5 = (bf16[2,192,384]{2,1,0:T(8,128)(2,1)S(1)}, bf16[2,192,384]{2,1,0:T(8,128)(2,1)S(1)}, u32[]{:S(2)}, u32[]{:S(2)}) collective-permute-start(bf16[2,192,384]{2,1,0:T(8,128)(2,1)S(1)} %fusion.3), channel_id=1, source_target_pairs={{0,64},{64,128},{128,192},{192,256},{256,320},{320,384},{384,448},... | collective-permute-start | bytes 884744 | tf_op jit(solution)/shard_map/ppermute | solution.py:31
  108.0 10.3 %collective-permute-start.12 = (bf16[2,192,384]{2,1,0:T(8,128)(2,1)S(1)}, bf16[2,192,384]{2,1,0:T(8,128)(2,1)S(1)}, u32[]{:S(2)}, u32[]{:S(2)}) collective-permute-start(bf16[2,192,384]{2,1,0:T(8,128)(2,1)S(1)} %fusion.3), channel_id=1, source_target_pairs={{64,0},{128,64},{192,128},{256,192},{320,256},{384,320},{448,384},... | collective-permute-start | bytes 884744 | tf_op jit(solution)/shard_map/ppermute | solution.py:32
  114.1 9.4 %collective-permute-start.6 = (bf16[2,192,384]{2,1,0:T(8,128)(2,1)S(1)}, bf16[2,192,384]{2,1,0:T(8,128)(2,1)S(1)}, u32[]{:S(2)}, u32[]{:S(2)}) collective-permute-start(bf16[2,192,384]{2,1,0:T(8,128)(2,1)S(1)} %collective-permute-done.5), channel_id=1, source_target_pairs={{0,64},{64,128},{128,192},{192,256},{256,320},{320,384},{384,448},... | collective-permute-start | bytes 884744 | tf_op jit(solution)/shard_map/ppermute | solution.py:31
  118.3 9.5 %collective-permute-start.13 = (bf16[2,192,384]{2,1,0:T(8,128)(2,1)S(1)}, bf16[2,192,384]{2,1,0:T(8,128)(2,1)S(1)}, u32[]{:S(2)}, u32[]{:S(2)}) collective-permute-start(bf16[2,192,384]{2,1,0:T(8,128)(2,1)S(1)} %collective-permute-done.12), channel_id=1, source_target_pairs={{64,0},{128,64},{192,128},{256,192},{320,256},{384,320},{448,384},... | collective-permute-start | bytes 884744 | tf_op jit(solution)/shard_map/ppermute | solution.py:32
  123.5 8.7 %collective-permute-start.7 = (bf16[2,192,384]{2,1,0:T(8,128)(2,1)S(1)}, bf16[2,192,384]{2,1,0:T(8,128)(2,1)S(1)}, u32[]{:S(2)}, u32[]{:S(2)}) collective-permute-start(bf16[2,192,384]{2,1,0:T(8,128)(2,1)S(1)} %collective-permute-done.6), channel_id=1, source_target_pairs={{0,64},{64,128},{128,192},{192,256},{256,320},{320,384},{384,448},... | collective-permute-start | bytes 884744 | tf_op jit(solution)/shard_map/ppermute | solution.py:31
  127.7 8.7 %collective-permute-start.14 = (bf16[2,192,384]{2,1,0:T(8,128)(2,1)S(1)}, bf16[2,192,384]{2,1,0:T(8,128)(2,1)S(1)}, u32[]{:S(2)}, u32[]{:S(2)}) collective-permute-start(bf16[2,192,384]{2,1,0:T(8,128)(2,1)S(1)} %collective-permute-done.13), channel_id=1, source_target_pairs={{64,0},{128,64},{192,128},{256,192},{320,256},{384,320},{448,384},... | collective-permute-start | bytes 884744 | tf_op jit(solution)/shard_map/ppermute | solution.py:32
  132.2 7.9 %collective-permute-start.8 = (bf16[2,192,384]{2,1,0:T(8,128)(2,1)S(1)}, bf16[2,192,384]{2,1,0:T(8,128)(2,1)S(1)}, u32[]{:S(2)}, u32[]{:S(2)}) collective-permute-start(bf16[2,192,384]{2,1,0:T(8,128)(2,1)S(1)} %collective-permute-done.7), channel_id=1, source_target_pairs={{0,64},{64,128},{128,192},{192,256},{256,320},{320,384},{384,448},... | collective-permute-start | bytes 884744 | tf_op jit(solution)/shard_map/ppermute | solution.py:31
  136.4 7.5 %collective-permute-start.15 = (bf16[2,192,384]{2,1,0:T(8,128)(2,1)S(1)}, bf16[2,192,384]{2,1,0:T(8,128)(2,1)S(1)}, u32[]{:S(2)}, u32[]{:S(2)}) collective-permute-start(bf16[2,192,384]{2,1,0:T(8,128)(2,1)S(1)} %collective-permute-done.14), channel_id=1, source_target_pairs={{64,0},{128,64},{192,128},{256,192},{320,256},{384,320},{448,384},... | collective-permute-start | bytes 884744 | tf_op jit(solution)/shard_map/ppermute | solution.py:32
  140.0 7.5 %collective-permute-start.9 = (bf16[2,192,384]{2,1,0:T(8,128)(2,1)S(1)}, bf16[2,192,384]{2,1,0:T(8,128)(2,1)S(1)}, u32[]{:S(2)}, u32[]{:S(2)}) collective-permute-start(bf16[2,192,384]{2,1,0:T(8,128)(2,1)S(1)} %collective-permute-done.8), channel_id=1, source_target_pairs={{0,64},{64,128},{128,192},{192,256},{256,320},{320,384},{384,448},... | collective-permute-start | bytes 884744 | tf_op jit(solution)/shard_map/ppermute | solution.py:31
  143.9 8.2 %collective-permute-start.16 = (bf16[2,192,384]{2,1,0:T(8,128)(2,1)S(1)}, bf16[2,192,384]{2,1,0:T(8,128)(2,1)S(1)}, u32[]{:S(2)}, u32[]{:S(2)}) collective-permute-start(bf16[2,192,384]{2,1,0:T(8,128)(2,1)S(1)} %collective-permute-done.15), channel_id=1, source_target_pairs={{64,0},{128,64},{192,128},{256,192},{320,256},{384,320},{448,384},... | collective-permute-start | bytes 884744 | tf_op jit(solution)/shard_map/ppermute | solution.py:32
  147.5 7.5 %collective-permute-start.10 = (bf16[2,192,384]{2,1,0:T(8,128)(2,1)S(1)}, bf16[2,192,384]{2,1,0:T(8,128)(2,1)}, u32[]{:S(2)}, u32[]{:S(2)}) collective-permute-start(bf16[2,192,384]{2,1,0:T(8,128)(2,1)S(1)} %collective-permute-done.9), channel_id=1, source_target_pairs={{0,64},{64,128},{128,192},{192,256},{256,320},{320,384},{384,448},... | collective-permute-start | bytes 884744 | tf_op jit(solution)/shard_map/ppermute | solution.py:31
  152.0 7.9 %collective-permute-start.17 = (bf16[2,192,384]{2,1,0:T(8,128)(2,1)S(1)}, bf16[2,192,384]{2,1,0:T(8,128)(2,1)S(1)}, u32[]{:S(2)}, u32[]{:S(2)}) collective-permute-start(bf16[2,192,384]{2,1,0:T(8,128)(2,1)S(1)} %collective-permute-done.16), channel_id=1, source_target_pairs={{64,0},{128,64},{192,128},{256,192},{320,256},{384,320},{448,384},... | collective-permute-start | bytes 884744 | tf_op jit(solution)/shard_map/ppermute | solution.py:32
  155.0 8.7 %collective-permute-start.11 = (bf16[2,192,384]{2,1,0:T(8,128)(2,1)}, bf16[2,192,384]{2,1,0:T(8,128)(2,1)}, u32[]{:S(2)}, u32[]{:S(2)}) collective-permute-start(bf16[2,192,384]{2,1,0:T(8,128)(2,1)} %collective-permute-done.10), channel_id=1, source_target_pairs={{0,64},{64,128},{128,192},{192,256},{256,320},{320,384},{384,448},... | collective-permute-start | bytes 884744 | tf_op jit(solution)/shard_map/ppermute | solution.py:31
  159.9 8.9 %collective-permute-start.18 = (bf16[2,192,384]{2,1,0:T(8,128)(2,1)S(1)}, bf16[2,192,384]{2,1,0:T(8,128)(2,1)S(1)}, u32[]{:S(2)}, u32[]{:S(2)}) collective-permute-start(bf16[2,192,384]{2,1,0:T(8,128)(2,1)S(1)} %collective-permute-done.17), channel_id=1, source_target_pairs={{64,0},{128,64},{192,128},{256,192},{320,256},{384,320},{448,384},... | collective-permute-start | bytes 884744 | tf_op jit(solution)/shard_map/ppermute | solution.py:32
  168.8 2.1 %copy-start = (bf16[15,2,192,384]{3,2,1,0:T(8,128)(2,1)}, bf16[15,2,192,384]{3,2,1,0:T(8,128)(2,1)S(1)}, u32[]{:S(2)}) copy-start(bf16[15,2,192,384]{3,2,1,0:T(8,128)(2,1)S(1)} %bitcast_dynamic-update-slice_fusion) | copy-start | bytes 13271044
  171.2 12.6 %collective-permute-start.19 = (bf16[8,2,192,384]{3,2,1,0:T(8,128)(2,1)S(1)}, bf16[8,2,192,384]{3,2,1,0:T(8,128)(2,1)}, u32[]{:S(2)}, u32[]{:S(2)}) collective-permute-start(bf16[8,2,192,384]{3,2,1,0:T(8,128)(2,1)S(1)} %constant_dynamic-slice_fusion), channel_id=1, source_target_pairs={{0,32},{32,0},{1,33},{33,1},{2,34},{34,2},{3,35},{35,3},{4,36},{36... | collective-permute-start | bytes 7077896 | tf_op jit(solution)/shard_map/ppermute | solution.py:37
  198.0 3.9 %copy-start.1 = (bf16[4,2,2,192,384]{4,3,1,0,2:T(8,128)(2,1)S(1)}, bf16[4,2,2,192,384]{4,3,1,0,2:T(8,128)(2,1)}, u32[]{:S(2)}) copy-start(bf16[4,2,2,192,384]{4,3,1,0,2:T(8,128)(2,1)} %copy.6) | copy-start | bytes 7077892
Sparse Core Ops, SparseCore 0:
  100.5 92.7 all-gather.2

commit v11 on v9

--- a/solution.py
+++ b/solution.py
@@ -70,11 +70,8 @@
         core_index == 0, jnp.stack([mine, other], axis=1), jnp.stack([other, mine], axis=1)
     ).reshape((2 * n_line,) + symmetric.shape)
 
-    def product(left, panel):
-        panel = panel.reshape(n_line, 2 * rows, parts, cols)
-        return jnp.einsum("jpxc,jcqn->pqxn", left, panel, preferred_element_type=jnp.float32)
-
-    terms = product(natural[:n_line], panels[0]) + product(natural[n_line:], panels[1])
+    panel = panels.reshape(2 * n_line, 2 * rows, parts, cols)
+    terms = jnp.einsum("jpxc,jcqn->pqxn", natural, panel, preferred_element_type=jnp.float32)
     factor = 1.0 / math.sqrt(N)
     real = (terms[0, 0] - terms[1, 1]) * factor
     imag = (terms[0, 1] + terms[1, 0]) * factor

time: 209 us -> 214 us (1.024)
  matrix products: 5.99 us -> 9 us
  other arithmetic: 6.35 us -> 8.74 us
    slice x4 -> x0, local copies, waits for them, and re-layouts: 8.73 us -> none  [the longest x1 4.72 us: local(): panels[0]]
    all_gather x0 -> x1, local copies, waits for them, and re-layouts: none -> 8.26 us  [local(): panels = lax.all_gather(pieces, ('y', 'x'), axis=1, tiled=False)]
    dot_general x2 -> x1, matrix products: 5.99 us -> 9 us  [local(): jnp.einsum('jpxc,jcqn->pqxn', natural, panel, preferred_element_type=jnp....]
    select_n x1, other arithmetic: 3.32 us -> 5.72 us  [local(): jnp.where(core_index == 0, jnp.stack([mine, other], axis=1), jnp.stack([o...]
    unnamed x20 -> x18, local copies, waits for them, and re-layouts: 4.98 us -> 4.99 us
  transfers between devices with their start and end apart: 19 -> 19, of which waited for: 17 -> 17; matrix products, arithmetic and copies ran while one was open for 6% -> 5% of each run, Pallas kernels for 0% -> 0%
where the time goes in v11:
time: 214 us; the launch traced here: 213 us
  starting transfers between devices  103 us (48%)
  waiting for transfers between devices  61.5 us (29%)
  local copies, waits for them, and re-layouts  16.7 us (8%)
  between operations  13.7 us (6%)
  matrix products  9 us (4%)
  other arithmetic  8.74 us (4%)
    ppermute x1, starting transfers between devices, local(): partner_block = lax.ppermute(symmetric, 'zh', [(0, 1), (1, 0)])  49.2 us
    ppermute x7, starting transfers between devices, gather_line(): lax.ppermute(rightward, 'zl', [(k, k + 1) for k in range(n_line - 1)])  29.2 us
    ppermute x7, waiting for transfers between devices, gather_line(): lax.ppermute(rightward, 'zl', [(k, k + 1) for k in range(n_line - 1)])  25.9 us
    all_gather x1, waiting for transfers between devices, local(): panels = lax.all_gather(pieces, ('y', 'x'), axis=1, tiled=False)  9.41 us
    ppermute x7, starting transfers between devices, gather_line(): lax.ppermute(leftward, 'zl', [(k + 1, k) for k in range(n_line - 1)])  9 us
    dot_general x1, matrix products, local(): jnp.einsum('jpxc,jcqn->pqxn', natural, panel, preferred_element_type=jnp....  9 us
    ppermute x2, starting transfers between devices, local(): lax.ppermute(piece, axes, mirror_pairs(n_recv, n_shot, flip))  8.58 us
    ppermute x7, waiting for transfers between devices, gather_line(): lax.ppermute(leftward, 'zl', [(k + 1, k) for k in range(n_line - 1)])  8.31 us
  transfers between devices with their start and end apart: 19, of which 17 were waited for; matrix products, arithmetic and copies ran while one was open for 5% of the time, Pallas kernels for 0%

profile of v11, /device:TPU:1, one launch (start us, length us, event | category | flops | bytes accessed | tf_op | source)
XLA Modules:
  0.0 212.9 jit_solution(17877112444489441244)
XLA Ops:
  6.5 0.0 all-gather.3.cloned.1.call-start
  6.5 1.2 constant_dynamic-slice_fusion.2
  7.7 0.1 copy.17
  7.9 6.0 %collective-permute-start = (bf16[2,192,192]{1,2,0:T(8,128)(2,1)S(1)}, bf16[2,192,192]{1,2,0:T(8,128)(2,1)S(1)}, u32[]{:S(2)}, u32[]{:S(2)}) collective-permute-start(bf16[2,192,192]{1,2,0:T(8,128)(2,1)S(1)} %copy.17), channel_id=1, source_target_pairs={{0,0},{32,2},{64,4},{96,6},{128,8},{160,10},{192,12},{224,14},{256... | collective-permute-start | bytes 442376 | tf_op jit(solution)/shard_map/ppermute | solution.py:52
  13.9 0.1 copy.18
  14.1 2.5 %collective-permute-start.1 = (bf16[2,192,192]{1,2,0:T(8,128)(2,1)S(1)}, bf16[2,192,192]{1,2,0:T(8,128)(2,1)S(1)}, u32[]{:S(2)}, u32[]{:S(2)}) collective-permute-start(bf16[2,192,192]{1,2,0:T(8,128)(2,1)S(1)} %copy.18), channel_id=1, source_target_pairs={{0,1},{32,3},{64,5},{96,7},{128,9},{160,11},{192,13},{224,15},{256... | collective-permute-start | bytes 442376 | tf_op jit(solution)/shard_map/ppermute | solution.py:52
  16.6 2.9 %collective-permute-done = bf16[2,192,192]{1,2,0:T(8,128)(2,1)S(1)} collective-permute-done((bf16[2,192,192]{1,2,0:T(8,128)(2,1)S(1)}, bf16[2,192,192]{1,2,0:T(8,128)(2,1)S(1)}, u32[]{:S(2)}, u32[]{:S(2)}) %collective-permute-start) | collective-permute-done | bytes 147488 | tf_op jit(solution)/shard_map/ppermute | solution.py:52
  19.5 5.1 %collective-permute-done.1 = bf16[2,192,192]{1,2,0:T(8,128)(2,1)S(1)} collective-permute-done((bf16[2,192,192]{1,2,0:T(8,128)(2,1)S(1)}, bf16[2,192,192]{1,2,0:T(8,128)(2,1)S(1)}, u32[]{:S(2)}, u32[]{:S(2)}) %collective-permute-start.1) | collective-permute-done | bytes 147488 | tf_op jit(solution)/shard_map/ppermute | solution.py:52
  24.6 1.1 fusion.7
  25.8 49.2 %collective-permute-start.2 = (bf16[2,192,384]{2,1,0:T(8,128)(2,1)S(1)}, bf16[2,192,384]{2,1,0:T(8,128)(2,1)S(1)}, u32[]{:S(2)}, u32[]{:S(2)}) collective-permute-start(bf16[2,192,384]{2,1,0:T(8,128)(2,1)S(1)} %fusion.7), channel_id=1, source_target_pairs={{0,16},{16,0},{1,17},{17,1},{2,18},{18,2},{3,19},{19,3},{4,20},{20... | collective-permute-start | bytes 884744 | tf_op jit(solution)/shard_map/ppermute | solution.py:60
  74.9 7.6 %collective-permute-done.2 = bf16[2,192,384]{2,1,0:T(8,128)(2,1)S(1)} collective-permute-done((bf16[2,192,384]{2,1,0:T(8,128)(2,1)S(1)}, bf16[2,192,384]{2,1,0:T(8,128)(2,1)S(1)}, u32[]{:S(2)}, u32[]{:S(2)}) %collective-permute-start.2) | collective-permute-done | bytes 294944 | tf_op jit(solution)/shard_map/ppermute | solution.py:60
  82.6 0.1 select_bitcast_fusion.1
  82.6 0.9 maximum_bitcast_fusion
  83.5 0.0 all-gather.3.cloned.1.call-update
  83.5 1.3 collective-permute-start.3
  84.8 1.3 collective-permute-start.10
  86.1 12.5 %collective-permute-done.3 = bf16[2,192,384]{2,1,0:T(8,128)(2,1)S(1)} collective-permute-done((bf16[2,192,384]{2,1,0:T(8,128)(2,1)S(1)}, bf16[2,192,384]{2,1,0:T(8,128)(2,1)S(1)}, u32[]{:S(2)}, u32[]{:S(2)}) %collective-permute-start.3) | collective-permute-done | bytes 294944 | tf_op jit(solution)/shard_map/ppermute | solution.py:27
  98.6 4.1 %collective-permute-start.4 = (bf16[2,192,384]{2,1,0:T(8,128)(2,1)S(1)}, bf16[2,192,384]{2,1,0:T(8,128)(2,1)S(1)}, u32[]{:S(2)}, u32[]{:S(2)}) collective-permute-start(bf16[2,192,384]{2,1,0:T(8,128)(2,1)S(1)} %collective-permute-done.3), channel_id=1, source_target_pairs={{0,64},{64,128},{128,192},{192,256},{256,320},{320,384},{384,448},... | collective-permute-start | bytes 884744 | tf_op jit(solution)/shard_map/ppermute | solution.py:27
  102.7 0.0 collective-permute-done.10
  102.7 1.3 collective-permute-start.11
  104.0 4.6 %collective-permute-done.4 = bf16[2,192,384]{2,1,0:T(8,128)(2,1)S(1)} collective-permute-done((bf16[2,192,384]{2,1,0:T(8,128)(2,1)S(1)}, bf16[2,192,384]{2,1,0:T(8,128)(2,1)S(1)}, u32[]{:S(2)}, u32[]{:S(2)}) %collective-permute-start.4) | collective-permute-done | bytes 294944 | tf_op jit(solution)/shard_map/ppermute | solution.py:27
  108.6 4.1 %collective-permute-start.5 = (bf16[2,192,384]{2,1,0:T(8,128)(2,1)S(1)}, bf16[2,192,384]{2,1,0:T(8,128)(2,1)S(1)}, u32[]{:S(2)}, u32[]{:S(2)}) collective-permute-start(bf16[2,192,384]{2,1,0:T(8,128)(2,1)S(1)} %collective-permute-done.4), channel_id=1, source_target_pairs={{0,64},{64,128},{128,192},{192,256},{256,320},{320,384},{384,448},... | collective-permute-start | bytes 884744 | tf_op jit(solution)/shard_map/ppermute | solution.py:27
  112.7 0.0 collective-permute-done.11
  112.7 1.3 collective-permute-start.12
  114.0 3.6 %collective-permute-done.5 = bf16[2,192,384]{2,1,0:T(8,128)(2,1)S(1)} collective-permute-done((bf16[2,192,384]{2,1,0:T(8,128)(2,1)S(1)}, bf16[2,192,384]{2,1,0:T(8,128)(2,1)S(1)}, u32[]{:S(2)}, u32[]{:S(2)}) %collective-permute-start.5) | collective-permute-done | bytes 294944 | tf_op jit(solution)/shard_map/ppermute | solution.py:27
  117.7 4.2 %collective-permute-start.6 = (bf16[2,192,384]{2,1,0:T(8,128)(2,1)S(1)}, bf16[2,192,384]{2,1,0:T(8,128)(2,1)S(1)}, u32[]{:S(2)}, u32[]{:S(2)}) collective-permute-start(bf16[2,192,384]{2,1,0:T(8,128)(2,1)S(1)} %collective-permute-done.5), channel_id=1, source_target_pairs={{0,64},{64,128},{128,192},{192,256},{256,320},{320,384},{384,448},... | collective-permute-start | bytes 884744 | tf_op jit(solution)/shard_map/ppermute | solution.py:27
  121.9 0.9 collective-permute-done.12
  122.8 1.3 collective-permute-start.13
  124.1 2.0 collective-permute-done.6
  126.1 4.2 %collective-permute-start.7 = (bf16[2,192,384]{2,1,0:T(8,128)(2,1)S(1)}, bf16[2,192,384]{2,1,0:T(8,128)(2,1)S(1)}, u32[]{:S(2)}, u32[]{:S(2)}) collective-permute-start(bf16[2,192,384]{2,1,0:T(8,128)(2,1)S(1)} %collective-permute-done.6), channel_id=1, source_target_pairs={{0,64},{64,128},{128,192},{192,256},{256,320},{320,384},{384,448},... | collective-permute-start | bytes 884744 | tf_op jit(solution)/shard_map/ppermute | solution.py:27
  130.3 0.6 collective-permute-done.13
  130.9 1.3 collective-permute-start.14
  132.2 1.7 collective-permute-done.7
  133.9 4.8 %collective-permute-start.8 = (bf16[2,192,384]{2,1,0:T(8,128)(2,1)S(1)}, bf16[2,192,384]{2,1,0:T(8,128)(2,1)}, u32[]{:S(2)}, u32[]{:S(2)}) collective-permute-start(bf16[2,192,384]{2,1,0:T(8,128)(2,1)S(1)} %collective-permute-done.7), channel_id=1, source_target_pairs={{0,64},{64,128},{128,192},{192,256},{256,320},{320,384},{384,448},... | collective-permute-start | bytes 884744 | tf_op jit(solution)/shard_map/ppermute | solution.py:27
  138.7 1.0 collective-permute-done.14
  139.8 1.3 collective-permute-start.15
  141.1 0.6 collective-permute-done.8
  141.7 6.4 %collective-permute-start.9 = (bf16[2,192,384]{2,1,0:T(8,128)(2,1)}, bf16[2,192,384]{2,1,0:T(8,128)(2,1)}, u32[]{:S(2)}, u32[]{:S(2)}) collective-permute-start(bf16[2,192,384]{2,1,0:T(8,128)(2,1)} %collective-permute-done.8), channel_id=1, source_target_pairs={{0,64},{64,128},{128,192},{192,256},{256,320},{320,384},{384,448},... | collective-permute-start | bytes 884744 | tf_op jit(solution)/shard_map/ppermute | solution.py:27
  148.0 1.1 collective-permute-done.15
  149.1 1.3 collective-permute-start.16
  150.4 0.9 collective-permute-done.9
  151.3 1.0 bitcast_dynamic-update-slice_fusion.14
  152.3 1.0 bitcast_dynamic-update-slice_fusion.13
  154.0 4.7 %collective-permute-done.16 = bf16[2,192,384]{2,1,0:T(8,128)(2,1)S(1)} collective-permute-done((bf16[2,192,384]{2,1,0:T(8,128)(2,1)S(1)}, bf16[2,192,384]{2,1,0:T(8,128)(2,1)S(1)}, u32[]{:S(2)}, u32[]{:S(2)}) %collective-permute-start.16) | collective-permute-done | bytes 294944 | tf_op jit(solution)/shard_map/ppermute | solution.py:28
  158.7 0.0 copy-start
  158.7 2.1 %copy-done = bf16[15,2,192,384]{3,2,1,0:T(8,128)(2,1)} copy-done((bf16[15,2,192,384]{3,2,1,0:T(8,128)(2,1)}, bf16[15,2,192,384]{3,2,1,0:T(8,128)(2,1)S(1)}, u32[]{:S(2)}) %copy-start) | copy-done | bytes 4423704
  160.9 0.2 constant_dynamic-slice_fusion
  161.1 7.3 %collective-permute-start.17 = (bf16[8,2,192,384]{3,2,1,0:T(8,128)(2,1)S(1)}, bf16[8,2,192,384]{3,2,1,0:T(8,128)(2,1)}, u32[]{:S(2)}, u32[]{:S(2)}) collective-permute-start(bf16[8,2,192,384]{3,2,1,0:T(8,128)(2,1)S(1)} %constant_dynamic-slice_fusion), channel_id=1, source_target_pairs={{0,32},{32,0},{1,33},{33,1},{2,34},{34,2},{3,35},{35,3},{4,36},{36... | collective-permute-start | bytes 7077896 | tf_op jit(solution)/shard_map/ppermute | solution.py:33
  168.5 2.0 fusion.14
  170.5 2.3 %collective-permute-done.17 = bf16[8,2,192,384]{3,2,1,0:T(8,128)(2,1)} collective-permute-done((bf16[8,2,192,384]{3,2,1,0:T(8,128)(2,1)S(1)}, bf16[8,2,192,384]{3,2,1,0:T(8,128)(2,1)}, u32[]{:S(2)}, u32[]{:S(2)}) %collective-permute-start.17) | collective-permute-done | bytes 2359328 | tf_op jit(solution)/shard_map/ppermute | solution.py:33
  172.8 5.7 %maximum_select_fusion = bf16[8,2,2,192,384]{4,3,2,1,0:T(8,128)(2,1)} fusion(bf16[8,1,2,192,384]{4,3,2,1,0:T(8,128)(2,1)} %bitcast.23, bf16[8,1,2,192,384]{4,3,2,1,0:T(8,128)(2,1)S(1)} %fusion.14, pred[]{:T(512)S(6)} %eq.17), kind=kLoop, calls=%fused_computation | loop fusion | flops 7077888 | bytes 9437185 | tf_op jit(solution)/shard_map/jit(_where)/select_n | solution.py:69
  178.5 9.4 %all-gather.3.cloned.1.call-done = bf16[2,3072,2,384]{3,1,2,0:T(8,128)(2,1)} async-done(((bf16[2,192,2,384]{3,1,2,0:T(8,128)(2,1)}), bf16[2,3072,2,384]{3,1,2,0:T(8,128)(2,1)}) %all-gather.3.cloned.1.call-update) | async-done | bytes 9437200 | tf_op jit(solution)/shard_map/all_gather | solution.py:64
  187.9 8.3 %copy.10 = bf16[2,3072,2,384]{3,1,0,2:T(8,128)(2,1)} copy(bf16[2,3072,2,384]{3,1,2,0:T(8,128)(2,1)} %all-gather.3.cloned.1.call-done) | data formatting | bytes 18874368 | tf_op jit(solution)/shard_map/all_gather | solution.py:64
  196.1 9.0 %fusion.3 = f32[2,2,192,384]{3,2,0,1:T(8,128)S(1)} fusion(bf16[16,384,2,384,1]{3,1,0,4,2:T(8,128)(2,1)} %bitcast.79, bf16[16,2,192,384]{3,2,1,0:T(8,128)(2,1)} %bitcast.80), kind=kOutput, calls=%fused_computation.4 | convolution fusion | flops 3623878656 | bytes 15335424 | tf_op jit(solution)/shard_map/jpxc,jcqn->pqxn/dot_general | solution.py:74
  205.2 0.9 pad_maximum_fusion
  (16 shorter events, 0.7 us)
Async XLA Ops:
  6.5 181.3 %all-gather.3.cloned.1.call-start = ((), (), s32[]{:S(2)}) async-start(), calls=%async_computation | async-start | bytes 10027008 | tf_op jit(solution)/shard_map/all_gather | solution.py:64
  7.9 11.7 %collective-permute-start = (bf16[2,192,192]{1,2,0:T(8,128)(2,1)S(1)}, bf16[2,192,192]{1,2,0:T(8,128)(2,1)S(1)}, u32[]{:S(2)}, u32[]{:S(2)}) collective-permute-start(bf16[2,192,192]{1,2,0:T(8,128)(2,1)S(1)} %copy.17), channel_id=1, source_target_pairs={{0,0},{32,2},{64,4},{96,6},{128,8},{160,10},{192,12},{224,14},{256... | collective-permute-start | bytes 442376 | tf_op jit(solution)/shard_map/ppermute | solution.py:52
  14.1 10.5 %collective-permute-start.1 = (bf16[2,192,192]{1,2,0:T(8,128)(2,1)S(1)}, bf16[2,192,192]{1,2,0:T(8,128)(2,1)S(1)}, u32[]{:S(2)}, u32[]{:S(2)}) collective-permute-start(bf16[2,192,192]{1,2,0:T(8,128)(2,1)S(1)} %copy.18), channel_id=1, source_target_pairs={{0,1},{32,3},{64,5},{96,7},{128,9},{160,11},{192,13},{224,15},{256... | collective-permute-start | bytes 442376 | tf_op jit(solution)/shard_map/ppermute | solution.py:52
  25.8 56.8 %collective-permute-start.2 = (bf16[2,192,384]{2,1,0:T(8,128)(2,1)S(1)}, bf16[2,192,384]{2,1,0:T(8,128)(2,1)S(1)}, u32[]{:S(2)}, u32[]{:S(2)}) collective-permute-start(bf16[2,192,384]{2,1,0:T(8,128)(2,1)S(1)} %fusion.7), channel_id=1, source_target_pairs={{0,16},{16,0},{1,17},{17,1},{2,18},{18,2},{3,19},{19,3},{4,20},{20... | collective-permute-start | bytes 884744 | tf_op jit(solution)/shard_map/ppermute | solution.py:60
  83.5 15.1 %collective-permute-start.3 = (bf16[2,192,384]{2,1,0:T(8,128)(2,1)S(1)}, bf16[2,192,384]{2,1,0:T(8,128)(2,1)S(1)}, u32[]{:S(2)}, u32[]{:S(2)}) collective-permute-start(bf16[2,192,384]{2,1,0:T(8,128)(2,1)S(1)} %fusion.7), channel_id=1, source_target_pairs={{0,64},{64,128},{128,192},{192,256},{256,320},{320,384},{384,448},... | collective-permute-start | bytes 884744 | tf_op jit(solution)/shard_map/ppermute | solution.py:27
  84.8 17.9 %collective-permute-start.10 = (bf16[2,192,384]{2,1,0:T(8,128)(2,1)S(1)}, bf16[2,192,384]{2,1,0:T(8,128)(2,1)S(1)}, u32[]{:S(2)}, u32[]{:S(2)}) collective-permute-start(bf16[2,192,384]{2,1,0:T(8,128)(2,1)S(1)} %fusion.7), channel_id=1, source_target_pairs={{64,0},{128,64},{192,128},{256,192},{320,256},{384,320},{448,384},... | collective-permute-start | bytes 884744 | tf_op jit(solution)/shard_map/ppermute | solution.py:28
  98.6 10.0 %collective-permute-start.4 = (bf16[2,192,384]{2,1,0:T(8,128)(2,1)S(1)}, bf16[2,192,384]{2,1,0:T(8,128)(2,1)S(1)}, u32[]{:S(2)}, u32[]{:S(2)}) collective-permute-start(bf16[2,192,384]{2,1,0:T(8,128)(2,1)S(1)} %collective-permute-done.3), channel_id=1, source_target_pairs={{0,64},{64,128},{128,192},{192,256},{256,320},{320,384},{384,448},... | collective-permute-start | bytes 884744 | tf_op jit(solution)/shard_map/ppermute | solution.py:27
  102.7 10.0 %collective-permute-start.11 = (bf16[2,192,384]{2,1,0:T(8,128)(2,1)S(1)}, bf16[2,192,384]{2,1,0:T(8,128)(2,1)S(1)}, u32[]{:S(2)}, u32[]{:S(2)}) collective-permute-start(bf16[2,192,384]{2,1,0:T(8,128)(2,1)S(1)} %collective-permute-done.10), channel_id=1, source_target_pairs={{64,0},{128,64},{192,128},{256,192},{320,256},{384,320},{448,384},... | collective-permute-start | bytes 884744 | tf_op jit(solution)/shard_map/ppermute | solution.py:28
  108.6 9.1 %collective-permute-start.5 = (bf16[2,192,384]{2,1,0:T(8,128)(2,1)S(1)}, bf16[2,192,384]{2,1,0:T(8,128)(2,1)S(1)}, u32[]{:S(2)}, u32[]{:S(2)}) collective-permute-start(bf16[2,192,384]{2,1,0:T(8,128)(2,1)S(1)} %collective-permute-done.4), channel_id=1, source_target_pairs={{0,64},{64,128},{128,192},{192,256},{256,320},{320,384},{384,448},... | collective-permute-start | bytes 884744 | tf_op jit(solution)/shard_map/ppermute | solution.py:27
  112.7 10.0 %collective-permute-start.12 = (bf16[2,192,384]{2,1,0:T(8,128)(2,1)S(1)}, bf16[2,192,384]{2,1,0:T(8,128)(2,1)S(1)}, u32[]{:S(2)}, u32[]{:S(2)}) collective-permute-start(bf16[2,192,384]{2,1,0:T(8,128)(2,1)S(1)} %collective-permute-done.11), channel_id=1, source_target_pairs={{64,0},{128,64},{192,128},{256,192},{320,256},{384,320},{448,384},... | collective-permute-start | bytes 884744 | tf_op jit(solution)/shard_map/ppermute | solution.py:28
  117.7 8.4 %collective-permute-start.6 = (bf16[2,192,384]{2,1,0:T(8,128)(2,1)S(1)}, bf16[2,192,384]{2,1,0:T(8,128)(2,1)S(1)}, u32[]{:S(2)}, u32[]{:S(2)}) collective-permute-start(bf16[2,192,384]{2,1,0:T(8,128)(2,1)S(1)} %collective-permute-done.5), channel_id=1, source_target_pairs={{0,64},{64,128},{128,192},{192,256},{256,320},{320,384},{384,448},... | collective-permute-start | bytes 884744 | tf_op jit(solution)/shard_map/ppermute | solution.py:27
  122.8 8.1 %collective-permute-start.13 = (bf16[2,192,384]{2,1,0:T(8,128)(2,1)S(1)}, bf16[2,192,384]{2,1,0:T(8,128)(2,1)S(1)}, u32[]{:S(2)}, u32[]{:S(2)}) collective-permute-start(bf16[2,192,384]{2,1,0:T(8,128)(2,1)S(1)} %collective-permute-done.12), channel_id=1, source_target_pairs={{64,0},{128,64},{192,128},{256,192},{320,256},{384,320},{448,384},... | collective-permute-start | bytes 884744 | tf_op jit(solution)/shard_map/ppermute | solution.py:28
  126.1 7.9 %collective-permute-start.7 = (bf16[2,192,384]{2,1,0:T(8,128)(2,1)S(1)}, bf16[2,192,384]{2,1,0:T(8,128)(2,1)S(1)}, u32[]{:S(2)}, u32[]{:S(2)}) collective-permute-start(bf16[2,192,384]{2,1,0:T(8,128)(2,1)S(1)} %collective-permute-done.6), channel_id=1, source_target_pairs={{0,64},{64,128},{128,192},{192,256},{256,320},{320,384},{384,448},... | collective-permute-start | bytes 884744 | tf_op jit(solution)/shard_map/ppermute | solution.py:27
  130.9 8.9 %collective-permute-start.14 = (bf16[2,192,384]{2,1,0:T(8,128)(2,1)S(1)}, bf16[2,192,384]{2,1,0:T(8,128)(2,1)S(1)}, u32[]{:S(2)}, u32[]{:S(2)}) collective-permute-start(bf16[2,192,384]{2,1,0:T(8,128)(2,1)S(1)} %collective-permute-done.13), channel_id=1, source_target_pairs={{64,0},{128,64},{192,128},{256,192},{320,256},{384,320},{448,384},... | collective-permute-start | bytes 884744 | tf_op jit(solution)/shard_map/ppermute | solution.py:28
  133.9 7.8 %collective-permute-start.8 = (bf16[2,192,384]{2,1,0:T(8,128)(2,1)S(1)}, bf16[2,192,384]{2,1,0:T(8,128)(2,1)}, u32[]{:S(2)}, u32[]{:S(2)}) collective-permute-start(bf16[2,192,384]{2,1,0:T(8,128)(2,1)S(1)} %collective-permute-done.7), channel_id=1, source_target_pairs={{0,64},{64,128},{128,192},{192,256},{256,320},{320,384},{384,448},... | collective-permute-start | bytes 884744 | tf_op jit(solution)/shard_map/ppermute | solution.py:27
  139.8 9.3 %collective-permute-start.15 = (bf16[2,192,384]{2,1,0:T(8,128)(2,1)S(1)}, bf16[2,192,384]{2,1,0:T(8,128)(2,1)S(1)}, u32[]{:S(2)}, u32[]{:S(2)}) collective-permute-start(bf16[2,192,384]{2,1,0:T(8,128)(2,1)S(1)} %collective-permute-done.14), channel_id=1, source_target_pairs={{64,0},{128,64},{192,128},{256,192},{320,256},{384,320},{448,384},... | collective-permute-start | bytes 884744 | tf_op jit(solution)/shard_map/ppermute | solution.py:28
  141.7 9.6 %collective-permute-start.9 = (bf16[2,192,384]{2,1,0:T(8,128)(2,1)}, bf16[2,192,384]{2,1,0:T(8,128)(2,1)}, u32[]{:S(2)}, u32[]{:S(2)}) collective-permute-start(bf16[2,192,384]{2,1,0:T(8,128)(2,1)} %collective-permute-done.8), channel_id=1, source_target_pairs={{0,64},{64,128},{128,192},{192,256},{256,320},{320,384},{384,448},... | collective-permute-start | bytes 884744 | tf_op jit(solution)/shard_map/ppermute | solution.py:27
  149.1 9.6 %collective-permute-start.16 = (bf16[2,192,384]{2,1,0:T(8,128)(2,1)S(1)}, bf16[2,192,384]{2,1,0:T(8,128)(2,1)S(1)}, u32[]{:S(2)}, u32[]{:S(2)}) collective-permute-start(bf16[2,192,384]{2,1,0:T(8,128)(2,1)S(1)} %collective-permute-done.15), channel_id=1, source_target_pairs={{64,0},{128,64},{192,128},{256,192},{320,256},{384,320},{448,384},... | collective-permute-start | bytes 884744 | tf_op jit(solution)/shard_map/ppermute | solution.py:28
  158.7 2.1 %copy-start = (bf16[15,2,192,384]{3,2,1,0:T(8,128)(2,1)}, bf16[15,2,192,384]{3,2,1,0:T(8,128)(2,1)S(1)}, u32[]{:S(2)}) copy-start(bf16[15,2,192,384]{3,2,1,0:T(8,128)(2,1)S(1)} %bitcast_dynamic-update-slice_fusion) | copy-start | bytes 13271044
  161.1 11.6 %collective-permute-start.17 = (bf16[8,2,192,384]{3,2,1,0:T(8,128)(2,1)S(1)}, bf16[8,2,192,384]{3,2,1,0:T(8,128)(2,1)}, u32[]{:S(2)}, u32[]{:S(2)}) collective-permute-start(bf16[8,2,192,384]{3,2,1,0:T(8,128)(2,1)S(1)} %constant_dynamic-slice_fusion), channel_id=1, source_target_pairs={{0,32},{32,0},{1,33},{33,1},{2,34},{34,2},{3,35},{35,3},{4,36},{36... | collective-permute-start | bytes 7077896 | tf_op jit(solution)/shard_map/ppermute | solution.py:33
Sparse Core Ops, SparseCore 0:
  83.6 104.1 all-gather.2

commit v12 on v9

--- a/solution.py
+++ b/solution.py
@@ -61,7 +61,11 @@
     top = jnp.where(half_index == 0, symmetric, partner_block)
     bottom = jnp.where(half_index == 0, partner_block, symmetric)
     pieces = jnp.swapaxes(jnp.stack([top, bottom]), 1, 2)
-    panels = lax.all_gather(pieces, ("y", "x"), axis=1, tiled=False)
+    n_plane = lax.axis_size("y") * lax.axis_size("x")
+    plane_index = lax.axis_index("y") * lax.axis_size("x") + lax.axis_index("x")
+    slots = jnp.zeros((pieces.shape[0], n_plane) + pieces.shape[1:], pieces.dtype)
+    slots = lax.dynamic_update_slice_in_dim(slots, pieces[:, None], plane_index, 1)
+    panels = lax.psum(slots, ("y", "x"))
     mine, other = gather_line(symmetric)
     core_index = lax.axis_index("core")
     n_line = mine.shape[0]

time: 209 us -> 302 us (1.44)
  waiting for transfers between devices: 59.9 us -> 145 us
  local copies, waits for them, and re-layouts: 17.2 us -> 22.3 us
  starting transfers between devices: 103 us -> 107 us
    psum x0 -> x1, waiting for transfers between devices: none -> 97.5 us  [local(): panels = lax.psum(slots, ('y', 'x'))]
    ppermute x7, waiting for transfers between devices: 25.9 us -> 15.5 us  [gather_line(): lax.ppermute(rightward, 'zl', [(k, k + 1) for k in range(n_line - 1)])]
    all_gather x1 -> x0, waiting for transfers between devices: 7.79 us -> none  [local(): panels = lax.all_gather(pieces, ('y', 'x'), axis=1, tiled=False)]
    ppermute x7, waiting for transfers between devices: 8.3 us -> 14.5 us  [gather_line(): lax.ppermute(leftward, 'zl', [(k + 1, k) for k in range(n_line - 1)])]
    broadcast_in_dim x0 -> x1, local copies, waits for them, and re-layouts: none -> 5.15 us  [local(): jnp.zeros((pieces.shape[0], n_plane) + pieces.shape[1:], pieces.dtype)]
    ppermute x7, starting transfers between devices: 29.2 us -> 33.1 us  [gather_line(): lax.ppermute(rightward, 'zl', [(k, k + 1) for k in range(n_line - 1)])]
  transfers between devices with their start and end apart: 19 -> 19, of which waited for: 17 -> 14; matrix products, arithmetic and copies ran while one was open for 6% -> 4% of each run, Pallas kernels for 0% -> 0%
where the time goes in v12:
time: 302 us; the launch traced here: 301 us
  waiting for transfers between devices  145 us (48%)
  starting transfers between devices  107 us (35%)
  local copies, waits for them, and re-layouts  22.3 us (7%)
  between operations  13.8 us (5%)
  other arithmetic  6.41 us (2%)
  matrix products  5.99 us (2%)
    psum x1, waiting for transfers between devices, local(): panels = lax.psum(slots, ('y', 'x'))  97.5 us
    ppermute x1, starting transfers between devices, local(): partner_block = lax.ppermute(symmetric, 'zh', [(0, 1), (1, 0)])  49.2 us
    ppermute x7, starting transfers between devices, gather_line(): lax.ppermute(rightward, 'zl', [(k, k + 1) for k in range(n_line - 1)])  33.1 us
    ppermute x7, waiting for transfers between devices, gather_line(): lax.ppermute(rightward, 'zl', [(k, k + 1) for k in range(n_line - 1)])  15.5 us
    ppermute x7, waiting for transfers between devices, gather_line(): lax.ppermute(leftward, 'zl', [(k + 1, k) for k in range(n_line - 1)])  14.5 us
    ppermute x7, starting transfers between devices, gather_line(): lax.ppermute(leftward, 'zl', [(k + 1, k) for k in range(n_line - 1)])  9 us
    ppermute x2, starting transfers between devices, local(): lax.ppermute(piece, axes, mirror_pairs(n_recv, n_shot, flip))  8.58 us
    ppermute x2, waiting for transfers between devices, local(): lax.ppermute(piece, axes, mirror_pairs(n_recv, n_shot, flip))  7.99 us
  transfers between devices with their start and end apart: 19, of which 14 were waited for; matrix products, arithmetic and copies ran while one was open for 4% of the time, Pallas kernels for 0%

profile of v12, /device:TPU:1, one launch (start us, length us, event | category | flops | bytes accessed | tf_op | source)
XLA Modules:
  0.0 301.0 jit_solution(3442308512333674745)
XLA Ops:
  6.5 0.0 all-reduce.2.cloned.1.call-start
  6.5 1.2 constant_dynamic-slice_fusion.2
  7.7 0.1 copy.14
  7.9 6.0 %collective-permute-start = (bf16[2,192,192]{1,2,0:T(8,128)(2,1)S(1)}, bf16[2,192,192]{1,2,0:T(8,128)(2,1)S(1)}, u32[]{:S(2)}, u32[]{:S(2)}) collective-permute-start(bf16[2,192,192]{1,2,0:T(8,128)(2,1)S(1)} %copy.14), channel_id=1, source_target_pairs={{0,0},{32,2},{64,4},{96,6},{128,8},{160,10},{192,12},{224,14},{256... | collective-permute-start | bytes 442376 | tf_op jit(solution)/shard_map/ppermute | solution.py:52
  13.9 0.1 copy.15
  14.1 2.5 collective-permute-start.1
  16.6 2.9 collective-permute-done
  19.5 5.1 %collective-permute-done.1 = bf16[2,192,192]{1,2,0:T(8,128)(2,1)S(1)} collective-permute-done((bf16[2,192,192]{1,2,0:T(8,128)(2,1)S(1)}, bf16[2,192,192]{1,2,0:T(8,128)(2,1)S(1)}, u32[]{:S(2)}, u32[]{:S(2)}) %collective-permute-start.1) | collective-permute-done | bytes 147488 | tf_op jit(solution)/shard_map/ppermute | solution.py:52
  24.6 1.1 fusion.4
  25.8 49.2 %collective-permute-start.2 = (bf16[2,192,384]{2,1,0:T(8,128)(2,1)S(1)}, bf16[2,192,384]{2,1,0:T(8,128)(2,1)S(1)}, u32[]{:S(2)}, u32[]{:S(2)}) collective-permute-start(bf16[2,192,384]{2,1,0:T(8,128)(2,1)S(1)} %fusion.4), channel_id=1, source_target_pairs={{0,16},{16,0},{1,17},{17,1},{2,18},{18,2},{3,19},{19,3},{4,20},{20... | collective-permute-start | bytes 884744 | tf_op jit(solution)/shard_map/ppermute | solution.py:60
  74.9 7.5 %collective-permute-done.2 = bf16[2,192,384]{2,1,0:T(8,128)(2,1)S(1)} collective-permute-done((bf16[2,192,384]{2,1,0:T(8,128)(2,1)S(1)}, bf16[2,192,384]{2,1,0:T(8,128)(2,1)S(1)}, u32[]{:S(2)}, u32[]{:S(2)}) %collective-permute-start.2) | collective-permute-done | bytes 294944 | tf_op jit(solution)/shard_map/ppermute | solution.py:60
  82.5 0.1 select_bitcast_fusion.1
  82.5 5.2 %broadcast_in_dim.6 = bf16[2,16,192,2,384]{4,2,1,3,0:T(8,128)(2,1)} broadcast(bf16[]{:T(256)} %constant.46.clone.1), dimensions={} | broadcast | bytes 9437186 | tf_op jit(solution)/shard_map/broadcast_in_dim | solution.py:66
  87.7 0.9 fusion.2
  88.5 0.0 all-reduce.2.cloned.1.call-update
  88.6 1.3 collective-permute-start.3
  89.9 1.3 collective-permute-start.10
  91.2 7.3 %collective-permute-done.3 = bf16[2,192,384]{2,1,0:T(8,128)(2,1)S(1)} collective-permute-done((bf16[2,192,384]{2,1,0:T(8,128)(2,1)S(1)}, bf16[2,192,384]{2,1,0:T(8,128)(2,1)S(1)}, u32[]{:S(2)}, u32[]{:S(2)}) %collective-permute-start.3) | collective-permute-done | bytes 294944 | tf_op jit(solution)/shard_map/ppermute | solution.py:27
  98.5 4.1 %collective-permute-start.4 = (bf16[2,192,384]{2,1,0:T(8,128)(2,1)S(1)}, bf16[2,192,384]{2,1,0:T(8,128)(2,1)S(1)}, u32[]{:S(2)}, u32[]{:S(2)}) collective-permute-start(bf16[2,192,384]{2,1,0:T(8,128)(2,1)S(1)} %collective-permute-done.3), channel_id=1, source_target_pairs={{0,64},{64,128},{128,192},{192,256},{256,320},{320,384},{384,448},... | collective-permute-start | bytes 884744 | tf_op jit(solution)/shard_map/ppermute | solution.py:27
  102.6 0.0 collective-permute-done.10
  102.6 1.3 collective-permute-start.11
  103.9 4.5 %collective-permute-done.4 = bf16[2,192,384]{2,1,0:T(8,128)(2,1)S(1)} collective-permute-done((bf16[2,192,384]{2,1,0:T(8,128)(2,1)S(1)}, bf16[2,192,384]{2,1,0:T(8,128)(2,1)S(1)}, u32[]{:S(2)}, u32[]{:S(2)}) %collective-permute-start.4) | collective-permute-done | bytes 294944 | tf_op jit(solution)/shard_map/ppermute | solution.py:27
  108.4 4.1 %collective-permute-start.5 = (bf16[2,192,384]{2,1,0:T(8,128)(2,1)S(1)}, bf16[2,192,384]{2,1,0:T(8,128)(2,1)S(1)}, u32[]{:S(2)}, u32[]{:S(2)}) collective-permute-start(bf16[2,192,384]{2,1,0:T(8,128)(2,1)S(1)} %collective-permute-done.4), channel_id=1, source_target_pairs={{0,64},{64,128},{128,192},{192,256},{256,320},{320,384},{384,448},... | collective-permute-start | bytes 884744 | tf_op jit(solution)/shard_map/ppermute | solution.py:27
  112.5 0.0 collective-permute-done.11
  112.5 1.3 collective-permute-start.12
  113.8 3.5 %collective-permute-done.5 = bf16[2,192,384]{2,1,0:T(8,128)(2,1)S(1)} collective-permute-done((bf16[2,192,384]{2,1,0:T(8,128)(2,1)S(1)}, bf16[2,192,384]{2,1,0:T(8,128)(2,1)S(1)}, u32[]{:S(2)}, u32[]{:S(2)}) %collective-permute-start.5) | collective-permute-done | bytes 294944 | tf_op jit(solution)/shard_map/ppermute | solution.py:27
  117.4 7.4 %collective-permute-start.6 = (bf16[2,192,384]{2,1,0:T(8,128)(2,1)S(1)}, bf16[2,192,384]{2,1,0:T(8,128)(2,1)S(1)}, u32[]{:S(2)}, u32[]{:S(2)}) collective-permute-start(bf16[2,192,384]{2,1,0:T(8,128)(2,1)S(1)} %collective-permute-done.5), channel_id=1, source_target_pairs={{0,64},{64,128},{128,192},{192,256},{256,320},{320,384},{384,448},... | collective-permute-start | bytes 884744 | tf_op jit(solution)/shard_map/ppermute | solution.py:27
  124.8 3.2 %collective-permute-done.12 = bf16[2,192,384]{2,1,0:T(8,128)(2,1)S(1)} collective-permute-done((bf16[2,192,384]{2,1,0:T(8,128)(2,1)S(1)}, bf16[2,192,384]{2,1,0:T(8,128)(2,1)S(1)}, u32[]{:S(2)}, u32[]{:S(2)}) %collective-permute-start.12) | collective-permute-done | bytes 294944 | tf_op jit(solution)/shard_map/ppermute | solution.py:28
  128.0 1.3 collective-permute-start.13
  129.3 0.0 collective-permute-done.6
  129.3 4.9 %collective-permute-start.7 = (bf16[2,192,384]{2,1,0:T(8,128)(2,1)S(1)}, bf16[2,192,384]{2,1,0:T(8,128)(2,1)S(1)}, u32[]{:S(2)}, u32[]{:S(2)}) collective-permute-start(bf16[2,192,384]{2,1,0:T(8,128)(2,1)S(1)} %collective-permute-done.6), channel_id=1, source_target_pairs={{0,64},{64,128},{128,192},{192,256},{256,320},{320,384},{384,448},... | collective-permute-start | bytes 884744 | tf_op jit(solution)/shard_map/ppermute | solution.py:27
  134.2 2.7 collective-permute-done.13
  136.8 1.3 collective-permute-start.14
  138.1 0.0 collective-permute-done.7
  138.1 5.3 %collective-permute-start.8 = (bf16[2,192,384]{2,1,0:T(8,128)(2,1)S(1)}, bf16[2,192,384]{2,1,0:T(8,128)(2,1)}, u32[]{:S(2)}, u32[]{:S(2)}) collective-permute-start(bf16[2,192,384]{2,1,0:T(8,128)(2,1)S(1)} %collective-permute-done.7), channel_id=1, source_target_pairs={{0,64},{64,128},{128,192},{192,256},{256,320},{320,384},{384,448},... | collective-permute-start | bytes 884744 | tf_op jit(solution)/shard_map/ppermute | solution.py:27
  143.4 1.8 collective-permute-done.14
  145.3 1.3 collective-permute-start.15
  146.6 0.0 collective-permute-done.8
  146.6 5.9 %collective-permute-start.9 = (bf16[2,192,384]{2,1,0:T(8,128)(2,1)}, bf16[2,192,384]{2,1,0:T(8,128)(2,1)}, u32[]{:S(2)}, u32[]{:S(2)}) collective-permute-start(bf16[2,192,384]{2,1,0:T(8,128)(2,1)} %collective-permute-done.8), channel_id=1, source_target_pairs={{0,64},{64,128},{128,192},{192,256},{256,320},{320,384},{384,448},... | collective-permute-start | bytes 884744 | tf_op jit(solution)/shard_map/ppermute | solution.py:27
  152.5 1.8 collective-permute-done.15
  154.4 1.3 collective-permute-start.16
  155.7 0.1 collective-permute-done.9
  155.8 1.0 bitcast_dynamic-update-slice_fusion.14
  156.8 1.0 bitcast_dynamic-update-slice_fusion.13
  158.5 5.0 %collective-permute-done.16 = bf16[2,192,384]{2,1,0:T(8,128)(2,1)S(1)} collective-permute-done((bf16[2,192,384]{2,1,0:T(8,128)(2,1)S(1)}, bf16[2,192,384]{2,1,0:T(8,128)(2,1)S(1)}, u32[]{:S(2)}, u32[]{:S(2)}) %collective-permute-start.16) | collective-permute-done | bytes 294944 | tf_op jit(solution)/shard_map/ppermute | solution.py:28
  163.5 0.0 copy-start
  163.5 2.1 copy-done
  165.6 0.2 constant_dynamic-slice_fusion
  165.8 7.5 %collective-permute-start.17 = (bf16[8,2,192,384]{3,2,1,0:T(8,128)(2,1)S(1)}, bf16[8,2,192,384]{3,2,1,0:T(8,128)(2,1)}, u32[]{:S(2)}, u32[]{:S(2)}) collective-permute-start(bf16[8,2,192,384]{3,2,1,0:T(8,128)(2,1)S(1)} %constant_dynamic-slice_fusion), channel_id=1, source_target_pairs={{0,32},{32,0},{1,33},{33,1},{2,34},{34,2},{3,35},{35,3},{4,36},{36... | collective-permute-start | bytes 7077896 | tf_op jit(solution)/shard_map/ppermute | solution.py:33
  173.3 1.9 fusion.16
  175.3 2.3 collective-permute-done.17
  177.6 3.4 %maximum_select_fusion = bf16[8,2,2,192,384]{4,3,2,0,1:T(8,128)(2,1)S(1)} fusion(bf16[8,1,2,192,384]{4,3,2,0,1:T(8,128)(2,1)} %bitcast.25, bf16[8,1,2,192,384]{4,3,2,0,1:T(8,128)(2,1)S(1)} %fusion.16, pred[]{:T(512)S(6)} %eq.17), kind=kLoop, calls=%fused_computation | loop fusion | flops 7077888 | bytes 9437185 | tf_op jit(solution)/shard_map/jit(_where)/select_n | solution.py:73
  181.0 0.7 fusion.11
  181.7 1.7 copy.6
  183.4 1.7 copy.5
  185.0 97.5 %all-reduce.2.cloned.1.call-done = bf16[2,16,192,2,384]{4,2,1,3,0:T(8,128)(2,1)} async-done(((bf16[2,16,192,2,384]{4,2,1,3,0:T(8,128)(2,1)}), bf16[2,16,192,2,384]{4,2,1,3,0:T(8,128)(2,1)}) %all-reduce.2.cloned.1.call-update) | async-done | bytes 9437200 | tf_op jit(solution)/shard_map/psum | solution.py:68
  282.5 4.7 %fusion.10 = (bf16[1,16,192,2,384]{4,2,1,3,0:T(8,128)(2,1)S(1)}, bf16[1,16,192,2,384]{4,2,1,3,0:T(8,128)(2,1)S(1)}) fusion(bf16[2,16,192,2,384]{4,2,1,3,0:T(8,128)(2,1)} %all-reduce.2.cloned.1.call-done), kind=kLoop, calls=%fused_computation.41 | loop fusion | bytes 18874368 | tf_op jit(solution)/shard_map/slice | solution.py:81
  287.2 0.0 copy-start.1
  287.2 3.9 %convolution_bitcast_fusion = f32[2,384,2,192]{1,3,2,0:T(8,128)S(1)} fusion(bf16[8,384,2,384,1]{3,1,0,4,2:T(8,128)(2,1)S(1)} %bitcast.101, bf16[8,2,192,384,1]{3,2,0,1,4:T(8,128)(2,1)} %bitcast.103), kind=kOutput, calls=%fused_computation.1 | convolution fusion | flops 1811939328 | bytes 8257536 | tf_op jit(solution)/shard_map/jpxc,jcqn->pqxn/dot_general | solution.py:79
  291.1 0.0 copy-done.1
  291.2 2.1 fusion.1
  293.3 0.9 pad_maximum_fusion
  (16 shorter events, 0.7 us)
Async XLA Ops:
  6.5 275.9 %all-reduce.2.cloned.1.call-start = ((), (), s32[]{:S(2)}) async-start(), calls=%async_computation | async-start | bytes 18874368 | tf_op jit(solution)/shard_map/psum | solution.py:68
  7.9 11.7 %collective-permute-start = (bf16[2,192,192]{1,2,0:T(8,128)(2,1)S(1)}, bf16[2,192,192]{1,2,0:T(8,128)(2,1)S(1)}, u32[]{:S(2)}, u32[]{:S(2)}) collective-permute-start(bf16[2,192,192]{1,2,0:T(8,128)(2,1)S(1)} %copy.14), channel_id=1, source_target_pairs={{0,0},{32,2},{64,4},{96,6},{128,8},{160,10},{192,12},{224,14},{256... | collective-permute-start | bytes 442376 | tf_op jit(solution)/shard_map/ppermute | solution.py:52
  14.1 10.5 %collective-permute-start.1 = (bf16[2,192,192]{1,2,0:T(8,128)(2,1)S(1)}, bf16[2,192,192]{1,2,0:T(8,128)(2,1)S(1)}, u32[]{:S(2)}, u32[]{:S(2)}) collective-permute-start(bf16[2,192,192]{1,2,0:T(8,128)(2,1)S(1)} %copy.15), channel_id=1, source_target_pairs={{0,1},{32,3},{64,5},{96,7},{128,9},{160,11},{192,13},{224,15},{256... | collective-permute-start | bytes 442376 | tf_op jit(solution)/shard_map/ppermute | solution.py:52
  25.8 56.7 %collective-permute-start.2 = (bf16[2,192,384]{2,1,0:T(8,128)(2,1)S(1)}, bf16[2,192,384]{2,1,0:T(8,128)(2,1)S(1)}, u32[]{:S(2)}, u32[]{:S(2)}) collective-permute-start(bf16[2,192,384]{2,1,0:T(8,128)(2,1)S(1)} %fusion.4), channel_id=1, source_target_pairs={{0,16},{16,0},{1,17},{17,1},{2,18},{18,2},{3,19},{19,3},{4,20},{20... | collective-permute-start | bytes 884744 | tf_op jit(solution)/shard_map/ppermute | solution.py:60
  88.6 9.9 %collective-permute-start.3 = (bf16[2,192,384]{2,1,0:T(8,128)(2,1)S(1)}, bf16[2,192,384]{2,1,0:T(8,128)(2,1)S(1)}, u32[]{:S(2)}, u32[]{:S(2)}) collective-permute-start(bf16[2,192,384]{2,1,0:T(8,128)(2,1)S(1)} %fusion.4), channel_id=1, source_target_pairs={{0,64},{64,128},{128,192},{192,256},{256,320},{320,384},{384,448},... | collective-permute-start | bytes 884744 | tf_op jit(solution)/shard_map/ppermute | solution.py:27
  89.9 12.7 %collective-permute-start.10 = (bf16[2,192,384]{2,1,0:T(8,128)(2,1)S(1)}, bf16[2,192,384]{2,1,0:T(8,128)(2,1)S(1)}, u32[]{:S(2)}, u32[]{:S(2)}) collective-permute-start(bf16[2,192,384]{2,1,0:T(8,128)(2,1)S(1)} %fusion.4), channel_id=1, source_target_pairs={{64,0},{128,64},{192,128},{256,192},{320,256},{384,320},{448,384},... | collective-permute-start | bytes 884744 | tf_op jit(solution)/shard_map/ppermute | solution.py:28
  98.5 9.9 %collective-permute-start.4 = (bf16[2,192,384]{2,1,0:T(8,128)(2,1)S(1)}, bf16[2,192,384]{2,1,0:T(8,128)(2,1)S(1)}, u32[]{:S(2)}, u32[]{:S(2)}) collective-permute-start(bf16[2,192,384]{2,1,0:T(8,128)(2,1)S(1)} %collective-permute-done.3), channel_id=1, source_target_pairs={{0,64},{64,128},{128,192},{192,256},{256,320},{320,384},{384,448},... | collective-permute-start | bytes 884744 | tf_op jit(solution)/shard_map/ppermute | solution.py:27
  102.6 9.9 %collective-permute-start.11 = (bf16[2,192,384]{2,1,0:T(8,128)(2,1)S(1)}, bf16[2,192,384]{2,1,0:T(8,128)(2,1)S(1)}, u32[]{:S(2)}, u32[]{:S(2)}) collective-permute-start(bf16[2,192,384]{2,1,0:T(8,128)(2,1)S(1)} %collective-permute-done.10), channel_id=1, source_target_pairs={{64,0},{128,64},{192,128},{256,192},{320,256},{384,320},{448,384},... | collective-permute-start | bytes 884744 | tf_op jit(solution)/shard_map/ppermute | solution.py:28
  108.4 9.0 %collective-permute-start.5 = (bf16[2,192,384]{2,1,0:T(8,128)(2,1)S(1)}, bf16[2,192,384]{2,1,0:T(8,128)(2,1)S(1)}, u32[]{:S(2)}, u32[]{:S(2)}) collective-permute-start(bf16[2,192,384]{2,1,0:T(8,128)(2,1)S(1)} %collective-permute-done.4), channel_id=1, source_target_pairs={{0,64},{64,128},{128,192},{192,256},{256,320},{320,384},{384,448},... | collective-permute-start | bytes 884744 | tf_op jit(solution)/shard_map/ppermute | solution.py:27
  112.5 15.5 %collective-permute-start.12 = (bf16[2,192,384]{2,1,0:T(8,128)(2,1)S(1)}, bf16[2,192,384]{2,1,0:T(8,128)(2,1)S(1)}, u32[]{:S(2)}, u32[]{:S(2)}) collective-permute-start(bf16[2,192,384]{2,1,0:T(8,128)(2,1)S(1)} %collective-permute-done.11), channel_id=1, source_target_pairs={{64,0},{128,64},{192,128},{256,192},{320,256},{384,320},{448,384},... | collective-permute-start | bytes 884744 | tf_op jit(solution)/shard_map/ppermute | solution.py:28
  117.4 11.9 %collective-permute-start.6 = (bf16[2,192,384]{2,1,0:T(8,128)(2,1)S(1)}, bf16[2,192,384]{2,1,0:T(8,128)(2,1)S(1)}, u32[]{:S(2)}, u32[]{:S(2)}) collective-permute-start(bf16[2,192,384]{2,1,0:T(8,128)(2,1)S(1)} %collective-permute-done.5), channel_id=1, source_target_pairs={{0,64},{64,128},{128,192},{192,256},{256,320},{320,384},{384,448},... | collective-permute-start | bytes 884744 | tf_op jit(solution)/shard_map/ppermute | solution.py:27
  128.0 8.9 %collective-permute-start.13 = (bf16[2,192,384]{2,1,0:T(8,128)(2,1)S(1)}, bf16[2,192,384]{2,1,0:T(8,128)(2,1)S(1)}, u32[]{:S(2)}, u32[]{:S(2)}) collective-permute-start(bf16[2,192,384]{2,1,0:T(8,128)(2,1)S(1)} %collective-permute-done.12), channel_id=1, source_target_pairs={{64,0},{128,64},{192,128},{256,192},{320,256},{384,320},{448,384},... | collective-permute-start | bytes 884744 | tf_op jit(solution)/shard_map/ppermute | solution.py:28
  129.3 8.9 %collective-permute-start.7 = (bf16[2,192,384]{2,1,0:T(8,128)(2,1)S(1)}, bf16[2,192,384]{2,1,0:T(8,128)(2,1)S(1)}, u32[]{:S(2)}, u32[]{:S(2)}) collective-permute-start(bf16[2,192,384]{2,1,0:T(8,128)(2,1)S(1)} %collective-permute-done.6), channel_id=1, source_target_pairs={{0,64},{64,128},{128,192},{192,256},{256,320},{320,384},{384,448},... | collective-permute-start | bytes 884744 | tf_op jit(solution)/shard_map/ppermute | solution.py:27
  136.8 8.4 %collective-permute-start.14 = (bf16[2,192,384]{2,1,0:T(8,128)(2,1)S(1)}, bf16[2,192,384]{2,1,0:T(8,128)(2,1)S(1)}, u32[]{:S(2)}, u32[]{:S(2)}) collective-permute-start(bf16[2,192,384]{2,1,0:T(8,128)(2,1)S(1)} %collective-permute-done.13), channel_id=1, source_target_pairs={{64,0},{128,64},{192,128},{256,192},{320,256},{384,320},{448,384},... | collective-permute-start | bytes 884744 | tf_op jit(solution)/shard_map/ppermute | solution.py:28
  138.1 8.4 %collective-permute-start.8 = (bf16[2,192,384]{2,1,0:T(8,128)(2,1)S(1)}, bf16[2,192,384]{2,1,0:T(8,128)(2,1)}, u32[]{:S(2)}, u32[]{:S(2)}) collective-permute-start(bf16[2,192,384]{2,1,0:T(8,128)(2,1)S(1)} %collective-permute-done.7), channel_id=1, source_target_pairs={{0,64},{64,128},{128,192},{192,256},{256,320},{320,384},{384,448},... | collective-permute-start | bytes 884744 | tf_op jit(solution)/shard_map/ppermute | solution.py:27
  145.3 9.1 %collective-permute-start.15 = (bf16[2,192,384]{2,1,0:T(8,128)(2,1)S(1)}, bf16[2,192,384]{2,1,0:T(8,128)(2,1)S(1)}, u32[]{:S(2)}, u32[]{:S(2)}) collective-permute-start(bf16[2,192,384]{2,1,0:T(8,128)(2,1)S(1)} %collective-permute-done.14), channel_id=1, source_target_pairs={{64,0},{128,64},{192,128},{256,192},{320,256},{384,320},{448,384},... | collective-permute-start | bytes 884744 | tf_op jit(solution)/shard_map/ppermute | solution.py:28
  146.6 9.2 %collective-permute-start.9 = (bf16[2,192,384]{2,1,0:T(8,128)(2,1)}, bf16[2,192,384]{2,1,0:T(8,128)(2,1)}, u32[]{:S(2)}, u32[]{:S(2)}) collective-permute-start(bf16[2,192,384]{2,1,0:T(8,128)(2,1)} %collective-permute-done.8), channel_id=1, source_target_pairs={{0,64},{64,128},{128,192},{192,256},{256,320},{320,384},{384,448},... | collective-permute-start | bytes 884744 | tf_op jit(solution)/shard_map/ppermute | solution.py:27
  154.4 9.1 %collective-permute-start.16 = (bf16[2,192,384]{2,1,0:T(8,128)(2,1)S(1)}, bf16[2,192,384]{2,1,0:T(8,128)(2,1)S(1)}, u32[]{:S(2)}, u32[]{:S(2)}) collective-permute-start(bf16[2,192,384]{2,1,0:T(8,128)(2,1)S(1)} %collective-permute-done.15), channel_id=1, source_target_pairs={{64,0},{128,64},{192,128},{256,192},{320,256},{384,320},{448,384},... | collective-permute-start | bytes 884744 | tf_op jit(solution)/shard_map/ppermute | solution.py:28
  163.5 2.1 copy-start
  165.8 11.8 %collective-permute-start.17 = (bf16[8,2,192,384]{3,2,1,0:T(8,128)(2,1)S(1)}, bf16[8,2,192,384]{3,2,1,0:T(8,128)(2,1)}, u32[]{:S(2)}, u32[]{:S(2)}) collective-permute-start(bf16[8,2,192,384]{3,2,1,0:T(8,128)(2,1)S(1)} %constant_dynamic-slice_fusion), channel_id=1, source_target_pairs={{0,32},{32,0},{1,33},{33,1},{2,34},{34,2},{3,35},{35,3},{4,36},{36... | collective-permute-start | bytes 7077896 | tf_op jit(solution)/shard_map/ppermute | solution.py:33
  287.2 3.9 %copy-start.1 = (bf16[4,2,2,192,384]{4,3,1,0,2:T(8,128)(2,1)S(1)}, bf16[4,2,2,192,384]{4,3,1,0,2:T(8,128)(2,1)}, u32[]{:S(2)}) copy-start(bf16[4,2,2,192,384]{4,3,1,0,2:T(8,128)(2,1)} %copy.5) | copy-start | bytes 7077892
Sparse Core Ops, SparseCore 0:
  88.7 193.7 all-reduce.1

commit v13 on v9

--- a/solution.py
+++ b/solution.py
@@ -57,10 +57,8 @@
         (pressure.astype(jnp.float32) + jnp.swapaxes(mirror, 1, 2).astype(jnp.float32)) * 0.5
     ).astype(jnp.bfloat16)
 
-    partner_block = lax.ppermute(symmetric, "zh", [(0, 1), (1, 0)])
-    top = jnp.where(half_index == 0, symmetric, partner_block)
-    bottom = jnp.where(half_index == 0, partner_block, symmetric)
-    pieces = jnp.swapaxes(jnp.stack([top, bottom]), 1, 2)
+    stacked = lax.all_to_all(jnp.stack([symmetric, symmetric]), "zh", 0, 0, tiled=True)
+    pieces = jnp.swapaxes(stacked, 1, 2)
     panels = lax.all_gather(pieces, ("y", "x"), axis=1, tiled=False)
     mine, other = gather_line(symmetric)
     core_index = lax.axis_index("core")

time: 209 us -> 214 us (1.024)
  blocking collectives: 0 us -> 60.9 us
  starting transfers between devices: 103 us -> 62.2 us
  waiting for transfers between devices: 59.9 us -> 47.6 us
    all_to_all x0 -> x1, blocking collectives: none -> 60.9 us  [local(): lax.all_to_all(jnp.stack([symmetric, symmetric]), 'zh', 0, 0, tiled=True)]
    ppermute x1 -> x0, starting transfers between devices: 49.2 us -> none  [local(): partner_block = lax.ppermute(symmetric, 'zh', [(0, 1), (1, 0)])]
    ppermute x7, waiting for transfers between devices: 25.9 us -> 10.3 us  [gather_line(): lax.ppermute(rightward, 'zl', [(k, k + 1) for k in range(n_line - 1)])]
    ppermute x1 -> x0, waiting for transfers between devices: 7.63 us -> none  [local(): partner_block = lax.ppermute(symmetric, 'zh', [(0, 1), (1, 0)])]
    ppermute x7, starting transfers between devices: 29.2 us -> 36.2 us  [gather_line(): lax.ppermute(rightward, 'zl', [(k, k + 1) for k in range(n_line - 1)])]
    all_gather x1, waiting for transfers between devices: 7.79 us -> 14.7 us  [local(): panels = lax.all_gather(pieces, ('y', 'x'), axis=1, tiled=False)]
    ppermute x7, waiting for transfers between devices: 8.3 us -> 12.3 us  [gather_line(): lax.ppermute(leftward, 'zl', [(k + 1, k) for k in range(n_line - 1)])]
  transfers between devices with their start and end apart: 19 -> 18, of which waited for: 17 -> 14; matrix products, arithmetic and copies ran while one was open for 6% -> 6% of each run, Pallas kernels for 0% -> 0%
where the time goes in v13:
time: 214 us; the launch traced here: 213 us
  starting transfers between devices  62.2 us (29%)
  blocking collectives  60.9 us (28%)
  waiting for transfers between devices  47.6 us (22%)
  local copies, waits for them, and re-layouts  17.1 us (8%)
  between operations  13.8 us (6%)
  matrix products  5.99 us (3%)
  other arithmetic  5.46 us (3%)
    all_to_all x1, blocking collectives, local(): lax.all_to_all(jnp.stack([symmetric, symmetric]), 'zh', 0, 0, tiled=True)  60.9 us
    ppermute x7, starting transfers between devices, gather_line(): lax.ppermute(rightward, 'zl', [(k, k + 1) for k in range(n_line - 1)])  36.2 us
    all_gather x1, waiting for transfers between devices, local(): panels = lax.all_gather(pieces, ('y', 'x'), axis=1, tiled=False)  14.7 us
    ppermute x7, waiting for transfers between devices, gather_line(): lax.ppermute(leftward, 'zl', [(k + 1, k) for k in range(n_line - 1)])  12.3 us
    ppermute x7, waiting for transfers between devices, gather_line(): lax.ppermute(rightward, 'zl', [(k, k + 1) for k in range(n_line - 1)])  10.3 us
    ppermute x7, starting transfers between devices, gather_line(): lax.ppermute(leftward, 'zl', [(k + 1, k) for k in range(n_line - 1)])  8.99 us
    ppermute x2, starting transfers between devices, local(): lax.ppermute(piece, axes, mirror_pairs(n_recv, n_shot, flip))  8.58 us
    ppermute x1, starting transfers between devices, gather_line(): other = lax.ppermute(mine, 'core', [(0, 1), (1, 0)])  8.47 us
  transfers between devices with their start and end apart: 18, of which 14 were waited for; matrix products, arithmetic and copies ran while one was open for 6% of the time, Pallas kernels for 0%

profile of v13, /device:TPU:1, one launch (start us, length us, event | category | flops | bytes accessed | tf_op | source)
XLA Modules:
  0.0 213.1 jit_solution(3693021554914877411)
XLA Ops:
  6.5 0.0 all-gather.3.cloned.1.call-start
  6.5 1.2 constant_dynamic-slice_fusion.2
  7.7 0.1 copy.13
  7.9 6.0 %collective-permute-start = (bf16[2,192,192]{1,2,0:T(8,128)(2,1)S(1)}, bf16[2,192,192]{1,2,0:T(8,128)(2,1)S(1)}, u32[]{:S(2)}, u32[]{:S(2)}) collective-permute-start(bf16[2,192,192]{1,2,0:T(8,128)(2,1)S(1)} %copy.13), channel_id=1, source_target_pairs={{0,0},{32,2},{64,4},{96,6},{128,8},{160,10},{192,12},{224,14},{256... | collective-permute-start | bytes 442376 | tf_op jit(solution)/shard_map/ppermute | solution.py:52
  13.9 0.1 copy.14
  14.1 2.5 %collective-permute-start.1 = (bf16[2,192,192]{1,2,0:T(8,128)(2,1)S(1)}, bf16[2,192,192]{1,2,0:T(8,128)(2,1)S(1)}, u32[]{:S(2)}, u32[]{:S(2)}) collective-permute-start(bf16[2,192,192]{1,2,0:T(8,128)(2,1)S(1)} %copy.14), channel_id=1, source_target_pairs={{0,1},{32,3},{64,5},{96,7},{128,9},{160,11},{192,13},{224,15},{256... | collective-permute-start | bytes 442376 | tf_op jit(solution)/shard_map/ppermute | solution.py:52
  16.6 2.9 %collective-permute-done = bf16[2,192,192]{1,2,0:T(8,128)(2,1)S(1)} collective-permute-done((bf16[2,192,192]{1,2,0:T(8,128)(2,1)S(1)}, bf16[2,192,192]{1,2,0:T(8,128)(2,1)S(1)}, u32[]{:S(2)}, u32[]{:S(2)}) %collective-permute-start) | collective-permute-done | bytes 147488 | tf_op jit(solution)/shard_map/ppermute | solution.py:52
  19.5 5.1 %collective-permute-done.1 = bf16[2,192,192]{1,2,0:T(8,128)(2,1)S(1)} collective-permute-done((bf16[2,192,192]{1,2,0:T(8,128)(2,1)S(1)}, bf16[2,192,192]{1,2,0:T(8,128)(2,1)S(1)}, u32[]{:S(2)}, u32[]{:S(2)}) %collective-permute-start.1) | collective-permute-done | bytes 147488 | tf_op jit(solution)/shard_map/ppermute | solution.py:52
  24.6 1.1 fusion.3
  25.8 0.1 pad_maximum_fusion
  25.8 60.9 %all_to_all.5 = bf16[2,2,192,384]{3,2,1,0:T(8,128)(2,1)} all-to-all(bf16[2,2,192,384]{3,2,1,0:T(8,128)(2,1)S(1)} %pad_maximum_fusion), channel_id=1, replica_groups=mesh['zl'=8,'core'=2,'zh'=2,'y'=4,'x'=4] {'zh'}, dimensions={0} | all-to-all | bytes 1179648 | tf_op jit(solution)/shard_map/all_to_all | solution.py:60
  86.7 0.0 all-gather.3.cloned.1.call-update
  86.7 1.3 collective-permute-start.2
  88.0 1.3 collective-permute-start.9
  89.3 4.3 %collective-permute-done.2 = bf16[2,192,384]{2,1,0:T(8,128)(2,1)S(1)} collective-permute-done((bf16[2,192,384]{2,1,0:T(8,128)(2,1)S(1)}, bf16[2,192,384]{2,1,0:T(8,128)(2,1)S(1)}, u32[]{:S(2)}, u32[]{:S(2)}) %collective-permute-start.2) | collective-permute-done | bytes 294944 | tf_op jit(solution)/shard_map/ppermute | solution.py:27
  93.6 3.8 %collective-permute-start.3 = (bf16[2,192,384]{2,1,0:T(8,128)(2,1)S(1)}, bf16[2,192,384]{2,1,0:T(8,128)(2,1)S(1)}, u32[]{:S(2)}, u32[]{:S(2)}) collective-permute-start(bf16[2,192,384]{2,1,0:T(8,128)(2,1)S(1)} %collective-permute-done.2), channel_id=1, source_target_pairs={{0,64},{64,128},{128,192},{192,256},{256,320},{320,384},{384,448},... | collective-permute-start | bytes 884744 | tf_op jit(solution)/shard_map/ppermute | solution.py:27
  97.4 0.0 collective-permute-done.9
  97.4 1.3 collective-permute-start.10
  98.7 2.3 %collective-permute-done.3 = bf16[2,192,384]{2,1,0:T(8,128)(2,1)S(1)} collective-permute-done((bf16[2,192,384]{2,1,0:T(8,128)(2,1)S(1)}, bf16[2,192,384]{2,1,0:T(8,128)(2,1)S(1)}, u32[]{:S(2)}, u32[]{:S(2)}) %collective-permute-start.3) | collective-permute-done | bytes 294944 | tf_op jit(solution)/shard_map/ppermute | solution.py:27
  101.1 3.8 %collective-permute-start.4 = (bf16[2,192,384]{2,1,0:T(8,128)(2,1)S(1)}, bf16[2,192,384]{2,1,0:T(8,128)(2,1)S(1)}, u32[]{:S(2)}, u32[]{:S(2)}) collective-permute-start(bf16[2,192,384]{2,1,0:T(8,128)(2,1)S(1)} %collective-permute-done.3), channel_id=1, source_target_pairs={{0,64},{64,128},{128,192},{192,256},{256,320},{320,384},{384,448},... | collective-permute-start | bytes 884744 | tf_op jit(solution)/shard_map/ppermute | solution.py:27
  104.9 0.0 collective-permute-done.10
  104.9 1.3 collective-permute-start.11
  106.2 2.6 %collective-permute-done.4 = bf16[2,192,384]{2,1,0:T(8,128)(2,1)S(1)} collective-permute-done((bf16[2,192,384]{2,1,0:T(8,128)(2,1)S(1)}, bf16[2,192,384]{2,1,0:T(8,128)(2,1)S(1)}, u32[]{:S(2)}, u32[]{:S(2)}) %collective-permute-start.4) | collective-permute-done | bytes 294944 | tf_op jit(solution)/shard_map/ppermute | solution.py:27
  108.8 10.8 %collective-permute-start.5 = (bf16[2,192,384]{2,1,0:T(8,128)(2,1)S(1)}, bf16[2,192,384]{2,1,0:T(8,128)(2,1)S(1)}, u32[]{:S(2)}, u32[]{:S(2)}) collective-permute-start(bf16[2,192,384]{2,1,0:T(8,128)(2,1)S(1)} %collective-permute-done.4), channel_id=1, source_target_pairs={{0,64},{64,128},{128,192},{192,256},{256,320},{320,384},{384,448},... | collective-permute-start | bytes 884744 | tf_op jit(solution)/shard_map/ppermute | solution.py:27
  119.6 3.1 %collective-permute-done.11 = bf16[2,192,384]{2,1,0:T(8,128)(2,1)S(1)} collective-permute-done((bf16[2,192,384]{2,1,0:T(8,128)(2,1)S(1)}, bf16[2,192,384]{2,1,0:T(8,128)(2,1)S(1)}, u32[]{:S(2)}, u32[]{:S(2)}) %collective-permute-start.11) | collective-permute-done | bytes 294944 | tf_op jit(solution)/shard_map/ppermute | solution.py:28
  122.7 1.3 collective-permute-start.12
  124.0 0.0 collective-permute-done.5
  124.0 4.7 %collective-permute-start.6 = (bf16[2,192,384]{2,1,0:T(8,128)(2,1)S(1)}, bf16[2,192,384]{2,1,0:T(8,128)(2,1)S(1)}, u32[]{:S(2)}, u32[]{:S(2)}) collective-permute-start(bf16[2,192,384]{2,1,0:T(8,128)(2,1)S(1)} %collective-permute-done.5), channel_id=1, source_target_pairs={{0,64},{64,128},{128,192},{192,256},{256,320},{320,384},{384,448},... | collective-permute-start | bytes 884744 | tf_op jit(solution)/shard_map/ppermute | solution.py:27
  128.7 2.5 %collective-permute-done.12 = bf16[2,192,384]{2,1,0:T(8,128)(2,1)S(1)} collective-permute-done((bf16[2,192,384]{2,1,0:T(8,128)(2,1)S(1)}, bf16[2,192,384]{2,1,0:T(8,128)(2,1)S(1)}, u32[]{:S(2)}, u32[]{:S(2)}) %collective-permute-start.12) | collective-permute-done | bytes 294944 | tf_op jit(solution)/shard_map/ppermute | solution.py:28
  131.2 1.3 collective-permute-start.13
  132.5 0.0 collective-permute-done.6
  132.5 5.7 %collective-permute-start.7 = (bf16[2,192,384]{2,1,0:T(8,128)(2,1)S(1)}, bf16[2,192,384]{2,1,0:T(8,128)(2,1)}, u32[]{:S(2)}, u32[]{:S(2)}) collective-permute-start(bf16[2,192,384]{2,1,0:T(8,128)(2,1)S(1)} %collective-permute-done.6), channel_id=1, source_target_pairs={{0,64},{64,128},{128,192},{192,256},{256,320},{320,384},{384,448},... | collective-permute-start | bytes 884744 | tf_op jit(solution)/shard_map/ppermute | solution.py:27
  138.2 1.4 collective-permute-done.13
  139.6 1.3 collective-permute-start.14
  140.9 0.3 collective-permute-done.7
  141.2 6.0 %collective-permute-start.8 = (bf16[2,192,384]{2,1,0:T(8,128)(2,1)}, bf16[2,192,384]{2,1,0:T(8,128)(2,1)}, u32[]{:S(2)}, u32[]{:S(2)}) collective-permute-start(bf16[2,192,384]{2,1,0:T(8,128)(2,1)} %collective-permute-done.7), channel_id=1, source_target_pairs={{0,64},{64,128},{128,192},{192,256},{256,320},{320,384},{384,448},... | collective-permute-start | bytes 884744 | tf_op jit(solution)/shard_map/ppermute | solution.py:27
  147.2 1.1 collective-permute-done.14
  148.3 1.3 collective-permute-start.15
  149.6 0.9 collective-permute-done.8
  150.4 1.0 bitcast_dynamic-update-slice_fusion.13
  151.4 1.0 bitcast_dynamic-update-slice_fusion.12
  153.1 4.2 %collective-permute-done.15 = bf16[2,192,384]{2,1,0:T(8,128)(2,1)S(1)} collective-permute-done((bf16[2,192,384]{2,1,0:T(8,128)(2,1)S(1)}, bf16[2,192,384]{2,1,0:T(8,128)(2,1)S(1)}, u32[]{:S(2)}, u32[]{:S(2)}) %collective-permute-start.15) | collective-permute-done | bytes 294944 | tf_op jit(solution)/shard_map/ppermute | solution.py:28
  157.4 0.0 copy-start
  157.4 2.1 %copy-done = bf16[15,2,192,384]{3,2,1,0:T(8,128)(2,1)} copy-done((bf16[15,2,192,384]{3,2,1,0:T(8,128)(2,1)}, bf16[15,2,192,384]{3,2,1,0:T(8,128)(2,1)S(1)}, u32[]{:S(2)}) %copy-start) | copy-done | bytes 4423704
  159.5 0.2 constant_dynamic-slice_fusion
  159.8 8.5 %collective-permute-start.16 = (bf16[8,2,192,384]{3,2,1,0:T(8,128)(2,1)S(1)}, bf16[8,2,192,384]{3,2,1,0:T(8,128)(2,1)}, u32[]{:S(2)}, u32[]{:S(2)}) collective-permute-start(bf16[8,2,192,384]{3,2,1,0:T(8,128)(2,1)S(1)} %constant_dynamic-slice_fusion), channel_id=1, source_target_pairs={{0,32},{32,0},{1,33},{33,1},{2,34},{34,2},{3,35},{35,3},{4,36},{36... | collective-permute-start | bytes 7077896 | tf_op jit(solution)/shard_map/ppermute | solution.py:33
  168.3 1.9 fusion.15
  170.2 2.3 %collective-permute-done.16 = bf16[8,2,192,384]{3,2,1,0:T(8,128)(2,1)} collective-permute-done((bf16[8,2,192,384]{3,2,1,0:T(8,128)(2,1)S(1)}, bf16[8,2,192,384]{3,2,1,0:T(8,128)(2,1)}, u32[]{:S(2)}, u32[]{:S(2)}) %collective-permute-start.16) | collective-permute-done | bytes 2359328 | tf_op jit(solution)/shard_map/ppermute | solution.py:33
  172.5 3.3 %maximum_select_fusion = bf16[8,2,2,192,384]{4,3,2,0,1:T(8,128)(2,1)S(1)} fusion(bf16[8,1,2,192,384]{4,3,2,0,1:T(8,128)(2,1)} %bitcast.21, bf16[8,1,2,192,384]{4,3,2,0,1:T(8,128)(2,1)S(1)} %fusion.15, pred[]{:T(512)S(6)} %eq.12), kind=kLoop, calls=%fused_computation | loop fusion | flops 7077888 | bytes 9437185 | tf_op jit(solution)/shard_map/jit(_where)/select_n | solution.py:67
  175.9 0.7 fusion.10
  176.5 1.6 copy.5
  178.2 1.7 copy.4
  179.9 14.7 %all-gather.3.cloned.1.call-done = bf16[2,3072,2,384]{3,1,2,0:T(8,128)(2,1)} async-done(((bf16[2,192,2,384]{3,1,2,0:T(8,128)(2,1)}), bf16[2,3072,2,384]{3,1,2,0:T(8,128)(2,1)}) %all-gather.3.cloned.1.call-update) | async-done | bytes 9437200 | tf_op jit(solution)/shard_map/all_gather | solution.py:62
  194.6 4.7 %fusion.9 = (bf16[1,3072,2,384]{3,1,2,0:T(8,128)(2,1)S(1)}, bf16[1,3072,2,384]{3,1,2,0:T(8,128)(2,1)S(1)}) fusion(bf16[2,3072,2,384]{3,1,2,0:T(8,128)(2,1)} %all-gather.3.cloned.1.call-done), kind=kLoop, calls=%fused_computation.38 | loop fusion | bytes 18874368 | tf_op jit(solution)/shard_map/slice | solution.py:75
  199.3 0.0 copy-start.1
  199.3 3.9 %convolution_bitcast_fusion = f32[2,384,2,192]{1,3,2,0:T(8,128)S(1)} fusion(bf16[8,384,2,384,1]{3,1,0,4,2:T(8,128)(2,1)S(1)} %bitcast.90, bf16[8,2,192,384,1]{3,2,0,1,4:T(8,128)(2,1)} %bitcast.93), kind=kOutput, calls=%fused_computation.1 | convolution fusion | flops 1811939328 | bytes 8257536 | tf_op jit(solution)/shard_map/jpxc,jcqn->pqxn/dot_general | solution.py:73
  203.2 0.0 copy-done.1
  203.2 2.1 fusion.1
  205.4 0.9 pad_maximum_fusion.1
  (16 shorter events, 0.7 us)
Async XLA Ops:
  6.5 188.0 %all-gather.3.cloned.1.call-start = ((), (), s32[]{:S(2)}) async-start(), calls=%async_computation.1 | async-start | bytes 10027008 | tf_op jit(solution)/shard_map/all_gather | solution.py:62
  7.9 11.7 %collective-permute-start = (bf16[2,192,192]{1,2,0:T(8,128)(2,1)S(1)}, bf16[2,192,192]{1,2,0:T(8,128)(2,1)S(1)}, u32[]{:S(2)}, u32[]{:S(2)}) collective-permute-start(bf16[2,192,192]{1,2,0:T(8,128)(2,1)S(1)} %copy.13), channel_id=1, source_target_pairs={{0,0},{32,2},{64,4},{96,6},{128,8},{160,10},{192,12},{224,14},{256... | collective-permute-start | bytes 442376 | tf_op jit(solution)/shard_map/ppermute | solution.py:52
  14.1 10.5 %collective-permute-start.1 = (bf16[2,192,192]{1,2,0:T(8,128)(2,1)S(1)}, bf16[2,192,192]{1,2,0:T(8,128)(2,1)S(1)}, u32[]{:S(2)}, u32[]{:S(2)}) collective-permute-start(bf16[2,192,192]{1,2,0:T(8,128)(2,1)S(1)} %copy.14), channel_id=1, source_target_pairs={{0,1},{32,3},{64,5},{96,7},{128,9},{160,11},{192,13},{224,15},{256... | collective-permute-start | bytes 442376 | tf_op jit(solution)/shard_map/ppermute | solution.py:52
  86.7 6.9 %collective-permute-start.2 = (bf16[2,192,384]{2,1,0:T(8,128)(2,1)S(1)}, bf16[2,192,384]{2,1,0:T(8,128)(2,1)S(1)}, u32[]{:S(2)}, u32[]{:S(2)}) collective-permute-start(bf16[2,192,384]{2,1,0:T(8,128)(2,1)S(1)} %fusion.3), channel_id=1, source_target_pairs={{0,64},{64,128},{128,192},{192,256},{256,320},{320,384},{384,448},... | collective-permute-start | bytes 884744 | tf_op jit(solution)/shard_map/ppermute | solution.py:27
  88.0 9.4 %collective-permute-start.9 = (bf16[2,192,384]{2,1,0:T(8,128)(2,1)S(1)}, bf16[2,192,384]{2,1,0:T(8,128)(2,1)S(1)}, u32[]{:S(2)}, u32[]{:S(2)}) collective-permute-start(bf16[2,192,384]{2,1,0:T(8,128)(2,1)S(1)} %fusion.3), channel_id=1, source_target_pairs={{64,0},{128,64},{192,128},{256,192},{320,256},{384,320},{448,384},... | collective-permute-start | bytes 884744 | tf_op jit(solution)/shard_map/ppermute | solution.py:28
  93.6 7.5 %collective-permute-start.3 = (bf16[2,192,384]{2,1,0:T(8,128)(2,1)S(1)}, bf16[2,192,384]{2,1,0:T(8,128)(2,1)S(1)}, u32[]{:S(2)}, u32[]{:S(2)}) collective-permute-start(bf16[2,192,384]{2,1,0:T(8,128)(2,1)S(1)} %collective-permute-done.2), channel_id=1, source_target_pairs={{0,64},{64,128},{128,192},{192,256},{256,320},{320,384},{384,448},... | collective-permute-start | bytes 884744 | tf_op jit(solution)/shard_map/ppermute | solution.py:27
  97.4 7.5 %collective-permute-start.10 = (bf16[2,192,384]{2,1,0:T(8,128)(2,1)S(1)}, bf16[2,192,384]{2,1,0:T(8,128)(2,1)S(1)}, u32[]{:S(2)}, u32[]{:S(2)}) collective-permute-start(bf16[2,192,384]{2,1,0:T(8,128)(2,1)S(1)} %collective-permute-done.9), channel_id=1, source_target_pairs={{64,0},{128,64},{192,128},{256,192},{320,256},{384,320},{448,384},... | collective-permute-start | bytes 884744 | tf_op jit(solution)/shard_map/ppermute | solution.py:28
  101.1 7.7 %collective-permute-start.4 = (bf16[2,192,384]{2,1,0:T(8,128)(2,1)S(1)}, bf16[2,192,384]{2,1,0:T(8,128)(2,1)S(1)}, u32[]{:S(2)}, u32[]{:S(2)}) collective-permute-start(bf16[2,192,384]{2,1,0:T(8,128)(2,1)S(1)} %collective-permute-done.3), channel_id=1, source_target_pairs={{0,64},{64,128},{128,192},{192,256},{256,320},{320,384},{384,448},... | collective-permute-start | bytes 884744 | tf_op jit(solution)/shard_map/ppermute | solution.py:27
  104.9 17.8 %collective-permute-start.11 = (bf16[2,192,384]{2,1,0:T(8,128)(2,1)S(1)}, bf16[2,192,384]{2,1,0:T(8,128)(2,1)S(1)}, u32[]{:S(2)}, u32[]{:S(2)}) collective-permute-start(bf16[2,192,384]{2,1,0:T(8,128)(2,1)S(1)} %collective-permute-done.10), channel_id=1, source_target_pairs={{64,0},{128,64},{192,128},{256,192},{320,256},{384,320},{448,384},... | collective-permute-start | bytes 884744 | tf_op jit(solution)/shard_map/ppermute | solution.py:28
  108.8 15.2 %collective-permute-start.5 = (bf16[2,192,384]{2,1,0:T(8,128)(2,1)S(1)}, bf16[2,192,384]{2,1,0:T(8,128)(2,1)S(1)}, u32[]{:S(2)}, u32[]{:S(2)}) collective-permute-start(bf16[2,192,384]{2,1,0:T(8,128)(2,1)S(1)} %collective-permute-done.4), channel_id=1, source_target_pairs={{0,64},{64,128},{128,192},{192,256},{256,320},{320,384},{384,448},... | collective-permute-start | bytes 884744 | tf_op jit(solution)/shard_map/ppermute | solution.py:27
  122.7 8.5 %collective-permute-start.12 = (bf16[2,192,384]{2,1,0:T(8,128)(2,1)S(1)}, bf16[2,192,384]{2,1,0:T(8,128)(2,1)S(1)}, u32[]{:S(2)}, u32[]{:S(2)}) collective-permute-start(bf16[2,192,384]{2,1,0:T(8,128)(2,1)S(1)} %collective-permute-done.11), channel_id=1, source_target_pairs={{64,0},{128,64},{192,128},{256,192},{320,256},{384,320},{448,384},... | collective-permute-start | bytes 884744 | tf_op jit(solution)/shard_map/ppermute | solution.py:28
  124.0 8.5 %collective-permute-start.6 = (bf16[2,192,384]{2,1,0:T(8,128)(2,1)S(1)}, bf16[2,192,384]{2,1,0:T(8,128)(2,1)S(1)}, u32[]{:S(2)}, u32[]{:S(2)}) collective-permute-start(bf16[2,192,384]{2,1,0:T(8,128)(2,1)S(1)} %collective-permute-done.5), channel_id=1, source_target_pairs={{0,64},{64,128},{128,192},{192,256},{256,320},{320,384},{384,448},... | collective-permute-start | bytes 884744 | tf_op jit(solution)/shard_map/ppermute | solution.py:27
  131.2 8.4 %collective-permute-start.13 = (bf16[2,192,384]{2,1,0:T(8,128)(2,1)S(1)}, bf16[2,192,384]{2,1,0:T(8,128)(2,1)S(1)}, u32[]{:S(2)}, u32[]{:S(2)}) collective-permute-start(bf16[2,192,384]{2,1,0:T(8,128)(2,1)S(1)} %collective-permute-done.12), channel_id=1, source_target_pairs={{64,0},{128,64},{192,128},{256,192},{320,256},{384,320},{448,384},... | collective-permute-start | bytes 884744 | tf_op jit(solution)/shard_map/ppermute | solution.py:28
  132.5 8.7 %collective-permute-start.7 = (bf16[2,192,384]{2,1,0:T(8,128)(2,1)S(1)}, bf16[2,192,384]{2,1,0:T(8,128)(2,1)}, u32[]{:S(2)}, u32[]{:S(2)}) collective-permute-start(bf16[2,192,384]{2,1,0:T(8,128)(2,1)S(1)} %collective-permute-done.6), channel_id=1, source_target_pairs={{0,64},{64,128},{128,192},{192,256},{256,320},{320,384},{384,448},... | collective-permute-start | bytes 884744 | tf_op jit(solution)/shard_map/ppermute | solution.py:27
  139.6 8.7 %collective-permute-start.14 = (bf16[2,192,384]{2,1,0:T(8,128)(2,1)S(1)}, bf16[2,192,384]{2,1,0:T(8,128)(2,1)S(1)}, u32[]{:S(2)}, u32[]{:S(2)}) collective-permute-start(bf16[2,192,384]{2,1,0:T(8,128)(2,1)S(1)} %collective-permute-done.13), channel_id=1, source_target_pairs={{64,0},{128,64},{192,128},{256,192},{320,256},{384,320},{448,384},... | collective-permute-start | bytes 884744 | tf_op jit(solution)/shard_map/ppermute | solution.py:28
  141.2 9.3 %collective-permute-start.8 = (bf16[2,192,384]{2,1,0:T(8,128)(2,1)}, bf16[2,192,384]{2,1,0:T(8,128)(2,1)}, u32[]{:S(2)}, u32[]{:S(2)}) collective-permute-start(bf16[2,192,384]{2,1,0:T(8,128)(2,1)} %collective-permute-done.7), channel_id=1, source_target_pairs={{0,64},{64,128},{128,192},{192,256},{256,320},{320,384},{384,448},... | collective-permute-start | bytes 884744 | tf_op jit(solution)/shard_map/ppermute | solution.py:27
  148.3 9.1 %collective-permute-start.15 = (bf16[2,192,384]{2,1,0:T(8,128)(2,1)S(1)}, bf16[2,192,384]{2,1,0:T(8,128)(2,1)S(1)}, u32[]{:S(2)}, u32[]{:S(2)}) collective-permute-start(bf16[2,192,384]{2,1,0:T(8,128)(2,1)S(1)} %collective-permute-done.14), channel_id=1, source_target_pairs={{64,0},{128,64},{192,128},{256,192},{320,256},{384,320},{448,384},... | collective-permute-start | bytes 884744 | tf_op jit(solution)/shard_map/ppermute | solution.py:28
  157.4 2.1 %copy-start = (bf16[15,2,192,384]{3,2,1,0:T(8,128)(2,1)}, bf16[15,2,192,384]{3,2,1,0:T(8,128)(2,1)S(1)}, u32[]{:S(2)}) copy-start(bf16[15,2,192,384]{3,2,1,0:T(8,128)(2,1)S(1)} %bitcast_dynamic-update-slice_fusion) | copy-start | bytes 13271044
  159.8 12.7 %collective-permute-start.16 = (bf16[8,2,192,384]{3,2,1,0:T(8,128)(2,1)S(1)}, bf16[8,2,192,384]{3,2,1,0:T(8,128)(2,1)}, u32[]{:S(2)}, u32[]{:S(2)}) collective-permute-start(bf16[8,2,192,384]{3,2,1,0:T(8,128)(2,1)S(1)} %constant_dynamic-slice_fusion), channel_id=1, source_target_pairs={{0,32},{32,0},{1,33},{33,1},{2,34},{34,2},{3,35},{35,3},{4,36},{36... | collective-permute-start | bytes 7077896 | tf_op jit(solution)/shard_map/ppermute | solution.py:33
  199.3 3.9 %copy-start.1 = (bf16[4,2,2,192,384]{4,3,1,0,2:T(8,128)(2,1)S(1)}, bf16[4,2,2,192,384]{4,3,1,0,2:T(8,128)(2,1)}, u32[]{:S(2)}) copy-start(bf16[4,2,2,192,384]{4,3,1,0,2:T(8,128)(2,1)} %copy.4) | copy-start | bytes 7077892
Sparse Core Ops, SparseCore 0:
  86.8 107.6 all-gather.2

commit v14 on v11

--- a/solution.py
+++ b/solution.py
@@ -1,3 +1,4 @@
+import functools
 import math
 
 import jax
@@ -5,6 +6,8 @@
 from jax import lax
 from jax.sharding import Mesh
 from jax.sharding import PartitionSpec as P
+from jax.experimental import pallas as pl
+from jax.experimental.pallas import tpu as pltpu
 
 N = 6144
 
@@ -34,6 +37,37 @@
     return mine, other
 
 
+def product_kernel(left_ref, panel_ref, out_ref, *, n_block, width, factor):
+    acc = [[None, None], [None, None]]
+    for half in range(2):
+        for block in range(n_block):
+            for p in range(2):
+                lhs = left_ref[half * n_block + block, p, :, :]
+                for q in range(2):
+                    rhs = panel_ref[half, q, pl.ds(block * width, width), :]
+                    term = jnp.dot(lhs, rhs, preferred_element_type=jnp.float32)
+                    acc[p][q] = term if acc[p][q] is None else acc[p][q] + term
+    out_ref[0, :, :] = (acc[0][0] - acc[1][1]) * factor
+    out_ref[1, :, :] = (acc[0][1] + acc[1][0]) * factor
+
+
+def product(left, panels, factor):
+    n_blocks, parts, rows, width = left.shape
+    cols = panels.shape[-1]
+    kernel = functools.partial(product_kernel, n_block=n_blocks // 2, width=width, factor=factor)
+    return pl.pallas_call(
+        kernel,
+        out_shape=jax.ShapeDtypeStruct((2, rows, cols), jnp.float32),
+        in_specs=[pl.BlockSpec(memory_space=pltpu.VMEM)] * 2,
+        out_specs=pl.BlockSpec(memory_space=pltpu.VMEM),
+        cost_estimate=pl.CostEstimate(
+            flops=2 * 4 * rows * cols * width * n_blocks,
+            transcendentals=0,
+            bytes_accessed=2 * (left.size + panels.size) + 4 * 2 * rows * cols,
+        ),
+    )(left, panels)
+
+
 def local(pressure):
     n_shot = lax.axis_size("zl") * lax.axis_size("core")
     n_half = lax.axis_size("y") * lax.axis_size("x")
@@ -60,22 +94,14 @@
     partner_block = lax.ppermute(symmetric, "zh", [(0, 1), (1, 0)])
     top = jnp.where(half_index == 0, symmetric, partner_block)
     bottom = jnp.where(half_index == 0, partner_block, symmetric)
-    pieces = jnp.swapaxes(jnp.stack([top, bottom]), 1, 2)
-    panels = lax.all_gather(pieces, ("y", "x"), axis=1, tiled=False)
+    panels = lax.all_gather(jnp.stack([top, bottom]), ("y", "x"), axis=2, tiled=True)
     mine, other = gather_line(symmetric)
     core_index = lax.axis_index("core")
     n_line = mine.shape[0]
-    parts, rows, cols = symmetric.shape
     natural = jnp.where(
         core_index == 0, jnp.stack([mine, other], axis=1), jnp.stack([other, mine], axis=1)
     ).reshape((2 * n_line,) + symmetric.shape)
-
-    panel = panels.reshape(2 * n_line, 2 * rows, parts, cols)
-    terms = jnp.einsum("jpxc,jcqn->pqxn", natural, panel, preferred_element_type=jnp.float32)
-    factor = 1.0 / math.sqrt(N)
-    real = (terms[0, 0] - terms[1, 1]) * factor
-    imag = (terms[0, 1] + terms[1, 0]) * factor
-    return jnp.stack([real, imag])
+    return product(natural, panels, 1.0 / math.sqrt(N))
 
 
 def solution(mesh):

time: 214 us -> 208 us (0.972)
  Pallas kernels: 0 us -> 12 us
  matrix products: 9 us -> 0 us
  local copies, waits for them, and re-layouts: 16.7 us -> 11.2 us
  other arithmetic: 8.74 us -> 5.41 us
    pallas_call x0 -> x1, Pallas kernels: none -> 12 us  [product(): pl.pallas_call(kernel, out_shape=jax.ShapeDtypeStruct((2, rows, cols), jn...]
    dot_general x1 -> x0, matrix products: 9 us -> none  [local(): jnp.einsum('jpxc,jcqn->pqxn', natural, panel, preferred_element_type=jnp....]
    all_gather x1 -> x0, local copies, waits for them, and re-layouts: 8.26 us -> none  [local(): panels = lax.all_gather(pieces, ('y', 'x'), axis=1, tiled=False)]
    select_n x0 -> x1, local copies, waits for them, and re-layouts: none -> 2.75 us  [local(): jnp.where(core_index == 0, jnp.stack([mine, other], axis=1), jnp.stack([o...]
    select_n x1, other arithmetic: 5.72 us -> 3.32 us  [local(): jnp.where(core_index == 0, jnp.stack([mine, other], axis=1), jnp.stack([o...]
where the time goes in v14:
time: 208 us; the launch traced here: 207 us
  starting transfers between devices  103 us (50%)
  waiting for transfers between devices  61.1 us (29%)
  between operations  13.7 us (7%)
  Pallas kernels  12 us (6%)
  local copies, waits for them, and re-layouts  11.2 us (5%)
  other arithmetic  5.41 us (3%)
    ppermute x1, starting transfers between devices, local(): partner_block = lax.ppermute(symmetric, 'zh', [(0, 1), (1, 0)])  49.2 us
    ppermute x7, starting transfers between devices, gather_line(): lax.ppermute(rightward, 'zl', [(k, k + 1) for k in range(n_line - 1)])  29.2 us
    ppermute x7, waiting for transfers between devices, gather_line(): lax.ppermute(rightward, 'zl', [(k, k + 1) for k in range(n_line - 1)])  25.9 us
    pallas_call x1, Pallas kernels, product(): pl.pallas_call(kernel, out_shape=jax.ShapeDtypeStruct((2, rows, cols), jn...  12 us
    all_gather x1, waiting for transfers between devices, local(): lax.all_gather(jnp.stack([top, bottom]), ('y', 'x'), axis=2, tiled=True)  9.05 us
    ppermute x7, starting transfers between devices, gather_line(): lax.ppermute(leftward, 'zl', [(k + 1, k) for k in range(n_line - 1)])  9 us
    ppermute x2, starting transfers between devices, local(): lax.ppermute(piece, axes, mirror_pairs(n_recv, n_shot, flip))  8.58 us
    ppermute x7, waiting for transfers between devices, gather_line(): lax.ppermute(leftward, 'zl', [(k + 1, k) for k in range(n_line - 1)])  8.31 us
  transfers between devices with their start and end apart: 19, of which 17 were waited for; matrix products, arithmetic and copies ran while one was open for 5% of the time, Pallas kernels for 0%

profile of v14, /device:TPU:1, one launch (start us, length us, event | category | flops | bytes accessed | tf_op | source)
XLA Modules:
  0.0 206.7 jit_solution(14260146271825020944)
XLA Ops:
  6.5 0.0 all-gather.2.cloned.1.call-start
  6.5 1.2 constant_dynamic-slice_fusion.2
  7.7 0.1 copy.7
  7.9 6.0 %collective-permute-start = (bf16[2,192,192]{1,2,0:T(8,128)(2,1)S(1)}, bf16[2,192,192]{1,2,0:T(8,128)(2,1)S(1)}, u32[]{:S(2)}, u32[]{:S(2)}) collective-permute-start(bf16[2,192,192]{1,2,0:T(8,128)(2,1)S(1)} %copy.7), channel_id=1, source_target_pairs={{0,0},{32,2},{64,4},{96,6},{128,8},{160,10},{192,12},{224,14},{256... | collective-permute-start | bytes 442376 | tf_op jit(solution)/shard_map/ppermute | solution.py:86
  13.9 0.1 copy.8
  14.1 2.5 %collective-permute-start.1 = (bf16[2,192,192]{1,2,0:T(8,128)(2,1)S(1)}, bf16[2,192,192]{1,2,0:T(8,128)(2,1)S(1)}, u32[]{:S(2)}, u32[]{:S(2)}) collective-permute-start(bf16[2,192,192]{1,2,0:T(8,128)(2,1)S(1)} %copy.8), channel_id=1, source_target_pairs={{0,1},{32,3},{64,5},{96,7},{128,9},{160,11},{192,13},{224,15},{256... | collective-permute-start | bytes 442376 | tf_op jit(solution)/shard_map/ppermute | solution.py:86
  16.6 2.9 %collective-permute-done = bf16[2,192,192]{1,2,0:T(8,128)(2,1)S(1)} collective-permute-done((bf16[2,192,192]{1,2,0:T(8,128)(2,1)S(1)}, bf16[2,192,192]{1,2,0:T(8,128)(2,1)S(1)}, u32[]{:S(2)}, u32[]{:S(2)}) %collective-permute-start) | collective-permute-done | bytes 147488 | tf_op jit(solution)/shard_map/ppermute | solution.py:86
  19.5 5.1 %collective-permute-done.1 = bf16[2,192,192]{1,2,0:T(8,128)(2,1)S(1)} collective-permute-done((bf16[2,192,192]{1,2,0:T(8,128)(2,1)S(1)}, bf16[2,192,192]{1,2,0:T(8,128)(2,1)S(1)}, u32[]{:S(2)}, u32[]{:S(2)}) %collective-permute-start.1) | collective-permute-done | bytes 147488 | tf_op jit(solution)/shard_map/ppermute | solution.py:86
  24.6 1.1 fusion.1
  25.8 49.2 %collective-permute-start.17 = (bf16[2,192,384]{2,1,0:T(8,128)(2,1)S(1)}, bf16[2,192,384]{2,1,0:T(8,128)(2,1)S(1)}, u32[]{:S(2)}, u32[]{:S(2)}) collective-permute-start(bf16[2,192,384]{2,1,0:T(8,128)(2,1)S(1)} %fusion.1), channel_id=1, source_target_pairs={{0,16},{16,0},{1,17},{17,1},{2,18},{18,2},{3,19},{19,3},{4,20},{20... | collective-permute-start | bytes 884744 | tf_op jit(solution)/shard_map/ppermute | solution.py:94
  74.9 7.6 %collective-permute-done.17 = bf16[2,192,384]{2,1,0:T(8,128)(2,1)S(1)} collective-permute-done((bf16[2,192,384]{2,1,0:T(8,128)(2,1)S(1)}, bf16[2,192,384]{2,1,0:T(8,128)(2,1)S(1)}, u32[]{:S(2)}, u32[]{:S(2)}) %collective-permute-start.17) | collective-permute-done | bytes 294944 | tf_op jit(solution)/shard_map/ppermute | solution.py:94
  82.6 0.1 select_bitcast_fusion.1
  82.6 0.9 pad_maximum_fusion
  83.5 0.0 all-gather.2.cloned.1.call-update
  83.5 1.3 collective-permute-start.2
  84.8 1.3 collective-permute-start.9
  86.1 12.5 %collective-permute-done.2 = bf16[2,192,384]{2,1,0:T(8,128)(2,1)S(1)} collective-permute-done((bf16[2,192,384]{2,1,0:T(8,128)(2,1)S(1)}, bf16[2,192,384]{2,1,0:T(8,128)(2,1)S(1)}, u32[]{:S(2)}, u32[]{:S(2)}) %collective-permute-start.2) | collective-permute-done | bytes 294944 | tf_op jit(solution)/shard_map/ppermute | solution.py:30
  98.6 4.1 %collective-permute-start.3 = (bf16[2,192,384]{2,1,0:T(8,128)(2,1)S(1)}, bf16[2,192,384]{2,1,0:T(8,128)(2,1)S(1)}, u32[]{:S(2)}, u32[]{:S(2)}) collective-permute-start(bf16[2,192,384]{2,1,0:T(8,128)(2,1)S(1)} %collective-permute-done.2), channel_id=1, source_target_pairs={{0,64},{64,128},{128,192},{192,256},{256,320},{320,384},{384,448},... | collective-permute-start | bytes 884744 | tf_op jit(solution)/shard_map/ppermute | solution.py:30
  102.7 0.0 collective-permute-done.9
  102.7 1.3 collective-permute-start.10
  104.0 4.6 %collective-permute-done.3 = bf16[2,192,384]{2,1,0:T(8,128)(2,1)S(1)} collective-permute-done((bf16[2,192,384]{2,1,0:T(8,128)(2,1)S(1)}, bf16[2,192,384]{2,1,0:T(8,128)(2,1)S(1)}, u32[]{:S(2)}, u32[]{:S(2)}) %collective-permute-start.3) | collective-permute-done | bytes 294944 | tf_op jit(solution)/shard_map/ppermute | solution.py:30
  108.6 4.1 %collective-permute-start.4 = (bf16[2,192,384]{2,1,0:T(8,128)(2,1)S(1)}, bf16[2,192,384]{2,1,0:T(8,128)(2,1)S(1)}, u32[]{:S(2)}, u32[]{:S(2)}) collective-permute-start(bf16[2,192,384]{2,1,0:T(8,128)(2,1)S(1)} %collective-permute-done.3), channel_id=1, source_target_pairs={{0,64},{64,128},{128,192},{192,256},{256,320},{320,384},{384,448},... | collective-permute-start | bytes 884744 | tf_op jit(solution)/shard_map/ppermute | solution.py:30
  112.7 0.0 collective-permute-done.10
  112.7 1.3 collective-permute-start.11
  114.0 3.6 %collective-permute-done.4 = bf16[2,192,384]{2,1,0:T(8,128)(2,1)S(1)} collective-permute-done((bf16[2,192,384]{2,1,0:T(8,128)(2,1)S(1)}, bf16[2,192,384]{2,1,0:T(8,128)(2,1)S(1)}, u32[]{:S(2)}, u32[]{:S(2)}) %collective-permute-start.4) | collective-permute-done | bytes 294944 | tf_op jit(solution)/shard_map/ppermute | solution.py:30
  117.7 4.2 %collective-permute-start.5 = (bf16[2,192,384]{2,1,0:T(8,128)(2,1)S(1)}, bf16[2,192,384]{2,1,0:T(8,128)(2,1)S(1)}, u32[]{:S(2)}, u32[]{:S(2)}) collective-permute-start(bf16[2,192,384]{2,1,0:T(8,128)(2,1)S(1)} %collective-permute-done.4), channel_id=1, source_target_pairs={{0,64},{64,128},{128,192},{192,256},{256,320},{320,384},{384,448},... | collective-permute-start | bytes 884744 | tf_op jit(solution)/shard_map/ppermute | solution.py:30
  121.9 0.9 collective-permute-done.11
  122.8 1.3 collective-permute-start.12
  124.1 2.0 collective-permute-done.5
  126.1 4.2 %collective-permute-start.6 = (bf16[2,192,384]{2,1,0:T(8,128)(2,1)S(1)}, bf16[2,192,384]{2,1,0:T(8,128)(2,1)S(1)}, u32[]{:S(2)}, u32[]{:S(2)}) collective-permute-start(bf16[2,192,384]{2,1,0:T(8,128)(2,1)S(1)} %collective-permute-done.5), channel_id=1, source_target_pairs={{0,64},{64,128},{128,192},{192,256},{256,320},{320,384},{384,448},... | collective-permute-start | bytes 884744 | tf_op jit(solution)/shard_map/ppermute | solution.py:30
  130.3 0.6 collective-permute-done.12
  130.9 1.3 collective-permute-start.13
  132.2 1.7 collective-permute-done.6
  133.9 4.8 %collective-permute-start.7 = (bf16[2,192,384]{2,1,0:T(8,128)(2,1)S(1)}, bf16[2,192,384]{2,1,0:T(8,128)(2,1)}, u32[]{:S(2)}, u32[]{:S(2)}) collective-permute-start(bf16[2,192,384]{2,1,0:T(8,128)(2,1)S(1)} %collective-permute-done.6), channel_id=1, source_target_pairs={{0,64},{64,128},{128,192},{192,256},{256,320},{320,384},{384,448},... | collective-permute-start | bytes 884744 | tf_op jit(solution)/shard_map/ppermute | solution.py:30
  138.7 1.0 collective-permute-done.13
  139.8 1.3 collective-permute-start.14
  141.1 0.6 collective-permute-done.7
  141.7 6.4 %collective-permute-start.8 = (bf16[2,192,384]{2,1,0:T(8,128)(2,1)}, bf16[2,192,384]{2,1,0:T(8,128)(2,1)}, u32[]{:S(2)}, u32[]{:S(2)}) collective-permute-start(bf16[2,192,384]{2,1,0:T(8,128)(2,1)} %collective-permute-done.7), channel_id=1, source_target_pairs={{0,64},{64,128},{128,192},{192,256},{256,320},{320,384},{384,448},... | collective-permute-start | bytes 884744 | tf_op jit(solution)/shard_map/ppermute | solution.py:30
  148.0 1.1 collective-permute-done.14
  149.1 1.3 collective-permute-start.15
  150.4 0.9 collective-permute-done.8
  151.3 1.0 bitcast_dynamic-update-slice_fusion.14
  152.3 1.0 bitcast_dynamic-update-slice_fusion.13
  154.0 4.7 %collective-permute-done.15 = bf16[2,192,384]{2,1,0:T(8,128)(2,1)S(1)} collective-permute-done((bf16[2,192,384]{2,1,0:T(8,128)(2,1)S(1)}, bf16[2,192,384]{2,1,0:T(8,128)(2,1)S(1)}, u32[]{:S(2)}, u32[]{:S(2)}) %collective-permute-start.15) | collective-permute-done | bytes 294944 | tf_op jit(solution)/shard_map/ppermute | solution.py:31
  158.7 0.0 copy-start
  158.7 2.1 %copy-done = bf16[15,2,192,384]{3,2,1,0:T(8,128)(2,1)} copy-done((bf16[15,2,192,384]{3,2,1,0:T(8,128)(2,1)}, bf16[15,2,192,384]{3,2,1,0:T(8,128)(2,1)S(1)}, u32[]{:S(2)}) %copy-start) | copy-done | bytes 4423704
  160.9 0.2 constant_dynamic-slice_fusion
  161.1 7.3 %collective-permute-start.16 = (bf16[8,2,192,384]{3,2,1,0:T(8,128)(2,1)S(1)}, bf16[8,2,192,384]{3,2,1,0:T(8,128)(2,1)}, u32[]{:S(2)}, u32[]{:S(2)}) collective-permute-start(bf16[8,2,192,384]{3,2,1,0:T(8,128)(2,1)S(1)} %constant_dynamic-slice_fusion), channel_id=1, source_target_pairs={{0,32},{32,0},{1,33},{33,1},{2,34},{34,2},{3,35},{35,3},{4,36},{36... | collective-permute-start | bytes 7077896 | tf_op jit(solution)/shard_map/ppermute | solution.py:36
  168.5 2.0 fusion.2
  170.5 2.3 %collective-permute-done.16 = bf16[8,2,192,384]{3,2,1,0:T(8,128)(2,1)} collective-permute-done((bf16[8,2,192,384]{3,2,1,0:T(8,128)(2,1)S(1)}, bf16[8,2,192,384]{3,2,1,0:T(8,128)(2,1)}, u32[]{:S(2)}, u32[]{:S(2)}) %collective-permute-start.16) | collective-permute-done | bytes 2359328 | tf_op jit(solution)/shard_map/ppermute | solution.py:36
  172.8 3.3 %maximum_select_fusion = bf16[8,2,2,192,384]{4,3,2,0,1:T(8,128)(2,1)S(1)} fusion(bf16[8,1,2,192,384]{4,3,2,0,1:T(8,128)(2,1)} %bitcast.17, bf16[8,1,2,192,384]{4,3,2,0,1:T(8,128)(2,1)S(1)} %fusion.2, pred[]{:T(512)S(6)} %eq.15), kind=kLoop, calls=%fused_computation | loop fusion | flops 7077888 | bytes 9437185 | tf_op jit(solution)/shard_map/jit(_where)/select_n | solution.py:101
  176.1 2.7 %copy.6 = bf16[8,2,2,192,384]{4,3,2,1,0:T(8,128)(2,1)} copy(bf16[8,2,2,192,384]{4,3,2,0,1:T(8,128)(2,1)S(1)} %maximum_select_fusion) | data formatting | bytes 9437184 | tf_op jit(solution)/shard_map/jit(_where)/select_n | solution.py:101
  178.8 9.1 %all-gather.2.cloned.1.call-done.panel_ref = bf16[2,2,3072,384]{3,2,1,0:T(8,128)(2,1)} async-done(((bf16[2,2,192,384]{3,2,1,0:T(8,128)(2,1)}), bf16[2,2,3072,384]{3,2,1,0:T(8,128)(2,1)}) %all-gather.2.cloned.1.call-update) | async-done | bytes 9437200 | tf_op jit(solution)/shard_map/all_gather | solution.py:97
  187.9 12.0 %shard_map.17 = f32[2,192,384]{2,1,0:T(8,128)} custom-call(bf16[16,2,192,384]{3,2,1,0:T(8,128)(2,1)} %bitcast.44, bf16[2,2,3072,384]{3,2,1,0:T(8,128)(2,1)} %all-gather.2.cloned.1.call-done.panel_ref), custom_call_target="tpu_custom_call" | custom-call | flops 3623878656 | bytes 14745600 | tf_op jit(solution)/shard_map/pallas_call | solution.py:58
  (14 shorter events, 0.7 us)
Async XLA Ops:
  6.5 181.3 %all-gather.2.cloned.1.call-start = ((), (), s32[]{:S(2)}) async-start(), calls=%async_computation | async-start | bytes 10027008 | tf_op jit(solution)/shard_map/all_gather | solution.py:97
  7.9 11.7 %collective-permute-start = (bf16[2,192,192]{1,2,0:T(8,128)(2,1)S(1)}, bf16[2,192,192]{1,2,0:T(8,128)(2,1)S(1)}, u32[]{:S(2)}, u32[]{:S(2)}) collective-permute-start(bf16[2,192,192]{1,2,0:T(8,128)(2,1)S(1)} %copy.7), channel_id=1, source_target_pairs={{0,0},{32,2},{64,4},{96,6},{128,8},{160,10},{192,12},{224,14},{256... | collective-permute-start | bytes 442376 | tf_op jit(solution)/shard_map/ppermute | solution.py:86
  14.1 10.5 %collective-permute-start.1 = (bf16[2,192,192]{1,2,0:T(8,128)(2,1)S(1)}, bf16[2,192,192]{1,2,0:T(8,128)(2,1)S(1)}, u32[]{:S(2)}, u32[]{:S(2)}) collective-permute-start(bf16[2,192,192]{1,2,0:T(8,128)(2,1)S(1)} %copy.8), channel_id=1, source_target_pairs={{0,1},{32,3},{64,5},{96,7},{128,9},{160,11},{192,13},{224,15},{256... | collective-permute-start | bytes 442376 | tf_op jit(solution)/shard_map/ppermute | solution.py:86
  25.8 56.8 %collective-permute-start.17 = (bf16[2,192,384]{2,1,0:T(8,128)(2,1)S(1)}, bf16[2,192,384]{2,1,0:T(8,128)(2,1)S(1)}, u32[]{:S(2)}, u32[]{:S(2)}) collective-permute-start(bf16[2,192,384]{2,1,0:T(8,128)(2,1)S(1)} %fusion.1), channel_id=1, source_target_pairs={{0,16},{16,0},{1,17},{17,1},{2,18},{18,2},{3,19},{19,3},{4,20},{20... | collective-permute-start | bytes 884744 | tf_op jit(solution)/shard_map/ppermute | solution.py:94
  83.5 15.1 %collective-permute-start.2 = (bf16[2,192,384]{2,1,0:T(8,128)(2,1)S(1)}, bf16[2,192,384]{2,1,0:T(8,128)(2,1)S(1)}, u32[]{:S(2)}, u32[]{:S(2)}) collective-permute-start(bf16[2,192,384]{2,1,0:T(8,128)(2,1)S(1)} %fusion.1), channel_id=1, source_target_pairs={{0,64},{64,128},{128,192},{192,256},{256,320},{320,384},{384,448},... | collective-permute-start | bytes 884744 | tf_op jit(solution)/shard_map/ppermute | solution.py:30
  84.8 17.9 %collective-permute-start.9 = (bf16[2,192,384]{2,1,0:T(8,128)(2,1)S(1)}, bf16[2,192,384]{2,1,0:T(8,128)(2,1)S(1)}, u32[]{:S(2)}, u32[]{:S(2)}) collective-permute-start(bf16[2,192,384]{2,1,0:T(8,128)(2,1)S(1)} %fusion.1), channel_id=1, source_target_pairs={{64,0},{128,64},{192,128},{256,192},{320,256},{384,320},{448,384},... | collective-permute-start | bytes 884744 | tf_op jit(solution)/shard_map/ppermute | solution.py:31
  98.6 10.0 %collective-permute-start.3 = (bf16[2,192,384]{2,1,0:T(8,128)(2,1)S(1)}, bf16[2,192,384]{2,1,0:T(8,128)(2,1)S(1)}, u32[]{:S(2)}, u32[]{:S(2)}) collective-permute-start(bf16[2,192,384]{2,1,0:T(8,128)(2,1)S(1)} %collective-permute-done.2), channel_id=1, source_target_pairs={{0,64},{64,128},{128,192},{192,256},{256,320},{320,384},{384,448},... | collective-permute-start | bytes 884744 | tf_op jit(solution)/shard_map/ppermute | solution.py:30
  102.7 10.0 %collective-permute-start.10 = (bf16[2,192,384]{2,1,0:T(8,128)(2,1)S(1)}, bf16[2,192,384]{2,1,0:T(8,128)(2,1)S(1)}, u32[]{:S(2)}, u32[]{:S(2)}) collective-permute-start(bf16[2,192,384]{2,1,0:T(8,128)(2,1)S(1)} %collective-permute-done.9), channel_id=1, source_target_pairs={{64,0},{128,64},{192,128},{256,192},{320,256},{384,320},{448,384},... | collective-permute-start | bytes 884744 | tf_op jit(solution)/shard_map/ppermute | solution.py:31
  108.6 9.1 %collective-permute-start.4 = (bf16[2,192,384]{2,1,0:T(8,128)(2,1)S(1)}, bf16[2,192,384]{2,1,0:T(8,128)(2,1)S(1)}, u32[]{:S(2)}, u32[]{:S(2)}) collective-permute-start(bf16[2,192,384]{2,1,0:T(8,128)(2,1)S(1)} %collective-permute-done.3), channel_id=1, source_target_pairs={{0,64},{64,128},{128,192},{192,256},{256,320},{320,384},{384,448},... | collective-permute-start | bytes 884744 | tf_op jit(solution)/shard_map/ppermute | solution.py:30
  112.7 10.0 %collective-permute-start.11 = (bf16[2,192,384]{2,1,0:T(8,128)(2,1)S(1)}, bf16[2,192,384]{2,1,0:T(8,128)(2,1)S(1)}, u32[]{:S(2)}, u32[]{:S(2)}) collective-permute-start(bf16[2,192,384]{2,1,0:T(8,128)(2,1)S(1)} %collective-permute-done.10), channel_id=1, source_target_pairs={{64,0},{128,64},{192,128},{256,192},{320,256},{384,320},{448,384},... | collective-permute-start | bytes 884744 | tf_op jit(solution)/shard_map/ppermute | solution.py:31
  117.7 8.4 %collective-permute-start.5 = (bf16[2,192,384]{2,1,0:T(8,128)(2,1)S(1)}, bf16[2,192,384]{2,1,0:T(8,128)(2,1)S(1)}, u32[]{:S(2)}, u32[]{:S(2)}) collective-permute-start(bf16[2,192,384]{2,1,0:T(8,128)(2,1)S(1)} %collective-permute-done.4), channel_id=1, source_target_pairs={{0,64},{64,128},{128,192},{192,256},{256,320},{320,384},{384,448},... | collective-permute-start | bytes 884744 | tf_op jit(solution)/shard_map/ppermute | solution.py:30
  122.8 8.1 %collective-permute-start.12 = (bf16[2,192,384]{2,1,0:T(8,128)(2,1)S(1)}, bf16[2,192,384]{2,1,0:T(8,128)(2,1)S(1)}, u32[]{:S(2)}, u32[]{:S(2)}) collective-permute-start(bf16[2,192,384]{2,1,0:T(8,128)(2,1)S(1)} %collective-permute-done.11), channel_id=1, source_target_pairs={{64,0},{128,64},{192,128},{256,192},{320,256},{384,320},{448,384},... | collective-permute-start | bytes 884744 | tf_op jit(solution)/shard_map/ppermute | solution.py:31
  126.1 7.9 %collective-permute-start.6 = (bf16[2,192,384]{2,1,0:T(8,128)(2,1)S(1)}, bf16[2,192,384]{2,1,0:T(8,128)(2,1)S(1)}, u32[]{:S(2)}, u32[]{:S(2)}) collective-permute-start(bf16[2,192,384]{2,1,0:T(8,128)(2,1)S(1)} %collective-permute-done.5), channel_id=1, source_target_pairs={{0,64},{64,128},{128,192},{192,256},{256,320},{320,384},{384,448},... | collective-permute-start | bytes 884744 | tf_op jit(solution)/shard_map/ppermute | solution.py:30
  130.9 8.9 %collective-permute-start.13 = (bf16[2,192,384]{2,1,0:T(8,128)(2,1)S(1)}, bf16[2,192,384]{2,1,0:T(8,128)(2,1)S(1)}, u32[]{:S(2)}, u32[]{:S(2)}) collective-permute-start(bf16[2,192,384]{2,1,0:T(8,128)(2,1)S(1)} %collective-permute-done.12), channel_id=1, source_target_pairs={{64,0},{128,64},{192,128},{256,192},{320,256},{384,320},{448,384},... | collective-permute-start | bytes 884744 | tf_op jit(solution)/shard_map/ppermute | solution.py:31
  133.9 7.8 %collective-permute-start.7 = (bf16[2,192,384]{2,1,0:T(8,128)(2,1)S(1)}, bf16[2,192,384]{2,1,0:T(8,128)(2,1)}, u32[]{:S(2)}, u32[]{:S(2)}) collective-permute-start(bf16[2,192,384]{2,1,0:T(8,128)(2,1)S(1)} %collective-permute-done.6), channel_id=1, source_target_pairs={{0,64},{64,128},{128,192},{192,256},{256,320},{320,384},{384,448},... | collective-permute-start | bytes 884744 | tf_op jit(solution)/shard_map/ppermute | solution.py:30
  139.8 9.3 %collective-permute-start.14 = (bf16[2,192,384]{2,1,0:T(8,128)(2,1)S(1)}, bf16[2,192,384]{2,1,0:T(8,128)(2,1)S(1)}, u32[]{:S(2)}, u32[]{:S(2)}) collective-permute-start(bf16[2,192,384]{2,1,0:T(8,128)(2,1)S(1)} %collective-permute-done.13), channel_id=1, source_target_pairs={{64,0},{128,64},{192,128},{256,192},{320,256},{384,320},{448,384},... | collective-permute-start | bytes 884744 | tf_op jit(solution)/shard_map/ppermute | solution.py:31
  141.7 9.6 %collective-permute-start.8 = (bf16[2,192,384]{2,1,0:T(8,128)(2,1)}, bf16[2,192,384]{2,1,0:T(8,128)(2,1)}, u32[]{:S(2)}, u32[]{:S(2)}) collective-permute-start(bf16[2,192,384]{2,1,0:T(8,128)(2,1)} %collective-permute-done.7), channel_id=1, source_target_pairs={{0,64},{64,128},{128,192},{192,256},{256,320},{320,384},{384,448},... | collective-permute-start | bytes 884744 | tf_op jit(solution)/shard_map/ppermute | solution.py:30
  149.1 9.6 %collective-permute-start.15 = (bf16[2,192,384]{2,1,0:T(8,128)(2,1)S(1)}, bf16[2,192,384]{2,1,0:T(8,128)(2,1)S(1)}, u32[]{:S(2)}, u32[]{:S(2)}) collective-permute-start(bf16[2,192,384]{2,1,0:T(8,128)(2,1)S(1)} %collective-permute-done.14), channel_id=1, source_target_pairs={{64,0},{128,64},{192,128},{256,192},{320,256},{384,320},{448,384},... | collective-permute-start | bytes 884744 | tf_op jit(solution)/shard_map/ppermute | solution.py:31
  158.7 2.1 %copy-start = (bf16[15,2,192,384]{3,2,1,0:T(8,128)(2,1)}, bf16[15,2,192,384]{3,2,1,0:T(8,128)(2,1)S(1)}, u32[]{:S(2)}) copy-start(bf16[15,2,192,384]{3,2,1,0:T(8,128)(2,1)S(1)} %bitcast_dynamic-update-slice_fusion) | copy-start | bytes 13271044
  161.1 11.6 %collective-permute-start.16 = (bf16[8,2,192,384]{3,2,1,0:T(8,128)(2,1)S(1)}, bf16[8,2,192,384]{3,2,1,0:T(8,128)(2,1)}, u32[]{:S(2)}, u32[]{:S(2)}) collective-permute-start(bf16[8,2,192,384]{3,2,1,0:T(8,128)(2,1)S(1)} %constant_dynamic-slice_fusion), channel_id=1, source_target_pairs={{0,32},{32,0},{1,33},{33,1},{2,34},{34,2},{3,35},{35,3},{4,36},{36... | collective-permute-start | bytes 7077896 | tf_op jit(solution)/shard_map/ppermute | solution.py:36
Sparse Core Ops, SparseCore 0:
  83.6 104.1 all-gather.1

commit v15 on v14

--- a/solution.py
+++ b/solution.py
@@ -37,29 +37,31 @@
     return mine, other
 
 
-def product_kernel(left_ref, panel_ref, out_ref, *, n_block, width, factor):
-    acc = [[None, None], [None, None]]
+def product_kernel(left_ref, panel_ref, out_ref, acc_ref, *, n_block, width, factor):
     for half in range(2):
         for block in range(n_block):
+            rhs = panel_ref[half, pl.ds(block * width, width), :]
             for p in range(2):
-                lhs = left_ref[half * n_block + block, p, :, :]
-                for q in range(2):
-                    rhs = panel_ref[half, q, pl.ds(block * width, width), :]
-                    term = jnp.dot(lhs, rhs, preferred_element_type=jnp.float32)
-                    acc[p][q] = term if acc[p][q] is None else acc[p][q] + term
-    out_ref[0, :, :] = (acc[0][0] - acc[1][1]) * factor
-    out_ref[1, :, :] = (acc[0][1] + acc[1][0]) * factor
+                term = jnp.dot(left_ref[half * n_block + block, p, :, :], rhs, preferred_element_type=jnp.float32)
+                if half == 0 and block == 0:
+                    acc_ref[p] = term
+                else:
+                    acc_ref[p] += term
+    cols = out_ref.shape[-1]
+    out_ref[0, :, :] = (acc_ref[0, :, :cols] - acc_ref[1, :, cols:]) * factor
+    out_ref[1, :, :] = (acc_ref[0, :, cols:] + acc_ref[1, :, :cols]) * factor
 
 
 def product(left, panels, factor):
     n_blocks, parts, rows, width = left.shape
-    cols = panels.shape[-1]
+    cols = panels.shape[-1] // 2
     kernel = functools.partial(product_kernel, n_block=n_blocks // 2, width=width, factor=factor)
     return pl.pallas_call(
         kernel,
         out_shape=jax.ShapeDtypeStruct((2, rows, cols), jnp.float32),
         in_specs=[pl.BlockSpec(memory_space=pltpu.VMEM)] * 2,
         out_specs=pl.BlockSpec(memory_space=pltpu.VMEM),
+        scratch_shapes=[pltpu.VMEM((2, rows, 2 * cols), jnp.float32)],
         cost_estimate=pl.CostEstimate(
             flops=2 * 4 * rows * cols * width * n_blocks,
             transcendentals=0,
@@ -94,7 +96,9 @@
     partner_block = lax.ppermute(symmetric, "zh", [(0, 1), (1, 0)])
     top = jnp.where(half_index == 0, symmetric, partner_block)
     bottom = jnp.where(half_index == 0, partner_block, symmetric)
-    panels = lax.all_gather(jnp.stack([top, bottom]), ("y", "x"), axis=2, tiled=True)
+    pieces = jnp.swapaxes(jnp.stack([top, bottom]), 1, 2)
+    panels = lax.all_gather(pieces, ("y", "x"), axis=1, tiled=True)
+    panels = panels.reshape(panels.shape[0], panels.shape[1], -1)
     mine, other = gather_line(symmetric)
     core_index = lax.axis_index("core")
     n_line = mine.shape[0]

time: 208 us -> 216 us (1.038)
  local copies, waits for them, and re-layouts: 11.2 us -> 19.5 us
    reshape x0 -> x1, local copies, waits for them, and re-layouts: none -> 8.26 us  [local(): panels = panels.reshape(panels.shape[0], panels.shape[1], -1)]
    ppermute x7, waiting for transfers between devices: 8.31 us -> 14.2 us  [gather_line(): lax.ppermute(leftward, 'zl', [(k + 1, k) for k in range(n_line - 1)])]
    ppermute x7, waiting for transfers between devices: 25.9 us -> 20.3 us  [gather_line(): lax.ppermute(rightward, 'zl', [(k, k + 1) for k in range(n_line - 1)])]
  transfers between devices with their start and end apart: 19 -> 19, of which waited for: 17 -> 15; matrix products, arithmetic and copies ran while one was open for 5% -> 5% of each run, Pallas kernels for 0% -> 0%
where the time goes in v15:
time: 216 us; the launch traced here: 215 us
  starting transfers between devices  104 us (48%)
  waiting for transfers between devices  61.5 us (28%)
  local copies, waits for them, and re-layouts  19.5 us (9%)
  between operations  13.7 us (6%)
  Pallas kernels  11 us (5%)
  other arithmetic  5.41 us (3%)
    ppermute x1, starting transfers between devices, local(): partner_block = lax.ppermute(symmetric, 'zh', [(0, 1), (1, 0)])  49.2 us
    ppermute x7, starting transfers between devices, gather_line(): lax.ppermute(rightward, 'zl', [(k, k + 1) for k in range(n_line - 1)])  29.7 us
    ppermute x7, waiting for transfers between devices, gather_line(): lax.ppermute(rightward, 'zl', [(k, k + 1) for k in range(n_line - 1)])  20.3 us
    ppermute x7, waiting for transfers between devices, gather_line(): lax.ppermute(leftward, 'zl', [(k + 1, k) for k in range(n_line - 1)])  14.2 us
    pallas_call x1, Pallas kernels, product(): pl.pallas_call(kernel, out_shape=jax.ShapeDtypeStruct((2, rows, cols), jn...  11 us
    ppermute x7, starting transfers between devices, gather_line(): lax.ppermute(leftward, 'zl', [(k + 1, k) for k in range(n_line - 1)])  9 us
    all_gather x1, waiting for transfers between devices, local(): panels = lax.all_gather(pieces, ('y', 'x'), axis=1, tiled=True)  8.84 us
    ppermute x2, waiting for transfers between devices, local(): lax.ppermute(piece, axes, mirror_pairs(n_recv, n_shot, flip))  8.52 us
  transfers between devices with their start and end apart: 19, of which 15 were waited for; matrix products, arithmetic and copies ran while one was open for 5% of the time, Pallas kernels for 0%

profile of v15, /device:TPU:1, one launch (start us, length us, event | category | flops | bytes accessed | tf_op | source)
XLA Modules:
  0.0 215.0 jit_solution(9095943073879669509)
XLA Ops:
  6.5 0.0 all-gather.2.cloned.1.call-start
  6.5 1.2 constant_dynamic-slice_fusion.2
  7.7 0.1 copy.7
  7.9 5.8 %collective-permute-start.1 = (bf16[2,192,192]{1,2,0:T(8,128)(2,1)S(1)}, bf16[2,192,192]{1,2,0:T(8,128)(2,1)S(1)}, u32[]{:S(2)}, u32[]{:S(2)}) collective-permute-start(bf16[2,192,192]{1,2,0:T(8,128)(2,1)S(1)} %copy.7), channel_id=1, source_target_pairs={{0,1},{32,3},{64,5},{96,7},{128,9},{160,11},{192,13},{224,15},{256... | collective-permute-start | bytes 442376 | tf_op jit(solution)/shard_map/ppermute | solution.py:88
  13.7 0.1 copy.6
  13.8 2.1 collective-permute-start
  16.0 1.4 collective-permute-done.1
  17.4 7.1 %collective-permute-done = bf16[2,192,192]{1,2,0:T(8,128)(2,1)S(1)} collective-permute-done((bf16[2,192,192]{1,2,0:T(8,128)(2,1)S(1)}, bf16[2,192,192]{1,2,0:T(8,128)(2,1)S(1)}, u32[]{:S(2)}, u32[]{:S(2)}) %collective-permute-start) | collective-permute-done | bytes 147488 | tf_op jit(solution)/shard_map/ppermute | solution.py:88
  24.6 1.1 fusion.1
  25.7 49.2 %collective-permute-start.17 = (bf16[2,192,384]{2,1,0:T(8,128)(2,1)S(1)}, bf16[2,192,384]{2,1,0:T(8,128)(2,1)S(1)}, u32[]{:S(2)}, u32[]{:S(2)}) collective-permute-start(bf16[2,192,384]{2,1,0:T(8,128)(2,1)S(1)} %fusion.1), channel_id=1, source_target_pairs={{0,16},{16,0},{1,17},{17,1},{2,18},{18,2},{3,19},{19,3},{4,20},{20... | collective-permute-start | bytes 884744 | tf_op jit(solution)/shard_map/ppermute | solution.py:96
  74.9 7.3 %collective-permute-done.17 = bf16[2,192,384]{2,1,0:T(8,128)(2,1)S(1)} collective-permute-done((bf16[2,192,384]{2,1,0:T(8,128)(2,1)S(1)}, bf16[2,192,384]{2,1,0:T(8,128)(2,1)S(1)}, u32[]{:S(2)}, u32[]{:S(2)}) %collective-permute-start.17) | collective-permute-done | bytes 294944 | tf_op jit(solution)/shard_map/ppermute | solution.py:96
  82.3 0.1 select_bitcast_fusion.1
  82.3 0.9 maximum_bitcast_fusion
  83.2 0.0 all-gather.2.cloned.1.call-update
  83.2 1.3 collective-permute-start.2
  84.6 1.3 collective-permute-start.9
  85.9 11.8 %collective-permute-done.2 = bf16[2,192,384]{2,1,0:T(8,128)(2,1)S(1)} collective-permute-done((bf16[2,192,384]{2,1,0:T(8,128)(2,1)S(1)}, bf16[2,192,384]{2,1,0:T(8,128)(2,1)S(1)}, u32[]{:S(2)}, u32[]{:S(2)}) %collective-permute-start.2) | collective-permute-done | bytes 294944 | tf_op jit(solution)/shard_map/ppermute | solution.py:30
  97.6 4.1 %collective-permute-start.3 = (bf16[2,192,384]{2,1,0:T(8,128)(2,1)S(1)}, bf16[2,192,384]{2,1,0:T(8,128)(2,1)S(1)}, u32[]{:S(2)}, u32[]{:S(2)}) collective-permute-start(bf16[2,192,384]{2,1,0:T(8,128)(2,1)S(1)} %collective-permute-done.2), channel_id=1, source_target_pairs={{0,64},{64,128},{128,192},{192,256},{256,320},{320,384},{384,448},... | collective-permute-start | bytes 884744 | tf_op jit(solution)/shard_map/ppermute | solution.py:30
  101.8 0.0 collective-permute-done.9
  101.8 1.3 collective-permute-start.10
  103.1 4.5 %collective-permute-done.3 = bf16[2,192,384]{2,1,0:T(8,128)(2,1)S(1)} collective-permute-done((bf16[2,192,384]{2,1,0:T(8,128)(2,1)S(1)}, bf16[2,192,384]{2,1,0:T(8,128)(2,1)S(1)}, u32[]{:S(2)}, u32[]{:S(2)}) %collective-permute-start.3) | collective-permute-done | bytes 294944 | tf_op jit(solution)/shard_map/ppermute | solution.py:30
  107.6 4.1 %collective-permute-start.4 = (bf16[2,192,384]{2,1,0:T(8,128)(2,1)S(1)}, bf16[2,192,384]{2,1,0:T(8,128)(2,1)S(1)}, u32[]{:S(2)}, u32[]{:S(2)}) collective-permute-start(bf16[2,192,384]{2,1,0:T(8,128)(2,1)S(1)} %collective-permute-done.3), channel_id=1, source_target_pairs={{0,64},{64,128},{128,192},{192,256},{256,320},{320,384},{384,448},... | collective-permute-start | bytes 884744 | tf_op jit(solution)/shard_map/ppermute | solution.py:30
  111.7 0.0 collective-permute-done.10
  111.7 1.3 collective-permute-start.11
  113.0 3.6 %collective-permute-done.4 = bf16[2,192,384]{2,1,0:T(8,128)(2,1)S(1)} collective-permute-done((bf16[2,192,384]{2,1,0:T(8,128)(2,1)S(1)}, bf16[2,192,384]{2,1,0:T(8,128)(2,1)S(1)}, u32[]{:S(2)}, u32[]{:S(2)}) %collective-permute-start.4) | collective-permute-done | bytes 294944 | tf_op jit(solution)/shard_map/ppermute | solution.py:30
  116.7 4.2 %collective-permute-start.5 = (bf16[2,192,384]{2,1,0:T(8,128)(2,1)S(1)}, bf16[2,192,384]{2,1,0:T(8,128)(2,1)S(1)}, u32[]{:S(2)}, u32[]{:S(2)}) collective-permute-start(bf16[2,192,384]{2,1,0:T(8,128)(2,1)S(1)} %collective-permute-done.4), channel_id=1, source_target_pairs={{0,64},{64,128},{128,192},{192,256},{256,320},{320,384},{384,448},... | collective-permute-start | bytes 884744 | tf_op jit(solution)/shard_map/ppermute | solution.py:30
  120.9 3.3 %collective-permute-done.11 = bf16[2,192,384]{2,1,0:T(8,128)(2,1)S(1)} collective-permute-done((bf16[2,192,384]{2,1,0:T(8,128)(2,1)S(1)}, bf16[2,192,384]{2,1,0:T(8,128)(2,1)S(1)}, u32[]{:S(2)}, u32[]{:S(2)}) %collective-permute-start.11) | collective-permute-done | bytes 294944 | tf_op jit(solution)/shard_map/ppermute | solution.py:31
  124.2 1.3 collective-permute-start.12
  125.4 0.0 collective-permute-done.5
  125.5 5.7 %collective-permute-start.6 = (bf16[2,192,384]{2,1,0:T(8,128)(2,1)S(1)}, bf16[2,192,384]{2,1,0:T(8,128)(2,1)S(1)}, u32[]{:S(2)}, u32[]{:S(2)}) collective-permute-start(bf16[2,192,384]{2,1,0:T(8,128)(2,1)S(1)} %collective-permute-done.5), channel_id=1, source_target_pairs={{0,64},{64,128},{128,192},{192,256},{256,320},{320,384},{384,448},... | collective-permute-start | bytes 884744 | tf_op jit(solution)/shard_map/ppermute | solution.py:30
  131.2 2.8 %collective-permute-done.12 = bf16[2,192,384]{2,1,0:T(8,128)(2,1)S(1)} collective-permute-done((bf16[2,192,384]{2,1,0:T(8,128)(2,1)S(1)}, bf16[2,192,384]{2,1,0:T(8,128)(2,1)S(1)}, u32[]{:S(2)}, u32[]{:S(2)}) %collective-permute-start.12) | collective-permute-done | bytes 294944 | tf_op jit(solution)/shard_map/ppermute | solution.py:31
  134.0 1.3 collective-permute-start.13
  135.3 0.0 collective-permute-done.6
  135.3 5.1 %collective-permute-start.7 = (bf16[2,192,384]{2,1,0:T(8,128)(2,1)S(1)}, bf16[2,192,384]{2,1,0:T(8,128)(2,1)}, u32[]{:S(2)}, u32[]{:S(2)}) collective-permute-start(bf16[2,192,384]{2,1,0:T(8,128)(2,1)S(1)} %collective-permute-done.6), channel_id=1, source_target_pairs={{0,64},{64,128},{128,192},{192,256},{256,320},{320,384},{384,448},... | collective-permute-start | bytes 884744 | tf_op jit(solution)/shard_map/ppermute | solution.py:30
  140.4 1.4 collective-permute-done.13
  141.8 1.3 collective-permute-start.14
  143.1 0.2 collective-permute-done.7
  143.3 5.1 %collective-permute-start.8 = (bf16[2,192,384]{2,1,0:T(8,128)(2,1)}, bf16[2,192,384]{2,1,0:T(8,128)(2,1)}, u32[]{:S(2)}, u32[]{:S(2)}) collective-permute-start(bf16[2,192,384]{2,1,0:T(8,128)(2,1)} %collective-permute-done.7), channel_id=1, source_target_pairs={{0,64},{64,128},{128,192},{192,256},{256,320},{320,384},{384,448},... | collective-permute-start | bytes 884744 | tf_op jit(solution)/shard_map/ppermute | solution.py:30
  148.4 1.8 collective-permute-done.14
  150.2 1.3 collective-permute-start.15
  151.5 0.2 collective-permute-done.8
  151.7 1.0 bitcast_dynamic-update-slice_fusion.14
  152.7 1.0 bitcast_dynamic-update-slice_fusion.13
  154.4 4.9 %collective-permute-done.15 = bf16[2,192,384]{2,1,0:T(8,128)(2,1)S(1)} collective-permute-done((bf16[2,192,384]{2,1,0:T(8,128)(2,1)S(1)}, bf16[2,192,384]{2,1,0:T(8,128)(2,1)S(1)}, u32[]{:S(2)}, u32[]{:S(2)}) %collective-permute-start.15) | collective-permute-done | bytes 294944 | tf_op jit(solution)/shard_map/ppermute | solution.py:31
  159.3 0.0 copy-start
  159.3 2.1 copy-done
  161.5 0.2 constant_dynamic-slice_fusion
  161.7 8.0 %collective-permute-start.16 = (bf16[8,2,192,384]{3,2,1,0:T(8,128)(2,1)S(1)}, bf16[8,2,192,384]{3,2,1,0:T(8,128)(2,1)}, u32[]{:S(2)}, u32[]{:S(2)}) collective-permute-start(bf16[8,2,192,384]{3,2,1,0:T(8,128)(2,1)S(1)} %constant_dynamic-slice_fusion), channel_id=1, source_target_pairs={{0,32},{32,0},{1,33},{33,1},{2,34},{34,2},{3,35},{35,3},{4,36},{36... | collective-permute-start | bytes 7077896 | tf_op jit(solution)/shard_map/ppermute | solution.py:36
  169.7 2.0 fusion.2
  171.8 2.2 %collective-permute-done.16 = bf16[8,2,192,384]{3,2,1,0:T(8,128)(2,1)} collective-permute-done((bf16[8,2,192,384]{3,2,1,0:T(8,128)(2,1)S(1)}, bf16[8,2,192,384]{3,2,1,0:T(8,128)(2,1)}, u32[]{:S(2)}, u32[]{:S(2)}) %collective-permute-start.16) | collective-permute-done | bytes 2359328 | tf_op jit(solution)/shard_map/ppermute | solution.py:36
  174.0 3.3 %maximum_select_fusion = bf16[8,2,2,192,384]{4,3,2,0,1:T(8,128)(2,1)S(1)} fusion(bf16[8,1,2,192,384]{4,3,2,0,1:T(8,128)(2,1)} %bitcast.17, bf16[8,1,2,192,384]{4,3,2,0,1:T(8,128)(2,1)S(1)} %fusion.2, pred[]{:T(512)S(6)} %eq.15), kind=kLoop, calls=%fused_computation | loop fusion | flops 7077888 | bytes 9437185 | tf_op jit(solution)/shard_map/jit(_where)/select_n | solution.py:105
  177.3 2.7 %copy.4 = bf16[8,2,2,192,384]{4,3,2,1,0:T(8,128)(2,1)} copy(bf16[8,2,2,192,384]{4,3,2,0,1:T(8,128)(2,1)S(1)} %maximum_select_fusion) | data formatting | bytes 9437184 | tf_op jit(solution)/shard_map/jit(_where)/select_n | solution.py:105
  180.1 8.8 %all-gather.2.cloned.1.call-done = bf16[2,3072,2,384]{3,1,2,0:T(8,128)(2,1)} async-done(((bf16[2,192,2,384]{3,1,2,0:T(8,128)(2,1)}), bf16[2,3072,2,384]{3,1,2,0:T(8,128)(2,1)}) %all-gather.2.cloned.1.call-update) | async-done | bytes 9437200 | tf_op jit(solution)/shard_map/all_gather | solution.py:100
  188.9 8.3 %copy.8 = bf16[2,2,384,8,384]{4,3,1,2,0:T(8,128)(2,1)} copy(bf16[2,2,384,8,384]{4,3,2,1,0:T(8,128)(2,1)} %bitcast.50) | data formatting | bytes 18874368 | tf_op jit(solution)/shard_map/reshape | solution.py:101
  197.2 11.0 %shard_map.17 = f32[2,192,384]{2,1,0:T(8,128)} custom-call(bf16[16,2,192,384]{3,2,1,0:T(8,128)(2,1)} %bitcast.49, bf16[2,3072,768]{2,1,0:T(8,128)(2,1)} %bitcast.48), custom_call_target="tpu_custom_call" | custom-call | flops 3623878656 | bytes 14745600 | tf_op jit(solution)/shard_map/pallas_call | solution.py:59
  (14 shorter events, 0.7 us)
Async XLA Ops:
  6.5 182.4 %all-gather.2.cloned.1.call-start = ((), (), s32[]{:S(2)}) async-start(), calls=%async_computation | async-start | bytes 10027008 | tf_op jit(solution)/shard_map/all_gather | solution.py:100
  7.9 9.5 %collective-permute-start.1 = (bf16[2,192,192]{1,2,0:T(8,128)(2,1)S(1)}, bf16[2,192,192]{1,2,0:T(8,128)(2,1)S(1)}, u32[]{:S(2)}, u32[]{:S(2)}) collective-permute-start(bf16[2,192,192]{1,2,0:T(8,128)(2,1)S(1)} %copy.7), channel_id=1, source_target_pairs={{0,1},{32,3},{64,5},{96,7},{128,9},{160,11},{192,13},{224,15},{256... | collective-permute-start | bytes 442376 | tf_op jit(solution)/shard_map/ppermute | solution.py:88
  13.8 10.7 %collective-permute-start = (bf16[2,192,192]{1,2,0:T(8,128)(2,1)S(1)}, bf16[2,192,192]{1,2,0:T(8,128)(2,1)S(1)}, u32[]{:S(2)}, u32[]{:S(2)}) collective-permute-start(bf16[2,192,192]{1,2,0:T(8,128)(2,1)S(1)} %copy.6), channel_id=1, source_target_pairs={{0,0},{32,2},{64,4},{96,6},{128,8},{160,10},{192,12},{224,14},{256... | collective-permute-start | bytes 442376 | tf_op jit(solution)/shard_map/ppermute | solution.py:88
  25.7 56.6 %collective-permute-start.17 = (bf16[2,192,384]{2,1,0:T(8,128)(2,1)S(1)}, bf16[2,192,384]{2,1,0:T(8,128)(2,1)S(1)}, u32[]{:S(2)}, u32[]{:S(2)}) collective-permute-start(bf16[2,192,384]{2,1,0:T(8,128)(2,1)S(1)} %fusion.1), channel_id=1, source_target_pairs={{0,16},{16,0},{1,17},{17,1},{2,18},{18,2},{3,19},{19,3},{4,20},{20... | collective-permute-start | bytes 884744 | tf_op jit(solution)/shard_map/ppermute | solution.py:96
  83.2 14.4 %collective-permute-start.2 = (bf16[2,192,384]{2,1,0:T(8,128)(2,1)S(1)}, bf16[2,192,384]{2,1,0:T(8,128)(2,1)S(1)}, u32[]{:S(2)}, u32[]{:S(2)}) collective-permute-start(bf16[2,192,384]{2,1,0:T(8,128)(2,1)S(1)} %fusion.1), channel_id=1, source_target_pairs={{0,64},{64,128},{128,192},{192,256},{256,320},{320,384},{384,448},... | collective-permute-start | bytes 884744 | tf_op jit(solution)/shard_map/ppermute | solution.py:30
  84.6 17.2 %collective-permute-start.9 = (bf16[2,192,384]{2,1,0:T(8,128)(2,1)S(1)}, bf16[2,192,384]{2,1,0:T(8,128)(2,1)S(1)}, u32[]{:S(2)}, u32[]{:S(2)}) collective-permute-start(bf16[2,192,384]{2,1,0:T(8,128)(2,1)S(1)} %fusion.1), channel_id=1, source_target_pairs={{64,0},{128,64},{192,128},{256,192},{320,256},{384,320},{448,384},... | collective-permute-start | bytes 884744 | tf_op jit(solution)/shard_map/ppermute | solution.py:31
  97.6 10.0 %collective-permute-start.3 = (bf16[2,192,384]{2,1,0:T(8,128)(2,1)S(1)}, bf16[2,192,384]{2,1,0:T(8,128)(2,1)S(1)}, u32[]{:S(2)}, u32[]{:S(2)}) collective-permute-start(bf16[2,192,384]{2,1,0:T(8,128)(2,1)S(1)} %collective-permute-done.2), channel_id=1, source_target_pairs={{0,64},{64,128},{128,192},{192,256},{256,320},{320,384},{384,448},... | collective-permute-start | bytes 884744 | tf_op jit(solution)/shard_map/ppermute | solution.py:30
  101.8 10.0 %collective-permute-start.10 = (bf16[2,192,384]{2,1,0:T(8,128)(2,1)S(1)}, bf16[2,192,384]{2,1,0:T(8,128)(2,1)S(1)}, u32[]{:S(2)}, u32[]{:S(2)}) collective-permute-start(bf16[2,192,384]{2,1,0:T(8,128)(2,1)S(1)} %collective-permute-done.9), channel_id=1, source_target_pairs={{64,0},{128,64},{192,128},{256,192},{320,256},{384,320},{448,384},... | collective-permute-start | bytes 884744 | tf_op jit(solution)/shard_map/ppermute | solution.py:31
  107.6 9.1 %collective-permute-start.4 = (bf16[2,192,384]{2,1,0:T(8,128)(2,1)S(1)}, bf16[2,192,384]{2,1,0:T(8,128)(2,1)S(1)}, u32[]{:S(2)}, u32[]{:S(2)}) collective-permute-start(bf16[2,192,384]{2,1,0:T(8,128)(2,1)S(1)} %collective-permute-done.3), channel_id=1, source_target_pairs={{0,64},{64,128},{128,192},{192,256},{256,320},{320,384},{384,448},... | collective-permute-start | bytes 884744 | tf_op jit(solution)/shard_map/ppermute | solution.py:30
  111.7 12.4 %collective-permute-start.11 = (bf16[2,192,384]{2,1,0:T(8,128)(2,1)S(1)}, bf16[2,192,384]{2,1,0:T(8,128)(2,1)S(1)}, u32[]{:S(2)}, u32[]{:S(2)}) collective-permute-start(bf16[2,192,384]{2,1,0:T(8,128)(2,1)S(1)} %collective-permute-done.10), channel_id=1, source_target_pairs={{64,0},{128,64},{192,128},{256,192},{320,256},{384,320},{448,384},... | collective-permute-start | bytes 884744 | tf_op jit(solution)/shard_map/ppermute | solution.py:31
  116.7 8.8 %collective-permute-start.5 = (bf16[2,192,384]{2,1,0:T(8,128)(2,1)S(1)}, bf16[2,192,384]{2,1,0:T(8,128)(2,1)S(1)}, u32[]{:S(2)}, u32[]{:S(2)}) collective-permute-start(bf16[2,192,384]{2,1,0:T(8,128)(2,1)S(1)} %collective-permute-done.4), channel_id=1, source_target_pairs={{0,64},{64,128},{128,192},{192,256},{256,320},{320,384},{384,448},... | collective-permute-start | bytes 884744 | tf_op jit(solution)/shard_map/ppermute | solution.py:30
  124.2 9.8 %collective-permute-start.12 = (bf16[2,192,384]{2,1,0:T(8,128)(2,1)S(1)}, bf16[2,192,384]{2,1,0:T(8,128)(2,1)S(1)}, u32[]{:S(2)}, u32[]{:S(2)}) collective-permute-start(bf16[2,192,384]{2,1,0:T(8,128)(2,1)S(1)} %collective-permute-done.11), channel_id=1, source_target_pairs={{64,0},{128,64},{192,128},{256,192},{320,256},{384,320},{448,384},... | collective-permute-start | bytes 884744 | tf_op jit(solution)/shard_map/ppermute | solution.py:31
  125.5 9.8 %collective-permute-start.6 = (bf16[2,192,384]{2,1,0:T(8,128)(2,1)S(1)}, bf16[2,192,384]{2,1,0:T(8,128)(2,1)S(1)}, u32[]{:S(2)}, u32[]{:S(2)}) collective-permute-start(bf16[2,192,384]{2,1,0:T(8,128)(2,1)S(1)} %collective-permute-done.5), channel_id=1, source_target_pairs={{0,64},{64,128},{128,192},{192,256},{256,320},{320,384},{384,448},... | collective-permute-start | bytes 884744 | tf_op jit(solution)/shard_map/ppermute | solution.py:30
  134.0 7.8 %collective-permute-start.13 = (bf16[2,192,384]{2,1,0:T(8,128)(2,1)S(1)}, bf16[2,192,384]{2,1,0:T(8,128)(2,1)S(1)}, u32[]{:S(2)}, u32[]{:S(2)}) collective-permute-start(bf16[2,192,384]{2,1,0:T(8,128)(2,1)S(1)} %collective-permute-done.12), channel_id=1, source_target_pairs={{64,0},{128,64},{192,128},{256,192},{320,256},{384,320},{448,384},... | collective-permute-start | bytes 884744 | tf_op jit(solution)/shard_map/ppermute | solution.py:31
  135.3 8.0 %collective-permute-start.7 = (bf16[2,192,384]{2,1,0:T(8,128)(2,1)S(1)}, bf16[2,192,384]{2,1,0:T(8,128)(2,1)}, u32[]{:S(2)}, u32[]{:S(2)}) collective-permute-start(bf16[2,192,384]{2,1,0:T(8,128)(2,1)S(1)} %collective-permute-done.6), channel_id=1, source_target_pairs={{0,64},{64,128},{128,192},{192,256},{256,320},{320,384},{384,448},... | collective-permute-start | bytes 884744 | tf_op jit(solution)/shard_map/ppermute | solution.py:30
  141.8 8.4 %collective-permute-start.14 = (bf16[2,192,384]{2,1,0:T(8,128)(2,1)S(1)}, bf16[2,192,384]{2,1,0:T(8,128)(2,1)S(1)}, u32[]{:S(2)}, u32[]{:S(2)}) collective-permute-start(bf16[2,192,384]{2,1,0:T(8,128)(2,1)S(1)} %collective-permute-done.13), channel_id=1, source_target_pairs={{64,0},{128,64},{192,128},{256,192},{320,256},{384,320},{448,384},... | collective-permute-start | bytes 884744 | tf_op jit(solution)/shard_map/ppermute | solution.py:31
  143.3 8.4 %collective-permute-start.8 = (bf16[2,192,384]{2,1,0:T(8,128)(2,1)}, bf16[2,192,384]{2,1,0:T(8,128)(2,1)}, u32[]{:S(2)}, u32[]{:S(2)}) collective-permute-start(bf16[2,192,384]{2,1,0:T(8,128)(2,1)} %collective-permute-done.7), channel_id=1, source_target_pairs={{0,64},{64,128},{128,192},{192,256},{256,320},{320,384},{384,448},... | collective-permute-start | bytes 884744 | tf_op jit(solution)/shard_map/ppermute | solution.py:30
  150.2 9.1 %collective-permute-start.15 = (bf16[2,192,384]{2,1,0:T(8,128)(2,1)S(1)}, bf16[2,192,384]{2,1,0:T(8,128)(2,1)S(1)}, u32[]{:S(2)}, u32[]{:S(2)}) collective-permute-start(bf16[2,192,384]{2,1,0:T(8,128)(2,1)S(1)} %collective-permute-done.14), channel_id=1, source_target_pairs={{64,0},{128,64},{192,128},{256,192},{320,256},{384,320},{448,384},... | collective-permute-start | bytes 884744 | tf_op jit(solution)/shard_map/ppermute | solution.py:31
  159.3 2.1 copy-start
  161.7 12.3 %collective-permute-start.16 = (bf16[8,2,192,384]{3,2,1,0:T(8,128)(2,1)S(1)}, bf16[8,2,192,384]{3,2,1,0:T(8,128)(2,1)}, u32[]{:S(2)}, u32[]{:S(2)}) collective-permute-start(bf16[8,2,192,384]{3,2,1,0:T(8,128)(2,1)S(1)} %constant_dynamic-slice_fusion), channel_id=1, source_target_pairs={{0,32},{32,0},{1,33},{33,1},{2,34},{34,2},{3,35},{35,3},{4,36},{36... | collective-permute-start | bytes 7077896 | tf_op jit(solution)/shard_map/ppermute | solution.py:36
Sparse Core Ops, SparseCore 0:
  83.4 105.4 all-gather.1

commit v16 on v14

--- a/solution.py
+++ b/solution.py
@@ -37,8 +37,7 @@
     return mine, other
 
 
-def product_kernel(left_ref, panel_ref, out_ref, *, n_block, width, factor):
-    acc = [[None, None], [None, None]]
+def product_kernel(left_ref, panel_ref, out_ref, acc_ref, *, n_block, width, factor):
     for half in range(2):
         for block in range(n_block):
             for p in range(2):
@@ -46,9 +45,12 @@
                 for q in range(2):
                     rhs = panel_ref[half, q, pl.ds(block * width, width), :]
                     term = jnp.dot(lhs, rhs, preferred_element_type=jnp.float32)
-                    acc[p][q] = term if acc[p][q] is None else acc[p][q] + term
-    out_ref[0, :, :] = (acc[0][0] - acc[1][1]) * factor
-    out_ref[1, :, :] = (acc[0][1] + acc[1][0]) * factor
+                    if half == 0 and block == 0:
+                        acc_ref[p, q] = term
+                    else:
+                        acc_ref[p, q] += term
+    out_ref[0, :, :] = (acc_ref[0, 0] - acc_ref[1, 1]) * factor
+    out_ref[1, :, :] = (acc_ref[0, 1] + acc_ref[1, 0]) * factor
 
 
 def product(left, panels, factor):
@@ -60,6 +62,7 @@
         out_shape=jax.ShapeDtypeStruct((2, rows, cols), jnp.float32),
         in_specs=[pl.BlockSpec(memory_space=pltpu.VMEM)] * 2,
         out_specs=pl.BlockSpec(memory_space=pltpu.VMEM),
+        scratch_shapes=[pltpu.VMEM((2, 2, rows, cols), jnp.float32)],
         cost_estimate=pl.CostEstimate(
             flops=2 * 4 * rows * cols * width * n_blocks,
             transcendentals=0,

time: 208 us -> 208 us (level)
  no operation moved by 1% of the time
where the time goes in v16:
time: 208 us; the launch traced here: 207 us
  starting transfers between devices  103 us (50%)
  waiting for transfers between devices  61.1 us (29%)
  between operations  13.7 us (7%)
  Pallas kernels  12 us (6%)
  local copies, waits for them, and re-layouts  11.2 us (5%)
  other arithmetic  5.41 us (3%)
    ppermute x1, starting transfers between devices, local(): partner_block = lax.ppermute(symmetric, 'zh', [(0, 1), (1, 0)])  49.2 us
    ppermute x7, starting transfers between devices, gather_line(): lax.ppermute(rightward, 'zl', [(k, k + 1) for k in range(n_line - 1)])  29.2 us
    ppermute x7, waiting for transfers between devices, gather_line(): lax.ppermute(rightward, 'zl', [(k, k + 1) for k in range(n_line - 1)])  25.9 us
    pallas_call x1, Pallas kernels, product(): pl.pallas_call(kernel, out_shape=jax.ShapeDtypeStruct((2, rows, cols), jn...  12 us
    all_gather x1, waiting for transfers between devices, local(): lax.all_gather(jnp.stack([top, bottom]), ('y', 'x'), axis=2, tiled=True)  9.05 us
    ppermute x7, starting transfers between devices, gather_line(): lax.ppermute(leftward, 'zl', [(k + 1, k) for k in range(n_line - 1)])  9 us
    ppermute x2, starting transfers between devices, local(): lax.ppermute(piece, axes, mirror_pairs(n_recv, n_shot, flip))  8.58 us
    ppermute x7, waiting for transfers between devices, gather_line(): lax.ppermute(leftward, 'zl', [(k + 1, k) for k in range(n_line - 1)])  8.31 us
  transfers between devices with their start and end apart: 19, of which 17 were waited for; matrix products, arithmetic and copies ran while one was open for 5% of the time, Pallas kernels for 0%

profile of v16, /device:TPU:1, one launch (start us, length us, event | category | flops | bytes accessed | tf_op | source)
XLA Modules:
  0.0 206.7 jit_solution(431224053162101048)
XLA Ops:
  6.5 0.0 all-gather.2.cloned.1.call-start
  6.5 1.2 constant_dynamic-slice_fusion.2
  7.7 0.1 copy.7
  7.9 6.0 %collective-permute-start = (bf16[2,192,192]{1,2,0:T(8,128)(2,1)S(1)}, bf16[2,192,192]{1,2,0:T(8,128)(2,1)S(1)}, u32[]{:S(2)}, u32[]{:S(2)}) collective-permute-start(bf16[2,192,192]{1,2,0:T(8,128)(2,1)S(1)} %copy.7), channel_id=1, source_target_pairs={{0,0},{32,2},{64,4},{96,6},{128,8},{160,10},{192,12},{224,14},{256... | collective-permute-start | bytes 442376 | tf_op jit(solution)/shard_map/ppermute | solution.py:89
  13.9 0.1 copy.8
  14.1 2.5 %collective-permute-start.1 = (bf16[2,192,192]{1,2,0:T(8,128)(2,1)S(1)}, bf16[2,192,192]{1,2,0:T(8,128)(2,1)S(1)}, u32[]{:S(2)}, u32[]{:S(2)}) collective-permute-start(bf16[2,192,192]{1,2,0:T(8,128)(2,1)S(1)} %copy.8), channel_id=1, source_target_pairs={{0,1},{32,3},{64,5},{96,7},{128,9},{160,11},{192,13},{224,15},{256... | collective-permute-start | bytes 442376 | tf_op jit(solution)/shard_map/ppermute | solution.py:89
  16.6 2.9 %collective-permute-done = bf16[2,192,192]{1,2,0:T(8,128)(2,1)S(1)} collective-permute-done((bf16[2,192,192]{1,2,0:T(8,128)(2,1)S(1)}, bf16[2,192,192]{1,2,0:T(8,128)(2,1)S(1)}, u32[]{:S(2)}, u32[]{:S(2)}) %collective-permute-start) | collective-permute-done | bytes 147488 | tf_op jit(solution)/shard_map/ppermute | solution.py:89
  19.5 5.1 %collective-permute-done.1 = bf16[2,192,192]{1,2,0:T(8,128)(2,1)S(1)} collective-permute-done((bf16[2,192,192]{1,2,0:T(8,128)(2,1)S(1)}, bf16[2,192,192]{1,2,0:T(8,128)(2,1)S(1)}, u32[]{:S(2)}, u32[]{:S(2)}) %collective-permute-start.1) | collective-permute-done | bytes 147488 | tf_op jit(solution)/shard_map/ppermute | solution.py:89
  24.6 1.1 fusion.1
  25.8 49.2 %collective-permute-start.17 = (bf16[2,192,384]{2,1,0:T(8,128)(2,1)S(1)}, bf16[2,192,384]{2,1,0:T(8,128)(2,1)S(1)}, u32[]{:S(2)}, u32[]{:S(2)}) collective-permute-start(bf16[2,192,384]{2,1,0:T(8,128)(2,1)S(1)} %fusion.1), channel_id=1, source_target_pairs={{0,16},{16,0},{1,17},{17,1},{2,18},{18,2},{3,19},{19,3},{4,20},{20... | collective-permute-start | bytes 884744 | tf_op jit(solution)/shard_map/ppermute | solution.py:97
  74.9 7.6 %collective-permute-done.17 = bf16[2,192,384]{2,1,0:T(8,128)(2,1)S(1)} collective-permute-done((bf16[2,192,384]{2,1,0:T(8,128)(2,1)S(1)}, bf16[2,192,384]{2,1,0:T(8,128)(2,1)S(1)}, u32[]{:S(2)}, u32[]{:S(2)}) %collective-permute-start.17) | collective-permute-done | bytes 294944 | tf_op jit(solution)/shard_map/ppermute | solution.py:97
  82.6 0.1 select_bitcast_fusion.1
  82.6 0.9 pad_maximum_fusion
  83.5 0.0 all-gather.2.cloned.1.call-update
  83.5 1.3 collective-permute-start.2
  84.8 1.3 collective-permute-start.9
  86.1 12.5 %collective-permute-done.2 = bf16[2,192,384]{2,1,0:T(8,128)(2,1)S(1)} collective-permute-done((bf16[2,192,384]{2,1,0:T(8,128)(2,1)S(1)}, bf16[2,192,384]{2,1,0:T(8,128)(2,1)S(1)}, u32[]{:S(2)}, u32[]{:S(2)}) %collective-permute-start.2) | collective-permute-done | bytes 294944 | tf_op jit(solution)/shard_map/ppermute | solution.py:30
  98.6 4.1 %collective-permute-start.3 = (bf16[2,192,384]{2,1,0:T(8,128)(2,1)S(1)}, bf16[2,192,384]{2,1,0:T(8,128)(2,1)S(1)}, u32[]{:S(2)}, u32[]{:S(2)}) collective-permute-start(bf16[2,192,384]{2,1,0:T(8,128)(2,1)S(1)} %collective-permute-done.2), channel_id=1, source_target_pairs={{0,64},{64,128},{128,192},{192,256},{256,320},{320,384},{384,448},... | collective-permute-start | bytes 884744 | tf_op jit(solution)/shard_map/ppermute | solution.py:30
  102.7 0.0 collective-permute-done.9
  102.7 1.3 collective-permute-start.10
  104.0 4.6 %collective-permute-done.3 = bf16[2,192,384]{2,1,0:T(8,128)(2,1)S(1)} collective-permute-done((bf16[2,192,384]{2,1,0:T(8,128)(2,1)S(1)}, bf16[2,192,384]{2,1,0:T(8,128)(2,1)S(1)}, u32[]{:S(2)}, u32[]{:S(2)}) %collective-permute-start.3) | collective-permute-done | bytes 294944 | tf_op jit(solution)/shard_map/ppermute | solution.py:30
  108.6 4.1 %collective-permute-start.4 = (bf16[2,192,384]{2,1,0:T(8,128)(2,1)S(1)}, bf16[2,192,384]{2,1,0:T(8,128)(2,1)S(1)}, u32[]{:S(2)}, u32[]{:S(2)}) collective-permute-start(bf16[2,192,384]{2,1,0:T(8,128)(2,1)S(1)} %collective-permute-done.3), channel_id=1, source_target_pairs={{0,64},{64,128},{128,192},{192,256},{256,320},{320,384},{384,448},... | collective-permute-start | bytes 884744 | tf_op jit(solution)/shard_map/ppermute | solution.py:30
  112.7 0.0 collective-permute-done.10
  112.7 1.3 collective-permute-start.11
  114.0 3.6 %collective-permute-done.4 = bf16[2,192,384]{2,1,0:T(8,128)(2,1)S(1)} collective-permute-done((bf16[2,192,384]{2,1,0:T(8,128)(2,1)S(1)}, bf16[2,192,384]{2,1,0:T(8,128)(2,1)S(1)}, u32[]{:S(2)}, u32[]{:S(2)}) %collective-permute-start.4) | collective-permute-done | bytes 294944 | tf_op jit(solution)/shard_map/ppermute | solution.py:30
  117.7 4.2 %collective-permute-start.5 = (bf16[2,192,384]{2,1,0:T(8,128)(2,1)S(1)}, bf16[2,192,384]{2,1,0:T(8,128)(2,1)S(1)}, u32[]{:S(2)}, u32[]{:S(2)}) collective-permute-start(bf16[2,192,384]{2,1,0:T(8,128)(2,1)S(1)} %collective-permute-done.4), channel_id=1, source_target_pairs={{0,64},{64,128},{128,192},{192,256},{256,320},{320,384},{384,448},... | collective-permute-start | bytes 884744 | tf_op jit(solution)/shard_map/ppermute | solution.py:30
  121.9 0.9 collective-permute-done.11
  122.8 1.3 collective-permute-start.12
  124.1 2.0 collective-permute-done.5
  126.1 4.2 %collective-permute-start.6 = (bf16[2,192,384]{2,1,0:T(8,128)(2,1)S(1)}, bf16[2,192,384]{2,1,0:T(8,128)(2,1)S(1)}, u32[]{:S(2)}, u32[]{:S(2)}) collective-permute-start(bf16[2,192,384]{2,1,0:T(8,128)(2,1)S(1)} %collective-permute-done.5), channel_id=1, source_target_pairs={{0,64},{64,128},{128,192},{192,256},{256,320},{320,384},{384,448},... | collective-permute-start | bytes 884744 | tf_op jit(solution)/shard_map/ppermute | solution.py:30
  130.3 0.6 collective-permute-done.12
  130.9 1.3 collective-permute-start.13
  132.2 1.7 collective-permute-done.6
  133.9 4.8 %collective-permute-start.7 = (bf16[2,192,384]{2,1,0:T(8,128)(2,1)S(1)}, bf16[2,192,384]{2,1,0:T(8,128)(2,1)}, u32[]{:S(2)}, u32[]{:S(2)}) collective-permute-start(bf16[2,192,384]{2,1,0:T(8,128)(2,1)S(1)} %collective-permute-done.6), channel_id=1, source_target_pairs={{0,64},{64,128},{128,192},{192,256},{256,320},{320,384},{384,448},... | collective-permute-start | bytes 884744 | tf_op jit(solution)/shard_map/ppermute | solution.py:30
  138.7 1.0 collective-permute-done.13
  139.8 1.3 collective-permute-start.14
  141.1 0.6 collective-permute-done.7
  141.7 6.4 %collective-permute-start.8 = (bf16[2,192,384]{2,1,0:T(8,128)(2,1)}, bf16[2,192,384]{2,1,0:T(8,128)(2,1)}, u32[]{:S(2)}, u32[]{:S(2)}) collective-permute-start(bf16[2,192,384]{2,1,0:T(8,128)(2,1)} %collective-permute-done.7), channel_id=1, source_target_pairs={{0,64},{64,128},{128,192},{192,256},{256,320},{320,384},{384,448},... | collective-permute-start | bytes 884744 | tf_op jit(solution)/shard_map/ppermute | solution.py:30
  148.0 1.1 collective-permute-done.14
  149.1 1.3 collective-permute-start.15
  150.4 0.9 collective-permute-done.8
  151.3 1.0 bitcast_dynamic-update-slice_fusion.14
  152.3 1.0 bitcast_dynamic-update-slice_fusion.13
  154.0 4.7 %collective-permute-done.15 = bf16[2,192,384]{2,1,0:T(8,128)(2,1)S(1)} collective-permute-done((bf16[2,192,384]{2,1,0:T(8,128)(2,1)S(1)}, bf16[2,192,384]{2,1,0:T(8,128)(2,1)S(1)}, u32[]{:S(2)}, u32[]{:S(2)}) %collective-permute-start.15) | collective-permute-done | bytes 294944 | tf_op jit(solution)/shard_map/ppermute | solution.py:31
  158.7 0.0 copy-start
  158.7 2.1 %copy-done = bf16[15,2,192,384]{3,2,1,0:T(8,128)(2,1)} copy-done((bf16[15,2,192,384]{3,2,1,0:T(8,128)(2,1)}, bf16[15,2,192,384]{3,2,1,0:T(8,128)(2,1)S(1)}, u32[]{:S(2)}) %copy-start) | copy-done | bytes 4423704
  160.9 0.2 constant_dynamic-slice_fusion
  161.1 7.3 %collective-permute-start.16 = (bf16[8,2,192,384]{3,2,1,0:T(8,128)(2,1)S(1)}, bf16[8,2,192,384]{3,2,1,0:T(8,128)(2,1)}, u32[]{:S(2)}, u32[]{:S(2)}) collective-permute-start(bf16[8,2,192,384]{3,2,1,0:T(8,128)(2,1)S(1)} %constant_dynamic-slice_fusion), channel_id=1, source_target_pairs={{0,32},{32,0},{1,33},{33,1},{2,34},{34,2},{3,35},{35,3},{4,36},{36... | collective-permute-start | bytes 7077896 | tf_op jit(solution)/shard_map/ppermute | solution.py:36
  168.5 2.0 fusion.2
  170.5 2.3 %collective-permute-done.16 = bf16[8,2,192,384]{3,2,1,0:T(8,128)(2,1)} collective-permute-done((bf16[8,2,192,384]{3,2,1,0:T(8,128)(2,1)S(1)}, bf16[8,2,192,384]{3,2,1,0:T(8,128)(2,1)}, u32[]{:S(2)}, u32[]{:S(2)}) %collective-permute-start.16) | collective-permute-done | bytes 2359328 | tf_op jit(solution)/shard_map/ppermute | solution.py:36
  172.8 3.3 %maximum_select_fusion = bf16[8,2,2,192,384]{4,3,2,0,1:T(8,128)(2,1)S(1)} fusion(bf16[8,1,2,192,384]{4,3,2,0,1:T(8,128)(2,1)} %bitcast.17, bf16[8,1,2,192,384]{4,3,2,0,1:T(8,128)(2,1)S(1)} %fusion.2, pred[]{:T(512)S(6)} %eq.15), kind=kLoop, calls=%fused_computation | loop fusion | flops 7077888 | bytes 9437185 | tf_op jit(solution)/shard_map/jit(_where)/select_n | solution.py:104
  176.1 2.7 %copy.6 = bf16[8,2,2,192,384]{4,3,2,1,0:T(8,128)(2,1)} copy(bf16[8,2,2,192,384]{4,3,2,0,1:T(8,128)(2,1)S(1)} %maximum_select_fusion) | data formatting | bytes 9437184 | tf_op jit(solution)/shard_map/jit(_where)/select_n | solution.py:104
  178.8 9.1 %all-gather.2.cloned.1.call-done.panel_ref = bf16[2,2,3072,384]{3,2,1,0:T(8,128)(2,1)} async-done(((bf16[2,2,192,384]{3,2,1,0:T(8,128)(2,1)}), bf16[2,2,3072,384]{3,2,1,0:T(8,128)(2,1)}) %all-gather.2.cloned.1.call-update) | async-done | bytes 9437200 | tf_op jit(solution)/shard_map/all_gather | solution.py:100
  187.9 12.0 %shard_map.17 = f32[2,192,384]{2,1,0:T(8,128)} custom-call(bf16[16,2,192,384]{3,2,1,0:T(8,128)(2,1)} %bitcast.44, bf16[2,2,3072,384]{3,2,1,0:T(8,128)(2,1)} %all-gather.2.cloned.1.call-done.panel_ref), custom_call_target="tpu_custom_call" | custom-call | flops 3623878656 | bytes 14745600 | tf_op jit(solution)/shard_map/pallas_call | solution.py:60
  (14 shorter events, 0.7 us)
Async XLA Ops:
  6.5 181.3 %all-gather.2.cloned.1.call-start = ((), (), s32[]{:S(2)}) async-start(), calls=%async_computation | async-start | bytes 10027008 | tf_op jit(solution)/shard_map/all_gather | solution.py:100
  7.9 11.7 %collective-permute-start = (bf16[2,192,192]{1,2,0:T(8,128)(2,1)S(1)}, bf16[2,192,192]{1,2,0:T(8,128)(2,1)S(1)}, u32[]{:S(2)}, u32[]{:S(2)}) collective-permute-start(bf16[2,192,192]{1,2,0:T(8,128)(2,1)S(1)} %copy.7), channel_id=1, source_target_pairs={{0,0},{32,2},{64,4},{96,6},{128,8},{160,10},{192,12},{224,14},{256... | collective-permute-start | bytes 442376 | tf_op jit(solution)/shard_map/ppermute | solution.py:89
  14.1 10.5 %collective-permute-start.1 = (bf16[2,192,192]{1,2,0:T(8,128)(2,1)S(1)}, bf16[2,192,192]{1,2,0:T(8,128)(2,1)S(1)}, u32[]{:S(2)}, u32[]{:S(2)}) collective-permute-start(bf16[2,192,192]{1,2,0:T(8,128)(2,1)S(1)} %copy.8), channel_id=1, source_target_pairs={{0,1},{32,3},{64,5},{96,7},{128,9},{160,11},{192,13},{224,15},{256... | collective-permute-start | bytes 442376 | tf_op jit(solution)/shard_map/ppermute | solution.py:89
  25.8 56.8 %collective-permute-start.17 = (bf16[2,192,384]{2,1,0:T(8,128)(2,1)S(1)}, bf16[2,192,384]{2,1,0:T(8,128)(2,1)S(1)}, u32[]{:S(2)}, u32[]{:S(2)}) collective-permute-start(bf16[2,192,384]{2,1,0:T(8,128)(2,1)S(1)} %fusion.1), channel_id=1, source_target_pairs={{0,16},{16,0},{1,17},{17,1},{2,18},{18,2},{3,19},{19,3},{4,20},{20... | collective-permute-start | bytes 884744 | tf_op jit(solution)/shard_map/ppermute | solution.py:97
  83.5 15.1 %collective-permute-start.2 = (bf16[2,192,384]{2,1,0:T(8,128)(2,1)S(1)}, bf16[2,192,384]{2,1,0:T(8,128)(2,1)S(1)}, u32[]{:S(2)}, u32[]{:S(2)}) collective-permute-start(bf16[2,192,384]{2,1,0:T(8,128)(2,1)S(1)} %fusion.1), channel_id=1, source_target_pairs={{0,64},{64,128},{128,192},{192,256},{256,320},{320,384},{384,448},... | collective-permute-start | bytes 884744 | tf_op jit(solution)/shard_map/ppermute | solution.py:30
  84.8 17.9 %collective-permute-start.9 = (bf16[2,192,384]{2,1,0:T(8,128)(2,1)S(1)}, bf16[2,192,384]{2,1,0:T(8,128)(2,1)S(1)}, u32[]{:S(2)}, u32[]{:S(2)}) collective-permute-start(bf16[2,192,384]{2,1,0:T(8,128)(2,1)S(1)} %fusion.1), channel_id=1, source_target_pairs={{64,0},{128,64},{192,128},{256,192},{320,256},{384,320},{448,384},... | collective-permute-start | bytes 884744 | tf_op jit(solution)/shard_map/ppermute | solution.py:31
  98.6 10.0 %collective-permute-start.3 = (bf16[2,192,384]{2,1,0:T(8,128)(2,1)S(1)}, bf16[2,192,384]{2,1,0:T(8,128)(2,1)S(1)}, u32[]{:S(2)}, u32[]{:S(2)}) collective-permute-start(bf16[2,192,384]{2,1,0:T(8,128)(2,1)S(1)} %collective-permute-done.2), channel_id=1, source_target_pairs={{0,64},{64,128},{128,192},{192,256},{256,320},{320,384},{384,448},... | collective-permute-start | bytes 884744 | tf_op jit(solution)/shard_map/ppermute | solution.py:30
  102.7 10.0 %collective-permute-start.10 = (bf16[2,192,384]{2,1,0:T(8,128)(2,1)S(1)}, bf16[2,192,384]{2,1,0:T(8,128)(2,1)S(1)}, u32[]{:S(2)}, u32[]{:S(2)}) collective-permute-start(bf16[2,192,384]{2,1,0:T(8,128)(2,1)S(1)} %collective-permute-done.9), channel_id=1, source_target_pairs={{64,0},{128,64},{192,128},{256,192},{320,256},{384,320},{448,384},... | collective-permute-start | bytes 884744 | tf_op jit(solution)/shard_map/ppermute | solution.py:31
  108.6 9.1 %collective-permute-start.4 = (bf16[2,192,384]{2,1,0:T(8,128)(2,1)S(1)}, bf16[2,192,384]{2,1,0:T(8,128)(2,1)S(1)}, u32[]{:S(2)}, u32[]{:S(2)}) collective-permute-start(bf16[2,192,384]{2,1,0:T(8,128)(2,1)S(1)} %collective-permute-done.3), channel_id=1, source_target_pairs={{0,64},{64,128},{128,192},{192,256},{256,320},{320,384},{384,448},... | collective-permute-start | bytes 884744 | tf_op jit(solution)/shard_map/ppermute | solution.py:30
  112.7 10.0 %collective-permute-start.11 = (bf16[2,192,384]{2,1,0:T(8,128)(2,1)S(1)}, bf16[2,192,384]{2,1,0:T(8,128)(2,1)S(1)}, u32[]{:S(2)}, u32[]{:S(2)}) collective-permute-start(bf16[2,192,384]{2,1,0:T(8,128)(2,1)S(1)} %collective-permute-done.10), channel_id=1, source_target_pairs={{64,0},{128,64},{192,128},{256,192},{320,256},{384,320},{448,384},... | collective-permute-start | bytes 884744 | tf_op jit(solution)/shard_map/ppermute | solution.py:31
  117.7 8.4 %collective-permute-start.5 = (bf16[2,192,384]{2,1,0:T(8,128)(2,1)S(1)}, bf16[2,192,384]{2,1,0:T(8,128)(2,1)S(1)}, u32[]{:S(2)}, u32[]{:S(2)}) collective-permute-start(bf16[2,192,384]{2,1,0:T(8,128)(2,1)S(1)} %collective-permute-done.4), channel_id=1, source_target_pairs={{0,64},{64,128},{128,192},{192,256},{256,320},{320,384},{384,448},... | collective-permute-start | bytes 884744 | tf_op jit(solution)/shard_map/ppermute | solution.py:30
  122.8 8.1 %collective-permute-start.12 = (bf16[2,192,384]{2,1,0:T(8,128)(2,1)S(1)}, bf16[2,192,384]{2,1,0:T(8,128)(2,1)S(1)}, u32[]{:S(2)}, u32[]{:S(2)}) collective-permute-start(bf16[2,192,384]{2,1,0:T(8,128)(2,1)S(1)} %collective-permute-done.11), channel_id=1, source_target_pairs={{64,0},{128,64},{192,128},{256,192},{320,256},{384,320},{448,384},... | collective-permute-start | bytes 884744 | tf_op jit(solution)/shard_map/ppermute | solution.py:31
  126.1 7.9 %collective-permute-start.6 = (bf16[2,192,384]{2,1,0:T(8,128)(2,1)S(1)}, bf16[2,192,384]{2,1,0:T(8,128)(2,1)S(1)}, u32[]{:S(2)}, u32[]{:S(2)}) collective-permute-start(bf16[2,192,384]{2,1,0:T(8,128)(2,1)S(1)} %collective-permute-done.5), channel_id=1, source_target_pairs={{0,64},{64,128},{128,192},{192,256},{256,320},{320,384},{384,448},... | collective-permute-start | bytes 884744 | tf_op jit(solution)/shard_map/ppermute | solution.py:30
  130.9 8.9 %collective-permute-start.13 = (bf16[2,192,384]{2,1,0:T(8,128)(2,1)S(1)}, bf16[2,192,384]{2,1,0:T(8,128)(2,1)S(1)}, u32[]{:S(2)}, u32[]{:S(2)}) collective-permute-start(bf16[2,192,384]{2,1,0:T(8,128)(2,1)S(1)} %collective-permute-done.12), channel_id=1, source_target_pairs={{64,0},{128,64},{192,128},{256,192},{320,256},{384,320},{448,384},... | collective-permute-start | bytes 884744 | tf_op jit(solution)/shard_map/ppermute | solution.py:31
  133.9 7.8 %collective-permute-start.7 = (bf16[2,192,384]{2,1,0:T(8,128)(2,1)S(1)}, bf16[2,192,384]{2,1,0:T(8,128)(2,1)}, u32[]{:S(2)}, u32[]{:S(2)}) collective-permute-start(bf16[2,192,384]{2,1,0:T(8,128)(2,1)S(1)} %collective-permute-done.6), channel_id=1, source_target_pairs={{0,64},{64,128},{128,192},{192,256},{256,320},{320,384},{384,448},... | collective-permute-start | bytes 884744 | tf_op jit(solution)/shard_map/ppermute | solution.py:30
  139.8 9.3 %collective-permute-start.14 = (bf16[2,192,384]{2,1,0:T(8,128)(2,1)S(1)}, bf16[2,192,384]{2,1,0:T(8,128)(2,1)S(1)}, u32[]{:S(2)}, u32[]{:S(2)}) collective-permute-start(bf16[2,192,384]{2,1,0:T(8,128)(2,1)S(1)} %collective-permute-done.13), channel_id=1, source_target_pairs={{64,0},{128,64},{192,128},{256,192},{320,256},{384,320},{448,384},... | collective-permute-start | bytes 884744 | tf_op jit(solution)/shard_map/ppermute | solution.py:31
  141.7 9.6 %collective-permute-start.8 = (bf16[2,192,384]{2,1,0:T(8,128)(2,1)}, bf16[2,192,384]{2,1,0:T(8,128)(2,1)}, u32[]{:S(2)}, u32[]{:S(2)}) collective-permute-start(bf16[2,192,384]{2,1,0:T(8,128)(2,1)} %collective-permute-done.7), channel_id=1, source_target_pairs={{0,64},{64,128},{128,192},{192,256},{256,320},{320,384},{384,448},... | collective-permute-start | bytes 884744 | tf_op jit(solution)/shard_map/ppermute | solution.py:30
  149.1 9.6 %collective-permute-start.15 = (bf16[2,192,384]{2,1,0:T(8,128)(2,1)S(1)}, bf16[2,192,384]{2,1,0:T(8,128)(2,1)S(1)}, u32[]{:S(2)}, u32[]{:S(2)}) collective-permute-start(bf16[2,192,384]{2,1,0:T(8,128)(2,1)S(1)} %collective-permute-done.14), channel_id=1, source_target_pairs={{64,0},{128,64},{192,128},{256,192},{320,256},{384,320},{448,384},... | collective-permute-start | bytes 884744 | tf_op jit(solution)/shard_map/ppermute | solution.py:31
  158.7 2.1 %copy-start = (bf16[15,2,192,384]{3,2,1,0:T(8,128)(2,1)}, bf16[15,2,192,384]{3,2,1,0:T(8,128)(2,1)S(1)}, u32[]{:S(2)}) copy-start(bf16[15,2,192,384]{3,2,1,0:T(8,128)(2,1)S(1)} %bitcast_dynamic-update-slice_fusion) | copy-start | bytes 13271044
  161.1 11.6 %collective-permute-start.16 = (bf16[8,2,192,384]{3,2,1,0:T(8,128)(2,1)S(1)}, bf16[8,2,192,384]{3,2,1,0:T(8,128)(2,1)}, u32[]{:S(2)}, u32[]{:S(2)}) collective-permute-start(bf16[8,2,192,384]{3,2,1,0:T(8,128)(2,1)S(1)} %constant_dynamic-slice_fusion), channel_id=1, source_target_pairs={{0,32},{32,0},{1,33},{33,1},{2,34},{34,2},{3,35},{35,3},{4,36},{36... | collective-permute-start | bytes 7077896 | tf_op jit(solution)/shard_map/ppermute | solution.py:36
Sparse Core Ops, SparseCore 0:
  83.6 104.1 all-gather.1

commit v17 on v16

--- a/solution.py
+++ b/solution.py
@@ -37,15 +37,32 @@
     return mine, other
 
 
-def product_kernel(left_ref, panel_ref, out_ref, acc_ref, *, n_block, width, factor):
-    for half in range(2):
+def product_kernel(left_ref, panel_hbm, out_ref, buffers, copied, acc_ref, *, n_block, width, factor):
+    chunk_rows = n_block * width
+    n_chunks = panel_hbm.shape[2] // chunk_rows
+    chunks = [(half, k) for half in range(2) for k in range(n_chunks)]
+
+    def fetch(index):
+        half, k = chunks[index]
+        return pltpu.make_async_copy(
+            panel_hbm.at[half, :, pl.ds(k * chunk_rows, chunk_rows), :],
+            buffers.at[index % 2],
+            copied.at[index % 2],
+        )
+
+    fetch(0).start()
+    for index, (half, k) in enumerate(chunks):
+        if index + 1 < len(chunks):
+            fetch(index + 1).start()
+        fetch(index).wait()
         for block in range(n_block):
+            lhs_index = (half * n_chunks + k) * n_block + block
             for p in range(2):
-                lhs = left_ref[half * n_block + block, p, :, :]
+                lhs = left_ref[lhs_index, p, :, :]
                 for q in range(2):
-                    rhs = panel_ref[half, q, pl.ds(block * width, width), :]
+                    rhs = buffers[index % 2, q, pl.ds(block * width, width), :]
                     term = jnp.dot(lhs, rhs, preferred_element_type=jnp.float32)
-                    if half == 0 and block == 0:
+                    if index == 0 and block == 0:
                         acc_ref[p, q] = term
                     else:
                         acc_ref[p, q] += term
@@ -56,13 +73,18 @@
 def product(left, panels, factor):
     n_blocks, parts, rows, width = left.shape
     cols = panels.shape[-1]
-    kernel = functools.partial(product_kernel, n_block=n_blocks // 2, width=width, factor=factor)
+    n_block = n_blocks // 4
+    kernel = functools.partial(product_kernel, n_block=n_block, width=width, factor=factor)
     return pl.pallas_call(
         kernel,
         out_shape=jax.ShapeDtypeStruct((2, rows, cols), jnp.float32),
-        in_specs=[pl.BlockSpec(memory_space=pltpu.VMEM)] * 2,
+        in_specs=[pl.BlockSpec(memory_space=pltpu.VMEM), pl.BlockSpec(memory_space=pl.ANY)],
         out_specs=pl.BlockSpec(memory_space=pltpu.VMEM),
-        scratch_shapes=[pltpu.VMEM((2, 2, rows, cols), jnp.float32)],
+        scratch_shapes=[
+            pltpu.VMEM((2, parts, n_block * width, cols), panels.dtype),
+            pltpu.SemaphoreType.DMA((2,)),
+            pltpu.VMEM((2, 2, rows, cols), jnp.float32),
+        ],
         cost_estimate=pl.CostEstimate(
             flops=2 * 4 * rows * cols * width * n_blocks,
             transcendentals=0,

time: 208 us -> 207 us (level)
  no operation moved by 1% of the time
where the time goes in v17:
time: 207 us; the launch traced here: 206 us
  starting transfers between devices  103 us (50%)
  waiting for transfers between devices  61.1 us (30%)
  between operations  13.7 us (7%)
  local copies, waits for them, and re-layouts  11.2 us (5%)
  Pallas kernels  11.2 us (5%)
  other arithmetic  5.41 us (3%)
    ppermute x1, starting transfers between devices, local(): partner_block = lax.ppermute(symmetric, 'zh', [(0, 1), (1, 0)])  49.2 us
    ppermute x7, starting transfers between devices, gather_line(): lax.ppermute(rightward, 'zl', [(k, k + 1) for k in range(n_line - 1)])  29.2 us
    ppermute x7, waiting for transfers between devices, gather_line(): lax.ppermute(rightward, 'zl', [(k, k + 1) for k in range(n_line - 1)])  25.9 us
    pallas_call x1, Pallas kernels, product(): pl.pallas_call(kernel, out_shape=jax.ShapeDtypeStruct((2, rows, cols), jn...  11.2 us
    all_gather x1, waiting for transfers between devices, local(): lax.all_gather(jnp.stack([top, bottom]), ('y', 'x'), axis=2, tiled=True)  9.05 us
    ppermute x7, starting transfers between devices, gather_line(): lax.ppermute(leftward, 'zl', [(k + 1, k) for k in range(n_line - 1)])  9 us
    ppermute x2, starting transfers between devices, local(): lax.ppermute(piece, axes, mirror_pairs(n_recv, n_shot, flip))  8.58 us
    ppermute x7, waiting for transfers between devices, gather_line(): lax.ppermute(leftward, 'zl', [(k + 1, k) for k in range(n_line - 1)])  8.31 us
  transfers between devices with their start and end apart: 19, of which 17 were waited for; matrix products, arithmetic and copies ran while one was open for 5% of the time, Pallas kernels for 0%

profile of v17, /device:TPU:1, one launch (start us, length us, event | category | flops | bytes accessed | tf_op | source)
XLA Modules:
  0.0 206.0 jit_solution(10417525841844150579)
XLA Ops:
  6.5 0.0 all-gather.2.cloned.1.call-start
  6.5 1.2 constant_dynamic-slice_fusion.2
  7.7 0.1 copy.7
  7.9 6.0 %collective-permute-start = (bf16[2,192,192]{1,2,0:T(8,128)(2,1)S(1)}, bf16[2,192,192]{1,2,0:T(8,128)(2,1)S(1)}, u32[]{:S(2)}, u32[]{:S(2)}) collective-permute-start(bf16[2,192,192]{1,2,0:T(8,128)(2,1)S(1)} %copy.7), channel_id=1, source_target_pairs={{0,0},{32,2},{64,4},{96,6},{128,8},{160,10},{192,12},{224,14},{256... | collective-permute-start | bytes 442376 | tf_op jit(solution)/shard_map/ppermute | solution.py:111
  13.9 0.1 copy.8
  14.1 2.5 %collective-permute-start.1 = (bf16[2,192,192]{1,2,0:T(8,128)(2,1)S(1)}, bf16[2,192,192]{1,2,0:T(8,128)(2,1)S(1)}, u32[]{:S(2)}, u32[]{:S(2)}) collective-permute-start(bf16[2,192,192]{1,2,0:T(8,128)(2,1)S(1)} %copy.8), channel_id=1, source_target_pairs={{0,1},{32,3},{64,5},{96,7},{128,9},{160,11},{192,13},{224,15},{256... | collective-permute-start | bytes 442376 | tf_op jit(solution)/shard_map/ppermute | solution.py:111
  16.6 2.9 %collective-permute-done = bf16[2,192,192]{1,2,0:T(8,128)(2,1)S(1)} collective-permute-done((bf16[2,192,192]{1,2,0:T(8,128)(2,1)S(1)}, bf16[2,192,192]{1,2,0:T(8,128)(2,1)S(1)}, u32[]{:S(2)}, u32[]{:S(2)}) %collective-permute-start) | collective-permute-done | bytes 147488 | tf_op jit(solution)/shard_map/ppermute | solution.py:111
  19.5 5.1 %collective-permute-done.1 = bf16[2,192,192]{1,2,0:T(8,128)(2,1)S(1)} collective-permute-done((bf16[2,192,192]{1,2,0:T(8,128)(2,1)S(1)}, bf16[2,192,192]{1,2,0:T(8,128)(2,1)S(1)}, u32[]{:S(2)}, u32[]{:S(2)}) %collective-permute-start.1) | collective-permute-done | bytes 147488 | tf_op jit(solution)/shard_map/ppermute | solution.py:111
  24.6 1.1 fusion.1
  25.8 49.2 %collective-permute-start.17 = (bf16[2,192,384]{2,1,0:T(8,128)(2,1)S(1)}, bf16[2,192,384]{2,1,0:T(8,128)(2,1)S(1)}, u32[]{:S(2)}, u32[]{:S(2)}) collective-permute-start(bf16[2,192,384]{2,1,0:T(8,128)(2,1)S(1)} %fusion.1), channel_id=1, source_target_pairs={{0,16},{16,0},{1,17},{17,1},{2,18},{18,2},{3,19},{19,3},{4,20},{20... | collective-permute-start | bytes 884744 | tf_op jit(solution)/shard_map/ppermute | solution.py:119
  74.9 7.6 %collective-permute-done.17 = bf16[2,192,384]{2,1,0:T(8,128)(2,1)S(1)} collective-permute-done((bf16[2,192,384]{2,1,0:T(8,128)(2,1)S(1)}, bf16[2,192,384]{2,1,0:T(8,128)(2,1)S(1)}, u32[]{:S(2)}, u32[]{:S(2)}) %collective-permute-start.17) | collective-permute-done | bytes 294944 | tf_op jit(solution)/shard_map/ppermute | solution.py:119
  82.6 0.1 select_bitcast_fusion.1
  82.6 0.9 pad_maximum_fusion
  83.5 0.0 all-gather.2.cloned.1.call-update
  83.5 1.3 collective-permute-start.2
  84.8 1.3 collective-permute-start.9
  86.1 12.5 %collective-permute-done.2 = bf16[2,192,384]{2,1,0:T(8,128)(2,1)S(1)} collective-permute-done((bf16[2,192,384]{2,1,0:T(8,128)(2,1)S(1)}, bf16[2,192,384]{2,1,0:T(8,128)(2,1)S(1)}, u32[]{:S(2)}, u32[]{:S(2)}) %collective-permute-start.2) | collective-permute-done | bytes 294944 | tf_op jit(solution)/shard_map/ppermute | solution.py:30
  98.6 4.1 %collective-permute-start.3 = (bf16[2,192,384]{2,1,0:T(8,128)(2,1)S(1)}, bf16[2,192,384]{2,1,0:T(8,128)(2,1)S(1)}, u32[]{:S(2)}, u32[]{:S(2)}) collective-permute-start(bf16[2,192,384]{2,1,0:T(8,128)(2,1)S(1)} %collective-permute-done.2), channel_id=1, source_target_pairs={{0,64},{64,128},{128,192},{192,256},{256,320},{320,384},{384,448},... | collective-permute-start | bytes 884744 | tf_op jit(solution)/shard_map/ppermute | solution.py:30
  102.7 0.0 collective-permute-done.9
  102.7 1.3 collective-permute-start.10
  104.0 4.6 %collective-permute-done.3 = bf16[2,192,384]{2,1,0:T(8,128)(2,1)S(1)} collective-permute-done((bf16[2,192,384]{2,1,0:T(8,128)(2,1)S(1)}, bf16[2,192,384]{2,1,0:T(8,128)(2,1)S(1)}, u32[]{:S(2)}, u32[]{:S(2)}) %collective-permute-start.3) | collective-permute-done | bytes 294944 | tf_op jit(solution)/shard_map/ppermute | solution.py:30
  108.6 4.1 %collective-permute-start.4 = (bf16[2,192,384]{2,1,0:T(8,128)(2,1)S(1)}, bf16[2,192,384]{2,1,0:T(8,128)(2,1)S(1)}, u32[]{:S(2)}, u32[]{:S(2)}) collective-permute-start(bf16[2,192,384]{2,1,0:T(8,128)(2,1)S(1)} %collective-permute-done.3), channel_id=1, source_target_pairs={{0,64},{64,128},{128,192},{192,256},{256,320},{320,384},{384,448},... | collective-permute-start | bytes 884744 | tf_op jit(solution)/shard_map/ppermute | solution.py:30
  112.7 0.0 collective-permute-done.10
  112.7 1.3 collective-permute-start.11
  114.0 3.6 %collective-permute-done.4 = bf16[2,192,384]{2,1,0:T(8,128)(2,1)S(1)} collective-permute-done((bf16[2,192,384]{2,1,0:T(8,128)(2,1)S(1)}, bf16[2,192,384]{2,1,0:T(8,128)(2,1)S(1)}, u32[]{:S(2)}, u32[]{:S(2)}) %collective-permute-start.4) | collective-permute-done | bytes 294944 | tf_op jit(solution)/shard_map/ppermute | solution.py:30
  117.7 4.2 %collective-permute-start.5 = (bf16[2,192,384]{2,1,0:T(8,128)(2,1)S(1)}, bf16[2,192,384]{2,1,0:T(8,128)(2,1)S(1)}, u32[]{:S(2)}, u32[]{:S(2)}) collective-permute-start(bf16[2,192,384]{2,1,0:T(8,128)(2,1)S(1)} %collective-permute-done.4), channel_id=1, source_target_pairs={{0,64},{64,128},{128,192},{192,256},{256,320},{320,384},{384,448},... | collective-permute-start | bytes 884744 | tf_op jit(solution)/shard_map/ppermute | solution.py:30
  121.9 0.9 collective-permute-done.11
  122.8 1.3 collective-permute-start.12
  124.1 2.0 collective-permute-done.5
  126.1 4.2 %collective-permute-start.6 = (bf16[2,192,384]{2,1,0:T(8,128)(2,1)S(1)}, bf16[2,192,384]{2,1,0:T(8,128)(2,1)S(1)}, u32[]{:S(2)}, u32[]{:S(2)}) collective-permute-start(bf16[2,192,384]{2,1,0:T(8,128)(2,1)S(1)} %collective-permute-done.5), channel_id=1, source_target_pairs={{0,64},{64,128},{128,192},{192,256},{256,320},{320,384},{384,448},... | collective-permute-start | bytes 884744 | tf_op jit(solution)/shard_map/ppermute | solution.py:30
  130.3 0.6 collective-permute-done.12
  130.9 1.3 collective-permute-start.13
  132.2 1.7 collective-permute-done.6
  133.9 4.8 %collective-permute-start.7 = (bf16[2,192,384]{2,1,0:T(8,128)(2,1)S(1)}, bf16[2,192,384]{2,1,0:T(8,128)(2,1)}, u32[]{:S(2)}, u32[]{:S(2)}) collective-permute-start(bf16[2,192,384]{2,1,0:T(8,128)(2,1)S(1)} %collective-permute-done.6), channel_id=1, source_target_pairs={{0,64},{64,128},{128,192},{192,256},{256,320},{320,384},{384,448},... | collective-permute-start | bytes 884744 | tf_op jit(solution)/shard_map/ppermute | solution.py:30
  138.7 1.0 collective-permute-done.13
  139.8 1.3 collective-permute-start.14
  141.1 0.6 collective-permute-done.7
  141.7 6.4 %collective-permute-start.8 = (bf16[2,192,384]{2,1,0:T(8,128)(2,1)}, bf16[2,192,384]{2,1,0:T(8,128)(2,1)}, u32[]{:S(2)}, u32[]{:S(2)}) collective-permute-start(bf16[2,192,384]{2,1,0:T(8,128)(2,1)} %collective-permute-done.7), channel_id=1, source_target_pairs={{0,64},{64,128},{128,192},{192,256},{256,320},{320,384},{384,448},... | collective-permute-start | bytes 884744 | tf_op jit(solution)/shard_map/ppermute | solution.py:30
  148.0 1.1 collective-permute-done.14
  149.1 1.3 collective-permute-start.15
  150.4 0.9 collective-permute-done.8
  151.3 1.0 bitcast_dynamic-update-slice_fusion.14
  152.3 1.0 bitcast_dynamic-update-slice_fusion.13
  154.0 4.7 %collective-permute-done.15 = bf16[2,192,384]{2,1,0:T(8,128)(2,1)S(1)} collective-permute-done((bf16[2,192,384]{2,1,0:T(8,128)(2,1)S(1)}, bf16[2,192,384]{2,1,0:T(8,128)(2,1)S(1)}, u32[]{:S(2)}, u32[]{:S(2)}) %collective-permute-start.15) | collective-permute-done | bytes 294944 | tf_op jit(solution)/shard_map/ppermute | solution.py:31
  158.7 0.0 copy-start
  158.7 2.1 %copy-done = bf16[15,2,192,384]{3,2,1,0:T(8,128)(2,1)} copy-done((bf16[15,2,192,384]{3,2,1,0:T(8,128)(2,1)}, bf16[15,2,192,384]{3,2,1,0:T(8,128)(2,1)S(1)}, u32[]{:S(2)}) %copy-start) | copy-done | bytes 4423704
  160.9 0.2 constant_dynamic-slice_fusion
  161.1 7.3 %collective-permute-start.16 = (bf16[8,2,192,384]{3,2,1,0:T(8,128)(2,1)S(1)}, bf16[8,2,192,384]{3,2,1,0:T(8,128)(2,1)}, u32[]{:S(2)}, u32[]{:S(2)}) collective-permute-start(bf16[8,2,192,384]{3,2,1,0:T(8,128)(2,1)S(1)} %constant_dynamic-slice_fusion), channel_id=1, source_target_pairs={{0,32},{32,0},{1,33},{33,1},{2,34},{34,2},{3,35},{35,3},{4,36},{36... | collective-permute-start | bytes 7077896 | tf_op jit(solution)/shard_map/ppermute | solution.py:36
  168.5 2.0 fusion.2
  170.5 2.3 %collective-permute-done.16 = bf16[8,2,192,384]{3,2,1,0:T(8,128)(2,1)} collective-permute-done((bf16[8,2,192,384]{3,2,1,0:T(8,128)(2,1)S(1)}, bf16[8,2,192,384]{3,2,1,0:T(8,128)(2,1)}, u32[]{:S(2)}, u32[]{:S(2)}) %collective-permute-start.16) | collective-permute-done | bytes 2359328 | tf_op jit(solution)/shard_map/ppermute | solution.py:36
  172.8 3.3 %maximum_select_fusion = bf16[8,2,2,192,384]{4,3,2,0,1:T(8,128)(2,1)S(1)} fusion(bf16[8,1,2,192,384]{4,3,2,0,1:T(8,128)(2,1)} %bitcast.17, bf16[8,1,2,192,384]{4,3,2,0,1:T(8,128)(2,1)S(1)} %fusion.2, pred[]{:T(512)S(6)} %eq.15), kind=kLoop, calls=%fused_computation | loop fusion | flops 7077888 | bytes 9437185 | tf_op jit(solution)/shard_map/jit(_where)/select_n | solution.py:126
  176.1 2.7 %copy.6 = bf16[8,2,2,192,384]{4,3,2,1,0:T(8,128)(2,1)} copy(bf16[8,2,2,192,384]{4,3,2,0,1:T(8,128)(2,1)S(1)} %maximum_select_fusion) | data formatting | bytes 9437184 | tf_op jit(solution)/shard_map/jit(_where)/select_n | solution.py:126
  178.8 9.1 %all-gather.2.cloned.1.call-done.panel_hbm = bf16[2,2,3072,384]{3,2,1,0:T(8,128)(2,1)} async-done(((bf16[2,2,192,384]{3,2,1,0:T(8,128)(2,1)}), bf16[2,2,3072,384]{3,2,1,0:T(8,128)(2,1)}) %all-gather.2.cloned.1.call-update) | async-done | bytes 9437200 | tf_op jit(solution)/shard_map/all_gather | solution.py:122
  187.9 11.2 %shard_map.17 = f32[2,192,384]{2,1,0:T(8,128)} custom-call(bf16[16,2,192,384]{3,2,1,0:T(8,128)(2,1)} %bitcast.44, bf16[2,2,3072,384]{3,2,1,0:T(8,128)(2,1)} %all-gather.2.cloned.1.call-done.panel_hbm), custom_call_target="tpu_custom_call" | custom-call | flops 3623878656 | bytes 14745600 | tf_op jit(solution)/shard_map/pallas_call | solution.py:78
  (14 shorter events, 0.7 us)
Async XLA Ops:
  6.5 181.3 %all-gather.2.cloned.1.call-start = ((), (), s32[]{:S(2)}) async-start(), calls=%async_computation | async-start | bytes 10027008 | tf_op jit(solution)/shard_map/all_gather | solution.py:122
  7.9 11.7 %collective-permute-start = (bf16[2,192,192]{1,2,0:T(8,128)(2,1)S(1)}, bf16[2,192,192]{1,2,0:T(8,128)(2,1)S(1)}, u32[]{:S(2)}, u32[]{:S(2)}) collective-permute-start(bf16[2,192,192]{1,2,0:T(8,128)(2,1)S(1)} %copy.7), channel_id=1, source_target_pairs={{0,0},{32,2},{64,4},{96,6},{128,8},{160,10},{192,12},{224,14},{256... | collective-permute-start | bytes 442376 | tf_op jit(solution)/shard_map/ppermute | solution.py:111
  14.1 10.5 %collective-permute-start.1 = (bf16[2,192,192]{1,2,0:T(8,128)(2,1)S(1)}, bf16[2,192,192]{1,2,0:T(8,128)(2,1)S(1)}, u32[]{:S(2)}, u32[]{:S(2)}) collective-permute-start(bf16[2,192,192]{1,2,0:T(8,128)(2,1)S(1)} %copy.8), channel_id=1, source_target_pairs={{0,1},{32,3},{64,5},{96,7},{128,9},{160,11},{192,13},{224,15},{256... | collective-permute-start | bytes 442376 | tf_op jit(solution)/shard_map/ppermute | solution.py:111
  25.8 56.8 %collective-permute-start.17 = (bf16[2,192,384]{2,1,0:T(8,128)(2,1)S(1)}, bf16[2,192,384]{2,1,0:T(8,128)(2,1)S(1)}, u32[]{:S(2)}, u32[]{:S(2)}) collective-permute-start(bf16[2,192,384]{2,1,0:T(8,128)(2,1)S(1)} %fusion.1), channel_id=1, source_target_pairs={{0,16},{16,0},{1,17},{17,1},{2,18},{18,2},{3,19},{19,3},{4,20},{20... | collective-permute-start | bytes 884744 | tf_op jit(solution)/shard_map/ppermute | solution.py:119
  83.5 15.1 %collective-permute-start.2 = (bf16[2,192,384]{2,1,0:T(8,128)(2,1)S(1)}, bf16[2,192,384]{2,1,0:T(8,128)(2,1)S(1)}, u32[]{:S(2)}, u32[]{:S(2)}) collective-permute-start(bf16[2,192,384]{2,1,0:T(8,128)(2,1)S(1)} %fusion.1), channel_id=1, source_target_pairs={{0,64},{64,128},{128,192},{192,256},{256,320},{320,384},{384,448},... | collective-permute-start | bytes 884744 | tf_op jit(solution)/shard_map/ppermute | solution.py:30
  84.8 17.9 %collective-permute-start.9 = (bf16[2,192,384]{2,1,0:T(8,128)(2,1)S(1)}, bf16[2,192,384]{2,1,0:T(8,128)(2,1)S(1)}, u32[]{:S(2)}, u32[]{:S(2)}) collective-permute-start(bf16[2,192,384]{2,1,0:T(8,128)(2,1)S(1)} %fusion.1), channel_id=1, source_target_pairs={{64,0},{128,64},{192,128},{256,192},{320,256},{384,320},{448,384},... | collective-permute-start | bytes 884744 | tf_op jit(solution)/shard_map/ppermute | solution.py:31
  98.6 10.0 %collective-permute-start.3 = (bf16[2,192,384]{2,1,0:T(8,128)(2,1)S(1)}, bf16[2,192,384]{2,1,0:T(8,128)(2,1)S(1)}, u32[]{:S(2)}, u32[]{:S(2)}) collective-permute-start(bf16[2,192,384]{2,1,0:T(8,128)(2,1)S(1)} %collective-permute-done.2), channel_id=1, source_target_pairs={{0,64},{64,128},{128,192},{192,256},{256,320},{320,384},{384,448},... | collective-permute-start | bytes 884744 | tf_op jit(solution)/shard_map/ppermute | solution.py:30
  102.7 10.0 %collective-permute-start.10 = (bf16[2,192,384]{2,1,0:T(8,128)(2,1)S(1)}, bf16[2,192,384]{2,1,0:T(8,128)(2,1)S(1)}, u32[]{:S(2)}, u32[]{:S(2)}) collective-permute-start(bf16[2,192,384]{2,1,0:T(8,128)(2,1)S(1)} %collective-permute-done.9), channel_id=1, source_target_pairs={{64,0},{128,64},{192,128},{256,192},{320,256},{384,320},{448,384},... | collective-permute-start | bytes 884744 | tf_op jit(solution)/shard_map/ppermute | solution.py:31
  108.6 9.1 %collective-permute-start.4 = (bf16[2,192,384]{2,1,0:T(8,128)(2,1)S(1)}, bf16[2,192,384]{2,1,0:T(8,128)(2,1)S(1)}, u32[]{:S(2)}, u32[]{:S(2)}) collective-permute-start(bf16[2,192,384]{2,1,0:T(8,128)(2,1)S(1)} %collective-permute-done.3), channel_id=1, source_target_pairs={{0,64},{64,128},{128,192},{192,256},{256,320},{320,384},{384,448},... | collective-permute-start | bytes 884744 | tf_op jit(solution)/shard_map/ppermute | solution.py:30
  112.7 10.0 %collective-permute-start.11 = (bf16[2,192,384]{2,1,0:T(8,128)(2,1)S(1)}, bf16[2,192,384]{2,1,0:T(8,128)(2,1)S(1)}, u32[]{:S(2)}, u32[]{:S(2)}) collective-permute-start(bf16[2,192,384]{2,1,0:T(8,128)(2,1)S(1)} %collective-permute-done.10), channel_id=1, source_target_pairs={{64,0},{128,64},{192,128},{256,192},{320,256},{384,320},{448,384},... | collective-permute-start | bytes 884744 | tf_op jit(solution)/shard_map/ppermute | solution.py:31
  117.7 8.4 %collective-permute-start.5 = (bf16[2,192,384]{2,1,0:T(8,128)(2,1)S(1)}, bf16[2,192,384]{2,1,0:T(8,128)(2,1)S(1)}, u32[]{:S(2)}, u32[]{:S(2)}) collective-permute-start(bf16[2,192,384]{2,1,0:T(8,128)(2,1)S(1)} %collective-permute-done.4), channel_id=1, source_target_pairs={{0,64},{64,128},{128,192},{192,256},{256,320},{320,384},{384,448},... | collective-permute-start | bytes 884744 | tf_op jit(solution)/shard_map/ppermute | solution.py:30
  122.8 8.1 %collective-permute-start.12 = (bf16[2,192,384]{2,1,0:T(8,128)(2,1)S(1)}, bf16[2,192,384]{2,1,0:T(8,128)(2,1)S(1)}, u32[]{:S(2)}, u32[]{:S(2)}) collective-permute-start(bf16[2,192,384]{2,1,0:T(8,128)(2,1)S(1)} %collective-permute-done.11), channel_id=1, source_target_pairs={{64,0},{128,64},{192,128},{256,192},{320,256},{384,320},{448,384},... | collective-permute-start | bytes 884744 | tf_op jit(solution)/shard_map/ppermute | solution.py:31
  126.1 7.9 %collective-permute-start.6 = (bf16[2,192,384]{2,1,0:T(8,128)(2,1)S(1)}, bf16[2,192,384]{2,1,0:T(8,128)(2,1)S(1)}, u32[]{:S(2)}, u32[]{:S(2)}) collective-permute-start(bf16[2,192,384]{2,1,0:T(8,128)(2,1)S(1)} %collective-permute-done.5), channel_id=1, source_target_pairs={{0,64},{64,128},{128,192},{192,256},{256,320},{320,384},{384,448},... | collective-permute-start | bytes 884744 | tf_op jit(solution)/shard_map/ppermute | solution.py:30
  130.9 8.9 %collective-permute-start.13 = (bf16[2,192,384]{2,1,0:T(8,128)(2,1)S(1)}, bf16[2,192,384]{2,1,0:T(8,128)(2,1)S(1)}, u32[]{:S(2)}, u32[]{:S(2)}) collective-permute-start(bf16[2,192,384]{2,1,0:T(8,128)(2,1)S(1)} %collective-permute-done.12), channel_id=1, source_target_pairs={{64,0},{128,64},{192,128},{256,192},{320,256},{384,320},{448,384},... | collective-permute-start | bytes 884744 | tf_op jit(solution)/shard_map/ppermute | solution.py:31
  133.9 7.8 %collective-permute-start.7 = (bf16[2,192,384]{2,1,0:T(8,128)(2,1)S(1)}, bf16[2,192,384]{2,1,0:T(8,128)(2,1)}, u32[]{:S(2)}, u32[]{:S(2)}) collective-permute-start(bf16[2,192,384]{2,1,0:T(8,128)(2,1)S(1)} %collective-permute-done.6), channel_id=1, source_target_pairs={{0,64},{64,128},{128,192},{192,256},{256,320},{320,384},{384,448},... | collective-permute-start | bytes 884744 | tf_op jit(solution)/shard_map/ppermute | solution.py:30
  139.8 9.3 %collective-permute-start.14 = (bf16[2,192,384]{2,1,0:T(8,128)(2,1)S(1)}, bf16[2,192,384]{2,1,0:T(8,128)(2,1)S(1)}, u32[]{:S(2)}, u32[]{:S(2)}) collective-permute-start(bf16[2,192,384]{2,1,0:T(8,128)(2,1)S(1)} %collective-permute-done.13), channel_id=1, source_target_pairs={{64,0},{128,64},{192,128},{256,192},{320,256},{384,320},{448,384},... | collective-permute-start | bytes 884744 | tf_op jit(solution)/shard_map/ppermute | solution.py:31
  141.7 9.6 %collective-permute-start.8 = (bf16[2,192,384]{2,1,0:T(8,128)(2,1)}, bf16[2,192,384]{2,1,0:T(8,128)(2,1)}, u32[]{:S(2)}, u32[]{:S(2)}) collective-permute-start(bf16[2,192,384]{2,1,0:T(8,128)(2,1)} %collective-permute-done.7), channel_id=1, source_target_pairs={{0,64},{64,128},{128,192},{192,256},{256,320},{320,384},{384,448},... | collective-permute-start | bytes 884744 | tf_op jit(solution)/shard_map/ppermute | solution.py:30
  149.1 9.6 %collective-permute-start.15 = (bf16[2,192,384]{2,1,0:T(8,128)(2,1)S(1)}, bf16[2,192,384]{2,1,0:T(8,128)(2,1)S(1)}, u32[]{:S(2)}, u32[]{:S(2)}) collective-permute-start(bf16[2,192,384]{2,1,0:T(8,128)(2,1)S(1)} %collective-permute-done.14), channel_id=1, source_target_pairs={{64,0},{128,64},{192,128},{256,192},{320,256},{384,320},{448,384},... | collective-permute-start | bytes 884744 | tf_op jit(solution)/shard_map/ppermute | solution.py:31
  158.7 2.1 %copy-start = (bf16[15,2,192,384]{3,2,1,0:T(8,128)(2,1)}, bf16[15,2,192,384]{3,2,1,0:T(8,128)(2,1)S(1)}, u32[]{:S(2)}) copy-start(bf16[15,2,192,384]{3,2,1,0:T(8,128)(2,1)S(1)} %bitcast_dynamic-update-slice_fusion) | copy-start | bytes 13271044
  161.1 11.6 %collective-permute-start.16 = (bf16[8,2,192,384]{3,2,1,0:T(8,128)(2,1)S(1)}, bf16[8,2,192,384]{3,2,1,0:T(8,128)(2,1)}, u32[]{:S(2)}, u32[]{:S(2)}) collective-permute-start(bf16[8,2,192,384]{3,2,1,0:T(8,128)(2,1)S(1)} %constant_dynamic-slice_fusion), channel_id=1, source_target_pairs={{0,32},{32,0},{1,33},{33,1},{2,34},{34,2},{3,35},{35,3},{4,36},{36... | collective-permute-start | bytes 7077896 | tf_op jit(solution)/shard_map/ppermute | solution.py:36
Sparse Core Ops, SparseCore 0:
  83.6 104.1 all-gather.1

commit v18 on v17

--- a/solution.py
+++ b/solution.py
@@ -57,17 +57,17 @@
         fetch(index).wait()
         for block in range(n_block):
             lhs_index = (half * n_chunks + k) * n_block + block
-            for p in range(2):
-                lhs = left_ref[lhs_index, p, :, :]
-                for q in range(2):
-                    rhs = buffers[index % 2, q, pl.ds(block * width, width), :]
-                    term = jnp.dot(lhs, rhs, preferred_element_type=jnp.float32)
-                    if index == 0 and block == 0:
-                        acc_ref[p, q] = term
-                    else:
-                        acc_ref[p, q] += term
-    out_ref[0, :, :] = (acc_ref[0, 0] - acc_ref[1, 1]) * factor
-    out_ref[1, :, :] = (acc_ref[0, 1] + acc_ref[1, 0]) * factor
+            lhs = left_ref[lhs_index].reshape(-1, left_ref.shape[-1])
+            for q in range(2):
+                rhs = buffers[index % 2, q, pl.ds(block * width, width), :]
+                term = jnp.dot(lhs, rhs, preferred_element_type=jnp.float32)
+                if index == 0 and block == 0:
+                    acc_ref[q] = term
+                else:
+                    acc_ref[q] += term
+    rows = out_ref.shape[1]
+    out_ref[0, :, :] = (acc_ref[0, :rows] - acc_ref[1, rows:]) * factor
+    out_ref[1, :, :] = (acc_ref[1, :rows] + acc_ref[0, rows:]) * factor
 
 
 def product(left, panels, factor):
@@ -83,7 +83,7 @@
         scratch_shapes=[
             pltpu.VMEM((2, parts, n_block * width, cols), panels.dtype),
             pltpu.SemaphoreType.DMA((2,)),
-            pltpu.VMEM((2, 2, rows, cols), jnp.float32),
+            pltpu.VMEM((2, parts * rows, cols), jnp.float32),
         ],
         cost_estimate=pl.CostEstimate(
             flops=2 * 4 * rows * cols * width * n_blocks,

time: 207 us -> 208 us (level)
  no operation moved by 1% of the time
where the time goes in v18:
time: 208 us; the launch traced here: 207 us
  starting transfers between devices  103 us (50%)
  waiting for transfers between devices  61.1 us (29%)
  between operations  13.7 us (7%)
  Pallas kernels  12 us (6%)
  local copies, waits for them, and re-layouts  11.2 us (5%)
  other arithmetic  5.41 us (3%)
    ppermute x1, starting transfers between devices, local(): partner_block = lax.ppermute(symmetric, 'zh', [(0, 1), (1, 0)])  49.2 us
    ppermute x7, starting transfers between devices, gather_line(): lax.ppermute(rightward, 'zl', [(k, k + 1) for k in range(n_line - 1)])  29.2 us
    ppermute x7, waiting for transfers between devices, gather_line(): lax.ppermute(rightward, 'zl', [(k, k + 1) for k in range(n_line - 1)])  25.9 us
    pallas_call x1, Pallas kernels, product(): pl.pallas_call(kernel, out_shape=jax.ShapeDtypeStruct((2, rows, cols), jn...  12 us
    all_gather x1, waiting for transfers between devices, local(): lax.all_gather(jnp.stack([top, bottom]), ('y', 'x'), axis=2, tiled=True)  9.05 us
    ppermute x7, starting transfers between devices, gather_line(): lax.ppermute(leftward, 'zl', [(k + 1, k) for k in range(n_line - 1)])  9 us
    ppermute x2, starting transfers between devices, local(): lax.ppermute(piece, axes, mirror_pairs(n_recv, n_shot, flip))  8.58 us
    ppermute x7, waiting for transfers between devices, gather_line(): lax.ppermute(leftward, 'zl', [(k + 1, k) for k in range(n_line - 1)])  8.31 us
  transfers between devices with their start and end apart: 19, of which 17 were waited for; matrix products, arithmetic and copies ran while one was open for 5% of the time, Pallas kernels for 0%

profile of v18, /device:TPU:1, one launch (start us, length us, event | category | flops | bytes accessed | tf_op | source)
XLA Modules:
  0.0 206.7 jit_solution(15264715534234516586)
XLA Ops:
  6.5 0.0 all-gather.2.cloned.1.call-start
  6.5 1.2 constant_dynamic-slice_fusion.2
  7.7 0.1 copy.7
  7.9 6.0 %collective-permute-start = (bf16[2,192,192]{1,2,0:T(8,128)(2,1)S(1)}, bf16[2,192,192]{1,2,0:T(8,128)(2,1)S(1)}, u32[]{:S(2)}, u32[]{:S(2)}) collective-permute-start(bf16[2,192,192]{1,2,0:T(8,128)(2,1)S(1)} %copy.7), channel_id=1, source_target_pairs={{0,0},{32,2},{64,4},{96,6},{128,8},{160,10},{192,12},{224,14},{256... | collective-permute-start | bytes 442376 | tf_op jit(solution)/shard_map/ppermute | solution.py:111
  13.9 0.1 copy.8
  14.1 2.5 %collective-permute-start.1 = (bf16[2,192,192]{1,2,0:T(8,128)(2,1)S(1)}, bf16[2,192,192]{1,2,0:T(8,128)(2,1)S(1)}, u32[]{:S(2)}, u32[]{:S(2)}) collective-permute-start(bf16[2,192,192]{1,2,0:T(8,128)(2,1)S(1)} %copy.8), channel_id=1, source_target_pairs={{0,1},{32,3},{64,5},{96,7},{128,9},{160,11},{192,13},{224,15},{256... | collective-permute-start | bytes 442376 | tf_op jit(solution)/shard_map/ppermute | solution.py:111
  16.6 2.9 %collective-permute-done = bf16[2,192,192]{1,2,0:T(8,128)(2,1)S(1)} collective-permute-done((bf16[2,192,192]{1,2,0:T(8,128)(2,1)S(1)}, bf16[2,192,192]{1,2,0:T(8,128)(2,1)S(1)}, u32[]{:S(2)}, u32[]{:S(2)}) %collective-permute-start) | collective-permute-done | bytes 147488 | tf_op jit(solution)/shard_map/ppermute | solution.py:111
  19.5 5.1 %collective-permute-done.1 = bf16[2,192,192]{1,2,0:T(8,128)(2,1)S(1)} collective-permute-done((bf16[2,192,192]{1,2,0:T(8,128)(2,1)S(1)}, bf16[2,192,192]{1,2,0:T(8,128)(2,1)S(1)}, u32[]{:S(2)}, u32[]{:S(2)}) %collective-permute-start.1) | collective-permute-done | bytes 147488 | tf_op jit(solution)/shard_map/ppermute | solution.py:111
  24.6 1.1 fusion.1
  25.8 49.2 %collective-permute-start.17 = (bf16[2,192,384]{2,1,0:T(8,128)(2,1)S(1)}, bf16[2,192,384]{2,1,0:T(8,128)(2,1)S(1)}, u32[]{:S(2)}, u32[]{:S(2)}) collective-permute-start(bf16[2,192,384]{2,1,0:T(8,128)(2,1)S(1)} %fusion.1), channel_id=1, source_target_pairs={{0,16},{16,0},{1,17},{17,1},{2,18},{18,2},{3,19},{19,3},{4,20},{20... | collective-permute-start | bytes 884744 | tf_op jit(solution)/shard_map/ppermute | solution.py:119
  74.9 7.6 %collective-permute-done.17 = bf16[2,192,384]{2,1,0:T(8,128)(2,1)S(1)} collective-permute-done((bf16[2,192,384]{2,1,0:T(8,128)(2,1)S(1)}, bf16[2,192,384]{2,1,0:T(8,128)(2,1)S(1)}, u32[]{:S(2)}, u32[]{:S(2)}) %collective-permute-start.17) | collective-permute-done | bytes 294944 | tf_op jit(solution)/shard_map/ppermute | solution.py:119
  82.6 0.1 select_bitcast_fusion.1
  82.6 0.9 pad_maximum_fusion
  83.5 0.0 all-gather.2.cloned.1.call-update
  83.5 1.3 collective-permute-start.2
  84.8 1.3 collective-permute-start.9
  86.1 12.5 %collective-permute-done.2 = bf16[2,192,384]{2,1,0:T(8,128)(2,1)S(1)} collective-permute-done((bf16[2,192,384]{2,1,0:T(8,128)(2,1)S(1)}, bf16[2,192,384]{2,1,0:T(8,128)(2,1)S(1)}, u32[]{:S(2)}, u32[]{:S(2)}) %collective-permute-start.2) | collective-permute-done | bytes 294944 | tf_op jit(solution)/shard_map/ppermute | solution.py:30
  98.6 4.1 %collective-permute-start.3 = (bf16[2,192,384]{2,1,0:T(8,128)(2,1)S(1)}, bf16[2,192,384]{2,1,0:T(8,128)(2,1)S(1)}, u32[]{:S(2)}, u32[]{:S(2)}) collective-permute-start(bf16[2,192,384]{2,1,0:T(8,128)(2,1)S(1)} %collective-permute-done.2), channel_id=1, source_target_pairs={{0,64},{64,128},{128,192},{192,256},{256,320},{320,384},{384,448},... | collective-permute-start | bytes 884744 | tf_op jit(solution)/shard_map/ppermute | solution.py:30
  102.7 0.0 collective-permute-done.9
  102.7 1.3 collective-permute-start.10
  104.0 4.6 %collective-permute-done.3 = bf16[2,192,384]{2,1,0:T(8,128)(2,1)S(1)} collective-permute-done((bf16[2,192,384]{2,1,0:T(8,128)(2,1)S(1)}, bf16[2,192,384]{2,1,0:T(8,128)(2,1)S(1)}, u32[]{:S(2)}, u32[]{:S(2)}) %collective-permute-start.3) | collective-permute-done | bytes 294944 | tf_op jit(solution)/shard_map/ppermute | solution.py:30
  108.6 4.1 %collective-permute-start.4 = (bf16[2,192,384]{2,1,0:T(8,128)(2,1)S(1)}, bf16[2,192,384]{2,1,0:T(8,128)(2,1)S(1)}, u32[]{:S(2)}, u32[]{:S(2)}) collective-permute-start(bf16[2,192,384]{2,1,0:T(8,128)(2,1)S(1)} %collective-permute-done.3), channel_id=1, source_target_pairs={{0,64},{64,128},{128,192},{192,256},{256,320},{320,384},{384,448},... | collective-permute-start | bytes 884744 | tf_op jit(solution)/shard_map/ppermute | solution.py:30
  112.7 0.0 collective-permute-done.10
  112.7 1.3 collective-permute-start.11
  114.0 3.6 %collective-permute-done.4 = bf16[2,192,384]{2,1,0:T(8,128)(2,1)S(1)} collective-permute-done((bf16[2,192,384]{2,1,0:T(8,128)(2,1)S(1)}, bf16[2,192,384]{2,1,0:T(8,128)(2,1)S(1)}, u32[]{:S(2)}, u32[]{:S(2)}) %collective-permute-start.4) | collective-permute-done | bytes 294944 | tf_op jit(solution)/shard_map/ppermute | solution.py:30
  117.7 4.2 %collective-permute-start.5 = (bf16[2,192,384]{2,1,0:T(8,128)(2,1)S(1)}, bf16[2,192,384]{2,1,0:T(8,128)(2,1)S(1)}, u32[]{:S(2)}, u32[]{:S(2)}) collective-permute-start(bf16[2,192,384]{2,1,0:T(8,128)(2,1)S(1)} %collective-permute-done.4), channel_id=1, source_target_pairs={{0,64},{64,128},{128,192},{192,256},{256,320},{320,384},{384,448},... | collective-permute-start | bytes 884744 | tf_op jit(solution)/shard_map/ppermute | solution.py:30
  121.9 0.9 collective-permute-done.11
  122.8 1.3 collective-permute-start.12
  124.1 2.0 collective-permute-done.5
  126.1 4.2 %collective-permute-start.6 = (bf16[2,192,384]{2,1,0:T(8,128)(2,1)S(1)}, bf16[2,192,384]{2,1,0:T(8,128)(2,1)S(1)}, u32[]{:S(2)}, u32[]{:S(2)}) collective-permute-start(bf16[2,192,384]{2,1,0:T(8,128)(2,1)S(1)} %collective-permute-done.5), channel_id=1, source_target_pairs={{0,64},{64,128},{128,192},{192,256},{256,320},{320,384},{384,448},... | collective-permute-start | bytes 884744 | tf_op jit(solution)/shard_map/ppermute | solution.py:30
  130.3 0.6 collective-permute-done.12
  130.9 1.3 collective-permute-start.13
  132.2 1.7 collective-permute-done.6
  133.9 4.8 %collective-permute-start.7 = (bf16[2,192,384]{2,1,0:T(8,128)(2,1)S(1)}, bf16[2,192,384]{2,1,0:T(8,128)(2,1)}, u32[]{:S(2)}, u32[]{:S(2)}) collective-permute-start(bf16[2,192,384]{2,1,0:T(8,128)(2,1)S(1)} %collective-permute-done.6), channel_id=1, source_target_pairs={{0,64},{64,128},{128,192},{192,256},{256,320},{320,384},{384,448},... | collective-permute-start | bytes 884744 | tf_op jit(solution)/shard_map/ppermute | solution.py:30
  138.7 1.0 collective-permute-done.13
  139.8 1.3 collective-permute-start.14
  141.1 0.6 collective-permute-done.7
  141.7 6.4 %collective-permute-start.8 = (bf16[2,192,384]{2,1,0:T(8,128)(2,1)}, bf16[2,192,384]{2,1,0:T(8,128)(2,1)}, u32[]{:S(2)}, u32[]{:S(2)}) collective-permute-start(bf16[2,192,384]{2,1,0:T(8,128)(2,1)} %collective-permute-done.7), channel_id=1, source_target_pairs={{0,64},{64,128},{128,192},{192,256},{256,320},{320,384},{384,448},... | collective-permute-start | bytes 884744 | tf_op jit(solution)/shard_map/ppermute | solution.py:30
  148.0 1.1 collective-permute-done.14
  149.1 1.3 collective-permute-start.15
  150.4 0.9 collective-permute-done.8
  151.3 1.0 bitcast_dynamic-update-slice_fusion.14
  152.3 1.0 bitcast_dynamic-update-slice_fusion.13
  154.0 4.7 %collective-permute-done.15 = bf16[2,192,384]{2,1,0:T(8,128)(2,1)S(1)} collective-permute-done((bf16[2,192,384]{2,1,0:T(8,128)(2,1)S(1)}, bf16[2,192,384]{2,1,0:T(8,128)(2,1)S(1)}, u32[]{:S(2)}, u32[]{:S(2)}) %collective-permute-start.15) | collective-permute-done | bytes 294944 | tf_op jit(solution)/shard_map/ppermute | solution.py:31
  158.7 0.0 copy-start
  158.7 2.1 %copy-done = bf16[15,2,192,384]{3,2,1,0:T(8,128)(2,1)} copy-done((bf16[15,2,192,384]{3,2,1,0:T(8,128)(2,1)}, bf16[15,2,192,384]{3,2,1,0:T(8,128)(2,1)S(1)}, u32[]{:S(2)}) %copy-start) | copy-done | bytes 4423704
  160.9 0.2 constant_dynamic-slice_fusion
  161.1 7.3 %collective-permute-start.16 = (bf16[8,2,192,384]{3,2,1,0:T(8,128)(2,1)S(1)}, bf16[8,2,192,384]{3,2,1,0:T(8,128)(2,1)}, u32[]{:S(2)}, u32[]{:S(2)}) collective-permute-start(bf16[8,2,192,384]{3,2,1,0:T(8,128)(2,1)S(1)} %constant_dynamic-slice_fusion), channel_id=1, source_target_pairs={{0,32},{32,0},{1,33},{33,1},{2,34},{34,2},{3,35},{35,3},{4,36},{36... | collective-permute-start | bytes 7077896 | tf_op jit(solution)/shard_map/ppermute | solution.py:36
  168.5 2.0 fusion.2
  170.5 2.3 %collective-permute-done.16 = bf16[8,2,192,384]{3,2,1,0:T(8,128)(2,1)} collective-permute-done((bf16[8,2,192,384]{3,2,1,0:T(8,128)(2,1)S(1)}, bf16[8,2,192,384]{3,2,1,0:T(8,128)(2,1)}, u32[]{:S(2)}, u32[]{:S(2)}) %collective-permute-start.16) | collective-permute-done | bytes 2359328 | tf_op jit(solution)/shard_map/ppermute | solution.py:36
  172.8 3.3 %maximum_select_fusion = bf16[8,2,2,192,384]{4,3,2,0,1:T(8,128)(2,1)S(1)} fusion(bf16[8,1,2,192,384]{4,3,2,0,1:T(8,128)(2,1)} %bitcast.17, bf16[8,1,2,192,384]{4,3,2,0,1:T(8,128)(2,1)S(1)} %fusion.2, pred[]{:T(512)S(6)} %eq.15), kind=kLoop, calls=%fused_computation | loop fusion | flops 7077888 | bytes 9437185 | tf_op jit(solution)/shard_map/jit(_where)/select_n | solution.py:126
  176.1 2.7 %copy.6 = bf16[8,2,2,192,384]{4,3,2,1,0:T(8,128)(2,1)} copy(bf16[8,2,2,192,384]{4,3,2,0,1:T(8,128)(2,1)S(1)} %maximum_select_fusion) | data formatting | bytes 9437184 | tf_op jit(solution)/shard_map/jit(_where)/select_n | solution.py:126
  178.8 9.1 %all-gather.2.cloned.1.call-done.panel_hbm = bf16[2,2,3072,384]{3,2,1,0:T(8,128)(2,1)} async-done(((bf16[2,2,192,384]{3,2,1,0:T(8,128)(2,1)}), bf16[2,2,3072,384]{3,2,1,0:T(8,128)(2,1)}) %all-gather.2.cloned.1.call-update) | async-done | bytes 9437200 | tf_op jit(solution)/shard_map/all_gather | solution.py:122
  187.9 12.0 %shard_map.17 = f32[2,192,384]{2,1,0:T(8,128)} custom-call(bf16[16,2,192,384]{3,2,1,0:T(8,128)(2,1)} %bitcast.44, bf16[2,2,3072,384]{3,2,1,0:T(8,128)(2,1)} %all-gather.2.cloned.1.call-done.panel_hbm), custom_call_target="tpu_custom_call" | custom-call | flops 3623878656 | bytes 14745600 | tf_op jit(solution)/shard_map/pallas_call | solution.py:78
  (14 shorter events, 0.7 us)
Async XLA Ops:
  6.5 181.3 %all-gather.2.cloned.1.call-start = ((), (), s32[]{:S(2)}) async-start(), calls=%async_computation | async-start | bytes 10027008 | tf_op jit(solution)/shard_map/all_gather | solution.py:122
  7.9 11.7 %collective-permute-start = (bf16[2,192,192]{1,2,0:T(8,128)(2,1)S(1)}, bf16[2,192,192]{1,2,0:T(8,128)(2,1)S(1)}, u32[]{:S(2)}, u32[]{:S(2)}) collective-permute-start(bf16[2,192,192]{1,2,0:T(8,128)(2,1)S(1)} %copy.7), channel_id=1, source_target_pairs={{0,0},{32,2},{64,4},{96,6},{128,8},{160,10},{192,12},{224,14},{256... | collective-permute-start | bytes 442376 | tf_op jit(solution)/shard_map/ppermute | solution.py:111
  14.1 10.5 %collective-permute-start.1 = (bf16[2,192,192]{1,2,0:T(8,128)(2,1)S(1)}, bf16[2,192,192]{1,2,0:T(8,128)(2,1)S(1)}, u32[]{:S(2)}, u32[]{:S(2)}) collective-permute-start(bf16[2,192,192]{1,2,0:T(8,128)(2,1)S(1)} %copy.8), channel_id=1, source_target_pairs={{0,1},{32,3},{64,5},{96,7},{128,9},{160,11},{192,13},{224,15},{256... | collective-permute-start | bytes 442376 | tf_op jit(solution)/shard_map/ppermute | solution.py:111
  25.8 56.8 %collective-permute-start.17 = (bf16[2,192,384]{2,1,0:T(8,128)(2,1)S(1)}, bf16[2,192,384]{2,1,0:T(8,128)(2,1)S(1)}, u32[]{:S(2)}, u32[]{:S(2)}) collective-permute-start(bf16[2,192,384]{2,1,0:T(8,128)(2,1)S(1)} %fusion.1), channel_id=1, source_target_pairs={{0,16},{16,0},{1,17},{17,1},{2,18},{18,2},{3,19},{19,3},{4,20},{20... | collective-permute-start | bytes 884744 | tf_op jit(solution)/shard_map/ppermute | solution.py:119
  83.5 15.1 %collective-permute-start.2 = (bf16[2,192,384]{2,1,0:T(8,128)(2,1)S(1)}, bf16[2,192,384]{2,1,0:T(8,128)(2,1)S(1)}, u32[]{:S(2)}, u32[]{:S(2)}) collective-permute-start(bf16[2,192,384]{2,1,0:T(8,128)(2,1)S(1)} %fusion.1), channel_id=1, source_target_pairs={{0,64},{64,128},{128,192},{192,256},{256,320},{320,384},{384,448},... | collective-permute-start | bytes 884744 | tf_op jit(solution)/shard_map/ppermute | solution.py:30
  84.8 17.9 %collective-permute-start.9 = (bf16[2,192,384]{2,1,0:T(8,128)(2,1)S(1)}, bf16[2,192,384]{2,1,0:T(8,128)(2,1)S(1)}, u32[]{:S(2)}, u32[]{:S(2)}) collective-permute-start(bf16[2,192,384]{2,1,0:T(8,128)(2,1)S(1)} %fusion.1), channel_id=1, source_target_pairs={{64,0},{128,64},{192,128},{256,192},{320,256},{384,320},{448,384},... | collective-permute-start | bytes 884744 | tf_op jit(solution)/shard_map/ppermute | solution.py:31
  98.6 10.0 %collective-permute-start.3 = (bf16[2,192,384]{2,1,0:T(8,128)(2,1)S(1)}, bf16[2,192,384]{2,1,0:T(8,128)(2,1)S(1)}, u32[]{:S(2)}, u32[]{:S(2)}) collective-permute-start(bf16[2,192,384]{2,1,0:T(8,128)(2,1)S(1)} %collective-permute-done.2), channel_id=1, source_target_pairs={{0,64},{64,128},{128,192},{192,256},{256,320},{320,384},{384,448},... | collective-permute-start | bytes 884744 | tf_op jit(solution)/shard_map/ppermute | solution.py:30
  102.7 10.0 %collective-permute-start.10 = (bf16[2,192,384]{2,1,0:T(8,128)(2,1)S(1)}, bf16[2,192,384]{2,1,0:T(8,128)(2,1)S(1)}, u32[]{:S(2)}, u32[]{:S(2)}) collective-permute-start(bf16[2,192,384]{2,1,0:T(8,128)(2,1)S(1)} %collective-permute-done.9), channel_id=1, source_target_pairs={{64,0},{128,64},{192,128},{256,192},{320,256},{384,320},{448,384},... | collective-permute-start | bytes 884744 | tf_op jit(solution)/shard_map/ppermute | solution.py:31
  108.6 9.1 %collective-permute-start.4 = (bf16[2,192,384]{2,1,0:T(8,128)(2,1)S(1)}, bf16[2,192,384]{2,1,0:T(8,128)(2,1)S(1)}, u32[]{:S(2)}, u32[]{:S(2)}) collective-permute-start(bf16[2,192,384]{2,1,0:T(8,128)(2,1)S(1)} %collective-permute-done.3), channel_id=1, source_target_pairs={{0,64},{64,128},{128,192},{192,256},{256,320},{320,384},{384,448},... | collective-permute-start | bytes 884744 | tf_op jit(solution)/shard_map/ppermute | solution.py:30
  112.7 10.0 %collective-permute-start.11 = (bf16[2,192,384]{2,1,0:T(8,128)(2,1)S(1)}, bf16[2,192,384]{2,1,0:T(8,128)(2,1)S(1)}, u32[]{:S(2)}, u32[]{:S(2)}) collective-permute-start(bf16[2,192,384]{2,1,0:T(8,128)(2,1)S(1)} %collective-permute-done.10), channel_id=1, source_target_pairs={{64,0},{128,64},{192,128},{256,192},{320,256},{384,320},{448,384},... | collective-permute-start | bytes 884744 | tf_op jit(solution)/shard_map/ppermute | solution.py:31
  117.7 8.4 %collective-permute-start.5 = (bf16[2,192,384]{2,1,0:T(8,128)(2,1)S(1)}, bf16[2,192,384]{2,1,0:T(8,128)(2,1)S(1)}, u32[]{:S(2)}, u32[]{:S(2)}) collective-permute-start(bf16[2,192,384]{2,1,0:T(8,128)(2,1)S(1)} %collective-permute-done.4), channel_id=1, source_target_pairs={{0,64},{64,128},{128,192},{192,256},{256,320},{320,384},{384,448},... | collective-permute-start | bytes 884744 | tf_op jit(solution)/shard_map/ppermute | solution.py:30
  122.8 8.1 %collective-permute-start.12 = (bf16[2,192,384]{2,1,0:T(8,128)(2,1)S(1)}, bf16[2,192,384]{2,1,0:T(8,128)(2,1)S(1)}, u32[]{:S(2)}, u32[]{:S(2)}) collective-permute-start(bf16[2,192,384]{2,1,0:T(8,128)(2,1)S(1)} %collective-permute-done.11), channel_id=1, source_target_pairs={{64,0},{128,64},{192,128},{256,192},{320,256},{384,320},{448,384},... | collective-permute-start | bytes 884744 | tf_op jit(solution)/shard_map/ppermute | solution.py:31
  126.1 7.9 %collective-permute-start.6 = (bf16[2,192,384]{2,1,0:T(8,128)(2,1)S(1)}, bf16[2,192,384]{2,1,0:T(8,128)(2,1)S(1)}, u32[]{:S(2)}, u32[]{:S(2)}) collective-permute-start(bf16[2,192,384]{2,1,0:T(8,128)(2,1)S(1)} %collective-permute-done.5), channel_id=1, source_target_pairs={{0,64},{64,128},{128,192},{192,256},{256,320},{320,384},{384,448},... | collective-permute-start | bytes 884744 | tf_op jit(solution)/shard_map/ppermute | solution.py:30
  130.9 8.9 %collective-permute-start.13 = (bf16[2,192,384]{2,1,0:T(8,128)(2,1)S(1)}, bf16[2,192,384]{2,1,0:T(8,128)(2,1)S(1)}, u32[]{:S(2)}, u32[]{:S(2)}) collective-permute-start(bf16[2,192,384]{2,1,0:T(8,128)(2,1)S(1)} %collective-permute-done.12), channel_id=1, source_target_pairs={{64,0},{128,64},{192,128},{256,192},{320,256},{384,320},{448,384},... | collective-permute-start | bytes 884744 | tf_op jit(solution)/shard_map/ppermute | solution.py:31
  133.9 7.8 %collective-permute-start.7 = (bf16[2,192,384]{2,1,0:T(8,128)(2,1)S(1)}, bf16[2,192,384]{2,1,0:T(8,128)(2,1)}, u32[]{:S(2)}, u32[]{:S(2)}) collective-permute-start(bf16[2,192,384]{2,1,0:T(8,128)(2,1)S(1)} %collective-permute-done.6), channel_id=1, source_target_pairs={{0,64},{64,128},{128,192},{192,256},{256,320},{320,384},{384,448},... | collective-permute-start | bytes 884744 | tf_op jit(solution)/shard_map/ppermute | solution.py:30
  139.8 9.3 %collective-permute-start.14 = (bf16[2,192,384]{2,1,0:T(8,128)(2,1)S(1)}, bf16[2,192,384]{2,1,0:T(8,128)(2,1)S(1)}, u32[]{:S(2)}, u32[]{:S(2)}) collective-permute-start(bf16[2,192,384]{2,1,0:T(8,128)(2,1)S(1)} %collective-permute-done.13), channel_id=1, source_target_pairs={{64,0},{128,64},{192,128},{256,192},{320,256},{384,320},{448,384},... | collective-permute-start | bytes 884744 | tf_op jit(solution)/shard_map/ppermute | solution.py:31
  141.7 9.6 %collective-permute-start.8 = (bf16[2,192,384]{2,1,0:T(8,128)(2,1)}, bf16[2,192,384]{2,1,0:T(8,128)(2,1)}, u32[]{:S(2)}, u32[]{:S(2)}) collective-permute-start(bf16[2,192,384]{2,1,0:T(8,128)(2,1)} %collective-permute-done.7), channel_id=1, source_target_pairs={{0,64},{64,128},{128,192},{192,256},{256,320},{320,384},{384,448},... | collective-permute-start | bytes 884744 | tf_op jit(solution)/shard_map/ppermute | solution.py:30
  149.1 9.6 %collective-permute-start.15 = (bf16[2,192,384]{2,1,0:T(8,128)(2,1)S(1)}, bf16[2,192,384]{2,1,0:T(8,128)(2,1)S(1)}, u32[]{:S(2)}, u32[]{:S(2)}) collective-permute-start(bf16[2,192,384]{2,1,0:T(8,128)(2,1)S(1)} %collective-permute-done.14), channel_id=1, source_target_pairs={{64,0},{128,64},{192,128},{256,192},{320,256},{384,320},{448,384},... | collective-permute-start | bytes 884744 | tf_op jit(solution)/shard_map/ppermute | solution.py:31
  158.7 2.1 %copy-start = (bf16[15,2,192,384]{3,2,1,0:T(8,128)(2,1)}, bf16[15,2,192,384]{3,2,1,0:T(8,128)(2,1)S(1)}, u32[]{:S(2)}) copy-start(bf16[15,2,192,384]{3,2,1,0:T(8,128)(2,1)S(1)} %bitcast_dynamic-update-slice_fusion) | copy-start | bytes 13271044
  161.1 11.6 %collective-permute-start.16 = (bf16[8,2,192,384]{3,2,1,0:T(8,128)(2,1)S(1)}, bf16[8,2,192,384]{3,2,1,0:T(8,128)(2,1)}, u32[]{:S(2)}, u32[]{:S(2)}) collective-permute-start(bf16[8,2,192,384]{3,2,1,0:T(8,128)(2,1)S(1)} %constant_dynamic-slice_fusion), channel_id=1, source_target_pairs={{0,32},{32,0},{1,33},{33,1},{2,34},{34,2},{3,35},{35,3},{4,36},{36... | collective-permute-start | bytes 7077896 | tf_op jit(solution)/shard_map/ppermute | solution.py:36
Sparse Core Ops, SparseCore 0:
  83.6 104.1 all-gather.1

commit v19 on v17

--- a/solution.py
+++ b/solution.py
@@ -37,28 +37,35 @@
     return mine, other
 
 
-def product_kernel(left_ref, panel_hbm, out_ref, buffers, copied, acc_ref, *, n_block, width, factor):
+def product_kernel(left_hbm, panel_hbm, out_ref, lefts, buffers, copied, acc_ref, *, n_block, width, factor):
     chunk_rows = n_block * width
     n_chunks = panel_hbm.shape[2] // chunk_rows
     chunks = [(half, k) for half in range(2) for k in range(n_chunks)]
 
     def fetch(index):
         half, k = chunks[index]
-        return pltpu.make_async_copy(
-            panel_hbm.at[half, :, pl.ds(k * chunk_rows, chunk_rows), :],
-            buffers.at[index % 2],
-            copied.at[index % 2],
+        return (
+            pltpu.make_async_copy(
+                panel_hbm.at[half, :, pl.ds(k * chunk_rows, chunk_rows), :],
+                buffers.at[index % 2],
+                copied.at[0, index % 2],
+            ),
+            pltpu.make_async_copy(
+                left_hbm.at[pl.ds(index * n_block, n_block)], lefts.at[index % 2], copied.at[1, index % 2]
+            ),
         )
 
-    fetch(0).start()
+    for copy in fetch(0):
+        copy.start()
     for index, (half, k) in enumerate(chunks):
         if index + 1 < len(chunks):
-            fetch(index + 1).start()
-        fetch(index).wait()
+            for copy in fetch(index + 1):
+                copy.start()
+        for copy in fetch(index):
+            copy.wait()
         for block in range(n_block):
-            lhs_index = (half * n_chunks + k) * n_block + block
             for p in range(2):
-                lhs = left_ref[lhs_index, p, :, :]
+                lhs = lefts[index % 2, block, p, :, :]
                 for q in range(2):
                     rhs = buffers[index % 2, q, pl.ds(block * width, width), :]
                     term = jnp.dot(lhs, rhs, preferred_element_type=jnp.float32)
@@ -78,11 +85,12 @@
     return pl.pallas_call(
         kernel,
         out_shape=jax.ShapeDtypeStruct((2, rows, cols), jnp.float32),
-        in_specs=[pl.BlockSpec(memory_space=pltpu.VMEM), pl.BlockSpec(memory_space=pl.ANY)],
+        in_specs=[pl.BlockSpec(memory_space=pl.ANY), pl.BlockSpec(memory_space=pl.ANY)],
         out_specs=pl.BlockSpec(memory_space=pltpu.VMEM),
         scratch_shapes=[
+            pltpu.VMEM((2, n_block, parts, rows, width), left.dtype),
             pltpu.VMEM((2, parts, n_block * width, cols), panels.dtype),
-            pltpu.SemaphoreType.DMA((2,)),
+            pltpu.SemaphoreType.DMA((2, 2)),
             pltpu.VMEM((2, 2, rows, cols), jnp.float32),
         ],
         cost_estimate=pl.CostEstimate(

time: 207 us -> 205 us (level)
  no operation moved by 1% of the time
where the time goes in v19:
time: 205 us; the launch traced here: 204 us
  starting transfers between devices  103 us (50%)
  waiting for transfers between devices  61.1 us (30%)
  between operations  13.7 us (7%)
  local copies, waits for them, and re-layouts  11.2 us (5%)
  Pallas kernels  9.6 us (5%)
  other arithmetic  5.41 us (3%)
    ppermute x1, starting transfers between devices, local(): partner_block = lax.ppermute(symmetric, 'zh', [(0, 1), (1, 0)])  49.2 us
    ppermute x7, starting transfers between devices, gather_line(): lax.ppermute(rightward, 'zl', [(k, k + 1) for k in range(n_line - 1)])  29.2 us
    ppermute x7, waiting for transfers between devices, gather_line(): lax.ppermute(rightward, 'zl', [(k, k + 1) for k in range(n_line - 1)])  25.9 us
    pallas_call x1, Pallas kernels, product(): pl.pallas_call(kernel, out_shape=jax.ShapeDtypeStruct((2, rows, cols), jn...  9.6 us
    all_gather x1, waiting for transfers between devices, local(): lax.all_gather(jnp.stack([top, bottom]), ('y', 'x'), axis=2, tiled=True)  9.05 us
    ppermute x7, starting transfers between devices, gather_line(): lax.ppermute(leftward, 'zl', [(k + 1, k) for k in range(n_line - 1)])  9 us
    ppermute x2, starting transfers between devices, local(): lax.ppermute(piece, axes, mirror_pairs(n_recv, n_shot, flip))  8.58 us
    ppermute x7, waiting for transfers between devices, gather_line(): lax.ppermute(leftward, 'zl', [(k + 1, k) for k in range(n_line - 1)])  8.31 us
  transfers between devices with their start and end apart: 19, of which 17 were waited for; matrix products, arithmetic and copies ran while one was open for 5% of the time, Pallas kernels for 0%

profile of v19, /device:TPU:1, one launch (start us, length us, event | category | flops | bytes accessed | tf_op | source)
XLA Modules:
  0.0 204.3 jit_solution(2706770297006851196)
XLA Ops:
  6.5 0.0 all-gather.2.cloned.1.call-start
  6.5 1.2 constant_dynamic-slice_fusion.2
  7.7 0.1 copy.7
  7.9 6.0 %collective-permute-start = (bf16[2,192,192]{1,2,0:T(8,128)(2,1)S(1)}, bf16[2,192,192]{1,2,0:T(8,128)(2,1)S(1)}, u32[]{:S(2)}, u32[]{:S(2)}) collective-permute-start(bf16[2,192,192]{1,2,0:T(8,128)(2,1)S(1)} %copy.7), channel_id=1, source_target_pairs={{0,0},{32,2},{64,4},{96,6},{128,8},{160,10},{192,12},{224,14},{256... | collective-permute-start | bytes 442376 | tf_op jit(solution)/shard_map/ppermute | solution.py:119
  13.9 0.1 copy.8
  14.1 2.5 %collective-permute-start.1 = (bf16[2,192,192]{1,2,0:T(8,128)(2,1)S(1)}, bf16[2,192,192]{1,2,0:T(8,128)(2,1)S(1)}, u32[]{:S(2)}, u32[]{:S(2)}) collective-permute-start(bf16[2,192,192]{1,2,0:T(8,128)(2,1)S(1)} %copy.8), channel_id=1, source_target_pairs={{0,1},{32,3},{64,5},{96,7},{128,9},{160,11},{192,13},{224,15},{256... | collective-permute-start | bytes 442376 | tf_op jit(solution)/shard_map/ppermute | solution.py:119
  16.6 2.9 %collective-permute-done = bf16[2,192,192]{1,2,0:T(8,128)(2,1)S(1)} collective-permute-done((bf16[2,192,192]{1,2,0:T(8,128)(2,1)S(1)}, bf16[2,192,192]{1,2,0:T(8,128)(2,1)S(1)}, u32[]{:S(2)}, u32[]{:S(2)}) %collective-permute-start) | collective-permute-done | bytes 147488 | tf_op jit(solution)/shard_map/ppermute | solution.py:119
  19.5 5.1 %collective-permute-done.1 = bf16[2,192,192]{1,2,0:T(8,128)(2,1)S(1)} collective-permute-done((bf16[2,192,192]{1,2,0:T(8,128)(2,1)S(1)}, bf16[2,192,192]{1,2,0:T(8,128)(2,1)S(1)}, u32[]{:S(2)}, u32[]{:S(2)}) %collective-permute-start.1) | collective-permute-done | bytes 147488 | tf_op jit(solution)/shard_map/ppermute | solution.py:119
  24.6 1.1 fusion.1
  25.8 49.2 %collective-permute-start.17 = (bf16[2,192,384]{2,1,0:T(8,128)(2,1)S(1)}, bf16[2,192,384]{2,1,0:T(8,128)(2,1)S(1)}, u32[]{:S(2)}, u32[]{:S(2)}) collective-permute-start(bf16[2,192,384]{2,1,0:T(8,128)(2,1)S(1)} %fusion.1), channel_id=1, source_target_pairs={{0,16},{16,0},{1,17},{17,1},{2,18},{18,2},{3,19},{19,3},{4,20},{20... | collective-permute-start | bytes 884744 | tf_op jit(solution)/shard_map/ppermute | solution.py:127
  74.9 7.6 %collective-permute-done.17 = bf16[2,192,384]{2,1,0:T(8,128)(2,1)S(1)} collective-permute-done((bf16[2,192,384]{2,1,0:T(8,128)(2,1)S(1)}, bf16[2,192,384]{2,1,0:T(8,128)(2,1)S(1)}, u32[]{:S(2)}, u32[]{:S(2)}) %collective-permute-start.17) | collective-permute-done | bytes 294944 | tf_op jit(solution)/shard_map/ppermute | solution.py:127
  82.6 0.1 select_bitcast_fusion.1
  82.6 0.9 pad_maximum_fusion
  83.5 0.0 all-gather.2.cloned.1.call-update
  83.5 1.3 collective-permute-start.2
  84.8 1.3 collective-permute-start.9
  86.1 12.5 %collective-permute-done.2 = bf16[2,192,384]{2,1,0:T(8,128)(2,1)S(1)} collective-permute-done((bf16[2,192,384]{2,1,0:T(8,128)(2,1)S(1)}, bf16[2,192,384]{2,1,0:T(8,128)(2,1)S(1)}, u32[]{:S(2)}, u32[]{:S(2)}) %collective-permute-start.2) | collective-permute-done | bytes 294944 | tf_op jit(solution)/shard_map/ppermute | solution.py:30
  98.6 4.1 %collective-permute-start.3 = (bf16[2,192,384]{2,1,0:T(8,128)(2,1)S(1)}, bf16[2,192,384]{2,1,0:T(8,128)(2,1)S(1)}, u32[]{:S(2)}, u32[]{:S(2)}) collective-permute-start(bf16[2,192,384]{2,1,0:T(8,128)(2,1)S(1)} %collective-permute-done.2), channel_id=1, source_target_pairs={{0,64},{64,128},{128,192},{192,256},{256,320},{320,384},{384,448},... | collective-permute-start | bytes 884744 | tf_op jit(solution)/shard_map/ppermute | solution.py:30
  102.7 0.0 collective-permute-done.9
  102.7 1.3 collective-permute-start.10
  104.0 4.6 %collective-permute-done.3 = bf16[2,192,384]{2,1,0:T(8,128)(2,1)S(1)} collective-permute-done((bf16[2,192,384]{2,1,0:T(8,128)(2,1)S(1)}, bf16[2,192,384]{2,1,0:T(8,128)(2,1)S(1)}, u32[]{:S(2)}, u32[]{:S(2)}) %collective-permute-start.3) | collective-permute-done | bytes 294944 | tf_op jit(solution)/shard_map/ppermute | solution.py:30
  108.6 4.1 %collective-permute-start.4 = (bf16[2,192,384]{2,1,0:T(8,128)(2,1)S(1)}, bf16[2,192,384]{2,1,0:T(8,128)(2,1)S(1)}, u32[]{:S(2)}, u32[]{:S(2)}) collective-permute-start(bf16[2,192,384]{2,1,0:T(8,128)(2,1)S(1)} %collective-permute-done.3), channel_id=1, source_target_pairs={{0,64},{64,128},{128,192},{192,256},{256,320},{320,384},{384,448},... | collective-permute-start | bytes 884744 | tf_op jit(solution)/shard_map/ppermute | solution.py:30
  112.7 0.0 collective-permute-done.10
  112.7 1.3 collective-permute-start.11
  114.0 3.6 %collective-permute-done.4 = bf16[2,192,384]{2,1,0:T(8,128)(2,1)S(1)} collective-permute-done((bf16[2,192,384]{2,1,0:T(8,128)(2,1)S(1)}, bf16[2,192,384]{2,1,0:T(8,128)(2,1)S(1)}, u32[]{:S(2)}, u32[]{:S(2)}) %collective-permute-start.4) | collective-permute-done | bytes 294944 | tf_op jit(solution)/shard_map/ppermute | solution.py:30
  117.7 4.2 %collective-permute-start.5 = (bf16[2,192,384]{2,1,0:T(8,128)(2,1)S(1)}, bf16[2,192,384]{2,1,0:T(8,128)(2,1)S(1)}, u32[]{:S(2)}, u32[]{:S(2)}) collective-permute-start(bf16[2,192,384]{2,1,0:T(8,128)(2,1)S(1)} %collective-permute-done.4), channel_id=1, source_target_pairs={{0,64},{64,128},{128,192},{192,256},{256,320},{320,384},{384,448},... | collective-permute-start | bytes 884744 | tf_op jit(solution)/shard_map/ppermute | solution.py:30
  121.9 0.9 collective-permute-done.11
  122.8 1.3 collective-permute-start.12
  124.1 2.0 collective-permute-done.5
  126.1 4.2 %collective-permute-start.6 = (bf16[2,192,384]{2,1,0:T(8,128)(2,1)S(1)}, bf16[2,192,384]{2,1,0:T(8,128)(2,1)S(1)}, u32[]{:S(2)}, u32[]{:S(2)}) collective-permute-start(bf16[2,192,384]{2,1,0:T(8,128)(2,1)S(1)} %collective-permute-done.5), channel_id=1, source_target_pairs={{0,64},{64,128},{128,192},{192,256},{256,320},{320,384},{384,448},... | collective-permute-start | bytes 884744 | tf_op jit(solution)/shard_map/ppermute | solution.py:30
  130.3 0.6 collective-permute-done.12
  130.9 1.3 collective-permute-start.13
  132.2 1.7 collective-permute-done.6
  133.9 4.8 %collective-permute-start.7 = (bf16[2,192,384]{2,1,0:T(8,128)(2,1)S(1)}, bf16[2,192,384]{2,1,0:T(8,128)(2,1)}, u32[]{:S(2)}, u32[]{:S(2)}) collective-permute-start(bf16[2,192,384]{2,1,0:T(8,128)(2,1)S(1)} %collective-permute-done.6), channel_id=1, source_target_pairs={{0,64},{64,128},{128,192},{192,256},{256,320},{320,384},{384,448},... | collective-permute-start | bytes 884744 | tf_op jit(solution)/shard_map/ppermute | solution.py:30
  138.7 1.0 collective-permute-done.13
  139.8 1.3 collective-permute-start.14
  141.1 0.6 collective-permute-done.7
  141.7 6.4 %collective-permute-start.8 = (bf16[2,192,384]{2,1,0:T(8,128)(2,1)}, bf16[2,192,384]{2,1,0:T(8,128)(2,1)}, u32[]{:S(2)}, u32[]{:S(2)}) collective-permute-start(bf16[2,192,384]{2,1,0:T(8,128)(2,1)} %collective-permute-done.7), channel_id=1, source_target_pairs={{0,64},{64,128},{128,192},{192,256},{256,320},{320,384},{384,448},... | collective-permute-start | bytes 884744 | tf_op jit(solution)/shard_map/ppermute | solution.py:30
  148.0 1.1 collective-permute-done.14
  149.1 1.3 collective-permute-start.15
  150.4 0.9 collective-permute-done.8
  151.3 1.0 bitcast_dynamic-update-slice_fusion.14
  152.3 1.0 bitcast_dynamic-update-slice_fusion.13
  154.0 4.7 %collective-permute-done.15 = bf16[2,192,384]{2,1,0:T(8,128)(2,1)S(1)} collective-permute-done((bf16[2,192,384]{2,1,0:T(8,128)(2,1)S(1)}, bf16[2,192,384]{2,1,0:T(8,128)(2,1)S(1)}, u32[]{:S(2)}, u32[]{:S(2)}) %collective-permute-start.15) | collective-permute-done | bytes 294944 | tf_op jit(solution)/shard_map/ppermute | solution.py:31
  158.7 0.0 copy-start
  158.7 2.1 %copy-done = bf16[15,2,192,384]{3,2,1,0:T(8,128)(2,1)} copy-done((bf16[15,2,192,384]{3,2,1,0:T(8,128)(2,1)}, bf16[15,2,192,384]{3,2,1,0:T(8,128)(2,1)S(1)}, u32[]{:S(2)}) %copy-start) | copy-done | bytes 4423704
  160.9 0.2 constant_dynamic-slice_fusion
  161.1 7.3 %collective-permute-start.16 = (bf16[8,2,192,384]{3,2,1,0:T(8,128)(2,1)S(1)}, bf16[8,2,192,384]{3,2,1,0:T(8,128)(2,1)}, u32[]{:S(2)}, u32[]{:S(2)}) collective-permute-start(bf16[8,2,192,384]{3,2,1,0:T(8,128)(2,1)S(1)} %constant_dynamic-slice_fusion), channel_id=1, source_target_pairs={{0,32},{32,0},{1,33},{33,1},{2,34},{34,2},{3,35},{35,3},{4,36},{36... | collective-permute-start | bytes 7077896 | tf_op jit(solution)/shard_map/ppermute | solution.py:36
  168.5 2.0 fusion.2
  170.5 2.3 %collective-permute-done.16 = bf16[8,2,192,384]{3,2,1,0:T(8,128)(2,1)} collective-permute-done((bf16[8,2,192,384]{3,2,1,0:T(8,128)(2,1)S(1)}, bf16[8,2,192,384]{3,2,1,0:T(8,128)(2,1)}, u32[]{:S(2)}, u32[]{:S(2)}) %collective-permute-start.16) | collective-permute-done | bytes 2359328 | tf_op jit(solution)/shard_map/ppermute | solution.py:36
  172.8 3.3 %maximum_select_fusion = bf16[8,2,2,192,384]{4,3,2,0,1:T(8,128)(2,1)S(1)} fusion(bf16[8,1,2,192,384]{4,3,2,0,1:T(8,128)(2,1)} %bitcast.17, bf16[8,1,2,192,384]{4,3,2,0,1:T(8,128)(2,1)S(1)} %fusion.2, pred[]{:T(512)S(6)} %eq.15), kind=kLoop, calls=%fused_computation | loop fusion | flops 7077888 | bytes 9437185 | tf_op jit(solution)/shard_map/jit(_where)/select_n | solution.py:134
  176.1 2.7 %copy.6 = bf16[8,2,2,192,384]{4,3,2,1,0:T(8,128)(2,1)} copy(bf16[8,2,2,192,384]{4,3,2,0,1:T(8,128)(2,1)S(1)} %maximum_select_fusion) | data formatting | bytes 9437184 | tf_op jit(solution)/shard_map/jit(_where)/select_n | solution.py:134
  178.8 9.1 %all-gather.2.cloned.1.call-done.panel_hbm = bf16[2,2,3072,384]{3,2,1,0:T(8,128)(2,1)} async-done(((bf16[2,2,192,384]{3,2,1,0:T(8,128)(2,1)}), bf16[2,2,3072,384]{3,2,1,0:T(8,128)(2,1)}) %all-gather.2.cloned.1.call-update) | async-done | bytes 9437200 | tf_op jit(solution)/shard_map/all_gather | solution.py:130
  187.9 9.6 %shard_map.17 = f32[2,192,384]{2,1,0:T(8,128)} custom-call(bf16[16,2,192,384]{3,2,1,0:T(8,128)(2,1)} %bitcast.44, bf16[2,2,3072,384]{3,2,1,0:T(8,128)(2,1)} %all-gather.2.cloned.1.call-done.panel_hbm), custom_call_target="tpu_custom_call" | custom-call | flops 3623878656 | bytes 14745600 | tf_op jit(solution)/shard_map/pallas_call | solution.py:85
  (14 shorter events, 0.7 us)
Async XLA Ops:
  6.5 181.3 %all-gather.2.cloned.1.call-start = ((), (), s32[]{:S(2)}) async-start(), calls=%async_computation | async-start | bytes 10027008 | tf_op jit(solution)/shard_map/all_gather | solution.py:130
  7.9 11.7 %collective-permute-start = (bf16[2,192,192]{1,2,0:T(8,128)(2,1)S(1)}, bf16[2,192,192]{1,2,0:T(8,128)(2,1)S(1)}, u32[]{:S(2)}, u32[]{:S(2)}) collective-permute-start(bf16[2,192,192]{1,2,0:T(8,128)(2,1)S(1)} %copy.7), channel_id=1, source_target_pairs={{0,0},{32,2},{64,4},{96,6},{128,8},{160,10},{192,12},{224,14},{256... | collective-permute-start | bytes 442376 | tf_op jit(solution)/shard_map/ppermute | solution.py:119
  14.1 10.5 %collective-permute-start.1 = (bf16[2,192,192]{1,2,0:T(8,128)(2,1)S(1)}, bf16[2,192,192]{1,2,0:T(8,128)(2,1)S(1)}, u32[]{:S(2)}, u32[]{:S(2)}) collective-permute-start(bf16[2,192,192]{1,2,0:T(8,128)(2,1)S(1)} %copy.8), channel_id=1, source_target_pairs={{0,1},{32,3},{64,5},{96,7},{128,9},{160,11},{192,13},{224,15},{256... | collective-permute-start | bytes 442376 | tf_op jit(solution)/shard_map/ppermute | solution.py:119
  25.8 56.8 %collective-permute-start.17 = (bf16[2,192,384]{2,1,0:T(8,128)(2,1)S(1)}, bf16[2,192,384]{2,1,0:T(8,128)(2,1)S(1)}, u32[]{:S(2)}, u32[]{:S(2)}) collective-permute-start(bf16[2,192,384]{2,1,0:T(8,128)(2,1)S(1)} %fusion.1), channel_id=1, source_target_pairs={{0,16},{16,0},{1,17},{17,1},{2,18},{18,2},{3,19},{19,3},{4,20},{20... | collective-permute-start | bytes 884744 | tf_op jit(solution)/shard_map/ppermute | solution.py:127
  83.5 15.1 %collective-permute-start.2 = (bf16[2,192,384]{2,1,0:T(8,128)(2,1)S(1)}, bf16[2,192,384]{2,1,0:T(8,128)(2,1)S(1)}, u32[]{:S(2)}, u32[]{:S(2)}) collective-permute-start(bf16[2,192,384]{2,1,0:T(8,128)(2,1)S(1)} %fusion.1), channel_id=1, source_target_pairs={{0,64},{64,128},{128,192},{192,256},{256,320},{320,384},{384,448},... | collective-permute-start | bytes 884744 | tf_op jit(solution)/shard_map/ppermute | solution.py:30
  84.8 17.9 %collective-permute-start.9 = (bf16[2,192,384]{2,1,0:T(8,128)(2,1)S(1)}, bf16[2,192,384]{2,1,0:T(8,128)(2,1)S(1)}, u32[]{:S(2)}, u32[]{:S(2)}) collective-permute-start(bf16[2,192,384]{2,1,0:T(8,128)(2,1)S(1)} %fusion.1), channel_id=1, source_target_pairs={{64,0},{128,64},{192,128},{256,192},{320,256},{384,320},{448,384},... | collective-permute-start | bytes 884744 | tf_op jit(solution)/shard_map/ppermute | solution.py:31
  98.6 10.0 %collective-permute-start.3 = (bf16[2,192,384]{2,1,0:T(8,128)(2,1)S(1)}, bf16[2,192,384]{2,1,0:T(8,128)(2,1)S(1)}, u32[]{:S(2)}, u32[]{:S(2)}) collective-permute-start(bf16[2,192,384]{2,1,0:T(8,128)(2,1)S(1)} %collective-permute-done.2), channel_id=1, source_target_pairs={{0,64},{64,128},{128,192},{192,256},{256,320},{320,384},{384,448},... | collective-permute-start | bytes 884744 | tf_op jit(solution)/shard_map/ppermute | solution.py:30
  102.7 10.0 %collective-permute-start.10 = (bf16[2,192,384]{2,1,0:T(8,128)(2,1)S(1)}, bf16[2,192,384]{2,1,0:T(8,128)(2,1)S(1)}, u32[]{:S(2)}, u32[]{:S(2)}) collective-permute-start(bf16[2,192,384]{2,1,0:T(8,128)(2,1)S(1)} %collective-permute-done.9), channel_id=1, source_target_pairs={{64,0},{128,64},{192,128},{256,192},{320,256},{384,320},{448,384},... | collective-permute-start | bytes 884744 | tf_op jit(solution)/shard_map/ppermute | solution.py:31
  108.6 9.1 %collective-permute-start.4 = (bf16[2,192,384]{2,1,0:T(8,128)(2,1)S(1)}, bf16[2,192,384]{2,1,0:T(8,128)(2,1)S(1)}, u32[]{:S(2)}, u32[]{:S(2)}) collective-permute-start(bf16[2,192,384]{2,1,0:T(8,128)(2,1)S(1)} %collective-permute-done.3), channel_id=1, source_target_pairs={{0,64},{64,128},{128,192},{192,256},{256,320},{320,384},{384,448},... | collective-permute-start | bytes 884744 | tf_op jit(solution)/shard_map/ppermute | solution.py:30
  112.7 10.0 %collective-permute-start.11 = (bf16[2,192,384]{2,1,0:T(8,128)(2,1)S(1)}, bf16[2,192,384]{2,1,0:T(8,128)(2,1)S(1)}, u32[]{:S(2)}, u32[]{:S(2)}) collective-permute-start(bf16[2,192,384]{2,1,0:T(8,128)(2,1)S(1)} %collective-permute-done.10), channel_id=1, source_target_pairs={{64,0},{128,64},{192,128},{256,192},{320,256},{384,320},{448,384},... | collective-permute-start | bytes 884744 | tf_op jit(solution)/shard_map/ppermute | solution.py:31
  117.7 8.4 %collective-permute-start.5 = (bf16[2,192,384]{2,1,0:T(8,128)(2,1)S(1)}, bf16[2,192,384]{2,1,0:T(8,128)(2,1)S(1)}, u32[]{:S(2)}, u32[]{:S(2)}) collective-permute-start(bf16[2,192,384]{2,1,0:T(8,128)(2,1)S(1)} %collective-permute-done.4), channel_id=1, source_target_pairs={{0,64},{64,128},{128,192},{192,256},{256,320},{320,384},{384,448},... | collective-permute-start | bytes 884744 | tf_op jit(solution)/shard_map/ppermute | solution.py:30
  122.8 8.1 %collective-permute-start.12 = (bf16[2,192,384]{2,1,0:T(8,128)(2,1)S(1)}, bf16[2,192,384]{2,1,0:T(8,128)(2,1)S(1)}, u32[]{:S(2)}, u32[]{:S(2)}) collective-permute-start(bf16[2,192,384]{2,1,0:T(8,128)(2,1)S(1)} %collective-permute-done.11), channel_id=1, source_target_pairs={{64,0},{128,64},{192,128},{256,192},{320,256},{384,320},{448,384},... | collective-permute-start | bytes 884744 | tf_op jit(solution)/shard_map/ppermute | solution.py:31
  126.1 7.9 %collective-permute-start.6 = (bf16[2,192,384]{2,1,0:T(8,128)(2,1)S(1)}, bf16[2,192,384]{2,1,0:T(8,128)(2,1)S(1)}, u32[]{:S(2)}, u32[]{:S(2)}) collective-permute-start(bf16[2,192,384]{2,1,0:T(8,128)(2,1)S(1)} %collective-permute-done.5), channel_id=1, source_target_pairs={{0,64},{64,128},{128,192},{192,256},{256,320},{320,384},{384,448},... | collective-permute-start | bytes 884744 | tf_op jit(solution)/shard_map/ppermute | solution.py:30
  130.9 8.9 %collective-permute-start.13 = (bf16[2,192,384]{2,1,0:T(8,128)(2,1)S(1)}, bf16[2,192,384]{2,1,0:T(8,128)(2,1)S(1)}, u32[]{:S(2)}, u32[]{:S(2)}) collective-permute-start(bf16[2,192,384]{2,1,0:T(8,128)(2,1)S(1)} %collective-permute-done.12), channel_id=1, source_target_pairs={{64,0},{128,64},{192,128},{256,192},{320,256},{384,320},{448,384},... | collective-permute-start | bytes 884744 | tf_op jit(solution)/shard_map/ppermute | solution.py:31
  133.9 7.8 %collective-permute-start.7 = (bf16[2,192,384]{2,1,0:T(8,128)(2,1)S(1)}, bf16[2,192,384]{2,1,0:T(8,128)(2,1)}, u32[]{:S(2)}, u32[]{:S(2)}) collective-permute-start(bf16[2,192,384]{2,1,0:T(8,128)(2,1)S(1)} %collective-permute-done.6), channel_id=1, source_target_pairs={{0,64},{64,128},{128,192},{192,256},{256,320},{320,384},{384,448},... | collective-permute-start | bytes 884744 | tf_op jit(solution)/shard_map/ppermute | solution.py:30
  139.8 9.3 %collective-permute-start.14 = (bf16[2,192,384]{2,1,0:T(8,128)(2,1)S(1)}, bf16[2,192,384]{2,1,0:T(8,128)(2,1)S(1)}, u32[]{:S(2)}, u32[]{:S(2)}) collective-permute-start(bf16[2,192,384]{2,1,0:T(8,128)(2,1)S(1)} %collective-permute-done.13), channel_id=1, source_target_pairs={{64,0},{128,64},{192,128},{256,192},{320,256},{384,320},{448,384},... | collective-permute-start | bytes 884744 | tf_op jit(solution)/shard_map/ppermute | solution.py:31
  141.7 9.6 %collective-permute-start.8 = (bf16[2,192,384]{2,1,0:T(8,128)(2,1)}, bf16[2,192,384]{2,1,0:T(8,128)(2,1)}, u32[]{:S(2)}, u32[]{:S(2)}) collective-permute-start(bf16[2,192,384]{2,1,0:T(8,128)(2,1)} %collective-permute-done.7), channel_id=1, source_target_pairs={{0,64},{64,128},{128,192},{192,256},{256,320},{320,384},{384,448},... | collective-permute-start | bytes 884744 | tf_op jit(solution)/shard_map/ppermute | solution.py:30
  149.1 9.6 %collective-permute-start.15 = (bf16[2,192,384]{2,1,0:T(8,128)(2,1)S(1)}, bf16[2,192,384]{2,1,0:T(8,128)(2,1)S(1)}, u32[]{:S(2)}, u32[]{:S(2)}) collective-permute-start(bf16[2,192,384]{2,1,0:T(8,128)(2,1)S(1)} %collective-permute-done.14), channel_id=1, source_target_pairs={{64,0},{128,64},{192,128},{256,192},{320,256},{384,320},{448,384},... | collective-permute-start | bytes 884744 | tf_op jit(solution)/shard_map/ppermute | solution.py:31
  158.7 2.1 %copy-start = (bf16[15,2,192,384]{3,2,1,0:T(8,128)(2,1)}, bf16[15,2,192,384]{3,2,1,0:T(8,128)(2,1)S(1)}, u32[]{:S(2)}) copy-start(bf16[15,2,192,384]{3,2,1,0:T(8,128)(2,1)S(1)} %bitcast_dynamic-update-slice_fusion) | copy-start | bytes 13271044
  161.1 11.6 %collective-permute-start.16 = (bf16[8,2,192,384]{3,2,1,0:T(8,128)(2,1)S(1)}, bf16[8,2,192,384]{3,2,1,0:T(8,128)(2,1)}, u32[]{:S(2)}, u32[]{:S(2)}) collective-permute-start(bf16[8,2,192,384]{3,2,1,0:T(8,128)(2,1)S(1)} %constant_dynamic-slice_fusion), channel_id=1, source_target_pairs={{0,32},{32,0},{1,33},{33,1},{2,34},{34,2},{3,35},{35,3},{4,36},{36... | collective-permute-start | bytes 7077896 | tf_op jit(solution)/shard_map/ppermute | solution.py:36
Sparse Core Ops, SparseCore 0:
  83.6 104.1 all-gather.1

commit v20 on v19

--- a/solution.py
+++ b/solution.py
@@ -80,7 +80,7 @@
 def product(left, panels, factor):
     n_blocks, parts, rows, width = left.shape
     cols = panels.shape[-1]
-    n_block = n_blocks // 4
+    n_block = n_blocks // 8
     kernel = functools.partial(product_kernel, n_block=n_block, width=width, factor=factor)
     return pl.pallas_call(
         kernel,

time: 205 us -> 207 us (level)
  no operation moved by 1% of the time
where the time goes in v20:
time: 207 us; the launch traced here: 206 us
  starting transfers between devices  103 us (50%)
  waiting for transfers between devices  61.1 us (30%)
  between operations  13.7 us (7%)
  local copies, waits for them, and re-layouts  11.2 us (5%)
  Pallas kernels  10.9 us (5%)
  other arithmetic  5.41 us (3%)
    ppermute x1, starting transfers between devices, local(): partner_block = lax.ppermute(symmetric, 'zh', [(0, 1), (1, 0)])  49.2 us
    ppermute x7, starting transfers between devices, gather_line(): lax.ppermute(rightward, 'zl', [(k, k + 1) for k in range(n_line - 1)])  29.2 us
    ppermute x7, waiting for transfers between devices, gather_line(): lax.ppermute(rightward, 'zl', [(k, k + 1) for k in range(n_line - 1)])  25.9 us
    pallas_call x1, Pallas kernels, product(): pl.pallas_call(kernel, out_shape=jax.ShapeDtypeStruct((2, rows, cols), jn...  10.9 us
    all_gather x1, waiting for transfers between devices, local(): lax.all_gather(jnp.stack([top, bottom]), ('y', 'x'), axis=2, tiled=True)  9.05 us
    ppermute x7, starting transfers between devices, gather_line(): lax.ppermute(leftward, 'zl', [(k + 1, k) for k in range(n_line - 1)])  9 us
    ppermute x2, starting transfers between devices, local(): lax.ppermute(piece, axes, mirror_pairs(n_recv, n_shot, flip))  8.58 us
    ppermute x7, waiting for transfers between devices, gather_line(): lax.ppermute(leftward, 'zl', [(k + 1, k) for k in range(n_line - 1)])  8.31 us
  transfers between devices with their start and end apart: 19, of which 17 were waited for; matrix products, arithmetic and copies ran while one was open for 5% of the time, Pallas kernels for 0%

profile of v20, /device:TPU:1, one launch (start us, length us, event | category | flops | bytes accessed | tf_op | source)
XLA Modules:
  0.0 205.6 jit_solution(16581121588408149398)
XLA Ops:
  6.5 0.0 all-gather.2.cloned.1.call-start
  6.5 1.2 constant_dynamic-slice_fusion.2
  7.7 0.1 copy.7
  7.9 6.0 %collective-permute-start = (bf16[2,192,192]{1,2,0:T(8,128)(2,1)S(1)}, bf16[2,192,192]{1,2,0:T(8,128)(2,1)S(1)}, u32[]{:S(2)}, u32[]{:S(2)}) collective-permute-start(bf16[2,192,192]{1,2,0:T(8,128)(2,1)S(1)} %copy.7), channel_id=1, source_target_pairs={{0,0},{32,2},{64,4},{96,6},{128,8},{160,10},{192,12},{224,14},{256... | collective-permute-start | bytes 442376 | tf_op jit(solution)/shard_map/ppermute | solution.py:119
  13.9 0.1 copy.8
  14.1 2.5 %collective-permute-start.1 = (bf16[2,192,192]{1,2,0:T(8,128)(2,1)S(1)}, bf16[2,192,192]{1,2,0:T(8,128)(2,1)S(1)}, u32[]{:S(2)}, u32[]{:S(2)}) collective-permute-start(bf16[2,192,192]{1,2,0:T(8,128)(2,1)S(1)} %copy.8), channel_id=1, source_target_pairs={{0,1},{32,3},{64,5},{96,7},{128,9},{160,11},{192,13},{224,15},{256... | collective-permute-start | bytes 442376 | tf_op jit(solution)/shard_map/ppermute | solution.py:119
  16.6 2.9 %collective-permute-done = bf16[2,192,192]{1,2,0:T(8,128)(2,1)S(1)} collective-permute-done((bf16[2,192,192]{1,2,0:T(8,128)(2,1)S(1)}, bf16[2,192,192]{1,2,0:T(8,128)(2,1)S(1)}, u32[]{:S(2)}, u32[]{:S(2)}) %collective-permute-start) | collective-permute-done | bytes 147488 | tf_op jit(solution)/shard_map/ppermute | solution.py:119
  19.5 5.1 %collective-permute-done.1 = bf16[2,192,192]{1,2,0:T(8,128)(2,1)S(1)} collective-permute-done((bf16[2,192,192]{1,2,0:T(8,128)(2,1)S(1)}, bf16[2,192,192]{1,2,0:T(8,128)(2,1)S(1)}, u32[]{:S(2)}, u32[]{:S(2)}) %collective-permute-start.1) | collective-permute-done | bytes 147488 | tf_op jit(solution)/shard_map/ppermute | solution.py:119
  24.6 1.1 fusion.1
  25.8 49.2 %collective-permute-start.17 = (bf16[2,192,384]{2,1,0:T(8,128)(2,1)S(1)}, bf16[2,192,384]{2,1,0:T(8,128)(2,1)S(1)}, u32[]{:S(2)}, u32[]{:S(2)}) collective-permute-start(bf16[2,192,384]{2,1,0:T(8,128)(2,1)S(1)} %fusion.1), channel_id=1, source_target_pairs={{0,16},{16,0},{1,17},{17,1},{2,18},{18,2},{3,19},{19,3},{4,20},{20... | collective-permute-start | bytes 884744 | tf_op jit(solution)/shard_map/ppermute | solution.py:127
  74.9 7.6 %collective-permute-done.17 = bf16[2,192,384]{2,1,0:T(8,128)(2,1)S(1)} collective-permute-done((bf16[2,192,384]{2,1,0:T(8,128)(2,1)S(1)}, bf16[2,192,384]{2,1,0:T(8,128)(2,1)S(1)}, u32[]{:S(2)}, u32[]{:S(2)}) %collective-permute-start.17) | collective-permute-done | bytes 294944 | tf_op jit(solution)/shard_map/ppermute | solution.py:127
  82.6 0.1 select_bitcast_fusion.1
  82.6 0.9 pad_maximum_fusion
  83.5 0.0 all-gather.2.cloned.1.call-update
  83.5 1.3 collective-permute-start.2
  84.8 1.3 collective-permute-start.9
  86.1 12.5 %collective-permute-done.2 = bf16[2,192,384]{2,1,0:T(8,128)(2,1)S(1)} collective-permute-done((bf16[2,192,384]{2,1,0:T(8,128)(2,1)S(1)}, bf16[2,192,384]{2,1,0:T(8,128)(2,1)S(1)}, u32[]{:S(2)}, u32[]{:S(2)}) %collective-permute-start.2) | collective-permute-done | bytes 294944 | tf_op jit(solution)/shard_map/ppermute | solution.py:30
  98.6 4.1 %collective-permute-start.3 = (bf16[2,192,384]{2,1,0:T(8,128)(2,1)S(1)}, bf16[2,192,384]{2,1,0:T(8,128)(2,1)S(1)}, u32[]{:S(2)}, u32[]{:S(2)}) collective-permute-start(bf16[2,192,384]{2,1,0:T(8,128)(2,1)S(1)} %collective-permute-done.2), channel_id=1, source_target_pairs={{0,64},{64,128},{128,192},{192,256},{256,320},{320,384},{384,448},... | collective-permute-start | bytes 884744 | tf_op jit(solution)/shard_map/ppermute | solution.py:30
  102.7 0.0 collective-permute-done.9
  102.7 1.3 collective-permute-start.10
  104.0 4.6 %collective-permute-done.3 = bf16[2,192,384]{2,1,0:T(8,128)(2,1)S(1)} collective-permute-done((bf16[2,192,384]{2,1,0:T(8,128)(2,1)S(1)}, bf16[2,192,384]{2,1,0:T(8,128)(2,1)S(1)}, u32[]{:S(2)}, u32[]{:S(2)}) %collective-permute-start.3) | collective-permute-done | bytes 294944 | tf_op jit(solution)/shard_map/ppermute | solution.py:30
  108.6 4.1 %collective-permute-start.4 = (bf16[2,192,384]{2,1,0:T(8,128)(2,1)S(1)}, bf16[2,192,384]{2,1,0:T(8,128)(2,1)S(1)}, u32[]{:S(2)}, u32[]{:S(2)}) collective-permute-start(bf16[2,192,384]{2,1,0:T(8,128)(2,1)S(1)} %collective-permute-done.3), channel_id=1, source_target_pairs={{0,64},{64,128},{128,192},{192,256},{256,320},{320,384},{384,448},... | collective-permute-start | bytes 884744 | tf_op jit(solution)/shard_map/ppermute | solution.py:30
  112.7 0.0 collective-permute-done.10
  112.7 1.3 collective-permute-start.11
  114.0 3.6 %collective-permute-done.4 = bf16[2,192,384]{2,1,0:T(8,128)(2,1)S(1)} collective-permute-done((bf16[2,192,384]{2,1,0:T(8,128)(2,1)S(1)}, bf16[2,192,384]{2,1,0:T(8,128)(2,1)S(1)}, u32[]{:S(2)}, u32[]{:S(2)}) %collective-permute-start.4) | collective-permute-done | bytes 294944 | tf_op jit(solution)/shard_map/ppermute | solution.py:30
  117.7 4.2 %collective-permute-start.5 = (bf16[2,192,384]{2,1,0:T(8,128)(2,1)S(1)}, bf16[2,192,384]{2,1,0:T(8,128)(2,1)S(1)}, u32[]{:S(2)}, u32[]{:S(2)}) collective-permute-start(bf16[2,192,384]{2,1,0:T(8,128)(2,1)S(1)} %collective-permute-done.4), channel_id=1, source_target_pairs={{0,64},{64,128},{128,192},{192,256},{256,320},{320,384},{384,448},... | collective-permute-start | bytes 884744 | tf_op jit(solution)/shard_map/ppermute | solution.py:30
  121.9 0.9 collective-permute-done.11
  122.8 1.3 collective-permute-start.12
  124.1 2.0 collective-permute-done.5
  126.1 4.2 %collective-permute-start.6 = (bf16[2,192,384]{2,1,0:T(8,128)(2,1)S(1)}, bf16[2,192,384]{2,1,0:T(8,128)(2,1)S(1)}, u32[]{:S(2)}, u32[]{:S(2)}) collective-permute-start(bf16[2,192,384]{2,1,0:T(8,128)(2,1)S(1)} %collective-permute-done.5), channel_id=1, source_target_pairs={{0,64},{64,128},{128,192},{192,256},{256,320},{320,384},{384,448},... | collective-permute-start | bytes 884744 | tf_op jit(solution)/shard_map/ppermute | solution.py:30
  130.3 0.6 collective-permute-done.12
  130.9 1.3 collective-permute-start.13
  132.2 1.7 collective-permute-done.6
  133.9 4.8 %collective-permute-start.7 = (bf16[2,192,384]{2,1,0:T(8,128)(2,1)S(1)}, bf16[2,192,384]{2,1,0:T(8,128)(2,1)}, u32[]{:S(2)}, u32[]{:S(2)}) collective-permute-start(bf16[2,192,384]{2,1,0:T(8,128)(2,1)S(1)} %collective-permute-done.6), channel_id=1, source_target_pairs={{0,64},{64,128},{128,192},{192,256},{256,320},{320,384},{384,448},... | collective-permute-start | bytes 884744 | tf_op jit(solution)/shard_map/ppermute | solution.py:30
  138.7 1.0 collective-permute-done.13
  139.8 1.3 collective-permute-start.14
  141.1 0.6 collective-permute-done.7
  141.7 6.4 %collective-permute-start.8 = (bf16[2,192,384]{2,1,0:T(8,128)(2,1)}, bf16[2,192,384]{2,1,0:T(8,128)(2,1)}, u32[]{:S(2)}, u32[]{:S(2)}) collective-permute-start(bf16[2,192,384]{2,1,0:T(8,128)(2,1)} %collective-permute-done.7), channel_id=1, source_target_pairs={{0,64},{64,128},{128,192},{192,256},{256,320},{320,384},{384,448},... | collective-permute-start | bytes 884744 | tf_op jit(solution)/shard_map/ppermute | solution.py:30
  148.0 1.1 collective-permute-done.14
  149.1 1.3 collective-permute-start.15
  150.4 0.9 collective-permute-done.8
  151.3 1.0 bitcast_dynamic-update-slice_fusion.14
  152.3 1.0 bitcast_dynamic-update-slice_fusion.13
  154.0 4.7 %collective-permute-done.15 = bf16[2,192,384]{2,1,0:T(8,128)(2,1)S(1)} collective-permute-done((bf16[2,192,384]{2,1,0:T(8,128)(2,1)S(1)}, bf16[2,192,384]{2,1,0:T(8,128)(2,1)S(1)}, u32[]{:S(2)}, u32[]{:S(2)}) %collective-permute-start.15) | collective-permute-done | bytes 294944 | tf_op jit(solution)/shard_map/ppermute | solution.py:31
  158.7 0.0 copy-start
  158.7 2.1 %copy-done = bf16[15,2,192,384]{3,2,1,0:T(8,128)(2,1)} copy-done((bf16[15,2,192,384]{3,2,1,0:T(8,128)(2,1)}, bf16[15,2,192,384]{3,2,1,0:T(8,128)(2,1)S(1)}, u32[]{:S(2)}) %copy-start) | copy-done | bytes 4423704
  160.9 0.2 constant_dynamic-slice_fusion
  161.1 7.3 %collective-permute-start.16 = (bf16[8,2,192,384]{3,2,1,0:T(8,128)(2,1)S(1)}, bf16[8,2,192,384]{3,2,1,0:T(8,128)(2,1)}, u32[]{:S(2)}, u32[]{:S(2)}) collective-permute-start(bf16[8,2,192,384]{3,2,1,0:T(8,128)(2,1)S(1)} %constant_dynamic-slice_fusion), channel_id=1, source_target_pairs={{0,32},{32,0},{1,33},{33,1},{2,34},{34,2},{3,35},{35,3},{4,36},{36... | collective-permute-start | bytes 7077896 | tf_op jit(solution)/shard_map/ppermute | solution.py:36
  168.5 2.0 fusion.2
  170.5 2.3 %collective-permute-done.16 = bf16[8,2,192,384]{3,2,1,0:T(8,128)(2,1)} collective-permute-done((bf16[8,2,192,384]{3,2,1,0:T(8,128)(2,1)S(1)}, bf16[8,2,192,384]{3,2,1,0:T(8,128)(2,1)}, u32[]{:S(2)}, u32[]{:S(2)}) %collective-permute-start.16) | collective-permute-done | bytes 2359328 | tf_op jit(solution)/shard_map/ppermute | solution.py:36
  172.8 3.3 %maximum_select_fusion = bf16[8,2,2,192,384]{4,3,2,0,1:T(8,128)(2,1)S(1)} fusion(bf16[8,1,2,192,384]{4,3,2,0,1:T(8,128)(2,1)} %bitcast.17, bf16[8,1,2,192,384]{4,3,2,0,1:T(8,128)(2,1)S(1)} %fusion.2, pred[]{:T(512)S(6)} %eq.15), kind=kLoop, calls=%fused_computation | loop fusion | flops 7077888 | bytes 9437185 | tf_op jit(solution)/shard_map/jit(_where)/select_n | solution.py:134
  176.1 2.7 %copy.6 = bf16[8,2,2,192,384]{4,3,2,1,0:T(8,128)(2,1)} copy(bf16[8,2,2,192,384]{4,3,2,0,1:T(8,128)(2,1)S(1)} %maximum_select_fusion) | data formatting | bytes 9437184 | tf_op jit(solution)/shard_map/jit(_where)/select_n | solution.py:134
  178.8 9.1 %all-gather.2.cloned.1.call-done.panel_hbm = bf16[2,2,3072,384]{3,2,1,0:T(8,128)(2,1)} async-done(((bf16[2,2,192,384]{3,2,1,0:T(8,128)(2,1)}), bf16[2,2,3072,384]{3,2,1,0:T(8,128)(2,1)}) %all-gather.2.cloned.1.call-update) | async-done | bytes 9437200 | tf_op jit(solution)/shard_map/all_gather | solution.py:130
  187.9 10.9 %shard_map.17 = f32[2,192,384]{2,1,0:T(8,128)} custom-call(bf16[16,2,192,384]{3,2,1,0:T(8,128)(2,1)} %bitcast.44, bf16[2,2,3072,384]{3,2,1,0:T(8,128)(2,1)} %all-gather.2.cloned.1.call-done.panel_hbm), custom_call_target="tpu_custom_call" | custom-call | flops 3623878656 | bytes 14745600 | tf_op jit(solution)/shard_map/pallas_call | solution.py:85
  (14 shorter events, 0.7 us)
Async XLA Ops:
  6.5 181.3 %all-gather.2.cloned.1.call-start = ((), (), s32[]{:S(2)}) async-start(), calls=%async_computation | async-start | bytes 10027008 | tf_op jit(solution)/shard_map/all_gather | solution.py:130
  7.9 11.7 %collective-permute-start = (bf16[2,192,192]{1,2,0:T(8,128)(2,1)S(1)}, bf16[2,192,192]{1,2,0:T(8,128)(2,1)S(1)}, u32[]{:S(2)}, u32[]{:S(2)}) collective-permute-start(bf16[2,192,192]{1,2,0:T(8,128)(2,1)S(1)} %copy.7), channel_id=1, source_target_pairs={{0,0},{32,2},{64,4},{96,6},{128,8},{160,10},{192,12},{224,14},{256... | collective-permute-start | bytes 442376 | tf_op jit(solution)/shard_map/ppermute | solution.py:119
  14.1 10.5 %collective-permute-start.1 = (bf16[2,192,192]{1,2,0:T(8,128)(2,1)S(1)}, bf16[2,192,192]{1,2,0:T(8,128)(2,1)S(1)}, u32[]{:S(2)}, u32[]{:S(2)}) collective-permute-start(bf16[2,192,192]{1,2,0:T(8,128)(2,1)S(1)} %copy.8), channel_id=1, source_target_pairs={{0,1},{32,3},{64,5},{96,7},{128,9},{160,11},{192,13},{224,15},{256... | collective-permute-start | bytes 442376 | tf_op jit(solution)/shard_map/ppermute | solution.py:119
  25.8 56.8 %collective-permute-start.17 = (bf16[2,192,384]{2,1,0:T(8,128)(2,1)S(1)}, bf16[2,192,384]{2,1,0:T(8,128)(2,1)S(1)}, u32[]{:S(2)}, u32[]{:S(2)}) collective-permute-start(bf16[2,192,384]{2,1,0:T(8,128)(2,1)S(1)} %fusion.1), channel_id=1, source_target_pairs={{0,16},{16,0},{1,17},{17,1},{2,18},{18,2},{3,19},{19,3},{4,20},{20... | collective-permute-start | bytes 884744 | tf_op jit(solution)/shard_map/ppermute | solution.py:127
  83.5 15.1 %collective-permute-start.2 = (bf16[2,192,384]{2,1,0:T(8,128)(2,1)S(1)}, bf16[2,192,384]{2,1,0:T(8,128)(2,1)S(1)}, u32[]{:S(2)}, u32[]{:S(2)}) collective-permute-start(bf16[2,192,384]{2,1,0:T(8,128)(2,1)S(1)} %fusion.1), channel_id=1, source_target_pairs={{0,64},{64,128},{128,192},{192,256},{256,320},{320,384},{384,448},... | collective-permute-start | bytes 884744 | tf_op jit(solution)/shard_map/ppermute | solution.py:30
  84.8 17.9 %collective-permute-start.9 = (bf16[2,192,384]{2,1,0:T(8,128)(2,1)S(1)}, bf16[2,192,384]{2,1,0:T(8,128)(2,1)S(1)}, u32[]{:S(2)}, u32[]{:S(2)}) collective-permute-start(bf16[2,192,384]{2,1,0:T(8,128)(2,1)S(1)} %fusion.1), channel_id=1, source_target_pairs={{64,0},{128,64},{192,128},{256,192},{320,256},{384,320},{448,384},... | collective-permute-start | bytes 884744 | tf_op jit(solution)/shard_map/ppermute | solution.py:31
  98.6 10.0 %collective-permute-start.3 = (bf16[2,192,384]{2,1,0:T(8,128)(2,1)S(1)}, bf16[2,192,384]{2,1,0:T(8,128)(2,1)S(1)}, u32[]{:S(2)}, u32[]{:S(2)}) collective-permute-start(bf16[2,192,384]{2,1,0:T(8,128)(2,1)S(1)} %collective-permute-done.2), channel_id=1, source_target_pairs={{0,64},{64,128},{128,192},{192,256},{256,320},{320,384},{384,448},... | collective-permute-start | bytes 884744 | tf_op jit(solution)/shard_map/ppermute | solution.py:30
  102.7 10.0 %collective-permute-start.10 = (bf16[2,192,384]{2,1,0:T(8,128)(2,1)S(1)}, bf16[2,192,384]{2,1,0:T(8,128)(2,1)S(1)}, u32[]{:S(2)}, u32[]{:S(2)}) collective-permute-start(bf16[2,192,384]{2,1,0:T(8,128)(2,1)S(1)} %collective-permute-done.9), channel_id=1, source_target_pairs={{64,0},{128,64},{192,128},{256,192},{320,256},{384,320},{448,384},... | collective-permute-start | bytes 884744 | tf_op jit(solution)/shard_map/ppermute | solution.py:31
  108.6 9.1 %collective-permute-start.4 = (bf16[2,192,384]{2,1,0:T(8,128)(2,1)S(1)}, bf16[2,192,384]{2,1,0:T(8,128)(2,1)S(1)}, u32[]{:S(2)}, u32[]{:S(2)}) collective-permute-start(bf16[2,192,384]{2,1,0:T(8,128)(2,1)S(1)} %collective-permute-done.3), channel_id=1, source_target_pairs={{0,64},{64,128},{128,192},{192,256},{256,320},{320,384},{384,448},... | collective-permute-start | bytes 884744 | tf_op jit(solution)/shard_map/ppermute | solution.py:30
  112.7 10.0 %collective-permute-start.11 = (bf16[2,192,384]{2,1,0:T(8,128)(2,1)S(1)}, bf16[2,192,384]{2,1,0:T(8,128)(2,1)S(1)}, u32[]{:S(2)}, u32[]{:S(2)}) collective-permute-start(bf16[2,192,384]{2,1,0:T(8,128)(2,1)S(1)} %collective-permute-done.10), channel_id=1, source_target_pairs={{64,0},{128,64},{192,128},{256,192},{320,256},{384,320},{448,384},... | collective-permute-start | bytes 884744 | tf_op jit(solution)/shard_map/ppermute | solution.py:31
  117.7 8.4 %collective-permute-start.5 = (bf16[2,192,384]{2,1,0:T(8,128)(2,1)S(1)}, bf16[2,192,384]{2,1,0:T(8,128)(2,1)S(1)}, u32[]{:S(2)}, u32[]{:S(2)}) collective-permute-start(bf16[2,192,384]{2,1,0:T(8,128)(2,1)S(1)} %collective-permute-done.4), channel_id=1, source_target_pairs={{0,64},{64,128},{128,192},{192,256},{256,320},{320,384},{384,448},... | collective-permute-start | bytes 884744 | tf_op jit(solution)/shard_map/ppermute | solution.py:30
  122.8 8.1 %collective-permute-start.12 = (bf16[2,192,384]{2,1,0:T(8,128)(2,1)S(1)}, bf16[2,192,384]{2,1,0:T(8,128)(2,1)S(1)}, u32[]{:S(2)}, u32[]{:S(2)}) collective-permute-start(bf16[2,192,384]{2,1,0:T(8,128)(2,1)S(1)} %collective-permute-done.11), channel_id=1, source_target_pairs={{64,0},{128,64},{192,128},{256,192},{320,256},{384,320},{448,384},... | collective-permute-start | bytes 884744 | tf_op jit(solution)/shard_map/ppermute | solution.py:31
  126.1 7.9 %collective-permute-start.6 = (bf16[2,192,384]{2,1,0:T(8,128)(2,1)S(1)}, bf16[2,192,384]{2,1,0:T(8,128)(2,1)S(1)}, u32[]{:S(2)}, u32[]{:S(2)}) collective-permute-start(bf16[2,192,384]{2,1,0:T(8,128)(2,1)S(1)} %collective-permute-done.5), channel_id=1, source_target_pairs={{0,64},{64,128},{128,192},{192,256},{256,320},{320,384},{384,448},... | collective-permute-start | bytes 884744 | tf_op jit(solution)/shard_map/ppermute | solution.py:30
  130.9 8.9 %collective-permute-start.13 = (bf16[2,192,384]{2,1,0:T(8,128)(2,1)S(1)}, bf16[2,192,384]{2,1,0:T(8,128)(2,1)S(1)}, u32[]{:S(2)}, u32[]{:S(2)}) collective-permute-start(bf16[2,192,384]{2,1,0:T(8,128)(2,1)S(1)} %collective-permute-done.12), channel_id=1, source_target_pairs={{64,0},{128,64},{192,128},{256,192},{320,256},{384,320},{448,384},... | collective-permute-start | bytes 884744 | tf_op jit(solution)/shard_map/ppermute | solution.py:31
  133.9 7.8 %collective-permute-start.7 = (bf16[2,192,384]{2,1,0:T(8,128)(2,1)S(1)}, bf16[2,192,384]{2,1,0:T(8,128)(2,1)}, u32[]{:S(2)}, u32[]{:S(2)}) collective-permute-start(bf16[2,192,384]{2,1,0:T(8,128)(2,1)S(1)} %collective-permute-done.6), channel_id=1, source_target_pairs={{0,64},{64,128},{128,192},{192,256},{256,320},{320,384},{384,448},... | collective-permute-start | bytes 884744 | tf_op jit(solution)/shard_map/ppermute | solution.py:30
  139.8 9.3 %collective-permute-start.14 = (bf16[2,192,384]{2,1,0:T(8,128)(2,1)S(1)}, bf16[2,192,384]{2,1,0:T(8,128)(2,1)S(1)}, u32[]{:S(2)}, u32[]{:S(2)}) collective-permute-start(bf16[2,192,384]{2,1,0:T(8,128)(2,1)S(1)} %collective-permute-done.13), channel_id=1, source_target_pairs={{64,0},{128,64},{192,128},{256,192},{320,256},{384,320},{448,384},... | collective-permute-start | bytes 884744 | tf_op jit(solution)/shard_map/ppermute | solution.py:31
  141.7 9.6 %collective-permute-start.8 = (bf16[2,192,384]{2,1,0:T(8,128)(2,1)}, bf16[2,192,384]{2,1,0:T(8,128)(2,1)}, u32[]{:S(2)}, u32[]{:S(2)}) collective-permute-start(bf16[2,192,384]{2,1,0:T(8,128)(2,1)} %collective-permute-done.7), channel_id=1, source_target_pairs={{0,64},{64,128},{128,192},{192,256},{256,320},{320,384},{384,448},... | collective-permute-start | bytes 884744 | tf_op jit(solution)/shard_map/ppermute | solution.py:30
  149.1 9.6 %collective-permute-start.15 = (bf16[2,192,384]{2,1,0:T(8,128)(2,1)S(1)}, bf16[2,192,384]{2,1,0:T(8,128)(2,1)S(1)}, u32[]{:S(2)}, u32[]{:S(2)}) collective-permute-start(bf16[2,192,384]{2,1,0:T(8,128)(2,1)S(1)} %collective-permute-done.14), channel_id=1, source_target_pairs={{64,0},{128,64},{192,128},{256,192},{320,256},{384,320},{448,384},... | collective-permute-start | bytes 884744 | tf_op jit(solution)/shard_map/ppermute | solution.py:31
  158.7 2.1 %copy-start = (bf16[15,2,192,384]{3,2,1,0:T(8,128)(2,1)}, bf16[15,2,192,384]{3,2,1,0:T(8,128)(2,1)S(1)}, u32[]{:S(2)}) copy-start(bf16[15,2,192,384]{3,2,1,0:T(8,128)(2,1)S(1)} %bitcast_dynamic-update-slice_fusion) | copy-start | bytes 13271044
  161.1 11.6 %collective-permute-start.16 = (bf16[8,2,192,384]{3,2,1,0:T(8,128)(2,1)S(1)}, bf16[8,2,192,384]{3,2,1,0:T(8,128)(2,1)}, u32[]{:S(2)}, u32[]{:S(2)}) collective-permute-start(bf16[8,2,192,384]{3,2,1,0:T(8,128)(2,1)S(1)} %constant_dynamic-slice_fusion), channel_id=1, source_target_pairs={{0,32},{32,0},{1,33},{33,1},{2,34},{34,2},{3,35},{35,3},{4,36},{36... | collective-permute-start | bytes 7077896 | tf_op jit(solution)/shard_map/ppermute | solution.py:36
Sparse Core Ops, SparseCore 0:
  83.6 104.1 all-gather.1
